TPU v7x, 128 devices: a whole 4x4x4 slice. The times are simulated.
128 devices in a mesh: req: 16 (over x, y), row: 8 (over z, core).
Axes of the slice: x: 4, y: 4, z: 4, core: 2. Of those that a mesh axis runs over, the one named last changes fastest.
Arguments:
- patches: bfloat16 [8, 2048, 1280], P('row', 'req'), may hold values from -6 to 6
- picture_ids: int32 [8, 2048], P('row'), may hold values from -1 to 15, as said below
- ln_attn: float32 [1280], replicated, may hold values from 0.1 to 1.9
- w_qkv: bfloat16 [3, 1280, 1280], P(None, None, 'req'), may hold values from -6 to 6
- w_out: bfloat16 [1280, 1280], P('req'), may hold values from -1.25 to 1.25
- ln_mlp: float32 [1280], replicated, may hold values from 0.1 to 1.9
- w_up: bfloat16 [1280, 5120], P(None, 'req'), may hold values from -0.15625 to 0.15625
- w_down: bfloat16 [5120, 1280], P('req'), may hold values from -0.3125 to 0.3125
- w_merge: bfloat16 [5120, 1280], replicated, may hold values from -0.078125 to 0.078125
- text_embed: bfloat16 [16384, 1280], P(('req', 'row')), may hold values from -6 to 6
- slot_dest: int32 [8, 512], P('row', 'req'), may hold values from -1 to 16383, as said below
Outputs:
- prompt_embed: bfloat16 [16384, 1280], P(('req', 'row'))
Inputs may be any that keep to these rules, and one draw needn't show every extreme that they name: `picture_ids`: each group holds whole pictures one after another from its first row, each picture's length a multiple of 4 and laid out so that every aligned run of four rows is one 2x2 window; rows after the last picture are padding. `slot_dest`: A merged row has a prompt row exactly when its patch rows belong to a picture; no prompt row is named twice; a merged row of group g (rows of the row index g) names a prompt row of a device with the same row index; at most 2 merged rows of one device name prompt rows of one device, and in every draw some device sends that many to one device.
All inputs are finite; a program needn't handle non-finite values.
Results may differ from a plain program's by a relative error of at most 0.023.
Values may be sent and summed in bfloat16 or wider, within the bound.
No kernel may reach another device: no remote copies, remote signals or barrier semaphores. Data moves between devices by JAX's collectives and lax.ppermute only.
A program may use at most 128 MiB of HBM per device.

v0:
```python
import math

import jax
import jax.numpy as jnp
from jax import lax
from jax.sharding import PartitionSpec as P

HEAD = 80


def layer_norm(rows, gain):
    rows32 = rows.astype(jnp.float32)
    center = rows32 - jnp.mean(rows32, axis=-1, keepdims=True)
    spread = jnp.mean(center * center, axis=-1, keepdims=True)
    return center * lax.rsqrt(spread + 1e-06) * gain


def local(
    patches,
    picture_ids,
    ln_attn,
    w_qkv,
    w_out,
    ln_mlp,
    w_up,
    w_down,
    w_merge,
    text_embed,
    slot_dest,
):
    rows = patches[0]
    local_rows = rows.shape[0]
    width = rows.shape[1]
    ids = picture_ids[0]
    group_rows = ids.shape[0]
    head_cols = w_out.shape[0]
    req_count = lax.axis_size("req")
    row_count = lax.axis_size("row")
    normed = layer_norm(rows, ln_attn).astype(jnp.bfloat16)
    qkv = jnp.einsum(
        "rd,tdc->trc",
        lax.all_gather(normed, "req", axis=0, tiled=True),
        w_qkv,
        preferred_element_type=jnp.float32,
    ).astype(jnp.bfloat16)
    keys = qkv[1]
    values = qkv[2]
    block = min(512, group_rows)
    blocks = group_rows // block
    scale = 1.0 / math.sqrt(HEAD)

    def attend(item):
        query_block, id_block = item
        same = id_block[:, None] == ids[None, :]
        scores = (
            jnp.einsum("qc,kc->qk", query_block, keys, preferred_element_type=jnp.float32) * scale
        )
        scores = jnp.where(same, scores, -1e30)
        top = jnp.max(scores, axis=1, keepdims=True)
        expo = jnp.exp(scores - top)
        probs = (expo / jnp.sum(expo, axis=1, keepdims=True)).astype(jnp.bfloat16)
        results = [jnp.dot(probs, values, preferred_element_type=jnp.float32).astype(jnp.bfloat16)]
        return jnp.concatenate(results, axis=1)

    attended = lax.map(
        attend, (qkv[0].reshape(blocks, block, head_cols), ids.reshape(blocks, block))
    )
    attended = attended.reshape(group_rows, head_cols)
    piece = lax.slice_in_dim(attended, 0, local_rows * lax.axis_size("req"), axis=0)
    attn = lax.psum_scatter(
        jnp.dot(piece, w_out, preferred_element_type=jnp.float32).astype(jnp.bfloat16),
        "req",
        scatter_dimension=0,
        tiled=True,
    ).astype(jnp.float32)
    resid = (rows.astype(jnp.float32) + attn).astype(jnp.bfloat16)
    normed_two = layer_norm(resid, ln_mlp).astype(jnp.bfloat16)
    hidden = jax.nn.gelu(
        jnp.dot(
            lax.all_gather(normed_two, "req", axis=0, tiled=True),
            w_up,
            preferred_element_type=jnp.float32,
        ),
        approximate=False,
    ).astype(jnp.bfloat16)
    piece = lax.slice_in_dim(hidden, 0, local_rows * lax.axis_size("req"), axis=0)
    mlp = lax.psum_scatter(
        jnp.dot(piece, w_down, preferred_element_type=jnp.float32).astype(jnp.bfloat16),
        "req",
        scatter_dimension=0,
        tiled=True,
    ).astype(jnp.float32)
    vision = (resid.astype(jnp.float32) + mlp).astype(jnp.bfloat16)
    merged = vision.reshape(local_rows // 4, 4 * width)
    merged_count = merged.shape[0]
    dest = slot_dest[0]
    prompt_rows = text_embed.shape[0]
    slot_cap = max(2, merged_count // req_count)
    owner = jnp.where(dest >= 0, dest // prompt_rows // row_count, -1)
    order = jnp.arange(merged_count)
    same_owner = (owner[:, None] == owner[None, :]) & (order[None, :] < order[:, None])
    ranks = jnp.sum(same_owner.astype(jnp.int32), axis=1)
    target = jnp.where(owner >= 0, owner * slot_cap + ranks, -1)
    select = target[None, :] == jnp.arange(req_count * slot_cap)[:, None]
    places = jnp.sum(jnp.where(select, (dest % prompt_rows + 1)[None, :], 0), axis=1) - 1
    chooser = select.astype(jnp.bfloat16)
    outgoing = jnp.dot(chooser, merged, preferred_element_type=jnp.float32).astype(jnp.bfloat16)
    arrived, landing = (
        lax.all_to_all(
            outgoing.reshape(req_count, slot_cap, -1),
            "req",
            split_axis=0,
            concat_axis=0,
            tiled=True,
        ),
        lax.all_to_all(
            places.reshape(req_count, slot_cap), "req", split_axis=0, concat_axis=0, tiled=True
        ),
    )
    arrived = arrived.reshape(req_count * slot_cap, -1)
    landing = landing.reshape(-1)
    incoming = jnp.dot(arrived, w_merge, preferred_element_type=jnp.float32).astype(jnp.bfloat16)
    placer = landing[None, :] == jnp.arange(prompt_rows)[:, None]
    placed = jnp.dot(
        placer.astype(jnp.bfloat16), incoming, preferred_element_type=jnp.float32
    ).astype(jnp.bfloat16)
    filled = jnp.any(placer, axis=1)
    return jnp.where(filled[:, None], placed, text_embed)


def solution(mesh):
    return jax.shard_map(
        local,
        mesh=mesh,
        in_specs=(
            P("row", "req", None),
            P("row", None),
            P(),
            P(None, None, "req"),
            P("req", None),
            P(),
            P(None, "req"),
            P("req", None),
            P(),
            P(("req", "row"), None),
            P("row", "req"),
        ),
        out_specs=P(("req", "row"), None),
        check_vma=False,
    )
```

profile of v0, /device:TPU:0, one launch (start us, length us, event | category | flops | bytes accessed | tf_op | source)
XLA Modules:
  0.0 349.8 jit_solution(17088282344082328541)
XLA Ops:
  6.5 0.0 copy-start
  6.5 0.0 all-gather.3.cloned.1.call-start
  6.5 1.2 convert_reduce_fusion.1
  7.7 1.2 fusion.59
  8.9 1.9 fusion.61
  10.9 0.0 all-gather.3.cloned.1.call-update
  10.9 0.0 reduce-scatter.3.cloned.1.call-start
  11.0 0.6 broadcast.226
  11.5 1.4 reduce.7
  12.9 56.8 %all-gather.3.cloned.1.call-done = bf16[2048,1280]{1,0:T(8,128)(2,1)} async-done(((bf16[128,1280]{1,0:T(8,128)(2,1)}), bf16[2048,1280]{1,0:T(8,128)(2,1)}) %all-gather.3.cloned.1.call-update) | async-done | bytes 5242896 | tf_op jit(solution)/shard_map/all_gather | solution.py:42
  69.8 4.2 %fusion.105 = f32[2048,240]{0,1:S(1)} fusion(bf16[2048,1280]{1,0:T(8,128)(2,1)} %all-gather.3.cloned.1.call-done, bf16[1280,240]{0,1:T(8,128)(2,1)} %bitcast.94), kind=kOutput, calls=%fused_computation.160 | convolution fusion | flops 1258291200 | bytes 7823360
  73.9 0.1 convert_bitcast_fusion
  74.1 0.0 copy-start.4
  74.1 0.1 slice_bitcast_fusion
  74.2 0.3 copy.29
  74.4 0.3 copy.26
  74.7 0.3 copy.27
  75.0 0.0 copy-done.4
  75.0 0.0 copy-start.3
  75.0 11.0 %while.10 = (s32[]{:T(128)}, bf16[4,512,80]{1,2,0:T(8,128)(2,1)S(1)}, s32[4,512]{1,0:T(4,128)S(1)}, s32[1,2048]{1,0:T(1,128)S(1)}, bf16[4,512,80]{2,1,0:T(8,128)...) while((s32[]{:T(128)}, bf16[4,512,80]{1,2,0:T(8,128)(2,1)S(1)}, ...), condition=%wide.region_8.9_spmd, body=%wide.region_5.8_spmd.sunk | while | flops 345021440 | bytes 13869153 | solution.py:65
  75.1 0.9 fusion.125
  76.0 0.7 fusion.126
  76.7 1.1 fusion.127
  77.8 0.9 fusion.125
  78.7 0.7 fusion.126
  79.4 1.1 fusion.127
  80.6 0.9 fusion.125
  81.5 0.7 fusion.126
  82.2 1.1 fusion.127
  83.3 0.9 fusion.125
  84.2 0.7 fusion.126
  84.9 1.1 fusion.127
  86.1 3.9 %convolution_convert_fusion.1 = bf16[2048,1280]{1,0:T(8,128)(2,1)} fusion(bf16[2048,80]{0,1:T(8,128)(2,1)S(1)} %bitcast.88, bf16[80,1280]{1,0:T(8,128)(2,1)S(1)} %copy-done.3), kind=kOutput, calls=%fused_computation.13 | convolution fusion | flops 422051840 | bytes 5775360 | tf_op jit(solution)/shard_map/dot_general | solution.py:71
  90.0 0.0 reduce-scatter.3.cloned.1.call-update
  90.0 0.0 all-gather.5.cloned.1.call-start
  90.0 78.7 %reduce-scatter.3.cloned.1.call-done = bf16[128,1280]{1,0:T(8,128)(2,1)} async-done(((bf16[2048,1280]{1,0:T(8,128)(2,1)}), bf16[128,1280]{1,0:T(8,128)(2,1)}) %reduce-scatter.3.cloned.1.call-update) | async-done | bytes 327696 | tf_op jit(solution)/shard_map/reduce_scatter | solution.py:70
  168.8 1.2 convert_reduce_fusion
  170.0 0.2 fusion.56
  170.2 0.0 copy-done.5
  170.2 1.0 fusion.58
  171.2 0.0 all-gather.5.cloned.1.call-update
  171.2 0.2 reduce-scatter.5.cloned.1.call-start
  171.4 55.5 %all-gather.5.cloned.1.call-done = bf16[2048,1280]{1,0:T(8,128)(2,1)} async-done(((bf16[128,1280]{1,0:T(8,128)(2,1)}), bf16[2048,1280]{1,0:T(8,128)(2,1)}) %all-gather.5.cloned.1.call-update) | async-done | bytes 5242896 | tf_op jit(solution)/shard_map/all_gather | solution.py:80
  226.9 0.0 copy-done.6
  226.9 13.4 %convolution_convert_fusion = bf16[2048,1280]{1,0:T(8,128)(2,1)} fusion(bf16[320,1280]{1,0:T(8,128)(2,1)S(1)} %copy-done, bf16[2048,1280]{1,0:T(8,128)(2,1)} %all-gather.5.cloned.1.call-done, bf16[1280,320]{0,1:T(8,128)(2,1)S(1)} %copy-done.6), kind=kOutput, calls=%fused_computation.12 | convolution fusion | flops 3400663040 | bytes 12124160 | tf_op jit(solution)/shard_map/dot_general | solution.py:88
  240.3 0.0 reduce-scatter.5.cloned.1.call-update
  240.3 0.6 copy-done.7
  241.0 0.2 convert_reduce_fusion.2
  241.2 0.1 select_reduce_fusion
  241.3 0.7 sub.48
  242.0 5.3 %all-to-all-start = ((s32[16,1,2]{2,1,0:T(1,128)}), s32[16,1,2]{2,1,0:T(1,128)S(1)}, u32[]{:S(2)}, u32[]{:S(2)}) async-start(s32[16,1,2]{2,1,0:T(1,128)} %bitcast.9), calls=%async_computation | async-start | bytes 16384 | tf_op jit(solution)/shard_map/all_to_all | solution.py:116
  247.3 71.8 %reduce-scatter.5.cloned.1.call-done = bf16[128,1280]{1,0:T(8,128)(2,1)} async-done(((bf16[2048,1280]{1,0:T(8,128)(2,1)}), bf16[128,1280]{1,0:T(8,128)(2,1)}) %reduce-scatter.5.cloned.1.call-update) | async-done | bytes 327696 | tf_op jit(solution)/shard_map/reduce_scatter | solution.py:87
  319.1 1.0 fusion.63
  320.1 0.2 reshape.112
  320.3 0.2 convolution_convert_fusion.2
  320.6 0.8 reshape.113
  321.4 0.0 all-to-all-done
  321.4 4.9 %all-to-all-start.1 = ((bf16[16,2,5120]{2,1,0:T(2,128)(2,1)}), bf16[16,2,5120]{2,1,0:T(2,128)(2,1)S(1)}, u32[]{:S(2)}, u32[]{:S(2)}) async-start(bf16[16,2,5120]{2,1,0:T(2,128)(2,1)} %reshape.113), calls=%async_computation.3 | async-start | bytes 655360 | tf_op jit(solution)/shard_map/all_to_all | solution.py:109
  326.4 0.7 reduce.8
  327.1 0.1 eq.69
  327.1 0.1 fusion.64
  327.2 7.9 %all-to-all-done.1 = bf16[16,2,5120]{2,1,0:T(2,128)(2,1)S(1)} async-done(((bf16[16,2,5120]{2,1,0:T(2,128)(2,1)}), bf16[16,2,5120]{2,1,0:T(2,128)(2,1)S(1)}, u32[]{:S(2)}, u32[]{:S(2)}) %all-to-all-start.1) | async-done | bytes 327712 | tf_op jit(solution)/shard_map/all_to_all | solution.py:109
  335.2 0.1 reshape.114
  335.3 8.0 %fusion.18 = bf16[128,1280]{1,0:T(8,128)(2,1)} fusion(bf16[128,1280]{1,0:T(8,128)(2,1)S(1)} %copy-done.2, bf16[32,5120]{1,0:T(8,128)(2,1)S(1)} %reshape.114, bf16[5120,1280]{1,0:T(8,128)(2,1)} %param.21, pred[128]{0:T(512)(128)(4,1)S(1)} %fusion.64, s32[32]{0:T(128)S(1)} %eq.69), kind=kOutput, calls=%fused_computation.35 | convolution fusion | flops 430288896 | bytes 14090496 | tf_op jit(solution)/shard_map/dot_general | solution.py:124
  (24 shorter events, 0.2 us)
Async XLA Ops:
  6.5 220.4 %copy-start = (bf16[320,1280]{1,0:T(8,128)(2,1)S(1)}, bf16[320,1280]{1,0:T(8,128)(2,1)}, u32[]{:S(2)}) copy-start(bf16[320,1280]{1,0:T(8,128)(2,1)} %param.20) | copy-start | bytes 2457604
  6.5 63.2 %all-gather.3.cloned.1.call-start = ((), (), s32[]{:S(2)}) async-start(), calls=%async_computation.4 | async-start | bytes 5570560 | tf_op jit(solution)/shard_map/all_gather | solution.py:42
  10.9 157.9 %reduce-scatter.3.cloned.1.call-start = ((), (), s32[]{:S(2)}) async-start(), calls=%async_computation.5 | async-start | bytes 5570560 | tf_op jit(solution)/shard_map/reduce_scatter | solution.py:70
  74.1 0.9 copy-start.4
  75.0 11.0 %copy-start.3 = (bf16[80,1280]{1,0:T(8,128)(2,1)S(1)}, bf16[80,1280]{1,0:T(8,128)(2,1)}, u32[]{:S(2)}) copy-start(bf16[80,1280]{1,0:T(8,128)(2,1)} %param.17) | copy-start | bytes 614404
  90.0 78.8 %copy-start.1 = (bf16[1,128,1280]{2,1,0:T(8,128)(2,1)S(1)}, bf16[1,128,1280]{2,1,0:T(8,128)(2,1)}, u32[]{:S(2)}) copy-start(bf16[1,128,1280]{2,1,0:T(8,128)(2,1)} %param.13) | copy-start | bytes 983044
  90.0 80.2 %copy-start.5 = (f32[1280]{0:T(1024)S(1)}, f32[1280]{0:T(1024)}, u32[]{:S(2)}) copy-start(f32[1280]{0:T(1024)} %param.18) | copy-start | bytes 15364
  90.0 137.0 %copy-start.6 = (bf16[1280,320]{0,1:T(8,128)(2,1)S(1)}, bf16[1280,320]{0,1:T(8,128)(2,1)}, u32[]{:S(2)}) copy-start(bf16[1280,320]{0,1:T(8,128)(2,1)} %param.19) | copy-start | bytes 2457604
  90.0 136.9 %all-gather.5.cloned.1.call-start = ((), (), s32[]{:S(2)}) async-start(), calls=%async_computation.6 | async-start | bytes 5570560 | tf_op jit(solution)/shard_map/all_gather | solution.py:80
  171.2 147.9 %reduce-scatter.5.cloned.1.call-start = ((), (), s32[]{:S(2)}) async-start(), calls=%async_computation.7 | async-start | bytes 5570560 | tf_op jit(solution)/shard_map/reduce_scatter | solution.py:87
  240.3 0.7 copy-start.7
  241.0 94.3 %copy-start.2 = (bf16[128,1280]{1,0:T(8,128)(2,1)S(1)}, bf16[128,1280]{1,0:T(8,128)(2,1)}, u32[]{:S(2)}) copy-start(bf16[128,1280]{1,0:T(8,128)(2,1)} %param.22) | copy-start | bytes 983044
  242.0 79.4 %all-to-all-start = ((s32[16,1,2]{2,1,0:T(1,128)}), s32[16,1,2]{2,1,0:T(1,128)S(1)}, u32[]{:S(2)}, u32[]{:S(2)}) async-start(s32[16,1,2]{2,1,0:T(1,128)} %bitcast.9), calls=%async_computation | async-start | bytes 16384 | tf_op jit(solution)/shard_map/all_to_all | solution.py:116
  321.4 13.8 %all-to-all-start.1 = ((bf16[16,2,5120]{2,1,0:T(2,128)(2,1)}), bf16[16,2,5120]{2,1,0:T(2,128)(2,1)S(1)}, u32[]{:S(2)}, u32[]{:S(2)}) async-start(bf16[16,2,5120]{2,1,0:T(2,128)(2,1)} %reshape.113), calls=%async_computation.3 | async-start | bytes 655360 | tf_op jit(solution)/shard_map/all_to_all | solution.py:109
Sparse Core Ops, SparseCore 0:
  11.0 58.7 all-gather.2
  90.1 78.6 reduce-scatter.2
  171.3 55.5 all-gather.4
  240.5 78.5 reduce-scatter.4
where the time goes:
time: 350 us
  waiting for transfers between devices  271 us (77%)
  matrix products  37.6 us (11%)
  between operations  13.3 us (4%)
  other arithmetic  13.2 us (4%)
  starting transfers between devices  10.5 us (3%)
  local copies, waits for them, and re-layouts  4.15 us (1%)
    reduce_scatter x1, waiting for transfers between devices, local(): lax.psum_scatter(jnp.dot(piece, w_out, preferred_element_type=jnp.float32...  78.7 us
    reduce_scatter x1, waiting for transfers between devices, local(): lax.psum_scatter(jnp.dot(piece, w_down, preferred_element_type=jnp.float3...  71.8 us
    all_gather x1, waiting for transfers between devices, local(): lax.all_gather(normed, 'req', axis=0, tiled=True)  56.8 us
    all_gather x1, waiting for transfers between devices, local(): lax.all_gather(normed_two, 'req', axis=0, tiled=True)  55.5 us
    dot_general x1, matrix products, local(): jnp.dot(piece, w_down, preferred_element_type=jnp.float32)  13.4 us
    dot_general x1, matrix products, local(): jnp.dot(placer.astype(jnp.bfloat16), incoming, preferred_element_type=jnp...  7.96 us
    all_to_all x1, waiting for transfers between devices, local(): lax.all_to_all(outgoing.reshape(req_count, slot_cap, -1), 'req', split_ax...  7.94 us
  transfers between devices with their start and end apart: 6, of which 5 were waited for; matrix products, arithmetic and copies ran while one was open for 2% of the time, Pallas kernels for 0%

commit v1 on v0

v1 whole, which is shorter than its diff:
```python
import math

import jax
import jax.numpy as jnp
from jax import lax
from jax.experimental import pallas as pl
from jax.experimental.pallas import tpu as pltpu
from jax.sharding import Mesh
from jax.sharding import PartitionSpec as P

HEAD = 80
N = 4
BF = jnp.bfloat16
F32 = jnp.float32
NT = (((1,), (1,)), ((), ()))
TN = (((0,), (0,)), ((), ()))
VMEM = pl.BlockSpec(memory_space=pltpu.VMEM)
SMEM = pl.BlockSpec(memory_space=pltpu.SMEM)
PARAMS = pltpu.CompilerParams(vmem_limit_bytes=56 << 20)


def norm_rows(rows32, gain):
    center = rows32 - jnp.mean(rows32, axis=-1, keepdims=True)
    spread = jnp.mean(center * center, axis=-1, keepdims=True)
    return center * lax.rsqrt(spread + 1e-06) * gain


def shift(value, axis, step):
    pairs = [(i, (i + step) % N) for i in range(N)]
    return lax.ppermute(value, axis, pairs)


def swap(value):
    return lax.ppermute(value, "c", [(0, 1), (1, 0)])


def qkv_kernel(pos, p0, p1, p2, p3, gain, w0, m1, m2, m3, s1, s2, s3, o0, o1, o2, o3, h1):
    y = pos[1]
    c = pos[3]
    half = h1.shape[2]
    rows = p0.shape[0]
    for k, piece in enumerate((p0, p1, p2, p3)):
        normed = norm_rows(piece[...].astype(F32), gain[...]).astype(BF)
        at = pl.ds(pl.multiple_of(lax.rem(y - k + N, N) * rows, rows), rows)
        h1[0, at, :] = normed[:, :half]
        h1[1, at, :] = normed[:, half:]
    own = lax.dot_general(w0[:, :half], h1[0], NT, preferred_element_type=F32)
    own += lax.dot_general(w0[:, half:], h1[1], NT, preferred_element_type=F32)
    o0[...] = own.astype(BF)
    for mine, other, out in ((m1, s1, o1), (m2, s2, o2), (m3, s3, o3)):
        total = lax.dot_general(mine[...], h1[c], NT, preferred_element_type=F32)
        total += lax.dot_general(other[...], h1[1 - c], NT, preferred_element_type=F32)
        out[...] = total.astype(BF)


def attend_kernel(pos, bounds, r0, r1, r2, r3, id_row, id_col, out, qs, ks, vs, scores):
    x = pos[0]
    chunk = ks.shape[2]
    block = qs.shape[2]
    per = block // chunk
    scale = math.log2(math.e) / math.sqrt(HEAD)
    for k, piece in enumerate((r0, r1, r2, r3)):
        at = lax.rem(x + k, N)
        qs[at] = piece[:HEAD, :]
        for j in range(per):
            cols = slice(j * chunk, (j + 1) * chunk)
            ks[at * per + j] = piece[HEAD : 2 * HEAD, cols]
            vs[at * per + j] = piece[2 * HEAD :, cols]

    for qb in range(N):
        low = bounds[0, qb]
        high = bounds[1, qb]
        query = qs[qb]
        query_ids = id_row[:, qb * block : (qb + 1) * block]

        def score(kc, query=query):
            return lax.dot_general(ks[kc], query, TN, preferred_element_type=F32)

        scores[0] = score(low)

        def step(i, carry, query=query, query_ids=query_ids, low=low, high=high):
            top, total, acc = carry
            slot = lax.rem(i - low, 2)
            raw = scores[slot]
            scores[1 - slot] = score(jnp.minimum(i + 1, high - 1))
            key_ids = id_col[pl.ds(pl.multiple_of(i * chunk, chunk), chunk), :]
            val = jnp.where(key_ids == query_ids, raw * scale, -1e30)
            new_top = jnp.maximum(top, jnp.max(val, axis=0, keepdims=True))
            alpha = jnp.exp2(top - new_top)
            expo = jnp.exp2(val - new_top)
            total = total * alpha + jnp.sum(expo, axis=0, keepdims=True)
            acc = acc * alpha + jnp.dot(vs[i], expo.astype(BF), preferred_element_type=F32)
            return new_top, total, acc

        start = (
            jnp.full((1, block), -1e30, F32),
            jnp.zeros((1, block), F32),
            jnp.zeros((HEAD, block), F32),
        )
        top, total, acc = lax.fori_loop(low, high, step, start)
        out[lax.rem(qb - x + N, N)] = (acc / total).astype(BF)


def mlp_kernel(pos, g0, g1, g2, g3, p0, p1, p2, p3, gain, w_mlp, w_out, part, own, att, resid):
    x = pos[0]
    y = pos[1]
    rows = p0.shape[0]
    for k, piece in enumerate((g0, g1, g2, g3)):
        for j in range(N):
            at = lax.rem(y - k + N, N) * N + lax.rem(x - j + N, N)
            att[at] = piece[j * HEAD : (j + 1) * HEAD, :]
    for k, piece in enumerate((p0, p1, p2, p3)):
        at = pl.ds(pl.multiple_of(lax.rem(y - k + N, N) * rows, rows), rows)
        resid[at, :] = piece[...].astype(F32)
    lhs = att[...].reshape(N * N * HEAD, N * rows)
    attn = lax.dot_general(lhs, w_out[...], TN, preferred_element_type=F32)
    resid[...] = (resid[...] + attn).astype(BF).astype(F32)
    own[...] = resid[pl.ds(pl.multiple_of(y * rows, rows), rows), :].astype(BF)
    normed = norm_rows(resid[...], gain[...]).astype(BF)
    units = 160
    up = jnp.concatenate([w_mlp[i, :units, :] for i in range(2 * N)], axis=0)
    down = jnp.concatenate([w_mlp[i, units : 2 * units, :] for i in range(2 * N)], axis=0)
    hidden = lax.dot_general(normed, up, NT, preferred_element_type=F32)
    hidden = (0.5 * hidden * (1.0 + lax.erf(hidden * math.sqrt(0.5)))).astype(BF)
    result = jnp.dot(hidden, down, preferred_element_type=F32).astype(BF)
    for yb in range(N):
        part[lax.rem(yb - y + N, N)] = result[yb * rows : (yb + 1) * rows, :]


def local(
    patches,
    picture_ids,
    ln_attn,
    w_qkv,
    w_out,
    ln_mlp,
    w_up,
    w_down,
    w_merge,
    text_embed,
    slot_dest,
):
    rows = patches[0]
    count, width = rows.shape
    x = lax.axis_index("x")
    y = lax.axis_index("y")
    c = lax.axis_index("c")
    pos = jnp.stack([x, y, lax.axis_index("z"), c]).astype(jnp.int32)
    ids = picture_ids[0]

    units = w_down.shape[0] // 2
    half_head = HEAD // 2
    packed = jnp.concatenate(
        [
            lax.dynamic_slice_in_dim(w_up.T, c * units, units, 0),
            lax.dynamic_slice_in_dim(w_down, c * units, units, 0),
            lax.dynamic_slice_in_dim(w_out, c * half_head, half_head, 0),
        ],
        axis=0,
    )

    pieces = [rows] + [shift(rows, "y", k) for k in (1, 2, 3)]
    w_heads = jnp.transpose(w_qkv, (0, 2, 1)).reshape(3 * HEAD, width)
    w_half = lax.dynamic_slice_in_dim(w_heads, c * (width // 2), width // 2, 1)
    mine = [shift(w_half, "x", k) for k in (1, 2, 3)]
    other = [swap(m) for m in mine]

    w_near = lax.all_gather(packed, ("x", "c"), axis=0, tiled=False)
    out_heads = w_near[:, 2 * units :, :].reshape(N, HEAD, width)
    out_half = lax.dynamic_slice_in_dim(out_heads, c * 2, 2, 0).reshape(2 * HEAD, width)
    w_out_all = lax.all_gather(out_half, ("y", "c"), axis=0, tiled=True)

    total_rows = count * N
    qkv = pl.pallas_call(
        qkv_kernel,
        out_shape=[jax.ShapeDtypeStruct((3 * HEAD, total_rows), BF)] * N,
        in_specs=[SMEM] + [VMEM] * 12,
        out_specs=[VMEM] * N,
        scratch_shapes=[pltpu.VMEM((2, total_rows, width // 2), BF)],
        compiler_params=PARAMS,
        name="qkv",
    )(pos, *pieces, ln_attn[None, :], w_heads, *mine, *other)
    blocks = [qkv[0]] + [shift(qkv[k], "x", -k) for k in (1, 2, 3)]

    group_rows = ids.shape[0]
    chunk = 256
    chunks = group_rows // chunk
    held = (ids[:, None] == jnp.arange(16)[None, :]).reshape(chunks, chunk, 16)
    held = jnp.any(held, axis=1)
    per = chunks // N
    wanted = jnp.any(held.reshape(N, per, 16), axis=1)
    need = jnp.any(wanted[:, None, :] & held[None, :, :], axis=2)
    where = jnp.arange(chunks)[None, :]
    low = jnp.min(jnp.where(need, where, chunks - 1), axis=1)
    high = jnp.max(jnp.where(need, where + 1, 1), axis=1)
    bounds = jnp.stack([jnp.minimum(low, high - 1), high]).astype(jnp.int32)

    attended = pl.pallas_call(
        attend_kernel,
        out_shape=jax.ShapeDtypeStruct((N, HEAD, total_rows), BF),
        in_specs=[SMEM, SMEM] + [VMEM] * 6,
        out_specs=VMEM,
        scratch_shapes=[
            pltpu.VMEM((N, HEAD, total_rows), BF),
            pltpu.VMEM((chunks, HEAD, chunk), BF),
            pltpu.VMEM((chunks, HEAD, chunk), BF),
            pltpu.VMEM((2, chunk, total_rows), F32),
        ],
        compiler_params=PARAMS,
        name="attend",
    )(pos, bounds, *blocks, ids[None, :], ids[:, None])
    heads = [attended[0]] + [shift(attended[k], "x", k) for k in (1, 2, 3)]
    heads = jnp.concatenate(heads, axis=0)
    gathered = [heads] + [shift(heads, "y", k) for k in (1, 2, 3)]

    part, resid = pl.pallas_call(
        mlp_kernel,
        out_shape=[
            jax.ShapeDtypeStruct((N, count, width), BF),
            jax.ShapeDtypeStruct((count, width), BF),
        ],
        in_specs=[SMEM] + [VMEM] * 11,
        out_specs=[VMEM] * 2,
        scratch_shapes=[
            pltpu.VMEM((N * N, HEAD, total_rows), BF),
            pltpu.VMEM((total_rows, width), F32),
        ],
        compiler_params=PARAMS,
        name="mlp",
    )(pos, *gathered, *pieces, ln_mlp[None, :], w_near, w_out_all)
    sums = part[0].astype(F32)
    for k in (1, 2, 3):
        sums = sums + shift(part[k], "y", k).astype(F32)
    vision = (resid.astype(F32) + sums).astype(BF)

    merged = vision.reshape(count // 4, 4 * width)
    projected = jnp.dot(merged, w_merge, preferred_element_type=F32).astype(BF)
    merged_count = merged.shape[0]
    dest = slot_dest[0]
    prompt_rows = text_embed.shape[0]
    req_count = N * N
    row_count = lax.axis_size("z") * lax.axis_size("c")
    slot_cap = 2
    owner = jnp.where(dest >= 0, dest // prompt_rows // row_count, -1)
    order = jnp.arange(merged_count)
    same_owner = (owner[:, None] == owner[None, :]) & (order[None, :] < order[:, None])
    ranks = jnp.sum(same_owner.astype(jnp.int32), axis=1)
    target = jnp.where(owner >= 0, owner * slot_cap + ranks, -1)
    select = target[None, :] == jnp.arange(req_count * slot_cap)[:, None]
    places = jnp.sum(jnp.where(select, (dest % prompt_rows + 1)[None, :], 0), axis=1)
    lane = jnp.arange(128)[None, :] == 0
    tail = jnp.where(lane, places[:, None], 0).astype(BF)
    outgoing = jnp.dot(select.astype(BF), projected, preferred_element_type=F32).astype(BF)
    outgoing = jnp.concatenate([outgoing, tail], axis=1)
    arrived = lax.all_to_all(
        outgoing.reshape(req_count, slot_cap, width + 128),
        ("x", "y"),
        split_axis=0,
        concat_axis=0,
        tiled=True,
    ).reshape(req_count * slot_cap, width + 128)
    landing = arrived[:, width].astype(jnp.int32) - 1
    placer = landing[None, :] == jnp.arange(prompt_rows)[:, None]
    placed = jnp.dot(
        placer.astype(BF), arrived[:, :width], preferred_element_type=F32
    ).astype(BF)
    filled = jnp.any(placer, axis=1)
    return jnp.where(filled[:, None], placed, text_embed)


def solution(mesh):
    grid = Mesh(mesh.devices.reshape(N, N, -1, 2), ("x", "y", "z", "c"))
    req = ("x", "y")
    row = ("z", "c")
    return jax.shard_map(
        local,
        mesh=grid,
        in_specs=(
            P(row, req, None),
            P(row, None),
            P(),
            P(None, None, req),
            P(req, None),
            P(),
            P(None, req),
            P(req, None),
            P(),
            P(("x", "y", "z", "c"), None),
            P(row, req),
        ),
        out_specs=P(("x", "y", "z", "c"), None),
        check_vma=False,
    )
```

time: 350 us -> 217 us (0.62)
  waiting for transfers between devices: 271 us -> 106 us
  matrix products: 37.6 us -> 8.28 us
  Pallas kernels: 0 us -> 27.5 us
  starting transfers between devices: 10.5 us -> 28.7 us
  blocking collectives: 0 us -> 13 us
  local copies, waits for them, and re-layouts: 4.15 us -> 14.1 us
  other arithmetic: 13.2 us -> 5.33 us
    reduce_scatter x2 -> x0, waiting for transfers between devices: 151 us -> none  [the longest x1 78.7 us: local(): lax.psum_scatter(jnp.dot(piece, w_out, preferred_element_type=jnp.float32...]
    all_gather x2, waiting for transfers between devices: 112 us -> 48 us  [the longest x1 47.9 us: local(): w_near = lax.all_gather(packed, ('x', 'c'), axis=0, tiled=False)]
    ppermute x0 -> x21, waiting for transfers between devices: none -> 57.7 us  [the longest x18 57.7 us: shift(): return lax.ppermute(value, axis, pairs)]
    ppermute x0 -> x21, starting transfers between devices: none -> 28.7 us  [the longest x18 28.1 us: shift(): return lax.ppermute(value, axis, pairs)]
    pallas_call x0 -> x3, Pallas kernels: none -> 27.5 us  [the longest x1 12.1 us: local(): pl.pallas_call(mlp_kernel, out_shape=[jax.ShapeDtypeStruct((N, count, wid...]
    dot_general x12 -> x2, matrix products: 33.4 us -> 8.28 us  [the longest x1 7.19 us: local(): jnp.dot(select.astype(BF), projected, preferred_element_type=F32).astype(BF)]
    all_to_all x0 -> x1, blocking collectives: none -> 13 us  [local(): lax.all_to_all(outgoing.reshape(req_count, slot_cap, width + 128), ('x',...]
    all_to_all x2 -> x0, starting transfers between devices: 10.2 us -> none  [the longest x1 5.26 us: local(): lax.all_to_all(places.reshape(req_count, slot_cap), 'req', split_axis=0,...]
  transfers between devices with their start and end apart: 6 -> 23, of which waited for: 5 -> 12; matrix products, arithmetic and copies ran while one was open for 2% -> 3% of each run, Pallas kernels for 0% -> 7%
where the time goes in v1:
time: 217 us; the launch traced here: 216 us
  waiting for transfers between devices  106 us (49%)
  starting transfers between devices  28.7 us (13%)
  Pallas kernels  27.5 us (13%)
  local copies, waits for them, and re-layouts  14.1 us (6%)
  between operations  13.7 us (6%)
  blocking collectives  13 us (6%)
  matrix products  8.28 us (4%)
  other arithmetic  5.33 us (2%)
    ppermute x18, waiting for transfers between devices, shift(): return lax.ppermute(value, axis, pairs)  57.7 us
    all_gather x1, waiting for transfers between devices, local(): w_near = lax.all_gather(packed, ('x', 'c'), axis=0, tiled=False)  47.9 us
    ppermute x18, starting transfers between devices, shift(): return lax.ppermute(value, axis, pairs)  28.1 us
    all_to_all x1, blocking collectives, local(): lax.all_to_all(outgoing.reshape(req_count, slot_cap, width + 128), ('x',...  13 us
    pallas_call x1, Pallas kernels, local(): pl.pallas_call(mlp_kernel, out_shape=[jax.ShapeDtypeStruct((N, count, wid...  12.1 us
    pallas_call x1, Pallas kernels, local(): pl.pallas_call(attend_kernel, out_shape=jax.ShapeDtypeStruct((N, HEAD, to...  10 us
    dot_general x1, matrix products, local(): jnp.dot(select.astype(BF), projected, preferred_element_type=F32).astype(BF)  7.19 us
    pallas_call x1, Pallas kernels, local(): pl.pallas_call(qkv_kernel, out_shape=[jax.ShapeDtypeStruct((3 * HEAD, tot...  5.4 us
  transfers between devices with their start and end apart: 23, of which 12 were waited for; matrix products, arithmetic and copies ran while one was open for 3% of the time, Pallas kernels for 7%

profile of v1, /device:TPU:0, one launch (start us, length us, event | category | flops | bytes accessed | tf_op | source)
XLA Modules:
  0.0 216.4 jit_solution(12226551172818861513)
XLA Ops:
  6.5 1.1 copy-done
  7.7 1.0 dynamic-slice_bitcast_fusion
  8.8 0.9 constant_dynamic-slice_fusion.1
  9.7 1.1 pad_maximum_fusion
  10.9 47.9 %all-gather.6.cloned.1.call-done = bf16[2880,1280]{1,0:T(8,128)(2,1)} async-done(((bf16[360,1280]{1,0:T(8,128)(2,1)}), bf16[2880,1280]{1,0:T(8,128)(2,1)}) %all-gather.6.cloned.1.call-update) | async-done | bytes 7372816 | tf_op jit(solution)/shard_map/all_gather | solution.py:168
  58.8 1.2 slice.48
  60.0 0.8 constant_dynamic-slice_fusion
  60.9 0.7 collective-permute-start.3
  61.6 1.7 collective-permute-start.4
  63.3 2.2 %collective-permute-start.5 = (bf16[240,640]{1,0:T(8,128)(2,1)S(1)}, bf16[240,640]{1,0:T(8,128)(2,1)S(1)}, u32[]{:S(2)}, u32[]{:S(2)}) collective-permute-start(bf16[240,640]{1,0:T(8,128)(2,1)S(1)} %constant_dynamic-slice_fusion.3), channel_id=1, source_target_pairs={{0,96},{32,0},{64,32},{96,64},{1,97},{33,1},{65,33},{97,65},{2,98}... | collective-permute-start | bytes 921608 | tf_op jit(solution)/shard_map/ppermute | solution.py:30
  65.4 1.5 collective-permute-start
  66.9 2.7 %collective-permute-start.1 = (bf16[128,1280]{1,0:T(8,128)(2,1)S(1)}, bf16[128,1280]{1,0:T(8,128)(2,1)S(1)}, u32[]{:S(2)}, u32[]{:S(2)}) collective-permute-start(bf16[128,1280]{1,0:T(8,128)(2,1)S(1)} %bitcast.66), channel_id=1, source_target_pairs={{0,16},{8,24},{16,0},{24,8},{1,17},{9,25},{17,1},{25,9},{2,18},{10... | collective-permute-start | bytes 983048 | tf_op jit(solution)/shard_map/ppermute | solution.py:30
  69.6 0.6 broadcast_in_dim.91.gain
  70.2 0.5 broadcast.195
  70.8 0.7 reduce.5
  71.4 0.2 fusion.5
  71.7 0.2 and_reduce_fusion
  71.9 0.2 select_reduce_fusion.2
  72.1 6.1 %collective-permute-done.3.m1 = bf16[240,640]{1,0:T(8,128)(2,1)S(1)} collective-permute-done((bf16[240,640]{1,0:T(8,128)(2,1)S(1)}, bf16[240,640]{1,0:T(8,128)(2,1)S(1)}, u32[]{:S(2)}, u32[]{:S(2)}) %collective-permute-start.3) | collective-permute-done | bytes 307232 | tf_op jit(solution)/shard_map/ppermute | solution.py:30
  78.2 2.7 %collective-permute-start.2 = (bf16[128,1280]{1,0:T(8,128)(2,1)S(1)}, bf16[128,1280]{1,0:T(8,128)(2,1)S(1)}, u32[]{:S(2)}, u32[]{:S(2)}) collective-permute-start(bf16[128,1280]{1,0:T(8,128)(2,1)S(1)} %bitcast.67), channel_id=1, source_target_pairs={{0,24},{8,0},{16,8},{24,16},{1,25},{9,1},{17,9},{25,17},{2,26},{10... | collective-permute-start | bytes 983048 | tf_op jit(solution)/shard_map/ppermute | solution.py:30
  80.9 0.5 collective-permute-start.7
  81.5 0.7 pad_add_fusion.1.pos
  82.2 11.7 %collective-permute-done.1.p2 = bf16[128,1280]{1,0:T(8,128)(2,1)S(1)} collective-permute-done((bf16[128,1280]{1,0:T(8,128)(2,1)S(1)}, bf16[128,1280]{1,0:T(8,128)(2,1)S(1)}, u32[]{:S(2)}, u32[]{:S(2)}) %collective-permute-start.1) | collective-permute-done | bytes 327712 | tf_op jit(solution)/shard_map/ppermute | solution.py:30
  93.9 1.5 collective-permute-done.2.p3
  95.5 0.7 copy-done.6
  96.2 0.1 copy-done.15
  96.3 0.1 copy-done.16
  96.4 0.7 copy-done.17
  97.1 5.4 %qkv.1 = (bf16[240,512]{1,0:T(8,128)(2,1)}, bf16[240,512]{1,0:T(8,128)(2,1)}, bf16[240,512]{1,0:T(8,128)(2,1)}, bf16[240,512]{1,0:T(8,128)(2,1)}) custom-call(s32[4]{0:T(128)} %pad_add_fusion.1.pos, bf16[128,1280]{1,0:T(8,128)(2,1)} %bitcast.63, bf16[128,1280]{1,0:T(8,128)(2,1)} %copy-done.4, bf16[128,1280]{1,0:T(8,128)(2,1)} %copy-done.5, ...), custom_call_target="tpu_custom_call" | custom-call | tf_op jit(solution)/shard_map/qkv/pallas_call | solution.py:174
  102.6 3.2 %collective-permute-start.9 = (bf16[240,512]{1,0:T(8,128)(2,1)}, bf16[240,512]{1,0:T(8,128)(2,1)S(1)}, u32[]{:S(2)}, u32[]{:S(2)}) collective-permute-start(bf16[240,512]{1,0:T(8,128)(2,1)} %get-tuple-element.12), channel_id=1, source_target_pairs={{0,96},{32,0},{64,32},{96,64},{1,97},{33,1},{65,33},{97,65},{2,98}... | collective-permute-start | bytes 737288 | tf_op jit(solution)/shard_map/ppermute | solution.py:30
  105.9 0.5 pad_add_fusion.bounds
  106.4 1.3 copy.15.id_col
  107.7 0.6 broadcast_in_dim.92.gain
  108.4 4.8 %collective-permute-done.10.r2 = bf16[240,512]{1,0:T(8,128)(2,1)S(1)} collective-permute-done((bf16[240,512]{1,0:T(8,128)(2,1)}, bf16[240,512]{1,0:T(8,128)(2,1)S(1)}, u32[]{:S(2)}, u32[]{:S(2)}) %collective-permute-start.10) | collective-permute-done | bytes 245792 | tf_op jit(solution)/shard_map/ppermute | solution.py:30
  113.2 2.9 %collective-permute-done.11.r3 = bf16[240,512]{1,0:T(8,128)(2,1)S(1)} collective-permute-done((bf16[240,512]{1,0:T(8,128)(2,1)}, bf16[240,512]{1,0:T(8,128)(2,1)S(1)}, u32[]{:S(2)}, u32[]{:S(2)}) %collective-permute-start.11) | collective-permute-done | bytes 245792 | tf_op jit(solution)/shard_map/ppermute | solution.py:30
  116.0 0.7 copy-done.19
  116.8 10.0 %attend.1 = bf16[4,80,512]{2,1,0:T(8,128)(2,1)} custom-call(s32[4]{0:T(128)} %pad_add_fusion.1.pos, s32[2,4]{1,0:T(2,128)} %pad_add_fusion.bounds, bf16[240,512]{1,0:T(8,128)(2,1)} %get-tuple-element.11.r0, bf16[240,512]{1,0:T(8,128)(2,1)} %copy-done.20, bf16[240,512]{1,0:T(8,128)(2,1)} %copy-done.18, bf16[240,512]{1,0:T(8,128)(2,1)} %copy-done.19, ...), custom_call_target="tpu_custom_call" | custom-call | tf_op jit(solution)/shard_map/attend/pallas_call | solution.py:198
  126.8 1.0 slice_bitcast_fusion.6
  127.9 2.3 %collective-permute-start.13 = (bf16[80,512]{1,0:T(8,128)(2,1)S(1)}, bf16[80,512]{1,0:T(8,128)(2,1)S(1)}, u32[]{:S(2)}, u32[]{:S(2)}) collective-permute-start(bf16[80,512]{1,0:T(8,128)(2,1)S(1)} %get-tuple-element.24), channel_id=1, source_target_pairs={{0,64},{32,96},{64,0},{96,32},{1,65},{33,97},{65,1},{97,33},{2,66}... | collective-permute-start | bytes 245768 | tf_op jit(solution)/shard_map/ppermute | solution.py:30
  130.2 1.0 collective-permute-start.14
  131.1 0.2 convert_reduce_fusion
  131.3 3.7 %collective-permute-done.12 = bf16[80,512]{1,0:T(8,128)(2,1)S(1)} collective-permute-done((bf16[80,512]{1,0:T(8,128)(2,1)S(1)}, bf16[80,512]{1,0:T(8,128)(2,1)S(1)}, u32[]{:S(2)}, u32[]{:S(2)}) %collective-permute-start.12) | collective-permute-done | bytes 81952 | tf_op jit(solution)/shard_map/ppermute | solution.py:30
  135.0 0.6 collective-permute-done.14
  135.6 2.0 collective-permute-start.15
  137.6 3.3 %collective-permute-start.16 = (bf16[320,512]{1,0:T(8,128)(2,1)S(1)}, bf16[320,512]{1,0:T(8,128)(2,1)S(1)}, u32[]{:S(2)}, u32[]{:S(2)}) collective-permute-start(bf16[320,512]{1,0:T(8,128)(2,1)S(1)} %pad_maximum_fusion.1.g0), channel_id=1, source_target_pairs={{0,16},{8,24},{16,0},{24,8},{1,17},{9,25},{17,1},{25,9},{2,18},{10... | collective-permute-start | bytes 983048 | tf_op jit(solution)/shard_map/ppermute | solution.py:30
  140.9 0.4 collective-permute-start.17
  141.4 0.1 select_reduce_fusion
  141.5 5.7 %collective-permute-done.15.g1 = bf16[320,512]{1,0:T(8,128)(2,1)S(1)} collective-permute-done((bf16[320,512]{1,0:T(8,128)(2,1)S(1)}, bf16[320,512]{1,0:T(8,128)(2,1)S(1)}, u32[]{:S(2)}, u32[]{:S(2)}) %collective-permute-start.15) | collective-permute-done | bytes 327712 | tf_op jit(solution)/shard_map/ppermute | solution.py:30
  147.2 6.9 %collective-permute-done.16.g2 = bf16[320,512]{1,0:T(8,128)(2,1)S(1)} collective-permute-done((bf16[320,512]{1,0:T(8,128)(2,1)S(1)}, bf16[320,512]{1,0:T(8,128)(2,1)S(1)}, u32[]{:S(2)}, u32[]{:S(2)}) %collective-permute-start.16) | collective-permute-done | bytes 327712 | tf_op jit(solution)/shard_map/ppermute | solution.py:30
  154.2 0.7 copy-done.8
  154.8 0.1 copy-done.9
  155.0 12.1 %mlp.1 = (bf16[4,128,1280]{2,1,0:T(8,128)(2,1)}, bf16[128,1280]{1,0:T(8,128)(2,1)}) custom-call(s32[4]{0:T(128)} %pad_add_fusion.1.pos, bf16[320,512]{1,0:T(8,128)(2,1)} %copy-done.2, bf16[320,512]{1,0:T(8,128)(2,1)} %copy-done.7, bf16[320,512]{1,0:T(8,128)(2,1)} %copy-done.8, bf16[320,512]{1,0:T(8,128)(2,1)} %copy-done.9, bf16[128,1280]{1,0:T(8,128)(2,1)} %bitcast.64, ...), custom_call_target="tpu_custom_call" | custom-call | tf_op jit(solution)/shard_map/mlp/pallas_call | solution.py:216
  167.1 1.3 slice_bitcast_fusion.2
  168.3 0.9 collective-permute-start.18
  169.3 2.6 %collective-permute-start.19 = (bf16[128,1280]{1,0:T(8,128)(2,1)S(1)}, bf16[128,1280]{1,0:T(8,128)(2,1)S(1)}, u32[]{:S(2)}, u32[]{:S(2)}) collective-permute-start(bf16[128,1280]{1,0:T(8,128)(2,1)S(1)} %get-tuple-element.21), channel_id=1, source_target_pairs={{0,16},{8,24},{16,0},{24,8},{1,17},{9,25},{17,1},{25,9},{2,18},{10... | collective-permute-start | bytes 983048 | tf_op jit(solution)/shard_map/ppermute | solution.py:30
  171.9 0.7 collective-permute-start.20
  172.6 5.7 %collective-permute-done.18 = bf16[128,1280]{1,0:T(8,128)(2,1)S(1)} collective-permute-done((bf16[128,1280]{1,0:T(8,128)(2,1)S(1)}, bf16[128,1280]{1,0:T(8,128)(2,1)S(1)}, u32[]{:S(2)}, u32[]{:S(2)}) %collective-permute-start.18) | collective-permute-done | bytes 327712 | tf_op jit(solution)/shard_map/ppermute | solution.py:30
  178.3 8.2 %collective-permute-done.19 = bf16[128,1280]{1,0:T(8,128)(2,1)S(1)} collective-permute-done((bf16[128,1280]{1,0:T(8,128)(2,1)S(1)}, bf16[128,1280]{1,0:T(8,128)(2,1)S(1)}, u32[]{:S(2)}, u32[]{:S(2)}) %collective-permute-start.19) | collective-permute-done | bytes 327712 | tf_op jit(solution)/shard_map/ppermute | solution.py:30
  186.5 1.2 fusion.4
  187.7 0.2 reshape.123
  187.9 7.2 %convolution_convert_fusion.1 = bf16[32,1280]{1,0:T(8,128)(2,1)S(1)} fusion(bf16[32,5120]{1,0:T(8,128)(2,1)S(1)} %reshape.123, bf16[5120,1280]{1,0:T(8,128)(2,1)} %param.19, s32[32]{0:T(128)S(1)} %fusion.11), kind=kOutput, calls=%fused_computation.2 | convolution fusion | flops 422134784 | bytes 13516928 | tf_op jit(solution)/shard_map/dot_general | solution.py:253
  195.2 13.0 %all_to_all.5 = bf16[16,2,1408]{2,1,0:T(2,128)(2,1)S(1)} all-to-all(bf16[16,2,1408]{2,1,0:T(2,128)(2,1)S(1)} %reshape.124), channel_id=1, replica_groups=mesh['x'=4,'y'=4,'z'=4,'c'=2] {'x','y'}, dimensions={0} | all-to-all | bytes 180224 | tf_op jit(solution)/shard_map/all_to_all | solution.py:255
  208.2 0.1 add_reduce_fusion
  208.5 1.1 fusion
  (79 shorter events, 1.0 us)
Async XLA Ops:
  6.5 1.1 copy-start
  6.5 52.3 %all-gather.6.cloned.1.call-start = ((), (), s32[]{:S(2)}) async-start(), calls=%async_computation.2 | async-start | bytes 8294400 | tf_op jit(solution)/shard_map/all_gather | solution.py:168
  10.7 50.1 %copy-start.1 = (bf16[3,1280,80]{1,2,0:T(8,128)(2,1)S(1)}, bf16[3,1280,80]{1,2,0:T(8,128)(2,1)}, u32[]{:S(2)}) copy-start(bf16[3,1280,80]{1,2,0:T(8,128)(2,1)} %param.14) | copy-start | bytes 1843204
  10.8 54.7 %copy-start.3 = (bf16[1,128,1280]{2,1,0:T(8,128)(2,1)S(1)}, bf16[1,128,1280]{2,1,0:T(8,128)(2,1)}, u32[]{:S(2)}) copy-start(bf16[1,128,1280]{2,1,0:T(8,128)(2,1)} %param.11) | copy-start | bytes 983044
  10.8 58.9 %copy-start.22 = (f32[1280]{0:T(1024)S(1)}, f32[1280]{0:T(1024)}, u32[]{:S(2)}) copy-start(f32[1280]{0:T(1024)} %param.13) | copy-start | bytes 15364
  10.8 60.0 %copy-start.21 = (s32[1,2048]{1,0:T(1,128)S(1)}, s32[1,2048]{1,0:T(1,128)}, u32[]{:S(2)}) copy-start(s32[1,2048]{1,0:T(1,128)} %id_row.1) | copy-start | bytes 24580
  10.8 61.2 %copy-start.24 = (s32[1,32]{1,0:T(1,128)S(1)}, s32[1,32]{1,0:T(1,128)}, u32[]{:S(2)}) copy-start(s32[1,32]{1,0:T(1,128)} %param.21) | copy-start | bytes 388
  10.8 143.3 %all-gather.4.cloned.1.call-start = ((), (), s32[]{:S(2)}) async-start(), calls=%async_computation.1 | async-start | bytes 3686400 | tf_op jit(solution)/shard_map/all_gather | solution.py:171
  60.9 17.3 %collective-permute-start.3 = (bf16[240,640]{1,0:T(8,128)(2,1)S(1)}, bf16[240,640]{1,0:T(8,128)(2,1)S(1)}, u32[]{:S(2)}, u32[]{:S(2)}) collective-permute-start(bf16[240,640]{1,0:T(8,128)(2,1)S(1)} %constant_dynamic-slice_fusion.3), channel_id=1, source_target_pairs={{0,32},{32,64},{64,96},{96,0},{1,33},{33,65},{65,97},{97,1},{2,34}... | collective-permute-start | bytes 921608 | tf_op jit(solution)/shard_map/ppermute | solution.py:30
  61.6 19.3 %collective-permute-start.4 = (bf16[240,640]{1,0:T(8,128)(2,1)S(1)}, bf16[240,640]{1,0:T(8,128)(2,1)S(1)}, u32[]{:S(2)}, u32[]{:S(2)}) collective-permute-start(bf16[240,640]{1,0:T(8,128)(2,1)S(1)} %constant_dynamic-slice_fusion.3), channel_id=1, source_target_pairs={{0,64},{32,96},{64,0},{96,32},{1,65},{33,97},{65,1},{97,33},{2,66}... | collective-permute-start | bytes 921608 | tf_op jit(solution)/shard_map/ppermute | solution.py:30
  63.3 17.7 %collective-permute-start.5 = (bf16[240,640]{1,0:T(8,128)(2,1)S(1)}, bf16[240,640]{1,0:T(8,128)(2,1)S(1)}, u32[]{:S(2)}, u32[]{:S(2)}) collective-permute-start(bf16[240,640]{1,0:T(8,128)(2,1)S(1)} %constant_dynamic-slice_fusion.3), channel_id=1, source_target_pairs={{0,96},{32,0},{64,32},{96,64},{1,97},{33,1},{65,33},{97,65},{2,98}... | collective-permute-start | bytes 921608 | tf_op jit(solution)/shard_map/ppermute | solution.py:30
  65.4 16.0 %collective-permute-start = (bf16[128,1280]{1,0:T(8,128)(2,1)S(1)}, bf16[128,1280]{1,0:T(8,128)(2,1)S(1)}, u32[]{:S(2)}, u32[]{:S(2)}) collective-permute-start(bf16[128,1280]{1,0:T(8,128)(2,1)S(1)} %bitcast.65), channel_id=1, source_target_pairs={{0,8},{8,16},{16,24},{24,0},{1,9},{9,17},{17,25},{25,1},{2,10},{10... | collective-permute-start | bytes 983048 | tf_op jit(solution)/shard_map/ppermute | solution.py:30
  66.9 27.0 %collective-permute-start.1 = (bf16[128,1280]{1,0:T(8,128)(2,1)S(1)}, bf16[128,1280]{1,0:T(8,128)(2,1)S(1)}, u32[]{:S(2)}, u32[]{:S(2)}) collective-permute-start(bf16[128,1280]{1,0:T(8,128)(2,1)S(1)} %bitcast.66), channel_id=1, source_target_pairs={{0,16},{8,24},{16,0},{24,8},{1,17},{9,25},{17,1},{25,9},{2,18},{10... | collective-permute-start | bytes 983048 | tf_op jit(solution)/shard_map/ppermute | solution.py:30
  78.2 17.3 %copy-start.12 = (bf16[240,640]{1,0:T(8,128)(2,1)}, bf16[240,640]{1,0:T(8,128)(2,1)S(1)}, u32[]{:S(2)}) copy-start(bf16[240,640]{1,0:T(8,128)(2,1)S(1)} %collective-permute-done.3.m1) | copy-start | bytes 921604
  78.2 17.2 %collective-permute-start.2 = (bf16[128,1280]{1,0:T(8,128)(2,1)S(1)}, bf16[128,1280]{1,0:T(8,128)(2,1)S(1)}, u32[]{:S(2)}, u32[]{:S(2)}) collective-permute-start(bf16[128,1280]{1,0:T(8,128)(2,1)S(1)} %bitcast.67), channel_id=1, source_target_pairs={{0,24},{8,0},{16,8},{24,16},{1,25},{9,1},{17,9},{25,17},{2,26},{10... | collective-permute-start | bytes 983048 | tf_op jit(solution)/shard_map/ppermute | solution.py:30
  80.9 14.5 %copy-start.13 = (bf16[240,640]{1,0:T(8,128)(2,1)}, bf16[240,640]{1,0:T(8,128)(2,1)S(1)}, u32[]{:S(2)}) copy-start(bf16[240,640]{1,0:T(8,128)(2,1)S(1)} %collective-permute-done.4.m2) | copy-start | bytes 921604
  80.9 14.5 %collective-permute-start.6 = (bf16[240,640]{1,0:T(8,128)(2,1)S(1)}, bf16[240,640]{1,0:T(8,128)(2,1)S(1)}, u32[]{:S(2)}, u32[]{:S(2)}) collective-permute-start(bf16[240,640]{1,0:T(8,128)(2,1)S(1)} %collective-permute-done.3.m1), channel_id=1, source_target_pairs={{0,1},{1,0},{2,3},{3,2},{4,5},{5,4},{6,7},{7,6},{8,9},{9,8},{10,11... | collective-permute-start | bytes 921608 | tf_op jit(solution)/shard_map/ppermute | solution.py:34
  80.9 14.5 %copy-start.14 = (bf16[240,640]{1,0:T(8,128)(2,1)}, bf16[240,640]{1,0:T(8,128)(2,1)S(1)}, u32[]{:S(2)}) copy-start(bf16[240,640]{1,0:T(8,128)(2,1)S(1)} %collective-permute-done.5.m3) | copy-start | bytes 921604
  80.9 14.5 %collective-permute-start.7 = (bf16[240,640]{1,0:T(8,128)(2,1)S(1)}, bf16[240,640]{1,0:T(8,128)(2,1)S(1)}, u32[]{:S(2)}, u32[]{:S(2)}) collective-permute-start(bf16[240,640]{1,0:T(8,128)(2,1)S(1)} %collective-permute-done.4.m2), channel_id=1, source_target_pairs={{0,1},{1,0},{2,3},{3,2},{4,5},{5,4},{6,7},{7,6},{8,9},{9,8},{10,11... | collective-permute-start | bytes 921608 | tf_op jit(solution)/shard_map/ppermute | solution.py:34
  81.4 14.0 %copy-start.4 = (bf16[128,1280]{1,0:T(8,128)(2,1)}, bf16[128,1280]{1,0:T(8,128)(2,1)S(1)}, u32[]{:S(2)}) copy-start(bf16[128,1280]{1,0:T(8,128)(2,1)S(1)} %collective-permute-done.p1) | copy-start | bytes 983044
  81.4 14.0 %collective-permute-start.8 = (bf16[240,640]{1,0:T(8,128)(2,1)S(1)}, bf16[240,640]{1,0:T(8,128)(2,1)S(1)}, u32[]{:S(2)}, u32[]{:S(2)}) collective-permute-start(bf16[240,640]{1,0:T(8,128)(2,1)S(1)} %collective-permute-done.5.m3), channel_id=1, source_target_pairs={{0,1},{1,0},{2,3},{3,2},{4,5},{5,4},{6,7},{7,6},{8,9},{9,8},{10,11... | collective-permute-start | bytes 921608 | tf_op jit(solution)/shard_map/ppermute | solution.py:34
  82.2 25.5 %copy-start.23 = (f32[1280]{0:T(1024)S(1)}, f32[1280]{0:T(1024)}, u32[]{:S(2)}) copy-start(f32[1280]{0:T(1024)} %param.16) | copy-start | bytes 15364
  93.9 1.6 copy-start.5
  95.4 0.8 copy-start.6
  95.4 0.9 copy-start.15
  95.4 1.0 copy-start.16
  96.4 0.7 copy-start.17
  102.5 10.6 %collective-permute-start.10 = (bf16[240,512]{1,0:T(8,128)(2,1)}, bf16[240,512]{1,0:T(8,128)(2,1)S(1)}, u32[]{:S(2)}, u32[]{:S(2)}) collective-permute-start(bf16[240,512]{1,0:T(8,128)(2,1)} %get-tuple-element.13), channel_id=1, source_target_pairs={{0,64},{32,96},{64,0},{96,32},{1,65},{33,97},{65,1},{97,33},{2,66}... | collective-permute-start | bytes 737288 | tf_op jit(solution)/shard_map/ppermute | solution.py:30
  102.5 13.5 %collective-permute-start.11 = (bf16[240,512]{1,0:T(8,128)(2,1)}, bf16[240,512]{1,0:T(8,128)(2,1)S(1)}, u32[]{:S(2)}, u32[]{:S(2)}) collective-permute-start(bf16[240,512]{1,0:T(8,128)(2,1)} %get-tuple-element.14), channel_id=1, source_target_pairs={{0,32},{32,64},{64,96},{96,0},{1,33},{33,65},{65,97},{97,1},{2,34}... | collective-permute-start | bytes 737288 | tf_op jit(solution)/shard_map/ppermute | solution.py:30
  102.6 13.4 %collective-permute-start.9 = (bf16[240,512]{1,0:T(8,128)(2,1)}, bf16[240,512]{1,0:T(8,128)(2,1)S(1)}, u32[]{:S(2)}, u32[]{:S(2)}) collective-permute-start(bf16[240,512]{1,0:T(8,128)(2,1)} %get-tuple-element.12), channel_id=1, source_target_pairs={{0,96},{32,0},{64,32},{96,64},{1,97},{33,1},{65,33},{97,65},{2,98}... | collective-permute-start | bytes 737288 | tf_op jit(solution)/shard_map/ppermute | solution.py:30
  113.2 2.9 %copy-start.18 = (bf16[240,512]{1,0:T(8,128)(2,1)}, bf16[240,512]{1,0:T(8,128)(2,1)S(1)}, u32[]{:S(2)}) copy-start(bf16[240,512]{1,0:T(8,128)(2,1)S(1)} %collective-permute-done.10.r2) | copy-start | bytes 737284
  116.0 0.7 copy-start.19
  116.0 0.8 copy-start.20
  127.8 7.2 %collective-permute-start.12 = (bf16[80,512]{1,0:T(8,128)(2,1)S(1)}, bf16[80,512]{1,0:T(8,128)(2,1)S(1)}, u32[]{:S(2)}, u32[]{:S(2)}) collective-permute-start(bf16[80,512]{1,0:T(8,128)(2,1)S(1)} %get-tuple-element.25), channel_id=1, source_target_pairs={{0,32},{32,64},{64,96},{96,0},{1,33},{33,65},{65,97},{97,1},{2,34}... | collective-permute-start | bytes 245768 | tf_op jit(solution)/shard_map/ppermute | solution.py:30
  127.9 7.1 %collective-permute-start.13 = (bf16[80,512]{1,0:T(8,128)(2,1)S(1)}, bf16[80,512]{1,0:T(8,128)(2,1)S(1)}, u32[]{:S(2)}, u32[]{:S(2)}) collective-permute-start(bf16[80,512]{1,0:T(8,128)(2,1)S(1)} %get-tuple-element.24), channel_id=1, source_target_pairs={{0,64},{32,96},{64,0},{96,32},{1,65},{33,97},{65,1},{97,33},{2,66}... | collective-permute-start | bytes 245768 | tf_op jit(solution)/shard_map/ppermute | solution.py:30
  130.2 5.4 %collective-permute-start.14 = (bf16[80,512]{1,0:T(8,128)(2,1)S(1)}, bf16[80,512]{1,0:T(8,128)(2,1)S(1)}, u32[]{:S(2)}, u32[]{:S(2)}) collective-permute-start(bf16[80,512]{1,0:T(8,128)(2,1)S(1)} %get-tuple-element.23), channel_id=1, source_target_pairs={{0,96},{32,0},{64,32},{96,64},{1,97},{33,1},{65,33},{97,65},{2,98}... | collective-permute-start | bytes 245768 | tf_op jit(solution)/shard_map/ppermute | solution.py:30
  135.6 18.5 %copy-start.2 = (bf16[320,512]{1,0:T(8,128)(2,1)}, bf16[320,512]{1,0:T(8,128)(2,1)S(1)}, u32[]{:S(2)}) copy-start(bf16[320,512]{1,0:T(8,128)(2,1)S(1)} %pad_maximum_fusion.1.g0) | copy-start | bytes 983044
  135.6 11.6 %collective-permute-start.15 = (bf16[320,512]{1,0:T(8,128)(2,1)S(1)}, bf16[320,512]{1,0:T(8,128)(2,1)S(1)}, u32[]{:S(2)}, u32[]{:S(2)}) collective-permute-start(bf16[320,512]{1,0:T(8,128)(2,1)S(1)} %pad_maximum_fusion.1.g0), channel_id=1, source_target_pairs={{0,8},{8,16},{16,24},{24,0},{1,9},{9,17},{17,25},{25,1},{2,10},{10... | collective-permute-start | bytes 983048 | tf_op jit(solution)/shard_map/ppermute | solution.py:30
  137.6 16.5 %collective-permute-start.16 = (bf16[320,512]{1,0:T(8,128)(2,1)S(1)}, bf16[320,512]{1,0:T(8,128)(2,1)S(1)}, u32[]{:S(2)}, u32[]{:S(2)}) collective-permute-start(bf16[320,512]{1,0:T(8,128)(2,1)S(1)} %pad_maximum_fusion.1.g0), channel_id=1, source_target_pairs={{0,16},{8,24},{16,0},{24,8},{1,17},{9,25},{17,1},{25,9},{2,18},{10... | collective-permute-start | bytes 983048 | tf_op jit(solution)/shard_map/ppermute | solution.py:30
  140.9 13.2 %collective-permute-start.17 = (bf16[320,512]{1,0:T(8,128)(2,1)S(1)}, bf16[320,512]{1,0:T(8,128)(2,1)S(1)}, u32[]{:S(2)}, u32[]{:S(2)}) collective-permute-start(bf16[320,512]{1,0:T(8,128)(2,1)S(1)} %pad_maximum_fusion.1.g0), channel_id=1, source_target_pairs={{0,24},{8,0},{16,8},{24,16},{1,25},{9,1},{17,9},{25,17},{2,26},{10... | collective-permute-start | bytes 983048 | tf_op jit(solution)/shard_map/ppermute | solution.py:30
  147.2 7.0 %copy-start.7 = (bf16[320,512]{1,0:T(8,128)(2,1)}, bf16[320,512]{1,0:T(8,128)(2,1)S(1)}, u32[]{:S(2)}) copy-start(bf16[320,512]{1,0:T(8,128)(2,1)S(1)} %collective-permute-done.15.g1) | copy-start | bytes 983044
  154.1 0.7 copy-start.8
  154.1 0.9 copy-start.9
  167.1 19.5 %copy-start.11 = (bf16[128,1280]{1,0:T(8,128)(2,1)S(1)}, bf16[128,1280]{1,0:T(8,128)(2,1)}, u32[]{:S(2)}) copy-start(bf16[128,1280]{1,0:T(8,128)(2,1)} %get-tuple-element.15) | copy-start | bytes 983044
  168.3 10.0 %collective-permute-start.18 = (bf16[128,1280]{1,0:T(8,128)(2,1)S(1)}, bf16[128,1280]{1,0:T(8,128)(2,1)S(1)}, u32[]{:S(2)}, u32[]{:S(2)}) collective-permute-start(bf16[128,1280]{1,0:T(8,128)(2,1)S(1)} %get-tuple-element.19), channel_id=1, source_target_pairs={{0,8},{8,16},{16,24},{24,0},{1,9},{9,17},{17,25},{25,1},{2,10},{10... | collective-permute-start | bytes 983048 | tf_op jit(solution)/shard_map/ppermute | solution.py:30
  169.3 17.2 %collective-permute-start.19 = (bf16[128,1280]{1,0:T(8,128)(2,1)S(1)}, bf16[128,1280]{1,0:T(8,128)(2,1)S(1)}, u32[]{:S(2)}, u32[]{:S(2)}) collective-permute-start(bf16[128,1280]{1,0:T(8,128)(2,1)S(1)} %get-tuple-element.21), channel_id=1, source_target_pairs={{0,16},{8,24},{16,0},{24,8},{1,17},{9,25},{17,1},{25,9},{2,18},{10... | collective-permute-start | bytes 983048 | tf_op jit(solution)/shard_map/ppermute | solution.py:30
  171.9 14.6 %collective-permute-start.20 = (bf16[128,1280]{1,0:T(8,128)(2,1)S(1)}, bf16[128,1280]{1,0:T(8,128)(2,1)S(1)}, u32[]{:S(2)}, u32[]{:S(2)}) collective-permute-start(bf16[128,1280]{1,0:T(8,128)(2,1)S(1)} %get-tuple-element.20), channel_id=1, source_target_pairs={{0,24},{8,0},{16,8},{24,16},{1,25},{9,1},{17,9},{25,17},{2,26},{10... | collective-permute-start | bytes 983048 | tf_op jit(solution)/shard_map/ppermute | solution.py:30
  187.9 20.5 %copy-start.10 = (bf16[128,1280]{1,0:T(8,128)(2,1)S(1)}, bf16[128,1280]{1,0:T(8,128)(2,1)}, u32[]{:S(2)}) copy-start(bf16[128,1280]{1,0:T(8,128)(2,1)} %param.20) | copy-start | bytes 983044
Sparse Core Ops, SparseCore 0:
  10.9 47.8 all-gather.5
  60.9 37.0 all-gather.3

commit v2 on v1

--- a/solution.py
+++ b/solution.py
@@ -16,7 +16,10 @@
 TN = (((0,), (0,)), ((), ()))
 VMEM = pl.BlockSpec(memory_space=pltpu.VMEM)
 SMEM = pl.BlockSpec(memory_space=pltpu.SMEM)
-PARAMS = pltpu.CompilerParams(vmem_limit_bytes=56 << 20)
+
+
+def params(mib):
+    return pltpu.CompilerParams(vmem_limit_bytes=mib << 20)
 
 
 def norm_rows(rows32, gain):
@@ -34,9 +37,8 @@
     return lax.ppermute(value, "c", [(0, 1), (1, 0)])
 
 
-def qkv_kernel(pos, p0, p1, p2, p3, gain, w0, m1, m2, m3, s1, s2, s3, o0, o1, o2, o3, h1):
+def norm_kernel(pos, p0, p1, p2, p3, gain, h1):
     y = pos[1]
-    c = pos[3]
     half = h1.shape[2]
     rows = p0.shape[0]
     for k, piece in enumerate((p0, p1, p2, p3)):
@@ -44,16 +46,20 @@
         at = pl.ds(pl.multiple_of(lax.rem(y - k + N, N) * rows, rows), rows)
         h1[0, at, :] = normed[:, :half]
         h1[1, at, :] = normed[:, half:]
-    own = lax.dot_general(w0[:, :half], h1[0], NT, preferred_element_type=F32)
-    own += lax.dot_general(w0[:, half:], h1[1], NT, preferred_element_type=F32)
-    o0[...] = own.astype(BF)
-    for mine, other, out in ((m1, s1, o1), (m2, s2, o2), (m3, s3, o3)):
-        total = lax.dot_general(mine[...], h1[c], NT, preferred_element_type=F32)
-        total += lax.dot_general(other[...], h1[1 - c], NT, preferred_element_type=F32)
+
+
+def qkv_kernel(pos, h1, w, o0, o1, o2, o3):
+    x = pos[0]
+    for k, out in enumerate((o0, o1, o2, o3)):
+        at = lax.rem(x - k + N, N) * 2
+        total = lax.dot_general(w[at], h1[0], NT, preferred_element_type=F32)
+        total += lax.dot_general(w[at + 1], h1[1], NT, preferred_element_type=F32)
         out[...] = total.astype(BF)
 
 
-def attend_kernel(pos, bounds, r0, r1, r2, r3, id_row, id_col, out, qs, ks, vs, scores):
+def attend_kernel(
+    pos, bounds, r0, r1, r2, r3, id_row, id_col, o0, o1, o2, o3, qs, ks, vs, scores, outs
+):
     x = pos[0]
     chunk = ks.shape[2]
     block = qs.shape[2]
@@ -98,33 +104,52 @@
             jnp.zeros((HEAD, block), F32),
         )
         top, total, acc = lax.fori_loop(low, high, step, start)
-        out[lax.rem(qb - x + N, N)] = (acc / total).astype(BF)
-
-
-def mlp_kernel(pos, g0, g1, g2, g3, p0, p1, p2, p3, gain, w_mlp, w_out, part, own, att, resid):
-    x = pos[0]
+        outs[lax.rem(qb - x + N, N)] = (acc / total).astype(BF)
+    for k, out in enumerate((o0, o1, o2, o3)):
+        out[...] = outs[k]
+
+
+def mlp_kernel(pos, *refs):
+    gathered = refs[0:4]
+    pieces = refs[4:8]
+    mine = refs[8:12]
+    other = refs[12:16]
+    gain, w_hbm, t0, t1, t2, t3, own, resid, w_mlp, sem = refs[16:]
     y = pos[1]
-    rows = p0.shape[0]
-    for k, piece in enumerate((g0, g1, g2, g3)):
-        for j in range(N):
-            at = lax.rem(y - k + N, N) * N + lax.rem(x - j + N, N)
-            att[at] = piece[j * HEAD : (j + 1) * HEAD, :]
-    for k, piece in enumerate((p0, p1, p2, p3)):
+    c = pos[3]
+    rows = pieces[0].shape[0]
+    copy = pltpu.make_async_copy(w_hbm, w_mlp, sem)
+    copy.start()
+    lhs = jnp.concatenate([g[...] for g in gathered], axis=0)
+    w_mine = jnp.concatenate([w[...] for w in mine], axis=0)
+    w_other = jnp.concatenate([w[...] for w in other], axis=0)
+    half = w_mine.shape[1]
+    resid[c] = lax.dot_general(lhs, w_mine, TN, preferred_element_type=F32)
+    resid[1 - c] = lax.dot_general(lhs, w_other, TN, preferred_element_type=F32)
+    for k, piece in enumerate(pieces):
         at = pl.ds(pl.multiple_of(lax.rem(y - k + N, N) * rows, rows), rows)
-        resid[at, :] = piece[...].astype(F32)
-    lhs = att[...].reshape(N * N * HEAD, N * rows)
-    attn = lax.dot_general(lhs, w_out[...], TN, preferred_element_type=F32)
-    resid[...] = (resid[...] + attn).astype(BF).astype(F32)
-    own[...] = resid[pl.ds(pl.multiple_of(y * rows, rows), rows), :].astype(BF)
-    normed = norm_rows(resid[...], gain[...]).astype(BF)
-    units = 160
-    up = jnp.concatenate([w_mlp[i, :units, :] for i in range(2 * N)], axis=0)
-    down = jnp.concatenate([w_mlp[i, units : 2 * units, :] for i in range(2 * N)], axis=0)
+        for h in (0, 1):
+            start = piece[:, h * half : (h + 1) * half].astype(F32)
+            resid[h, at, :] = (resid[h, at, :] + start).astype(BF).astype(F32)
+            if k == 0:
+                own[:, h * half : (h + 1) * half] = resid[h, at, :].astype(BF)
+    full = jnp.concatenate([resid[0], resid[1]], axis=1)
+    normed = norm_rows(full, gain[...]).astype(BF)
+    copy.wait()
+    count = w_mlp.shape[0]
+    units = w_mlp.shape[1] // 2
+    up = jnp.concatenate([w_mlp[i, :units, :] for i in range(count)], axis=0)
+    down = jnp.concatenate([w_mlp[i, units:, :] for i in range(count)], axis=0)
     hidden = lax.dot_general(normed, up, NT, preferred_element_type=F32)
     hidden = (0.5 * hidden * (1.0 + lax.erf(hidden * math.sqrt(0.5)))).astype(BF)
-    result = jnp.dot(hidden, down, preferred_element_type=F32).astype(BF)
-    for yb in range(N):
-        part[lax.rem(yb - y + N, N)] = result[yb * rows : (yb + 1) * rows, :]
+    result = jnp.dot(hidden, down, preferred_element_type=F32)
+    for h in range(N):
+        resid[0, h * rows : (h + 1) * rows, :] = result[h * rows : (h + 1) * rows, :half]
+        resid[1, h * rows : (h + 1) * rows, :] = result[h * rows : (h + 1) * rows, half:]
+    for k, out in enumerate((t0, t1, t2, t3)):
+        at = pl.ds(pl.multiple_of(lax.rem(y + k, N) * rows, rows), rows)
+        out[:, :half] = resid[0, at, :].astype(BF)
+        out[:, half:] = resid[1, at, :].astype(BF)
 
 
 def local(
@@ -148,38 +173,45 @@
     pos = jnp.stack([x, y, lax.axis_index("z"), c]).astype(jnp.int32)
     ids = picture_ids[0]
 
+    half = width // 2
+    w_heads = jnp.transpose(w_qkv, (0, 2, 1)).reshape(3 * HEAD, width)
+    w_half = lax.dynamic_slice_in_dim(w_heads, c * half, half, 1)
+    w_heads = lax.all_gather(w_half, ("x", "c"), axis=0, tiled=False)
     units = w_down.shape[0] // 2
-    half_head = HEAD // 2
     packed = jnp.concatenate(
         [
             lax.dynamic_slice_in_dim(w_up.T, c * units, units, 0),
             lax.dynamic_slice_in_dim(w_down, c * units, units, 0),
-            lax.dynamic_slice_in_dim(w_out, c * half_head, half_head, 0),
         ],
         axis=0,
     )
+    packed, _ = lax.optimization_barrier((packed, w_half))
+    w_near = lax.all_gather(packed, ("x", "c"), axis=0, tiled=False)
 
     pieces = [rows] + [shift(rows, "y", k) for k in (1, 2, 3)]
-    w_heads = jnp.transpose(w_qkv, (0, 2, 1)).reshape(3 * HEAD, width)
-    w_half = lax.dynamic_slice_in_dim(w_heads, c * (width // 2), width // 2, 1)
-    mine = [shift(w_half, "x", k) for k in (1, 2, 3)]
-    other = [swap(m) for m in mine]
-
-    w_near = lax.all_gather(packed, ("x", "c"), axis=0, tiled=False)
-    out_heads = w_near[:, 2 * units :, :].reshape(N, HEAD, width)
-    out_half = lax.dynamic_slice_in_dim(out_heads, c * 2, 2, 0).reshape(2 * HEAD, width)
-    w_out_all = lax.all_gather(out_half, ("y", "c"), axis=0, tiled=True)
+    out_half = lax.dynamic_slice_in_dim(w_out, c * half, half, 1)
+    out_near = [out_half] + [shift(out_half, "x", k) for k in (1, 2, 3)]
+    out_near = jnp.concatenate(out_near, axis=0)
+    out_mine = [out_near] + [shift(out_near, "y", k) for k in (1, 2, 3)]
+    out_other = [swap(m) for m in out_mine]
 
     total_rows = count * N
+    h1 = pl.pallas_call(
+        norm_kernel,
+        out_shape=jax.ShapeDtypeStruct((2, total_rows, half), BF),
+        in_specs=[SMEM] + [VMEM] * 5,
+        out_specs=VMEM,
+        compiler_params=params(16),
+        name="norm",
+    )(pos, *pieces, ln_attn[None, :])
     qkv = pl.pallas_call(
         qkv_kernel,
         out_shape=[jax.ShapeDtypeStruct((3 * HEAD, total_rows), BF)] * N,
-        in_specs=[SMEM] + [VMEM] * 12,
+        in_specs=[SMEM] + [VMEM] * 2,
         out_specs=[VMEM] * N,
-        scratch_shapes=[pltpu.VMEM((2, total_rows, width // 2), BF)],
-        compiler_params=PARAMS,
+        compiler_params=params(16),
         name="qkv",
-    )(pos, *pieces, ln_attn[None, :], w_heads, *mine, *other)
+    )(pos, h1, w_heads)
     blocks = [qkv[0]] + [shift(qkv[k], "x", -k) for k in (1, 2, 3)]
 
     group_rows = ids.shape[0]
@@ -197,37 +229,36 @@
 
     attended = pl.pallas_call(
         attend_kernel,
-        out_shape=jax.ShapeDtypeStruct((N, HEAD, total_rows), BF),
+        out_shape=[jax.ShapeDtypeStruct((HEAD, total_rows), BF)] * N,
         in_specs=[SMEM, SMEM] + [VMEM] * 6,
-        out_specs=VMEM,
+        out_specs=[VMEM] * N,
         scratch_shapes=[
             pltpu.VMEM((N, HEAD, total_rows), BF),
             pltpu.VMEM((chunks, HEAD, chunk), BF),
             pltpu.VMEM((chunks, HEAD, chunk), BF),
             pltpu.VMEM((2, chunk, total_rows), F32),
+            pltpu.VMEM((N, HEAD, total_rows), BF),
         ],
-        compiler_params=PARAMS,
+        compiler_params=params(16),
         name="attend",
     )(pos, bounds, *blocks, ids[None, :], ids[:, None])
     heads = [attended[0]] + [shift(attended[k], "x", k) for k in (1, 2, 3)]
     heads = jnp.concatenate(heads, axis=0)
     gathered = [heads] + [shift(heads, "y", k) for k in (1, 2, 3)]
 
-    part, resid = pl.pallas_call(
+    *part, resid = pl.pallas_call(
         mlp_kernel,
-        out_shape=[
-            jax.ShapeDtypeStruct((N, count, width), BF),
-            jax.ShapeDtypeStruct((count, width), BF),
+        out_shape=[jax.ShapeDtypeStruct((count, width), BF)] * (N + 1),
+        in_specs=[SMEM] + [VMEM] * 17 + [pl.BlockSpec(memory_space=pl.ANY)],
+        out_specs=[VMEM] * (N + 1),
+        scratch_shapes=[
+            pltpu.VMEM((2, total_rows, half), F32),
+            pltpu.VMEM(w_near.shape, BF),
+            pltpu.SemaphoreType.DMA(()),
         ],
-        in_specs=[SMEM] + [VMEM] * 11,
-        out_specs=[VMEM] * 2,
-        scratch_shapes=[
-            pltpu.VMEM((N * N, HEAD, total_rows), BF),
-            pltpu.VMEM((total_rows, width), F32),
-        ],
-        compiler_params=PARAMS,
+        compiler_params=params(40),
         name="mlp",
-    )(pos, *gathered, *pieces, ln_mlp[None, :], w_near, w_out_all)
+    )(pos, *gathered, *pieces, *out_mine, *out_other, ln_mlp[None, :], w_near)
     sums = part[0].astype(F32)
     for k in (1, 2, 3):
         sums = sums + shift(part[k], "y", k).astype(F32)

time: 217 us -> 180 us (0.83); the launches traced: 216 us -> 177 us
  waiting for transfers between devices: 106 us -> 58.8 us
  local copies, waits for them, and re-layouts: 14.1 us -> 21.9 us
  Pallas kernels: 27.5 us -> 21.7 us
  other arithmetic: 5.33 us -> 8.71 us
    all_gather x1, waiting for transfers between devices: 47.9 us -> 0.01 us  [local(): w_near = lax.all_gather(packed, ('x', 'c'), axis=0, tiled=False)]
    unnamed x51 -> x44, local copies, waits for them, and re-layouts: 4.96 us -> 16.7 us
    pallas_call x2 -> x3, Pallas kernels: 22.1 us -> 18.7 us  [the longest x1 9.33 us: local(): pl.pallas_call(mlp_kernel, out_shape=[jax.ShapeDtypeStruct((count, width)...]
    pallas_call x1, Pallas kernels: 5.4 us -> 3.03 us  [local(): pl.pallas_call(qkv_kernel, out_shape=[jax.ShapeDtypeStruct((3 * HEAD, tot...]
    squeeze x2 -> x0, local copies, waits for them, and re-layouts: 2.31 us -> none  [the longest x1 1.28 us: local(): sums = sums + shift(part[k], 'y', k).astype(F32)]
    ppermute x18 -> x21, starting transfers between devices: 28.1 us -> 29.5 us  [shift(): return lax.ppermute(value, axis, pairs)]
    ppermute x18 -> x21, waiting for transfers between devices: 57.7 us -> 58.8 us  [shift(): return lax.ppermute(value, axis, pairs)]
  transfers between devices with their start and end apart: 23 -> 27, of which waited for: 12 -> 13; matrix products, arithmetic and copies ran while one was open for 3% -> 7% of each run, Pallas kernels for 7% -> 7%
where the time goes in v2:
time: 180 us; the launch traced here: 177 us
  waiting for transfers between devices  58.8 us (33%)
  starting transfers between devices  30.1 us (17%)
  local copies, waits for them, and re-layouts  21.9 us (12%)
  Pallas kernels  21.7 us (12%)
  blocking collectives  13.8 us (8%)
  between operations  13.7 us (8%)
  other arithmetic  8.71 us (5%)
  matrix products  8.29 us (5%)
    ppermute x21, waiting for transfers between devices, shift(): return lax.ppermute(value, axis, pairs)  58.8 us
    ppermute x21, starting transfers between devices, shift(): return lax.ppermute(value, axis, pairs)  29.5 us
    unnamed x44, local copies, waits for them, and re-layouts  16.7 us
    all_to_all x1, blocking collectives, local(): lax.all_to_all(outgoing.reshape(req_count, slot_cap, width + 128), ('x',...  13.8 us
    pallas_call x1, Pallas kernels, local(): pl.pallas_call(mlp_kernel, out_shape=[jax.ShapeDtypeStruct((count, width)...  9.33 us
    pallas_call x1, Pallas kernels, local(): pl.pallas_call(attend_kernel, out_shape=[jax.ShapeDtypeStruct((HEAD, tota...  7.93 us
    dot_general x1, matrix products, local(): jnp.dot(select.astype(BF), projected, preferred_element_type=F32).astype(BF)  7.2 us
  transfers between devices with their start and end apart: 27, of which 13 were waited for; matrix products, arithmetic and copies ran while one was open for 7% of the time, Pallas kernels for 7%

profile of v2, /device:TPU:0, one launch (start us, length us, event | category | flops | bytes accessed | tf_op | source)
XLA Modules:
  0.0 176.9 jit_solution(13268619282874222627)
XLA Ops:
  6.5 1.8 %constant_dynamic-slice_fusion.2 = bf16[240,640]{1,0:T(8,128)(2,1)} fusion(bf16[240,1280]{1,0:T(8,128)(2,1)} %bitcast.47, s32[]{:T(128)S(6)} %select_n.84), kind=kLoop, calls=%fused_computation.53 | loop fusion | bytes 614404 | tf_op jit(solution)/shard_map/dynamic_slice | solution.py:178
  8.5 1.0 dynamic-slice_bitcast_fusion
  9.5 1.0 pad_maximum_fusion
  10.5 1.7 collective-permute-start
  12.2 2.9 %collective-permute-start.1 = (bf16[128,1280]{1,0:T(8,128)(2,1)}, bf16[128,1280]{1,0:T(8,128)(2,1)S(1)}, u32[]{:S(2)}, u32[]{:S(2)}) collective-permute-start(bf16[128,1280]{1,0:T(8,128)(2,1)} %bitcast.42), channel_id=1, source_target_pairs={{0,16},{8,24},{16,0},{24,8},{1,17},{9,25},{17,1},{25,9},{2,18},{10... | collective-permute-start | bytes 983048 | tf_op jit(solution)/shard_map/ppermute | solution.py:33
  15.1 0.9 constant_dynamic-slice_fusion.1
  16.0 1.6 collective-permute-start.12
  17.6 2.7 %collective-permute-start.13 = (bf16[80,640]{1,0:T(8,128)(2,1)S(1)}, bf16[80,640]{1,0:T(8,128)(2,1)S(1)}, u32[]{:S(2)}, u32[]{:S(2)}) collective-permute-start(bf16[80,640]{1,0:T(8,128)(2,1)S(1)} %constant_dynamic-slice_fusion.1), channel_id=1, source_target_pairs={{0,64},{32,96},{64,0},{96,32},{1,65},{33,97},{65,1},{97,33},{2,66}... | collective-permute-start | bytes 307208 | tf_op jit(solution)/shard_map/ppermute | solution.py:33
  20.3 1.4 collective-permute-start.14
  21.8 0.7 broadcast_in_dim.91.gain
  22.5 0.6 broadcast.195
  23.0 1.4 reduce.5
  24.9 1.2 compare_select_fusion.2
  26.1 1.4 collective-permute-start.2
  27.6 0.7 collective-permute-start.15
  28.5 0.5 bitcast_minimum_fusion
  29.1 0.8 collective-permute-start.16
  29.9 1.9 %collective-permute-start.17 = (bf16[320,640]{1,0:T(8,128)(2,1)S(1)}, bf16[320,640]{1,0:T(8,128)(2,1)}, u32[]{:S(2)}, u32[]{:S(2)}) collective-permute-start(bf16[320,640]{1,0:T(8,128)(2,1)S(1)} %pad_maximum_fusion.1.refs_8_), channel_id=1, source_target_pairs={{0,24},{8,0},{16,8},{24,16},{1,25},{9,1},{17,9},{25,17},{2,26},{10... | collective-permute-start | bytes 1228808 | tf_op jit(solution)/shard_map/ppermute | solution.py:33
  31.8 12.4 %collective-permute-done.2.p3.refs_7_ = bf16[128,1280]{1,0:T(8,128)(2,1)S(1)} collective-permute-done((bf16[128,1280]{1,0:T(8,128)(2,1)}, bf16[128,1280]{1,0:T(8,128)(2,1)S(1)}, u32[]{:S(2)}, u32[]{:S(2)}) %collective-permute-start.2) | collective-permute-done | bytes 327712 | tf_op jit(solution)/shard_map/ppermute | solution.py:33
  44.1 1.0 copy-done.3
  45.1 1.4 norm.1.h1
  46.5 0.7 copy-done.5
  47.2 1.9 %copy-done.2 = bf16[1920,640]{1,0:T(8,128)(2,1)S(1)} copy-done((bf16[1920,640]{1,0:T(8,128)(2,1)S(1)}, bf16[1920,640]{1,0:T(8,128)(2,1)}, u32[]{:S(2)}) %copy-start.2) | copy-done | bytes 2457624
  49.1 3.0 %qkv.1 = (bf16[240,512]{1,0:T(8,128)(2,1)S(1)}, bf16[240,512]{1,0:T(8,128)(2,1)}, bf16[240,512]{1,0:T(8,128)(2,1)}, bf16[240,512]{1,0:T(8,128)(2,1)}) custom-call(s32[4]{0:T(128)S(1)} %pad_add_fusion.1.pos, bf16[2,512,640]{2,1,0:T(8,128)(2,1)S(1)} %norm.1.h1, bf16[8,240,640]{2,1,0:T(8,128)(2,1)S(1)} %bitcast.40), custom_call_target="tpu_custom_call" | custom-call | tf_op jit(solution)/shard_map/qkv/pallas_call | solution.py:207
  52.1 0.7 copy-done.15
  52.8 2.5 %collective-permute-start.4 = (bf16[240,512]{1,0:T(8,128)(2,1)}, bf16[240,512]{1,0:T(8,128)(2,1)}, u32[]{:S(2)}, u32[]{:S(2)}) collective-permute-start(bf16[240,512]{1,0:T(8,128)(2,1)} %get-tuple-element.21), channel_id=1, source_target_pairs={{0,64},{32,96},{64,0},{96,32},{1,65},{33,97},{65,1},{97,33},{2,66}... | collective-permute-start | bytes 737288 | tf_op jit(solution)/shard_map/ppermute | solution.py:33
  55.3 0.7 compare_select_fusion
  56.4 0.6 pad_add_fusion.bounds
  57.0 0.8 convert_reduce_fusion
  58.4 6.0 %collective-permute-done.3.r1 = bf16[240,512]{1,0:T(8,128)(2,1)S(1)} collective-permute-done((bf16[240,512]{1,0:T(8,128)(2,1)}, bf16[240,512]{1,0:T(8,128)(2,1)S(1)}, u32[]{:S(2)}, u32[]{:S(2)}) %collective-permute-start.3) | collective-permute-done | bytes 245792 | tf_op jit(solution)/shard_map/ppermute | solution.py:33
  64.5 1.6 collective-permute-done.4.r2
  66.1 6.4 %collective-permute-done.5.r3 = bf16[240,512]{1,0:T(8,128)(2,1)} collective-permute-done((bf16[240,512]{1,0:T(8,128)(2,1)}, bf16[240,512]{1,0:T(8,128)(2,1)}, u32[]{:S(2)}, u32[]{:S(2)}) %collective-permute-start.5) | collective-permute-done | bytes 245792 | tf_op jit(solution)/shard_map/ppermute | solution.py:33
  72.5 0.9 copy-done.16
  73.4 7.9 %attend.1 = (bf16[80,512]{1,0:T(8,128)(2,1)S(1)}, bf16[80,512]{1,0:T(8,128)(2,1)S(1)}, bf16[80,512]{1,0:T(8,128)(2,1)S(1)}, bf16[80,512]{1,0:T(8,128)(2,1)S(1)}) custom-call(s32[4]{0:T(128)S(1)} %pad_add_fusion.1.pos, s32[2,4]{1,0:T(2,128)S(1)} %pad_add_fusion.bounds, bf16[240,512]{1,0:T(8,128)(2,1)S(1)} %copy-done.16, ...), custom_call_target="tpu_custom_call" | custom-call | tf_op jit(solution)/shard_map/attend/pallas_call | solution.py:230
  81.4 2.5 %collective-permute-start.6 = (bf16[80,512]{1,0:T(8,128)(2,1)S(1)}, bf16[80,512]{1,0:T(8,128)(2,1)S(1)}, u32[]{:S(2)}, u32[]{:S(2)}) collective-permute-start(bf16[80,512]{1,0:T(8,128)(2,1)S(1)} %get-tuple-element.24), channel_id=1, source_target_pairs={{0,32},{32,64},{64,96},{96,0},{1,33},{33,65},{65,97},{97,1},{2,34}... | collective-permute-start | bytes 245768 | tf_op jit(solution)/shard_map/ppermute | solution.py:33
  83.9 4.2 %collective-permute-done.6 = bf16[80,512]{1,0:T(8,128)(2,1)S(1)} collective-permute-done((bf16[80,512]{1,0:T(8,128)(2,1)S(1)}, bf16[80,512]{1,0:T(8,128)(2,1)S(1)}, u32[]{:S(2)}, u32[]{:S(2)}) %collective-permute-start.6) | collective-permute-done | bytes 81952 | tf_op jit(solution)/shard_map/ppermute | solution.py:33
  88.0 1.1 collective-permute-start.7
  89.2 4.8 %collective-permute-done.7 = bf16[80,512]{1,0:T(8,128)(2,1)S(1)} collective-permute-done((bf16[80,512]{1,0:T(8,128)(2,1)S(1)}, bf16[80,512]{1,0:T(8,128)(2,1)S(1)}, u32[]{:S(2)}, u32[]{:S(2)}) %collective-permute-start.7) | collective-permute-done | bytes 81952 | tf_op jit(solution)/shard_map/ppermute | solution.py:33
  94.0 0.6 collective-permute-start.8
  94.6 3.8 %collective-permute-done.8 = bf16[80,512]{1,0:T(8,128)(2,1)S(1)} collective-permute-done((bf16[80,512]{1,0:T(8,128)(2,1)S(1)}, bf16[80,512]{1,0:T(8,128)(2,1)S(1)}, u32[]{:S(2)}, u32[]{:S(2)}) %collective-permute-start.8) | collective-permute-done | bytes 81952 | tf_op jit(solution)/shard_map/ppermute | solution.py:33
  98.5 0.8 copy-done.7
  99.2 3.4 %collective-permute-start.11 = (bf16[320,512]{1,0:T(8,128)(2,1)S(1)}, bf16[320,512]{1,0:T(8,128)(2,1)S(1)}, u32[]{:S(2)}, u32[]{:S(2)}) collective-permute-start(bf16[320,512]{1,0:T(8,128)(2,1)S(1)} %constant_dynamic-update-slice_fusion.refs_0_), channel_id=1, source_target_pairs={{0,24},{8,0},{16,8},{24,16},{1,25},{9,1},{17,9},{25,17},{2,26},{10... | collective-permute-start | bytes 983048 | tf_op jit(solution)/shard_map/ppermute | solution.py:33
  102.6 0.7 copy-done.9
  103.4 0.8 collective-permute-start.9
  104.2 0.6 fusion.7
  104.8 0.7 select_reduce_fusion
  105.6 0.7 copy-done.11
  106.4 0.8 copy-done.13
  107.1 3.3 %collective-permute-done.10.refs_2_ = bf16[320,512]{1,0:T(8,128)(2,1)S(1)} collective-permute-done((bf16[320,512]{1,0:T(8,128)(2,1)S(1)}, bf16[320,512]{1,0:T(8,128)(2,1)S(1)}, u32[]{:S(2)}, u32[]{:S(2)}) %collective-permute-start.10) | collective-permute-done | bytes 327712 | tf_op jit(solution)/shard_map/ppermute | solution.py:33
  110.4 2.7 %collective-permute-done.11.refs_3_ = bf16[320,512]{1,0:T(8,128)(2,1)S(1)} collective-permute-done((bf16[320,512]{1,0:T(8,128)(2,1)S(1)}, bf16[320,512]{1,0:T(8,128)(2,1)S(1)}, u32[]{:S(2)}, u32[]{:S(2)}) %collective-permute-start.11) | collective-permute-done | bytes 327712 | tf_op jit(solution)/shard_map/ppermute | solution.py:33
  113.1 0.8 collective-permute-done.9.refs_1_
  113.9 2.9 %copy-done.1 = bf16[2560,1280]{1,0:T(8,128)(2,1)S(1)} copy-done((bf16[2560,1280]{1,0:T(8,128)(2,1)S(1)}, bf16[2560,1280]{1,0:T(8,128)(2,1)}, u32[]{:S(2)}) %copy-start.1) | copy-done | bytes 6553624
  116.8 1.0 copy-done.6
  117.8 1.0 copy-done.8
  118.8 1.0 copy-done.10
  119.8 1.0 copy-done.12
  120.8 1.0 copy-done.14
  121.8 9.3 %mlp.1 = (bf16[128,1280]{1,0:T(8,128)(2,1)S(1)}, bf16[128,1280]{1,0:T(8,128)(2,1)S(1)}, bf16[128,1280]{1,0:T(8,128)(2,1)S(1)}, bf16[128,1280]{1,0:T(8,128)(2,1)S(1)}, bf16[128,1280]{1,0:T(8,128)(2,1)S(1)}) custom-call(s32[4]{0:T(128)S(1)} %pad_add_fusion.1.pos, bf16[320,512]{1,0:T(8,128)(2,1)S(1)} %constant_dynamic-update-slice_fusion.refs_0_, ...), custom_call_target="tpu_custom_call" | custom-call | tf_op jit(solution)/shard_map/mlp/pallas_call | solution.py:249
  131.2 3.2 %collective-permute-start.23 = (bf16[128,1280]{1,0:T(8,128)(2,1)S(1)}, bf16[128,1280]{1,0:T(8,128)(2,1)S(1)}, u32[]{:S(2)}, u32[]{:S(2)}) collective-permute-start(bf16[128,1280]{1,0:T(8,128)(2,1)S(1)} %get-tuple-element.31), channel_id=1, source_target_pairs={{0,16},{8,24},{16,0},{24,8},{1,17},{9,25},{17,1},{25,9},{2,18},{10... | collective-permute-start | bytes 983048 | tf_op jit(solution)/shard_map/ppermute | solution.py:33
  134.5 7.7 %collective-permute-done.22 = bf16[128,1280]{1,0:T(8,128)(2,1)S(1)} collective-permute-done((bf16[128,1280]{1,0:T(8,128)(2,1)S(1)}, bf16[128,1280]{1,0:T(8,128)(2,1)S(1)}, u32[]{:S(2)}, u32[]{:S(2)}) %collective-permute-start.22) | collective-permute-done | bytes 327712 | tf_op jit(solution)/shard_map/ppermute | solution.py:33
  142.3 4.8 %collective-permute-done.23 = bf16[128,1280]{1,0:T(8,128)(2,1)S(1)} collective-permute-done((bf16[128,1280]{1,0:T(8,128)(2,1)S(1)}, bf16[128,1280]{1,0:T(8,128)(2,1)S(1)}, u32[]{:S(2)}, u32[]{:S(2)}) %collective-permute-start.23) | collective-permute-done | bytes 327712 | tf_op jit(solution)/shard_map/ppermute | solution.py:33
  147.7 7.2 %convolution_convert_fusion.1 = bf16[32,1280]{1,0:T(8,128)(2,1)S(1)} fusion(bf16[32,5120]{1,0:T(8,128)(2,1)S(1)} %reshape.113, bf16[5120,1280]{1,0:T(8,128)(2,1)} %param.19, s32[32]{0:T(128)S(1)} %fusion.7), kind=kOutput, calls=%fused_computation.2 | convolution fusion | flops 422134784 | bytes 13516928 | tf_op jit(solution)/shard_map/dot_general | solution.py:284
  155.0 13.8 %all_to_all.5 = bf16[16,2,1408]{2,1,0:T(2,128)(2,1)S(1)} all-to-all(bf16[16,2,1408]{2,1,0:T(2,128)(2,1)S(1)} %reshape.114), channel_id=1, replica_groups=mesh['x'=4,'y'=4,'z'=4,'c'=2] {'x','y'}, dimensions={0} | all-to-all | bytes 180224 | tf_op jit(solution)/shard_map/all_to_all | solution.py:286
  169.0 1.1 fusion
  (78 shorter events, 3.0 us)
Async XLA Ops:
  6.5 1.9 %copy-start = (bf16[320,1280]{1,0:T(8,128)(2,1)S(1)}, bf16[320,1280]{1,0:T(8,128)(2,1)}, u32[]{:S(2)}) copy-start(bf16[320,1280]{1,0:T(8,128)(2,1)} %param.18) | copy-start | bytes 2457604
  6.5 49.5 %copy-start.17 = (s32[1,2048]{1,0:T(1,128)S(1)}, s32[1,2048]{1,0:T(1,128)}, u32[]{:S(2)}) copy-start(s32[1,2048]{1,0:T(1,128)} %id_row.1) | copy-start | bytes 24580
  6.5 40.7 %all-gather.5.cloned.1.call-start = ((), (), s32[]{:S(2)}) async-start(), calls=%async_computation.1 | async-start | bytes 2764800 | tf_op jit(solution)/shard_map/all_gather | solution.py:179
  8.3 48.1 %copy-start.19 = (f32[1280]{0:T(1024)S(1)}, f32[1280]{0:T(1024)}, u32[]{:S(2)}) copy-start(f32[1280]{0:T(1024)} %param.16) | copy-start | bytes 15364
  8.4 105.6 %all-gather.7.cloned.1.call-start = ((), (), s32[]{:S(2)}) async-start(), calls=%async_computation.2 | async-start | bytes 7372800 | tf_op jit(solution)/shard_map/all_gather | solution.py:189
  9.5 104.4 %copy-start.4 = (bf16[1,128,1280]{2,1,0:T(8,128)(2,1)S(1)}, bf16[1,128,1280]{2,1,0:T(8,128)(2,1)}, u32[]{:S(2)}) copy-start(bf16[1,128,1280]{2,1,0:T(8,128)(2,1)} %param.11) | copy-start | bytes 983044
  10.5 19.4 %collective-permute-start = (bf16[128,1280]{1,0:T(8,128)(2,1)}, bf16[128,1280]{1,0:T(8,128)(2,1)S(1)}, u32[]{:S(2)}, u32[]{:S(2)}) collective-permute-start(bf16[128,1280]{1,0:T(8,128)(2,1)} %bitcast.41), channel_id=1, source_target_pairs={{0,8},{8,16},{16,24},{24,0},{1,9},{9,17},{17,25},{25,1},{2,10},{10... | collective-permute-start | bytes 983048 | tf_op jit(solution)/shard_map/ppermute | solution.py:33
  12.2 19.5 %collective-permute-start.1 = (bf16[128,1280]{1,0:T(8,128)(2,1)}, bf16[128,1280]{1,0:T(8,128)(2,1)S(1)}, u32[]{:S(2)}, u32[]{:S(2)}) collective-permute-start(bf16[128,1280]{1,0:T(8,128)(2,1)} %bitcast.42), channel_id=1, source_target_pairs={{0,16},{8,24},{16,0},{24,8},{1,17},{9,25},{17,1},{25,9},{2,18},{10... | collective-permute-start | bytes 983048 | tf_op jit(solution)/shard_map/ppermute | solution.py:33
  16.0 10.1 %collective-permute-start.12 = (bf16[80,640]{1,0:T(8,128)(2,1)S(1)}, bf16[80,640]{1,0:T(8,128)(2,1)S(1)}, u32[]{:S(2)}, u32[]{:S(2)}) collective-permute-start(bf16[80,640]{1,0:T(8,128)(2,1)S(1)} %constant_dynamic-slice_fusion.1), channel_id=1, source_target_pairs={{0,32},{32,64},{64,96},{96,0},{1,33},{33,65},{65,97},{97,1},{2,34}... | collective-permute-start | bytes 307208 | tf_op jit(solution)/shard_map/ppermute | solution.py:33
  17.6 9.9 %collective-permute-start.13 = (bf16[80,640]{1,0:T(8,128)(2,1)S(1)}, bf16[80,640]{1,0:T(8,128)(2,1)S(1)}, u32[]{:S(2)}, u32[]{:S(2)}) collective-permute-start(bf16[80,640]{1,0:T(8,128)(2,1)S(1)} %constant_dynamic-slice_fusion.1), channel_id=1, source_target_pairs={{0,64},{32,96},{64,0},{96,32},{1,65},{33,97},{65,1},{97,33},{2,66}... | collective-permute-start | bytes 307208 | tf_op jit(solution)/shard_map/ppermute | solution.py:33
  20.3 7.2 %collective-permute-start.14 = (bf16[80,640]{1,0:T(8,128)(2,1)S(1)}, bf16[80,640]{1,0:T(8,128)(2,1)S(1)}, u32[]{:S(2)}, u32[]{:S(2)}) collective-permute-start(bf16[80,640]{1,0:T(8,128)(2,1)S(1)} %constant_dynamic-slice_fusion.1), channel_id=1, source_target_pairs={{0,96},{32,0},{64,32},{96,64},{1,97},{33,1},{65,33},{97,65},{2,98}... | collective-permute-start | bytes 307208 | tf_op jit(solution)/shard_map/ppermute | solution.py:33
  26.1 18.0 %collective-permute-start.2 = (bf16[128,1280]{1,0:T(8,128)(2,1)}, bf16[128,1280]{1,0:T(8,128)(2,1)S(1)}, u32[]{:S(2)}, u32[]{:S(2)}) collective-permute-start(bf16[128,1280]{1,0:T(8,128)(2,1)} %bitcast.43), channel_id=1, source_target_pairs={{0,24},{8,0},{16,8},{24,16},{1,25},{9,1},{17,9},{25,17},{2,26},{10... | collective-permute-start | bytes 983048 | tf_op jit(solution)/shard_map/ppermute | solution.py:33
  27.6 27.8 %collective-permute-start.15 = (bf16[320,640]{1,0:T(8,128)(2,1)S(1)}, bf16[320,640]{1,0:T(8,128)(2,1)}, u32[]{:S(2)}, u32[]{:S(2)}) collective-permute-start(bf16[320,640]{1,0:T(8,128)(2,1)S(1)} %pad_maximum_fusion.1.refs_8_), channel_id=1, source_target_pairs={{0,8},{8,16},{16,24},{24,0},{1,9},{9,17},{17,25},{25,1},{2,10},{10... | collective-permute-start | bytes 1228808 | tf_op jit(solution)/shard_map/ppermute | solution.py:33
  29.1 28.8 %collective-permute-start.16 = (bf16[320,640]{1,0:T(8,128)(2,1)S(1)}, bf16[320,640]{1,0:T(8,128)(2,1)}, u32[]{:S(2)}, u32[]{:S(2)}) collective-permute-start(bf16[320,640]{1,0:T(8,128)(2,1)S(1)} %pad_maximum_fusion.1.refs_8_), channel_id=1, source_target_pairs={{0,16},{8,24},{16,0},{24,8},{1,17},{9,25},{17,1},{25,9},{2,18},{10... | collective-permute-start | bytes 1228808 | tf_op jit(solution)/shard_map/ppermute | solution.py:33
  29.9 28.0 %collective-permute-start.17 = (bf16[320,640]{1,0:T(8,128)(2,1)S(1)}, bf16[320,640]{1,0:T(8,128)(2,1)}, u32[]{:S(2)}, u32[]{:S(2)}) collective-permute-start(bf16[320,640]{1,0:T(8,128)(2,1)S(1)} %pad_maximum_fusion.1.refs_8_), channel_id=1, source_target_pairs={{0,24},{8,0},{16,8},{24,16},{1,25},{9,1},{17,9},{25,17},{2,26},{10... | collective-permute-start | bytes 1228808 | tf_op jit(solution)/shard_map/ppermute | solution.py:33
  44.1 1.0 copy-start.3
  46.5 0.7 copy-start.5
  47.2 1.9 %copy-start.2 = (bf16[1920,640]{1,0:T(8,128)(2,1)S(1)}, bf16[1920,640]{1,0:T(8,128)(2,1)}, u32[]{:S(2)}) copy-start(bf16[1920,640]{1,0:T(8,128)(2,1)} %all-gather.5.cloned.1.call-done) | copy-start | bytes 7372804
  52.1 0.7 copy-start.15
  52.8 11.6 %collective-permute-start.3 = (bf16[240,512]{1,0:T(8,128)(2,1)}, bf16[240,512]{1,0:T(8,128)(2,1)S(1)}, u32[]{:S(2)}, u32[]{:S(2)}) collective-permute-start(bf16[240,512]{1,0:T(8,128)(2,1)} %get-tuple-element.20), channel_id=1, source_target_pairs={{0,96},{32,0},{64,32},{96,64},{1,97},{33,1},{65,33},{97,65},{2,98}... | collective-permute-start | bytes 737288 | tf_op jit(solution)/shard_map/ppermute | solution.py:33
  52.8 13.3 %collective-permute-start.4 = (bf16[240,512]{1,0:T(8,128)(2,1)}, bf16[240,512]{1,0:T(8,128)(2,1)}, u32[]{:S(2)}, u32[]{:S(2)}) collective-permute-start(bf16[240,512]{1,0:T(8,128)(2,1)} %get-tuple-element.21), channel_id=1, source_target_pairs={{0,64},{32,96},{64,0},{96,32},{1,65},{33,97},{65,1},{97,33},{2,66}... | collective-permute-start | bytes 737288 | tf_op jit(solution)/shard_map/ppermute | solution.py:33
  55.3 17.2 %collective-permute-start.5 = (bf16[240,512]{1,0:T(8,128)(2,1)}, bf16[240,512]{1,0:T(8,128)(2,1)}, u32[]{:S(2)}, u32[]{:S(2)}) collective-permute-start(bf16[240,512]{1,0:T(8,128)(2,1)} %get-tuple-element.22), channel_id=1, source_target_pairs={{0,32},{32,64},{64,96},{96,0},{1,33},{33,65},{65,97},{97,1},{2,34}... | collective-permute-start | bytes 737288 | tf_op jit(solution)/shard_map/ppermute | solution.py:33
  57.8 40.6 %collective-permute-start.18 = (bf16[320,640]{1,0:T(8,128)(2,1)S(1)}, bf16[320,640]{1,0:T(8,128)(2,1)S(1)}, u32[]{:S(2)}, u32[]{:S(2)}) collective-permute-start(bf16[320,640]{1,0:T(8,128)(2,1)S(1)} %pad_maximum_fusion.1.refs_8_), channel_id=1, source_target_pairs={{0,1},{1,0},{2,3},{3,2},{4,5},{5,4},{6,7},{7,6},{8,9},{9,8},{10,11... | collective-permute-start | bytes 1228808 | tf_op jit(solution)/shard_map/ppermute | solution.py:37
  57.9 44.7 %collective-permute-start.19 = (bf16[320,640]{1,0:T(8,128)(2,1)}, bf16[320,640]{1,0:T(8,128)(2,1)S(1)}, u32[]{:S(2)}, u32[]{:S(2)}) collective-permute-start(bf16[320,640]{1,0:T(8,128)(2,1)} %collective-permute-done.15.refs_9_), channel_id=1, source_target_pairs={{0,1},{1,0},{2,3},{3,2},{4,5},{5,4},{6,7},{7,6},{8,9},{9,8},{10,11... | collective-permute-start | bytes 1228808 | tf_op jit(solution)/shard_map/ppermute | solution.py:37
  64.5 41.1 %collective-permute-start.20 = (bf16[320,640]{1,0:T(8,128)(2,1)}, bf16[320,640]{1,0:T(8,128)(2,1)S(1)}, u32[]{:S(2)}, u32[]{:S(2)}) collective-permute-start(bf16[320,640]{1,0:T(8,128)(2,1)} %collective-permute-done.16.refs_10_), channel_id=1, source_target_pairs={{0,1},{1,0},{2,3},{3,2},{4,5},{5,4},{6,7},{7,6},{8,9},{9,8},{10,11... | collective-permute-start | bytes 1228808 | tf_op jit(solution)/shard_map/ppermute | solution.py:37
  66.1 40.3 %collective-permute-start.21 = (bf16[320,640]{1,0:T(8,128)(2,1)}, bf16[320,640]{1,0:T(8,128)(2,1)S(1)}, u32[]{:S(2)}, u32[]{:S(2)}) collective-permute-start(bf16[320,640]{1,0:T(8,128)(2,1)} %collective-permute-done.17.refs_11_), channel_id=1, source_target_pairs={{0,1},{1,0},{2,3},{3,2},{4,5},{5,4},{6,7},{7,6},{8,9},{9,8},{10,11... | collective-permute-start | bytes 1228808 | tf_op jit(solution)/shard_map/ppermute | solution.py:37
  72.5 0.9 copy-start.16
  81.4 6.7 %collective-permute-start.6 = (bf16[80,512]{1,0:T(8,128)(2,1)S(1)}, bf16[80,512]{1,0:T(8,128)(2,1)S(1)}, u32[]{:S(2)}, u32[]{:S(2)}) collective-permute-start(bf16[80,512]{1,0:T(8,128)(2,1)S(1)} %get-tuple-element.24), channel_id=1, source_target_pairs={{0,32},{32,64},{64,96},{96,0},{1,33},{33,65},{65,97},{97,1},{2,34}... | collective-permute-start | bytes 245768 | tf_op jit(solution)/shard_map/ppermute | solution.py:33
  88.0 5.9 %collective-permute-start.7 = (bf16[80,512]{1,0:T(8,128)(2,1)S(1)}, bf16[80,512]{1,0:T(8,128)(2,1)S(1)}, u32[]{:S(2)}, u32[]{:S(2)}) collective-permute-start(bf16[80,512]{1,0:T(8,128)(2,1)S(1)} %get-tuple-element.25), channel_id=1, source_target_pairs={{0,64},{32,96},{64,0},{96,32},{1,65},{33,97},{65,1},{97,33},{2,66}... | collective-permute-start | bytes 245768 | tf_op jit(solution)/shard_map/ppermute | solution.py:33
  94.0 4.4 %collective-permute-start.8 = (bf16[80,512]{1,0:T(8,128)(2,1)S(1)}, bf16[80,512]{1,0:T(8,128)(2,1)S(1)}, u32[]{:S(2)}, u32[]{:S(2)}) collective-permute-start(bf16[80,512]{1,0:T(8,128)(2,1)S(1)} %get-tuple-element.26), channel_id=1, source_target_pairs={{0,96},{32,0},{64,32},{96,64},{1,97},{33,1},{65,33},{97,65},{2,98}... | collective-permute-start | bytes 245768 | tf_op jit(solution)/shard_map/ppermute | solution.py:33
  98.4 12.0 %collective-permute-start.10 = (bf16[320,512]{1,0:T(8,128)(2,1)S(1)}, bf16[320,512]{1,0:T(8,128)(2,1)S(1)}, u32[]{:S(2)}, u32[]{:S(2)}) collective-permute-start(bf16[320,512]{1,0:T(8,128)(2,1)S(1)} %constant_dynamic-update-slice_fusion.refs_0_), channel_id=1, source_target_pairs={{0,16},{8,24},{16,0},{24,8},{1,17},{9,25},{17,1},{25,9},{2,18},{10... | collective-permute-start | bytes 983048 | tf_op jit(solution)/shard_map/ppermute | solution.py:33
  98.4 0.8 copy-start.7
  99.2 13.9 %collective-permute-start.11 = (bf16[320,512]{1,0:T(8,128)(2,1)S(1)}, bf16[320,512]{1,0:T(8,128)(2,1)S(1)}, u32[]{:S(2)}, u32[]{:S(2)}) collective-permute-start(bf16[320,512]{1,0:T(8,128)(2,1)S(1)} %constant_dynamic-update-slice_fusion.refs_0_), channel_id=1, source_target_pairs={{0,24},{8,0},{16,8},{24,16},{1,25},{9,1},{17,9},{25,17},{2,26},{10... | collective-permute-start | bytes 983048 | tf_op jit(solution)/shard_map/ppermute | solution.py:33
  102.6 0.7 copy-start.9
  103.4 10.6 %collective-permute-start.9 = (bf16[320,512]{1,0:T(8,128)(2,1)S(1)}, bf16[320,512]{1,0:T(8,128)(2,1)S(1)}, u32[]{:S(2)}, u32[]{:S(2)}) collective-permute-start(bf16[320,512]{1,0:T(8,128)(2,1)S(1)} %constant_dynamic-update-slice_fusion.refs_0_), channel_id=1, source_target_pairs={{0,8},{8,16},{16,24},{24,0},{1,9},{9,17},{17,25},{25,1},{2,10},{10... | collective-permute-start | bytes 983048 | tf_op jit(solution)/shard_map/ppermute | solution.py:33
  105.6 0.8 copy-start.11
  106.4 0.8 copy-start.13
  113.9 2.9 %copy-start.1 = (bf16[2560,1280]{1,0:T(8,128)(2,1)S(1)}, bf16[2560,1280]{1,0:T(8,128)(2,1)}, u32[]{:S(2)}) copy-start(bf16[2560,1280]{1,0:T(8,128)(2,1)} %all-gather.7.cloned.1.call-done) | copy-start | bytes 19660804
  116.8 1.0 copy-start.6
  117.8 1.0 copy-start.8
  118.8 1.0 copy-start.10
  119.8 1.0 copy-start.12
  120.8 1.0 copy-start.14
  131.1 11.1 %collective-permute-start.22 = (bf16[128,1280]{1,0:T(8,128)(2,1)S(1)}, bf16[128,1280]{1,0:T(8,128)(2,1)S(1)}, u32[]{:S(2)}, u32[]{:S(2)}) collective-permute-start(bf16[128,1280]{1,0:T(8,128)(2,1)S(1)} %get-tuple-element.30), channel_id=1, source_target_pairs={{0,8},{8,16},{16,24},{24,0},{1,9},{9,17},{17,25},{25,1},{2,10},{10... | collective-permute-start | bytes 983048 | tf_op jit(solution)/shard_map/ppermute | solution.py:33
  131.2 15.8 %collective-permute-start.23 = (bf16[128,1280]{1,0:T(8,128)(2,1)S(1)}, bf16[128,1280]{1,0:T(8,128)(2,1)S(1)}, u32[]{:S(2)}, u32[]{:S(2)}) collective-permute-start(bf16[128,1280]{1,0:T(8,128)(2,1)S(1)} %get-tuple-element.31), channel_id=1, source_target_pairs={{0,16},{8,24},{16,0},{24,8},{1,17},{9,25},{17,1},{25,9},{2,18},{10... | collective-permute-start | bytes 983048 | tf_op jit(solution)/shard_map/ppermute | solution.py:33
  134.4 12.8 %collective-permute-start.24 = (bf16[128,1280]{1,0:T(8,128)(2,1)S(1)}, bf16[128,1280]{1,0:T(8,128)(2,1)S(1)}, u32[]{:S(2)}, u32[]{:S(2)}) collective-permute-start(bf16[128,1280]{1,0:T(8,128)(2,1)S(1)} %get-tuple-element.32), channel_id=1, source_target_pairs={{0,24},{8,0},{16,8},{24,16},{1,25},{9,1},{17,9},{25,17},{2,26},{10... | collective-permute-start | bytes 983048 | tf_op jit(solution)/shard_map/ppermute | solution.py:33
  147.7 21.3 %copy-start.18 = (bf16[128,1280]{1,0:T(8,128)(2,1)S(1)}, bf16[128,1280]{1,0:T(8,128)(2,1)}, u32[]{:S(2)}) copy-start(bf16[128,1280]{1,0:T(8,128)(2,1)} %param.20) | copy-start | bytes 983044
Sparse Core Ops, SparseCore 0:
  9.0 28.3 all-gather.4
  39.1 50.0 all-gather.6

commit v3 on v2

--- a/solution.py
+++ b/solution.py
@@ -14,6 +14,7 @@
 F32 = jnp.float32
 NT = (((1,), (1,)), ((), ()))
 TN = (((0,), (0,)), ((), ()))
+HBM = pl.BlockSpec(memory_space=pltpu.HBM)
 VMEM = pl.BlockSpec(memory_space=pltpu.VMEM)
 SMEM = pl.BlockSpec(memory_space=pltpu.SMEM)
 
@@ -31,6 +32,10 @@
 def shift(value, axis, step):
     pairs = [(i, (i + step) % N) for i in range(N)]
     return lax.ppermute(value, axis, pairs)
+
+
+def far(value):
+    return pltpu.with_memory_space_constraint(value, pltpu.HBM)
 
 
 def swap(value):
@@ -48,8 +53,11 @@
         h1[1, at, :] = normed[:, half:]
 
 
-def qkv_kernel(pos, h1, w, o0, o1, o2, o3):
+def qkv_kernel(pos, h1, w_hbm, o0, o1, o2, o3, w, sem):
     x = pos[0]
+    copy = pltpu.make_async_copy(w_hbm.at[:, : w.shape[1], :], w, sem)
+    copy.start()
+    copy.wait()
     for k, out in enumerate((o0, o1, o2, o3)):
         at = lax.rem(x - k + N, N) * 2
         total = lax.dot_general(w[at], h1[0], NT, preferred_element_type=F32)
@@ -109,23 +117,50 @@
         out[...] = outs[k]
 
 
+def pack_kernel(pos, g0, g1, g2, g3, out):
+    x = pos[0]
+    for k, piece in enumerate((g0, g1, g2, g3)):
+        out[lax.rem(x - k + N, N)] = piece[...]
+
+
 def mlp_kernel(pos, *refs):
     gathered = refs[0:4]
     pieces = refs[4:8]
-    mine = refs[8:12]
-    other = refs[12:16]
-    gain, w_hbm, t0, t1, t2, t3, own, resid, w_mlp, sem = refs[16:]
+    gain, near, w_hbm = refs[8:11]
+    mine = refs[11:14]
+    other = refs[14:17]
+    merge_hbm = refs[17]
+    t0, t1, t2, t3, own, w_merge, resid, w_mine, w_other, up, down, sems = refs[18:]
     y = pos[1]
     c = pos[3]
     rows = pieces[0].shape[0]
-    copy = pltpu.make_async_copy(w_hbm, w_mlp, sem)
-    copy.start()
-    lhs = jnp.concatenate([g[...] for g in gathered], axis=0)
-    w_mine = jnp.concatenate([w[...] for w in mine], axis=0)
-    w_other = jnp.concatenate([w[...] for w in other], axis=0)
     half = w_mine.shape[1]
-    resid[c] = lax.dot_general(lhs, w_mine, TN, preferred_element_type=F32)
-    resid[1 - c] = lax.dot_general(lhs, w_other, TN, preferred_element_type=F32)
+    group = N * HEAD
+    skip = near.shape[1] - HEAD
+    first = []
+    for j in range(N):
+        to = pl.ds(j * HEAD, HEAD)
+        src = near.at[2 * j + c, skip : skip + HEAD, :]
+        first.append(pltpu.make_async_copy(src, w_mine.at[to, :], sems.at[j]))
+        src = near.at[2 * j + 1 - c, skip : skip + HEAD, :]
+        first.append(pltpu.make_async_copy(src, w_other.at[to, :], sems.at[N + j]))
+    for k in range(N - 1):
+        to = pl.ds((k + 1) * group, group)
+        first.append(pltpu.make_async_copy(mine[k], w_mine.at[to, :], sems.at[2 * N + k]))
+        first.append(pltpu.make_async_copy(other[k], w_other.at[to, :], sems.at[3 * N + k]))
+    units = up.shape[1]
+    second = [
+        pltpu.make_async_copy(w_hbm.at[:, :units, :], up, sems.at[4 * N]),
+        pltpu.make_async_copy(w_hbm.at[:, units:, :], down, sems.at[4 * N + 1]),
+    ]
+    ahead = pltpu.make_async_copy(merge_hbm, w_merge, sems.at[4 * N + 2])
+    for copy in first + second + [ahead]:
+        copy.start()
+    lhs = jnp.concatenate([g[...].reshape(group, N * rows) for g in gathered], axis=0)
+    for copy in first:
+        copy.wait()
+    resid[c] = lax.dot_general(lhs, w_mine[...], TN, preferred_element_type=F32)
+    resid[1 - c] = lax.dot_general(lhs, w_other[...], TN, preferred_element_type=F32)
     for k, piece in enumerate(pieces):
         at = pl.ds(pl.multiple_of(lax.rem(y - k + N, N) * rows, rows), rows)
         for h in (0, 1):
@@ -135,21 +170,40 @@
                 own[:, h * half : (h + 1) * half] = resid[h, at, :].astype(BF)
     full = jnp.concatenate([resid[0], resid[1]], axis=1)
     normed = norm_rows(full, gain[...]).astype(BF)
-    copy.wait()
-    count = w_mlp.shape[0]
-    units = w_mlp.shape[1] // 2
-    up = jnp.concatenate([w_mlp[i, :units, :] for i in range(count)], axis=0)
-    down = jnp.concatenate([w_mlp[i, units:, :] for i in range(count)], axis=0)
-    hidden = lax.dot_general(normed, up, NT, preferred_element_type=F32)
+    width = 2 * half
+    count = up.shape[0] * units
+    second[0].wait()
+    hidden = lax.dot_general(
+        normed, up[...].reshape(count, width), NT, preferred_element_type=F32
+    )
     hidden = (0.5 * hidden * (1.0 + lax.erf(hidden * math.sqrt(0.5)))).astype(BF)
-    result = jnp.dot(hidden, down, preferred_element_type=F32)
-    for h in range(N):
-        resid[0, h * rows : (h + 1) * rows, :] = result[h * rows : (h + 1) * rows, :half]
-        resid[1, h * rows : (h + 1) * rows, :] = result[h * rows : (h + 1) * rows, half:]
+    second[1].wait()
+    result = jnp.dot(hidden, down[...].reshape(count, width), preferred_element_type=F32)
+    resid[0] = result[:, :half]
+    resid[1] = result[:, half:]
     for k, out in enumerate((t0, t1, t2, t3)):
         at = pl.ds(pl.multiple_of(lax.rem(y + k, N) * rows, rows), rows)
         out[:, :half] = resid[0, at, :].astype(BF)
         out[:, half:] = resid[1, at, :].astype(BF)
+    ahead.wait()
+
+
+def merge_kernel(resid, t0, t1, t2, t3, w, select, tail, out, vision):
+    sums = t0[...].astype(F32) + t1[...].astype(F32) + t2[...].astype(F32) + t3[...].astype(F32)
+    sums = (resid[...].astype(F32) + sums).astype(BF).astype(F32)
+    full, width = resid.shape
+    count = full // 4
+    tiles = width // 128
+    for i in range(tiles):
+        vision[i * full : (i + 1) * full, :] = sums[:, i * 128 : (i + 1) * 128]
+    total = jnp.zeros((count, width), F32)
+    for j in range(4):
+        rows = [vision[pl.ds(i * full + j, count, stride=4), :] for i in range(tiles)]
+        rows = jnp.concatenate(rows, axis=1).astype(BF)
+        total += jnp.dot(rows, w[j * width : (j + 1) * width, :], preferred_element_type=F32)
+    sent = jnp.dot(select[...], total.astype(BF), preferred_element_type=F32)
+    out[:, :width] = sent.astype(BF)
+    out[:, width:] = tail[...]
 
 
 def local(
@@ -175,8 +229,9 @@
 
     half = width // 2
     w_heads = jnp.transpose(w_qkv, (0, 2, 1)).reshape(3 * HEAD, width)
+    w_heads = jnp.concatenate([w_heads, w_out], axis=0)
     w_half = lax.dynamic_slice_in_dim(w_heads, c * half, half, 1)
-    w_heads = lax.all_gather(w_half, ("x", "c"), axis=0, tiled=False)
+    near = lax.all_gather(w_half, ("x", "c"), axis=0, tiled=False)
     units = w_down.shape[0] // 2
     packed = jnp.concatenate(
         [
@@ -189,11 +244,11 @@
     w_near = lax.all_gather(packed, ("x", "c"), axis=0, tiled=False)
 
     pieces = [rows] + [shift(rows, "y", k) for k in (1, 2, 3)]
-    out_half = lax.dynamic_slice_in_dim(w_out, c * half, half, 1)
-    out_near = [out_half] + [shift(out_half, "x", k) for k in (1, 2, 3)]
-    out_near = jnp.concatenate(out_near, axis=0)
-    out_mine = [out_near] + [shift(out_near, "y", k) for k in (1, 2, 3)]
-    out_other = [swap(m) for m in out_mine]
+    mine = near.reshape(N, 2, near.shape[1], half)
+    mine = lax.dynamic_index_in_dim(mine, c, axis=1, keepdims=False)[:, 3 * HEAD :, :]
+    mine = mine.reshape(N * HEAD, half)
+    mine1 = shift(mine, "y", 1)
+    mine3 = shift(mine, "y", 3)
 
     total_rows = count * N
     h1 = pl.pallas_call(
@@ -207,12 +262,20 @@
     qkv = pl.pallas_call(
         qkv_kernel,
         out_shape=[jax.ShapeDtypeStruct((3 * HEAD, total_rows), BF)] * N,
-        in_specs=[SMEM] + [VMEM] * 2,
+        in_specs=[SMEM, VMEM, HBM],
         out_specs=[VMEM] * N,
+        scratch_shapes=[
+            pltpu.VMEM((2 * N, 3 * HEAD, half), BF),
+            pltpu.SemaphoreType.DMA(()),
+        ],
         compiler_params=params(16),
         name="qkv",
-    )(pos, h1, w_heads)
+    )(pos, h1, far(near))
     blocks = [qkv[0]] + [shift(qkv[k], "x", -k) for k in (1, 2, 3)]
+    blocks, mine, mine1, mine3 = lax.optimization_barrier((blocks, mine, mine1, mine3))
+    mine2 = shift(mine, "y", 2)
+    other1 = swap(mine1)
+    other3 = swap(mine3)
 
     group_rows = ids.shape[0]
     chunk = 256
@@ -242,31 +305,48 @@
         compiler_params=params(16),
         name="attend",
     )(pos, bounds, *blocks, ids[None, :], ids[:, None])
+    attended, mine2, other1, other3 = lax.optimization_barrier(
+        (attended, mine2, other1, other3)
+    )
+    other2 = swap(mine2)
     heads = [attended[0]] + [shift(attended[k], "x", k) for k in (1, 2, 3)]
-    heads = jnp.concatenate(heads, axis=0)
+    heads = pl.pallas_call(
+        pack_kernel,
+        out_shape=jax.ShapeDtypeStruct((N, HEAD, total_rows), BF),
+        in_specs=[SMEM] + [VMEM] * N,
+        out_specs=VMEM,
+        compiler_params=params(8),
+        name="pack",
+    )(pos, *heads)
     gathered = [heads] + [shift(heads, "y", k) for k in (1, 2, 3)]
 
-    *part, resid = pl.pallas_call(
+    *part, resid, w_merge = pl.pallas_call(
         mlp_kernel,
-        out_shape=[jax.ShapeDtypeStruct((count, width), BF)] * (N + 1),
-        in_specs=[SMEM] + [VMEM] * 17 + [pl.BlockSpec(memory_space=pl.ANY)],
-        out_specs=[VMEM] * (N + 1),
+        out_shape=[jax.ShapeDtypeStruct((count, width), BF)] * (N + 1)
+        + [jax.ShapeDtypeStruct(w_merge.shape, BF)],
+        in_specs=[SMEM] + [VMEM] * 9 + [HBM] * 9,
+        out_specs=[VMEM] * (N + 2),
         scratch_shapes=[
             pltpu.VMEM((2, total_rows, half), F32),
-            pltpu.VMEM(w_near.shape, BF),
-            pltpu.SemaphoreType.DMA(()),
+            pltpu.VMEM((N * N * HEAD, half), BF),
+            pltpu.VMEM((N * N * HEAD, half), BF),
+            pltpu.VMEM((2 * N, units, width), BF),
+            pltpu.VMEM((2 * N, units, width), BF),
+            pltpu.SemaphoreType.DMA((4 * N + 3,)),
         ],
-        compiler_params=params(40),
+        compiler_params=params(32),
         name="mlp",
-    )(pos, *gathered, *pieces, *out_mine, *out_other, ln_mlp[None, :], w_near)
-    sums = part[0].astype(F32)
-    for k in (1, 2, 3):
-        sums = sums + shift(part[k], "y", k).astype(F32)
-    vision = (resid.astype(F32) + sums).astype(BF)
-
-    merged = vision.reshape(count // 4, 4 * width)
-    projected = jnp.dot(merged, w_merge, preferred_element_type=F32).astype(BF)
-    merged_count = merged.shape[0]
+    )(
+        pos,
+        *gathered,
+        *pieces,
+        ln_mlp[None, :],
+        *[far(v) for v in (near, w_near, mine1, mine2, mine3)],
+        *[far(v) for v in (other1, other2, other3, w_merge)],
+    )
+    sums = [part[0]] + [shift(part[k], "y", k) for k in (1, 2, 3)]
+
+    merged_count = count // 4
     dest = slot_dest[0]
     prompt_rows = text_embed.shape[0]
     req_count = N * N
@@ -281,8 +361,15 @@
     places = jnp.sum(jnp.where(select, (dest % prompt_rows + 1)[None, :], 0), axis=1)
     lane = jnp.arange(128)[None, :] == 0
     tail = jnp.where(lane, places[:, None], 0).astype(BF)
-    outgoing = jnp.dot(select.astype(BF), projected, preferred_element_type=F32).astype(BF)
-    outgoing = jnp.concatenate([outgoing, tail], axis=1)
+    outgoing = pl.pallas_call(
+        merge_kernel,
+        out_shape=jax.ShapeDtypeStruct((req_count * slot_cap, width + 128), BF),
+        in_specs=[VMEM] * 8,
+        out_specs=VMEM,
+        scratch_shapes=[pltpu.VMEM((count * width // 128, 128), F32)],
+        compiler_params=params(8),
+        name="merge",
+    )(resid, *sums, w_merge, select.astype(BF), tail)
     arrived = lax.all_to_all(
         outgoing.reshape(req_count, slot_cap, width + 128),
         ("x", "y"),

time: 180 us -> 171 us (0.950); the launches traced: 177 us -> 170 us
  waiting for transfers between devices: 58.8 us -> 77.8 us
  local copies, waits for them, and re-layouts: 21.9 us -> 3.56 us
  matrix products: 8.29 us -> 1.09 us
  Pallas kernels: 21.7 us -> 27.8 us
  other arithmetic: 8.71 us -> 4.85 us
    all_gather x1, waiting for transfers between devices: 0.01 us -> 22.4 us  [local(): near = lax.all_gather(w_half, ('x', 'c'), axis=0, tiled=False)]
    unnamed x44 -> x23, local copies, waits for them, and re-layouts: 16.7 us -> 0.63 us
    dot_general x1 -> x0, matrix products: 7.2 us -> none  [local(): jnp.dot(select.astype(BF), projected, preferred_element_type=F32).astype(BF)]
    ppermute x21 -> x18, waiting for transfers between devices: 58.8 us -> 55.4 us  [shift(): return lax.ppermute(value, axis, pairs)]
    pallas_call x0 -> x2, Pallas kernels: none -> 3.09 us  [the longest x1 2.53 us: local(): pl.pallas_call(merge_kernel, out_shape=jax.ShapeDtypeStruct((req_count *...]
    dynamic_slice x2 -> x0, local copies, waits for them, and re-layouts: 2.69 us -> none  [the longest x1 1.79 us: local(): w_half = lax.dynamic_slice_in_dim(w_heads, c * half, half, 1)]
    select_n x2 -> x1, other arithmetic: 1.88 us -> 0.02 us  [local(): owner = jnp.where(dest >= 0, dest // prompt_rows // row_count, -1)]
    concatenate x2 -> x1, other arithmetic: 0.05 us -> 1.9 us  [local(): w_heads = jnp.concatenate([w_heads, w_out], axis=0)]
  transfers between devices with their start and end apart: 27 -> 23, of which waited for: 13 -> 12; matrix products, arithmetic and copies ran while one was open for 7% -> 4% of each run, Pallas kernels for 7% -> 8%
where the time goes in v3:
time: 171 us; the launch traced here: 170 us
  waiting for transfers between devices  77.8 us (45%)
  starting transfers between devices  28.5 us (17%)
  Pallas kernels  27.8 us (16%)
  between operations  13.7 us (8%)
  blocking collectives  13 us (8%)
  other arithmetic  4.85 us (3%)
  local copies, waits for them, and re-layouts  3.56 us (2%)
    ppermute x18, waiting for transfers between devices, shift(): return lax.ppermute(value, axis, pairs)  55.4 us
    ppermute x18, starting transfers between devices, shift(): return lax.ppermute(value, axis, pairs)  28.3 us
    all_gather x1, waiting for transfers between devices, local(): near = lax.all_gather(w_half, ('x', 'c'), axis=0, tiled=False)  22.4 us
    all_to_all x1, blocking collectives, local(): lax.all_to_all(outgoing.reshape(req_count, slot_cap, width + 128), ('x',...  13 us
    pallas_call x1, Pallas kernels, local(): pl.pallas_call(mlp_kernel, out_shape=[jax.ShapeDtypeStruct((count, width)...  10.9 us
    pallas_call x1, Pallas kernels, local(): pl.pallas_call(attend_kernel, out_shape=[jax.ShapeDtypeStruct((HEAD, tota...  7.59 us
    pallas_call x1, Pallas kernels, local(): pl.pallas_call(qkv_kernel, out_shape=[jax.ShapeDtypeStruct((3 * HEAD, tot...  4.74 us
  transfers between devices with their start and end apart: 23, of which 12 were waited for; matrix products, arithmetic and copies ran while one was open for 4% of the time, Pallas kernels for 8%

profile of v3, /device:TPU:0, one launch (start us, length us, event | category | flops | bytes accessed | tf_op | source)
XLA Modules:
  0.0 170.3 jit_solution(901918314319612022)
XLA Ops:
  6.5 1.9 %fusion.1 = bf16[320,640]{1,0:T(8,128)(2,1)} fusion(s32[]{:T(128)S(6)} %select_n.80, bf16[240,1280]{1,0:T(8,128)(2,1)} %bitcast.53, bf16[80,1280]{1,0:T(8,128)(2,1)} %param.15), kind=kLoop, calls=%fused_computation.6 | loop fusion | flops 819200 | bytes 1228804 | tf_op jit(solution)/shard_map/concatenate | solution.py:232
  8.4 0.0 all-gather.5.cloned.1.call-update
  8.5 0.0 all-gather.7.cloned.1.call-start
  8.6 0.0 copy-start.1
  8.6 0.0 copy-start.8
  8.6 0.0 copy-start.2
  8.6 0.0 copy-start.10
  8.7 1.0 pad_maximum_fusion
  9.6 0.0 all-gather.7.cloned.1.call-update
  9.7 1.7 %collective-permute-start = (bf16[128,1280]{1,0:T(8,128)(2,1)S(1)}, bf16[128,1280]{1,0:T(8,128)(2,1)S(1)}, u32[]{:S(2)}, u32[]{:S(2)}) collective-permute-start(bf16[128,1280]{1,0:T(8,128)(2,1)S(1)} %bitcast.43), channel_id=1, source_target_pairs={{0,8},{8,16},{16,24},{24,0},{1,9},{9,17},{17,25},{25,1},{2,10},{10... | collective-permute-start | bytes 983048 | tf_op jit(solution)/shard_map/ppermute | solution.py:34
  11.4 2.9 %collective-permute-start.1 = (bf16[128,1280]{1,0:T(8,128)(2,1)S(1)}, bf16[128,1280]{1,0:T(8,128)(2,1)S(1)}, u32[]{:S(2)}, u32[]{:S(2)}) collective-permute-start(bf16[128,1280]{1,0:T(8,128)(2,1)S(1)} %bitcast.44), channel_id=1, source_target_pairs={{0,16},{8,24},{16,0},{24,8},{1,17},{9,25},{17,1},{25,9},{2,18},{10... | collective-permute-start | bytes 983048 | tf_op jit(solution)/shard_map/ppermute | solution.py:34
  14.3 1.3 collective-permute-start.2
  15.7 0.6 broadcast.195
  16.2 0.7 reduce.5
  17.0 0.2 fusion.2
  17.2 0.2 and_reduce_fusion
  17.4 22.4 %all-gather.5.cloned.1.call-done = bf16[2560,640]{1,0:T(8,128)(2,1)} async-done(((bf16[320,640]{1,0:T(8,128)(2,1)}), bf16[2560,640]{1,0:T(8,128)(2,1)}) %all-gather.5.cloned.1.call-update) | async-done | bytes 3276816 | tf_op jit(solution)/shard_map/all_gather | solution.py:234
  39.8 1.6 dynamic-slice_bitcast_fusion
  41.4 0.8 slice.12
  42.2 1.5 collective-permute-start.6
  43.7 1.8 %collective-permute-start.7 = (bf16[320,640]{1,0:T(8,128)(2,1)}, bf16[320,640]{1,0:T(8,128)(2,1)}, u32[]{:S(2)}, u32[]{:S(2)}) collective-permute-start(bf16[320,640]{1,0:T(8,128)(2,1)} %bitcast.12), channel_id=1, source_target_pairs={{0,24},{8,0},{16,8},{24,16},{1,25},{9,1},{17,9},{25,17},{2,26},{10... | collective-permute-start | bytes 1228808 | tf_op jit(solution)/shard_map/ppermute | solution.py:34
  45.4 0.1 pad_add_fusion.1.pos
  45.5 1.4 norm.1.h1
  46.9 4.7 %qkv.1 = (bf16[240,512]{1,0:T(8,128)(2,1)S(1)}, bf16[240,512]{1,0:T(8,128)(2,1)}, bf16[240,512]{1,0:T(8,128)(2,1)}, bf16[240,512]{1,0:T(8,128)(2,1)}) custom-call(s32[4]{0:T(128)S(1)} %pad_add_fusion.1.pos, bf16[2,512,640]{2,1,0:T(8,128)(2,1)S(1)} %norm.1.h1, bf16[8,320,640]{2,1,0:T(8,128)(2,1)} %bitcast.50), custom_call_target="tpu_custom_call" | custom-call | tf_op jit(solution)/shard_map/qkv/pallas_call | solution.py:262
  51.7 1.5 collective-permute-start.3
  53.2 1.0 collective-permute-start.4
  54.2 0.6 collective-permute-start.5
  54.8 0.1 select_reduce_fusion.2
  54.9 0.4 copy.19.id_col
  55.3 10.3 %collective-permute-done.3.r1 = bf16[240,512]{1,0:T(8,128)(2,1)} collective-permute-done((bf16[240,512]{1,0:T(8,128)(2,1)}, bf16[240,512]{1,0:T(8,128)(2,1)}, u32[]{:S(2)}, u32[]{:S(2)}) %collective-permute-start.3) | collective-permute-done | bytes 245792 | tf_op jit(solution)/shard_map/ppermute | solution.py:34
  65.6 3.4 %collective-permute-done.4.r2 = bf16[240,512]{1,0:T(8,128)(2,1)} collective-permute-done((bf16[240,512]{1,0:T(8,128)(2,1)}, bf16[240,512]{1,0:T(8,128)(2,1)}, u32[]{:S(2)}, u32[]{:S(2)}) %collective-permute-start.4) | collective-permute-done | bytes 245792 | tf_op jit(solution)/shard_map/ppermute | solution.py:34
  69.1 7.0 %collective-permute-done.5.r3 = bf16[240,512]{1,0:T(8,128)(2,1)} collective-permute-done((bf16[240,512]{1,0:T(8,128)(2,1)}, bf16[240,512]{1,0:T(8,128)(2,1)}, u32[]{:S(2)}, u32[]{:S(2)}) %collective-permute-start.5) | collective-permute-done | bytes 245792 | tf_op jit(solution)/shard_map/ppermute | solution.py:34
  76.1 1.8 %collective-permute-start.8 = (bf16[320,640]{1,0:T(8,128)(2,1)}, bf16[320,640]{1,0:T(8,128)(2,1)S(1)}, u32[]{:S(2)}, u32[]{:S(2)}) collective-permute-start(bf16[320,640]{1,0:T(8,128)(2,1)} %bitcast.12), channel_id=1, source_target_pairs={{0,16},{8,24},{16,0},{24,8},{1,17},{9,25},{17,1},{25,9},{2,18},{10... | collective-permute-start | bytes 1228808 | tf_op jit(solution)/shard_map/ppermute | solution.py:34
  77.9 0.2 collective-permute-start.9
  78.1 0.2 convert_reduce_fusion
  78.3 7.6 %attend.1 = (bf16[80,512]{1,0:T(8,128)(2,1)S(1)}, bf16[80,512]{1,0:T(8,128)(2,1)S(1)}, bf16[80,512]{1,0:T(8,128)(2,1)S(1)}, bf16[80,512]{1,0:T(8,128)(2,1)S(1)}) custom-call(s32[4]{0:T(128)S(1)} %pad_add_fusion.1.pos, s32[2,4]{1,0:T(2,128)S(1)} %pad_add_fusion.bounds, bf16[240,512]{1,0:T(8,128)(2,1)S(1)} %get-tuple-element.38.r0, ...), custom_call_target="tpu_custom_call" | custom-call | tf_op jit(solution)/shard_map/attend/pallas_call | solution.py:293
  85.9 3.8 %collective-permute-done.8.refs_12_ = bf16[320,640]{1,0:T(8,128)(2,1)S(1)} collective-permute-done((bf16[320,640]{1,0:T(8,128)(2,1)}, bf16[320,640]{1,0:T(8,128)(2,1)S(1)}, u32[]{:S(2)}, u32[]{:S(2)}) %collective-permute-start.8) | collective-permute-done | bytes 409632 | tf_op jit(solution)/shard_map/ppermute | solution.py:34
  89.7 2.5 %collective-permute-start.11 = (bf16[80,512]{1,0:T(8,128)(2,1)S(1)}, bf16[80,512]{1,0:T(8,128)(2,1)S(1)}, u32[]{:S(2)}, u32[]{:S(2)}) collective-permute-start(bf16[80,512]{1,0:T(8,128)(2,1)S(1)} %get-tuple-element.50), channel_id=1, source_target_pairs={{0,32},{32,64},{64,96},{96,0},{1,33},{33,65},{65,97},{97,1},{2,34}... | collective-permute-start | bytes 245768 | tf_op jit(solution)/shard_map/ppermute | solution.py:34
  92.3 2.4 %collective-permute-start.12 = (bf16[80,512]{1,0:T(8,128)(2,1)S(1)}, bf16[80,512]{1,0:T(8,128)(2,1)S(1)}, u32[]{:S(2)}, u32[]{:S(2)}) collective-permute-start(bf16[80,512]{1,0:T(8,128)(2,1)S(1)} %get-tuple-element.51), channel_id=1, source_target_pairs={{0,64},{32,96},{64,0},{96,32},{1,65},{33,97},{65,1},{97,33},{2,66}... | collective-permute-start | bytes 245768 | tf_op jit(solution)/shard_map/ppermute | solution.py:34
  94.7 0.3 collective-permute-start.13
  95.1 0.6 collective-permute-done.11.g1
  95.7 2.8 %collective-permute-done.12.g2 = bf16[80,512]{1,0:T(8,128)(2,1)S(1)} collective-permute-done((bf16[80,512]{1,0:T(8,128)(2,1)S(1)}, bf16[80,512]{1,0:T(8,128)(2,1)S(1)}, u32[]{:S(2)}, u32[]{:S(2)}) %collective-permute-start.12) | collective-permute-done | bytes 81952 | tf_op jit(solution)/shard_map/ppermute | solution.py:34
  98.4 0.7 collective-permute-done.13.g3
  99.2 0.6 pack.1.refs_0_
  99.7 0.3 collective-permute-start.14
  100.0 2.7 %collective-permute-start.15 = (bf16[4,80,512]{2,1,0:T(8,128)(2,1)S(1)}, bf16[4,80,512]{2,1,0:T(8,128)(2,1)S(1)}, u32[]{:S(2)}, u32[]{:S(2)}) collective-permute-start(bf16[4,80,512]{2,1,0:T(8,128)(2,1)S(1)} %pack.1.refs_0_), channel_id=1, source_target_pairs={{0,16},{8,24},{16,0},{24,8},{1,17},{9,25},{17,1},{25,9},{2,18},{10... | collective-permute-start | bytes 983048 | tf_op jit(solution)/shard_map/ppermute | solution.py:34
  102.7 1.4 collective-permute-start.16
  104.2 0.1 select_reduce_fusion
  104.3 11.8 %collective-permute-done.14.refs_1_ = bf16[4,80,512]{2,1,0:T(8,128)(2,1)S(1)} collective-permute-done((bf16[4,80,512]{2,1,0:T(8,128)(2,1)S(1)}, bf16[4,80,512]{2,1,0:T(8,128)(2,1)S(1)}, u32[]{:S(2)}, u32[]{:S(2)}) %collective-permute-start.14) | collective-permute-done | bytes 327712 | tf_op jit(solution)/shard_map/ppermute | solution.py:34
  116.1 0.6 collective-permute-done.16.refs_3_
  116.7 0.0 all-gather.7.cloned.1.call-done
  116.8 10.9 %mlp.1 = (bf16[128,1280]{1,0:T(8,128)(2,1)S(1)}, bf16[128,1280]{1,0:T(8,128)(2,1)S(1)}, bf16[128,1280]{1,0:T(8,128)(2,1)S(1)}, bf16[128,1280]{1,0:T(8,128)(2,1)S...) custom-call(s32[4]{0:T(128)S(1)} %pad_add_fusion.1.pos, bf16[4,80,512]{2,1,0:T(8,128)(2,1)S(1)} %pack.1.refs_0_, ...), custom_call_target="tpu_custom_call" | custom-call | tf_op jit(solution)/shard_map/mlp/pallas_call | solution.py:323
  127.7 1.2 collective-permute-start.18
  128.9 3.0 %collective-permute-start.19 = (bf16[128,1280]{1,0:T(8,128)(2,1)S(1)}, bf16[128,1280]{1,0:T(8,128)(2,1)S(1)}, u32[]{:S(2)}, u32[]{:S(2)}) collective-permute-start(bf16[128,1280]{1,0:T(8,128)(2,1)S(1)} %get-tuple-element.60), channel_id=1, source_target_pairs={{0,16},{8,24},{16,0},{24,8},{1,17},{9,25},{17,1},{25,9},{2,18},{10... | collective-permute-start | bytes 983048 | tf_op jit(solution)/shard_map/ppermute | solution.py:34
  131.9 0.3 collective-permute-start.20
  132.2 0.1 select_convert_fusion.tail
  132.3 6.1 %collective-permute-done.18.t1 = bf16[128,1280]{1,0:T(8,128)(2,1)S(1)} collective-permute-done((bf16[128,1280]{1,0:T(8,128)(2,1)S(1)}, bf16[128,1280]{1,0:T(8,128)(2,1)S(1)}, u32[]{:S(2)}, u32[]{:S(2)}) %collective-permute-start.18) | collective-permute-done | bytes 327712 | tf_op jit(solution)/shard_map/ppermute | solution.py:34
  138.3 8.2 %collective-permute-done.19.t2 = bf16[128,1280]{1,0:T(8,128)(2,1)S(1)} collective-permute-done((bf16[128,1280]{1,0:T(8,128)(2,1)S(1)}, bf16[128,1280]{1,0:T(8,128)(2,1)S(1)}, u32[]{:S(2)}, u32[]{:S(2)}) %collective-permute-start.19) | collective-permute-done | bytes 327712 | tf_op jit(solution)/shard_map/ppermute | solution.py:34
  146.5 2.5 %merge.1 = bf16[32,1408]{1,0:T(8,128)(2,1)S(1)} custom-call(bf16[128,1280]{1,0:T(8,128)(2,1)S(1)} %get-tuple-element.57.resid, bf16[128,1280]{1,0:T(8,128)(2,1)S(1)} %get-tuple-element.58.t0, bf16[128,1280]{1,0:T(8,128)(2,1)S(1)} %collective-permute-done.18.t1, bf16[128,1280]{1,0:T(8,128)(2,1)S(1)} %collective-permute-done.19.t2, ...), custom_call_target="tpu_custom_call" | custom-call | tf_op jit(solution)/shard_map/merge/pallas_call | solution.py:364
  149.1 0.1 reshape.118
  149.1 13.0 %all_to_all.5 = bf16[16,2,1408]{2,1,0:T(2,128)(2,1)S(1)} all-to-all(bf16[16,2,1408]{2,1,0:T(2,128)(2,1)S(1)} %reshape.118), channel_id=1, replica_groups=mesh['x'=4,'y'=4,'z'=4,'c'=2] {'x','y'}, dimensions={0} | all-to-all | bytes 180224 | tf_op jit(solution)/shard_map/all_to_all | solution.py:373
  162.2 0.1 add_reduce_fusion
  162.3 0.1 fusion.4
  162.4 1.1 fusion
  (47 shorter events, 0.3 us)
Async XLA Ops:
  6.5 2.0 %copy-start = (bf16[320,1280]{1,0:T(8,128)(2,1)S(1)}, bf16[320,1280]{1,0:T(8,128)(2,1)}, u32[]{:S(2)}) copy-start(bf16[320,1280]{1,0:T(8,128)(2,1)} %param.18) | copy-start | bytes 2457604
  6.5 2.0 %copy-start.7 = (bf16[1280,320]{0,1:T(8,128)(2,1)S(1)}, bf16[1280,320]{0,1:T(8,128)(2,1)}, u32[]{:S(2)}) copy-start(bf16[1280,320]{0,1:T(8,128)(2,1)} %param.17) | copy-start | bytes 2457604
  6.5 33.3 %all-gather.5.cloned.1.call-start = ((), (), s32[]{:S(2)}) async-start(), calls=%async_computation.1 | async-start | bytes 3686400 | tf_op jit(solution)/shard_map/all_gather | solution.py:234
  8.5 108.3 %all-gather.7.cloned.1.call-start = ((), (), s32[]{:S(2)}) async-start(), calls=%async_computation.2 | async-start | bytes 7372800 | tf_op jit(solution)/shard_map/all_gather | solution.py:244
  8.6 1.1 copy-start.1
  8.6 7.1 %copy-start.8 = (f32[1280]{0:T(1024)S(1)}, f32[1280]{0:T(1024)}, u32[]{:S(2)}) copy-start(f32[1280]{0:T(1024)} %param.13) | copy-start | bytes 15364
  8.6 7.6 %copy-start.2 = (s32[1,2048]{1,0:T(1,128)S(1)}, s32[1,2048]{1,0:T(1,128)}, u32[]{:S(2)}) copy-start(s32[1,2048]{1,0:T(1,128)} %id_row.1) | copy-start | bytes 24580
  8.6 8.8 %copy-start.10 = (s32[1,32]{1,0:T(1,128)S(1)}, s32[1,32]{1,0:T(1,128)}, u32[]{:S(2)}) copy-start(s32[1,32]{1,0:T(1,128)} %param.21) | copy-start | bytes 388
  9.7 35.8 %collective-permute-start = (bf16[128,1280]{1,0:T(8,128)(2,1)S(1)}, bf16[128,1280]{1,0:T(8,128)(2,1)S(1)}, u32[]{:S(2)}, u32[]{:S(2)}) collective-permute-start(bf16[128,1280]{1,0:T(8,128)(2,1)S(1)} %bitcast.43), channel_id=1, source_target_pairs={{0,8},{8,16},{16,24},{24,0},{1,9},{9,17},{17,25},{25,1},{2,10},{10... | collective-permute-start | bytes 983048 | tf_op jit(solution)/shard_map/ppermute | solution.py:34
  11.4 34.1 %collective-permute-start.1 = (bf16[128,1280]{1,0:T(8,128)(2,1)S(1)}, bf16[128,1280]{1,0:T(8,128)(2,1)S(1)}, u32[]{:S(2)}, u32[]{:S(2)}) collective-permute-start(bf16[128,1280]{1,0:T(8,128)(2,1)S(1)} %bitcast.44), channel_id=1, source_target_pairs={{0,16},{8,24},{16,0},{24,8},{1,17},{9,25},{17,1},{25,9},{2,18},{10... | collective-permute-start | bytes 983048 | tf_op jit(solution)/shard_map/ppermute | solution.py:34
  14.3 31.2 %collective-permute-start.2 = (bf16[128,1280]{1,0:T(8,128)(2,1)S(1)}, bf16[128,1280]{1,0:T(8,128)(2,1)S(1)}, u32[]{:S(2)}, u32[]{:S(2)}) collective-permute-start(bf16[128,1280]{1,0:T(8,128)(2,1)S(1)} %bitcast.45), channel_id=1, source_target_pairs={{0,24},{8,0},{16,8},{24,16},{1,25},{9,1},{17,9},{25,17},{2,26},{10... | collective-permute-start | bytes 983048 | tf_op jit(solution)/shard_map/ppermute | solution.py:34
  42.2 33.9 %collective-permute-start.6 = (bf16[320,640]{1,0:T(8,128)(2,1)}, bf16[320,640]{1,0:T(8,128)(2,1)}, u32[]{:S(2)}, u32[]{:S(2)}) collective-permute-start(bf16[320,640]{1,0:T(8,128)(2,1)} %bitcast.12), channel_id=1, source_target_pairs={{0,8},{8,16},{16,24},{24,0},{1,9},{9,17},{17,25},{25,1},{2,10},{10... | collective-permute-start | bytes 1228808 | tf_op jit(solution)/shard_map/ppermute | solution.py:34
  43.7 32.4 %collective-permute-start.7 = (bf16[320,640]{1,0:T(8,128)(2,1)}, bf16[320,640]{1,0:T(8,128)(2,1)}, u32[]{:S(2)}, u32[]{:S(2)}) collective-permute-start(bf16[320,640]{1,0:T(8,128)(2,1)} %bitcast.12), channel_id=1, source_target_pairs={{0,24},{8,0},{16,8},{24,16},{1,25},{9,1},{17,9},{25,17},{2,26},{10... | collective-permute-start | bytes 1228808 | tf_op jit(solution)/shard_map/ppermute | solution.py:34
  51.7 43.4 %copy-start.9 = (f32[1280]{0:T(1024)S(1)}, f32[1280]{0:T(1024)}, u32[]{:S(2)}) copy-start(f32[1280]{0:T(1024)} %param.16) | copy-start | bytes 15364
  51.7 14.0 %collective-permute-start.3 = (bf16[240,512]{1,0:T(8,128)(2,1)}, bf16[240,512]{1,0:T(8,128)(2,1)}, u32[]{:S(2)}, u32[]{:S(2)}) collective-permute-start(bf16[240,512]{1,0:T(8,128)(2,1)} %get-tuple-element.35), channel_id=1, source_target_pairs={{0,96},{32,0},{64,32},{96,64},{1,97},{33,1},{65,33},{97,65},{2,98}... | collective-permute-start | bytes 737288 | tf_op jit(solution)/shard_map/ppermute | solution.py:34
  53.2 15.9 %collective-permute-start.4 = (bf16[240,512]{1,0:T(8,128)(2,1)}, bf16[240,512]{1,0:T(8,128)(2,1)}, u32[]{:S(2)}, u32[]{:S(2)}) collective-permute-start(bf16[240,512]{1,0:T(8,128)(2,1)} %get-tuple-element.36), channel_id=1, source_target_pairs={{0,64},{32,96},{64,0},{96,32},{1,65},{33,97},{65,1},{97,33},{2,66}... | collective-permute-start | bytes 737288 | tf_op jit(solution)/shard_map/ppermute | solution.py:34
  54.2 21.9 %collective-permute-start.5 = (bf16[240,512]{1,0:T(8,128)(2,1)}, bf16[240,512]{1,0:T(8,128)(2,1)}, u32[]{:S(2)}, u32[]{:S(2)}) collective-permute-start(bf16[240,512]{1,0:T(8,128)(2,1)} %get-tuple-element.37), channel_id=1, source_target_pairs={{0,32},{32,64},{64,96},{96,0},{1,33},{33,65},{65,97},{97,1},{2,34}... | collective-permute-start | bytes 737288 | tf_op jit(solution)/shard_map/ppermute | solution.py:34
  76.1 9.8 %collective-permute-start.10 = (bf16[320,640]{1,0:T(8,128)(2,1)}, bf16[320,640]{1,0:T(8,128)(2,1)S(1)}, u32[]{:S(2)}, u32[]{:S(2)}) collective-permute-start(bf16[320,640]{1,0:T(8,128)(2,1)} %collective-permute-done.7.refs_13_), channel_id=1, source_target_pairs={{0,1},{1,0},{2,3},{3,2},{4,5},{5,4},{6,7},{7,6},{8,9},{9,8},{10,11... | collective-permute-start | bytes 1228808 | tf_op jit(solution)/shard_map/ppermute | solution.py:42
  76.1 13.6 %collective-permute-start.8 = (bf16[320,640]{1,0:T(8,128)(2,1)}, bf16[320,640]{1,0:T(8,128)(2,1)S(1)}, u32[]{:S(2)}, u32[]{:S(2)}) collective-permute-start(bf16[320,640]{1,0:T(8,128)(2,1)} %bitcast.12), channel_id=1, source_target_pairs={{0,16},{8,24},{16,0},{24,8},{1,17},{9,25},{17,1},{25,9},{2,18},{10... | collective-permute-start | bytes 1228808 | tf_op jit(solution)/shard_map/ppermute | solution.py:34
  77.9 11.8 %collective-permute-start.9 = (bf16[320,640]{1,0:T(8,128)(2,1)}, bf16[320,640]{1,0:T(8,128)(2,1)S(1)}, u32[]{:S(2)}, u32[]{:S(2)}) collective-permute-start(bf16[320,640]{1,0:T(8,128)(2,1)} %collective-permute-done.6.refs_11_), channel_id=1, source_target_pairs={{0,1},{1,0},{2,3},{3,2},{4,5},{5,4},{6,7},{7,6},{8,9},{9,8},{10,11... | collective-permute-start | bytes 1228808 | tf_op jit(solution)/shard_map/ppermute | solution.py:42
  85.9 30.9 %copy-start.3 = (bf16[320,640]{1,0:T(8,128)(2,1)}, bf16[320,640]{1,0:T(8,128)(2,1)S(1)}, u32[]{:S(2)}) copy-start(bf16[320,640]{1,0:T(8,128)(2,1)S(1)} %collective-permute-done.10.refs_16_) | copy-start | bytes 1228804
  89.7 27.0 %copy-start.4 = (bf16[320,640]{1,0:T(8,128)(2,1)}, bf16[320,640]{1,0:T(8,128)(2,1)S(1)}, u32[]{:S(2)}) copy-start(bf16[320,640]{1,0:T(8,128)(2,1)S(1)} %collective-permute-done.8.refs_12_) | copy-start | bytes 1228804
  89.7 27.0 %copy-start.5 = (bf16[320,640]{1,0:T(8,128)(2,1)}, bf16[320,640]{1,0:T(8,128)(2,1)S(1)}, u32[]{:S(2)}) copy-start(bf16[320,640]{1,0:T(8,128)(2,1)S(1)} %collective-permute-done.9.refs_14_) | copy-start | bytes 1228804
  89.7 6.0 %collective-permute-start.11 = (bf16[80,512]{1,0:T(8,128)(2,1)S(1)}, bf16[80,512]{1,0:T(8,128)(2,1)S(1)}, u32[]{:S(2)}, u32[]{:S(2)}) collective-permute-start(bf16[80,512]{1,0:T(8,128)(2,1)S(1)} %get-tuple-element.50), channel_id=1, source_target_pairs={{0,32},{32,64},{64,96},{96,0},{1,33},{33,65},{65,97},{97,1},{2,34}... | collective-permute-start | bytes 245768 | tf_op jit(solution)/shard_map/ppermute | solution.py:34
  92.3 6.2 %collective-permute-start.12 = (bf16[80,512]{1,0:T(8,128)(2,1)S(1)}, bf16[80,512]{1,0:T(8,128)(2,1)S(1)}, u32[]{:S(2)}, u32[]{:S(2)}) collective-permute-start(bf16[80,512]{1,0:T(8,128)(2,1)S(1)} %get-tuple-element.51), channel_id=1, source_target_pairs={{0,64},{32,96},{64,0},{96,32},{1,65},{33,97},{65,1},{97,33},{2,66}... | collective-permute-start | bytes 245768 | tf_op jit(solution)/shard_map/ppermute | solution.py:34
  94.7 4.4 %collective-permute-start.13 = (bf16[80,512]{1,0:T(8,128)(2,1)S(1)}, bf16[80,512]{1,0:T(8,128)(2,1)S(1)}, u32[]{:S(2)}, u32[]{:S(2)}) collective-permute-start(bf16[80,512]{1,0:T(8,128)(2,1)S(1)} %get-tuple-element.52), channel_id=1, source_target_pairs={{0,96},{32,0},{64,32},{96,64},{1,97},{33,1},{65,33},{97,65},{2,98}... | collective-permute-start | bytes 245768 | tf_op jit(solution)/shard_map/ppermute | solution.py:34
  95.0 21.7 %collective-permute-start.17 = (bf16[320,640]{1,0:T(8,128)(2,1)S(1)}, bf16[320,640]{1,0:T(8,128)(2,1)}, u32[]{:S(2)}, u32[]{:S(2)}) collective-permute-start(bf16[320,640]{1,0:T(8,128)(2,1)S(1)} %collective-permute-done.8.refs_12_), channel_id=1, source_target_pairs={{0,1},{1,0},{2,3},{3,2},{4,5},{5,4},{6,7},{7,6},{8,9},{9,8},{10,11... | collective-permute-start | bytes 1228808 | tf_op jit(solution)/shard_map/ppermute | solution.py:42
  99.7 16.4 %collective-permute-start.14 = (bf16[4,80,512]{2,1,0:T(8,128)(2,1)S(1)}, bf16[4,80,512]{2,1,0:T(8,128)(2,1)S(1)}, u32[]{:S(2)}, u32[]{:S(2)}) collective-permute-start(bf16[4,80,512]{2,1,0:T(8,128)(2,1)S(1)} %pack.1.refs_0_), channel_id=1, source_target_pairs={{0,8},{8,16},{16,24},{24,0},{1,9},{9,17},{17,25},{25,1},{2,10},{10... | collective-permute-start | bytes 983048 | tf_op jit(solution)/shard_map/ppermute | solution.py:34
  100.0 16.1 %collective-permute-start.15 = (bf16[4,80,512]{2,1,0:T(8,128)(2,1)S(1)}, bf16[4,80,512]{2,1,0:T(8,128)(2,1)S(1)}, u32[]{:S(2)}, u32[]{:S(2)}) collective-permute-start(bf16[4,80,512]{2,1,0:T(8,128)(2,1)S(1)} %pack.1.refs_0_), channel_id=1, source_target_pairs={{0,16},{8,24},{16,0},{24,8},{1,17},{9,25},{17,1},{25,9},{2,18},{10... | collective-permute-start | bytes 983048 | tf_op jit(solution)/shard_map/ppermute | solution.py:34
  102.7 14.0 %collective-permute-start.16 = (bf16[4,80,512]{2,1,0:T(8,128)(2,1)S(1)}, bf16[4,80,512]{2,1,0:T(8,128)(2,1)S(1)}, u32[]{:S(2)}, u32[]{:S(2)}) collective-permute-start(bf16[4,80,512]{2,1,0:T(8,128)(2,1)S(1)} %pack.1.refs_0_), channel_id=1, source_target_pairs={{0,24},{8,0},{16,8},{24,16},{1,25},{9,1},{17,9},{25,17},{2,26},{10... | collective-permute-start | bytes 983048 | tf_op jit(solution)/shard_map/ppermute | solution.py:34
  127.7 10.6 %collective-permute-start.18 = (bf16[128,1280]{1,0:T(8,128)(2,1)S(1)}, bf16[128,1280]{1,0:T(8,128)(2,1)S(1)}, u32[]{:S(2)}, u32[]{:S(2)}) collective-permute-start(bf16[128,1280]{1,0:T(8,128)(2,1)S(1)} %get-tuple-element.59), channel_id=1, source_target_pairs={{0,8},{8,16},{16,24},{24,0},{1,9},{9,17},{17,25},{25,1},{2,10},{10... | collective-permute-start | bytes 983048 | tf_op jit(solution)/shard_map/ppermute | solution.py:34
  128.9 17.6 %collective-permute-start.19 = (bf16[128,1280]{1,0:T(8,128)(2,1)S(1)}, bf16[128,1280]{1,0:T(8,128)(2,1)S(1)}, u32[]{:S(2)}, u32[]{:S(2)}) collective-permute-start(bf16[128,1280]{1,0:T(8,128)(2,1)S(1)} %get-tuple-element.60), channel_id=1, source_target_pairs={{0,16},{8,24},{16,0},{24,8},{1,17},{9,25},{17,1},{25,9},{2,18},{10... | collective-permute-start | bytes 983048 | tf_op jit(solution)/shard_map/ppermute | solution.py:34
  131.9 14.6 %collective-permute-start.20 = (bf16[128,1280]{1,0:T(8,128)(2,1)S(1)}, bf16[128,1280]{1,0:T(8,128)(2,1)S(1)}, u32[]{:S(2)}, u32[]{:S(2)}) collective-permute-start(bf16[128,1280]{1,0:T(8,128)(2,1)S(1)} %get-tuple-element.61), channel_id=1, source_target_pairs={{0,24},{8,0},{16,8},{24,16},{1,25},{9,1},{17,9},{25,17},{2,26},{10... | collective-permute-start | bytes 983048 | tf_op jit(solution)/shard_map/ppermute | solution.py:34
  146.5 15.9 %copy-start.6 = (bf16[128,1280]{1,0:T(8,128)(2,1)S(1)}, bf16[128,1280]{1,0:T(8,128)(2,1)}, u32[]{:S(2)}) copy-start(bf16[128,1280]{1,0:T(8,128)(2,1)} %param.20) | copy-start | bytes 983044
Sparse Core Ops, SparseCore 0:
  9.0 30.7 all-gather.4
  41.5 52.4 all-gather.6

commit v4 on v3

--- a/solution.py
+++ b/solution.py
@@ -42,27 +42,44 @@
     return lax.ppermute(value, "c", [(0, 1), (1, 0)])
 
 
-def norm_kernel(pos, p0, p1, p2, p3, gain, h1):
+def norm_kernel(pos, p0, p1, p2, p3, gain, h1, held, sems):
     y = pos[1]
     half = h1.shape[2]
     rows = p0.shape[0]
+    copies = []
     for k, piece in enumerate((p0, p1, p2, p3)):
-        normed = norm_rows(piece[...].astype(F32), gain[...]).astype(BF)
+        copies.append(pltpu.make_async_copy(piece, held.at[k], sems.at[k]))
+    for copy in copies:
+        copy.start()
+    for k in range(N):
+        copies[k].wait()
+        normed = norm_rows(held[k].astype(F32), gain[...]).astype(BF)
         at = pl.ds(pl.multiple_of(lax.rem(y - k + N, N) * rows, rows), rows)
         h1[0, at, :] = normed[:, :half]
         h1[1, at, :] = normed[:, half:]
 
 
-def qkv_kernel(pos, h1, w_hbm, o0, o1, o2, o3, w, sem):
+def qkv_kernel(pos, h1, w_hbm, o0, o1, o2, o3, share, w, sems):
     x = pos[0]
-    copy = pltpu.make_async_copy(w_hbm.at[:, : w.shape[1], :], w, sem)
-    copy.start()
-    copy.wait()
+    c = pos[3]
+    cols = w.shape[1]
+    copies = []
+    for k in range(N):
+        at = pl.ds(lax.rem(x - k + N, N) * 2, 2)
+        copies.append(pltpu.make_async_copy(w_hbm.at[at, :cols, :], w.at[at], sems.at[k]))
+    for j in range(N):
+        src = w_hbm.at[2 * j + c, cols : cols + HEAD, :]
+        copies.append(pltpu.make_async_copy(src, share.at[j], sems.at[N + j]))
+    for copy in copies:
+        copy.start()
     for k, out in enumerate((o0, o1, o2, o3)):
         at = lax.rem(x - k + N, N) * 2
+        copies[k].wait()
         total = lax.dot_general(w[at], h1[0], NT, preferred_element_type=F32)
         total += lax.dot_general(w[at + 1], h1[1], NT, preferred_element_type=F32)
         out[...] = total.astype(BF)
+    for copy in copies[N:]:
+        copy.wait()
 
 
 def attend_kernel(
@@ -73,6 +90,8 @@
     block = qs.shape[2]
     per = block // chunk
     scale = math.log2(math.e) / math.sqrt(HEAD)
+    rows = block // N
+    y = pos[1]
     for k, piece in enumerate((r0, r1, r2, r3)):
         at = lax.rem(x + k, N)
         qs[at] = piece[:HEAD, :]
@@ -112,15 +131,18 @@
             jnp.zeros((HEAD, block), F32),
         )
         top, total, acc = lax.fori_loop(low, high, step, start)
-        outs[lax.rem(qb - x + N, N)] = (acc / total).astype(BF)
+        result = (acc / total).astype(BF)
+        for yb in range(N):
+            part = result[:, yb * rows : (yb + 1) * rows]
+            outs[lax.rem(yb - y + N, N), :, qb * rows : (qb + 1) * rows] = part
     for k, out in enumerate((o0, o1, o2, o3)):
         out[...] = outs[k]
 
 
 def pack_kernel(pos, g0, g1, g2, g3, out):
-    x = pos[0]
+    y = pos[1]
     for k, piece in enumerate((g0, g1, g2, g3)):
-        out[lax.rem(x - k + N, N)] = piece[...]
+        out[lax.rem(y - k + N, N)] = piece[...]
 
 
 def mlp_kernel(pos, *refs):
@@ -130,7 +152,8 @@
     mine = refs[11:14]
     other = refs[14:17]
     merge_hbm = refs[17]
-    t0, t1, t2, t3, own, w_merge, resid, w_mine, w_other, up, down, sems = refs[18:]
+    t0, t1, t2, t3, own, w_merge, resid, w_mine, w_other, up, down, held, sems = refs[18:]
+    x = pos[0]
     y = pos[1]
     c = pos[3]
     rows = pieces[0].shape[0]
@@ -138,22 +161,29 @@
     group = N * HEAD
     skip = near.shape[1] - HEAD
     first = []
-    for j in range(N):
-        to = pl.ds(j * HEAD, HEAD)
-        src = near.at[2 * j + c, skip : skip + HEAD, :]
-        first.append(pltpu.make_async_copy(src, w_mine.at[to, :], sems.at[j]))
-        src = near.at[2 * j + 1 - c, skip : skip + HEAD, :]
-        first.append(pltpu.make_async_copy(src, w_other.at[to, :], sems.at[N + j]))
-    for k in range(N - 1):
-        to = pl.ds((k + 1) * group, group)
-        first.append(pltpu.make_async_copy(mine[k], w_mine.at[to, :], sems.at[2 * N + k]))
-        first.append(pltpu.make_async_copy(other[k], w_other.at[to, :], sems.at[3 * N + k]))
+    for k in range(N):
+        for j in range(N):
+            at = (lax.rem(x - j + N, N) * N + lax.rem(y - k + N, N)) * HEAD
+            to = pl.ds(pl.multiple_of(at, 16), HEAD)
+            if k == 0:
+                sources = (
+                    near.at[2 * j + c, skip : skip + HEAD, :],
+                    near.at[2 * j + 1 - c, skip : skip + HEAD, :],
+                )
+            else:
+                sources = (mine[k - 1].at[j], other[k - 1].at[j])
+            for src, dst in zip(sources, (w_mine, w_other)):
+                sem = sems.at[len(first)]
+                first.append(pltpu.make_async_copy(src, dst.at[to, :], sem))
+    for k in range(N):
+        sem = sems.at[len(first)]
+        first.append(pltpu.make_async_copy(pieces[k], held.at[k], sem))
     units = up.shape[1]
     second = [
-        pltpu.make_async_copy(w_hbm.at[:, :units, :], up, sems.at[4 * N]),
-        pltpu.make_async_copy(w_hbm.at[:, units:, :], down, sems.at[4 * N + 1]),
+        pltpu.make_async_copy(w_hbm.at[:, :units, :], up, sems.at[36]),
+        pltpu.make_async_copy(w_hbm.at[:, units:, :], down, sems.at[37]),
     ]
-    ahead = pltpu.make_async_copy(merge_hbm, w_merge, sems.at[4 * N + 2])
+    ahead = pltpu.make_async_copy(merge_hbm, w_merge, sems.at[38])
     for copy in first + second + [ahead]:
         copy.start()
     lhs = jnp.concatenate([g[...].reshape(group, N * rows) for g in gathered], axis=0)
@@ -161,10 +191,10 @@
         copy.wait()
     resid[c] = lax.dot_general(lhs, w_mine[...], TN, preferred_element_type=F32)
     resid[1 - c] = lax.dot_general(lhs, w_other[...], TN, preferred_element_type=F32)
-    for k, piece in enumerate(pieces):
-        at = pl.ds(pl.multiple_of(lax.rem(y - k + N, N) * rows, rows), rows)
+    for k in range(N):
+        at = pl.ds(pl.multiple_of(lax.rem(x - k + N, N) * rows, rows), rows)
         for h in (0, 1):
-            start = piece[:, h * half : (h + 1) * half].astype(F32)
+            start = held[k, :, h * half : (h + 1) * half].astype(F32)
             resid[h, at, :] = (resid[h, at, :] + start).astype(BF).astype(F32)
             if k == 0:
                 own[:, h * half : (h + 1) * half] = resid[h, at, :].astype(BF)
@@ -182,7 +212,7 @@
     resid[0] = result[:, :half]
     resid[1] = result[:, half:]
     for k, out in enumerate((t0, t1, t2, t3)):
-        at = pl.ds(pl.multiple_of(lax.rem(y + k, N) * rows, rows), rows)
+        at = pl.ds(pl.multiple_of(lax.rem(x + k, N) * rows, rows), rows)
         out[:, :half] = resid[0, at, :].astype(BF)
         out[:, half:] = resid[1, at, :].astype(BF)
     ahead.wait()
@@ -241,41 +271,45 @@
         axis=0,
     )
     packed, _ = lax.optimization_barrier((packed, w_half))
-    w_near = lax.all_gather(packed, ("x", "c"), axis=0, tiled=False)
+    w_near = lax.all_gather(packed, ("y", "c"), axis=0, tiled=False)
 
     pieces = [rows] + [shift(rows, "y", k) for k in (1, 2, 3)]
-    mine = near.reshape(N, 2, near.shape[1], half)
-    mine = lax.dynamic_index_in_dim(mine, c, axis=1, keepdims=False)[:, 3 * HEAD :, :]
-    mine = mine.reshape(N * HEAD, half)
-    mine1 = shift(mine, "y", 1)
-    mine3 = shift(mine, "y", 3)
+    across = [rows] + [shift(rows, "x", k) for k in (1, 2, 3)]
 
     total_rows = count * N
     h1 = pl.pallas_call(
         norm_kernel,
         out_shape=jax.ShapeDtypeStruct((2, total_rows, half), BF),
-        in_specs=[SMEM] + [VMEM] * 5,
+        in_specs=[SMEM] + [HBM] * N + [VMEM],
         out_specs=VMEM,
+        scratch_shapes=[
+            pltpu.VMEM((N, count, width), BF),
+            pltpu.SemaphoreType.DMA((N,)),
+        ],
         compiler_params=params(16),
         name="norm",
-    )(pos, *pieces, ln_attn[None, :])
-    qkv = pl.pallas_call(
+    )(pos, *[far(piece) for piece in pieces], ln_attn[None, :])
+    near, h1, across = lax.optimization_barrier((near, h1, across))
+    *qkv, mine = pl.pallas_call(
         qkv_kernel,
-        out_shape=[jax.ShapeDtypeStruct((3 * HEAD, total_rows), BF)] * N,
+        out_shape=[jax.ShapeDtypeStruct((3 * HEAD, total_rows), BF)] * N
+        + [jax.ShapeDtypeStruct((N, HEAD, half), BF)],
         in_specs=[SMEM, VMEM, HBM],
-        out_specs=[VMEM] * N,
+        out_specs=[VMEM] * (N + 1),
         scratch_shapes=[
             pltpu.VMEM((2 * N, 3 * HEAD, half), BF),
-            pltpu.SemaphoreType.DMA(()),
+            pltpu.SemaphoreType.DMA((2 * N,)),
         ],
         compiler_params=params(16),
         name="qkv",
     )(pos, h1, far(near))
     blocks = [qkv[0]] + [shift(qkv[k], "x", -k) for k in (1, 2, 3)]
-    blocks, mine, mine1, mine3 = lax.optimization_barrier((blocks, mine, mine1, mine3))
-    mine2 = shift(mine, "y", 2)
-    other1 = swap(mine1)
-    other3 = swap(mine3)
+    pass1 = shift(mine, "y", 1)
+    pass3 = shift(mine, "y", 3)
+    blocks, mine, pass1, pass3 = lax.optimization_barrier((blocks, mine, pass1, pass3))
+    pass2 = shift(mine, "y", 2)
+    swap1 = swap(pass1)
+    swap3 = swap(pass3)
 
     group_rows = ids.shape[0]
     chunk = 256
@@ -305,11 +339,8 @@
         compiler_params=params(16),
         name="attend",
     )(pos, bounds, *blocks, ids[None, :], ids[:, None])
-    attended, mine2, other1, other3 = lax.optimization_barrier(
-        (attended, mine2, other1, other3)
-    )
-    other2 = swap(mine2)
-    heads = [attended[0]] + [shift(attended[k], "x", k) for k in (1, 2, 3)]
+    attended, pass2, swap1, swap3 = lax.optimization_barrier((attended, pass2, swap1, swap3))
+    heads = [attended[0]] + [shift(attended[k], "y", k) for k in (1, 2, 3)]
     heads = pl.pallas_call(
         pack_kernel,
         out_shape=jax.ShapeDtypeStruct((N, HEAD, total_rows), BF),
@@ -318,13 +349,16 @@
         compiler_params=params(8),
         name="pack",
     )(pos, *heads)
-    gathered = [heads] + [shift(heads, "y", k) for k in (1, 2, 3)]
+    gathered = [heads] + [shift(heads, "x", k) for k in (1, 2, 3)]
+    swap2 = swap(pass2)
+    passed = [pass1, pass2, pass3]
+    swapped = [swap1, swap2, swap3]
 
     *part, resid, w_merge = pl.pallas_call(
         mlp_kernel,
         out_shape=[jax.ShapeDtypeStruct((count, width), BF)] * (N + 1)
         + [jax.ShapeDtypeStruct(w_merge.shape, BF)],
-        in_specs=[SMEM] + [VMEM] * 9 + [HBM] * 9,
+        in_specs=[SMEM] + [VMEM] * N + [HBM] * N + [VMEM] + [HBM] * 9,
         out_specs=[VMEM] * (N + 2),
         scratch_shapes=[
             pltpu.VMEM((2, total_rows, half), F32),
@@ -332,19 +366,19 @@
             pltpu.VMEM((N * N * HEAD, half), BF),
             pltpu.VMEM((2 * N, units, width), BF),
             pltpu.VMEM((2 * N, units, width), BF),
-            pltpu.SemaphoreType.DMA((4 * N + 3,)),
+            pltpu.VMEM((N, count, width), BF),
+            pltpu.SemaphoreType.DMA((39,)),
         ],
         compiler_params=params(32),
         name="mlp",
     )(
         pos,
         *gathered,
-        *pieces,
+        *[far(v) for v in across],
         ln_mlp[None, :],
-        *[far(v) for v in (near, w_near, mine1, mine2, mine3)],
-        *[far(v) for v in (other1, other2, other3, w_merge)],
+        *[far(v) for v in (near, w_near, *passed, *swapped, w_merge)],
     )
-    sums = [part[0]] + [shift(part[k], "y", k) for k in (1, 2, 3)]
+    sums = [part[0]] + [shift(part[k], "x", k) for k in (1, 2, 3)]
 
     merged_count = count // 4
     dest = slot_dest[0]

time: 171 us -> 177 us (1.035)
  starting transfers between devices: 28.5 us -> 32.9 us
    ppermute x18 -> x21, waiting for transfers between devices: 55.4 us -> 74.2 us  [shift(): return lax.ppermute(value, axis, pairs)]
    all_gather x1, waiting for transfers between devices: 22.4 us -> 3.62 us  [local(): near = lax.all_gather(w_half, ('x', 'c'), axis=0, tiled=False)]
    ppermute x18 -> x21, starting transfers between devices: 28.3 us -> 32.3 us  [shift(): return lax.ppermute(value, axis, pairs)]
    unnamed x23 -> x29, local copies, waits for them, and re-layouts: 0.63 us -> 2.74 us
  transfers between devices with their start and end apart: 23 -> 26, of which waited for: 12 -> 12; matrix products, arithmetic and copies ran while one was open for 4% -> 4% of each run, Pallas kernels for 8% -> 9%
where the time goes in v4:
time: 177 us
  waiting for transfers between devices  77.9 us (44%)
  starting transfers between devices  32.9 us (19%)
  Pallas kernels  29.4 us (17%)
  between operations  13.7 us (8%)
  blocking collectives  11.3 us (6%)
  other arithmetic  6.54 us (4%)
  local copies, waits for them, and re-layouts  4.29 us (2%)
    ppermute x21, waiting for transfers between devices, shift(): return lax.ppermute(value, axis, pairs)  74.2 us
    ppermute x21, starting transfers between devices, shift(): return lax.ppermute(value, axis, pairs)  32.3 us
    pallas_call x1, Pallas kernels, local(): pl.pallas_call(mlp_kernel, out_shape=[jax.ShapeDtypeStruct((count, width)...  11.5 us
    all_to_all x1, blocking collectives, local(): lax.all_to_all(outgoing.reshape(req_count, slot_cap, width + 128), ('x',...  11.3 us
    pallas_call x1, Pallas kernels, local(): pl.pallas_call(attend_kernel, out_shape=[jax.ShapeDtypeStruct((HEAD, tota...  7.28 us
    pallas_call x1, Pallas kernels, local(): pl.pallas_call(qkv_kernel, out_shape=[jax.ShapeDtypeStruct((3 * HEAD, tot...  4.85 us
    all_gather x1, waiting for transfers between devices, local(): near = lax.all_gather(w_half, ('x', 'c'), axis=0, tiled=False)  3.62 us
  transfers between devices with their start and end apart: 26, of which 12 were waited for; matrix products, arithmetic and copies ran while one was open for 4% of the time, Pallas kernels for 9%

profile of v4, /device:TPU:0, one launch (start us, length us, event | category | flops | bytes accessed | tf_op | source)
XLA Modules:
  0.0 177.0 jit_solution(2081909741361841196)
XLA Ops:
  6.5 0.0 all-gather.5.cloned.1.call-start
  6.6 1.9 %fusion.1 = bf16[320,640]{1,0:T(8,128)(2,1)} fusion(s32[]{:T(128)S(6)} %select_n.76, bf16[240,1280]{1,0:T(8,128)(2,1)} %bitcast.49, bf16[80,1280]{1,0:T(8,128)(2,1)} %param.15), kind=kLoop, calls=%fused_computation.5 | loop fusion | flops 819200 | bytes 1228804 | tf_op jit(solution)/shard_map/concatenate | solution.py:262
  8.5 0.0 all-gather.7.cloned.1.call-start
  8.6 1.0 dynamic-slice_bitcast_fusion
  9.6 1.0 pad_maximum_fusion
  10.6 1.7 collective-permute-start
  12.4 2.9 %collective-permute-start.1 = (bf16[128,1280]{1,0:T(8,128)(2,1)S(1)}, bf16[128,1280]{1,0:T(8,128)(2,1)S(1)}, u32[]{:S(2)}, u32[]{:S(2)}) collective-permute-start(bf16[128,1280]{1,0:T(8,128)(2,1)S(1)} %bitcast.44), channel_id=1, source_target_pairs={{0,16},{8,24},{16,0},{24,8},{1,17},{9,25},{17,1},{25,9},{2,18},{10... | collective-permute-start | bytes 983048 | tf_op jit(solution)/shard_map/ppermute | solution.py:34
  15.3 1.3 collective-permute-start.2
  16.6 1.5 collective-permute-start.3
  18.1 2.7 %collective-permute-start.4 = (bf16[128,1280]{1,0:T(8,128)(2,1)S(1)}, bf16[128,1280]{1,0:T(8,128)(2,1)}, u32[]{:S(2)}, u32[]{:S(2)}) collective-permute-start(bf16[128,1280]{1,0:T(8,128)(2,1)S(1)} %bitcast.47), channel_id=1, source_target_pairs={{0,64},{32,96},{64,0},{96,32},{1,65},{33,97},{65,1},{97,33},{2,66}... | collective-permute-start | bytes 983048 | tf_op jit(solution)/shard_map/ppermute | solution.py:34
  20.9 0.5 broadcast.195
  21.4 0.7 reduce.5
  22.1 0.2 fusion.2
  22.3 0.2 and_reduce_fusion
  22.5 1.8 %collective-permute-start.5 = (bf16[128,1280]{1,0:T(8,128)(2,1)S(1)}, bf16[128,1280]{1,0:T(8,128)(2,1)}, u32[]{:S(2)}, u32[]{:S(2)}) collective-permute-start(bf16[128,1280]{1,0:T(8,128)(2,1)S(1)} %bitcast.48), channel_id=1, source_target_pairs={{0,96},{32,0},{64,32},{96,64},{1,97},{33,1},{65,33},{97,65},{2,98}... | collective-permute-start | bytes 983048 | tf_op jit(solution)/shard_map/ppermute | solution.py:34
  24.3 0.1 pad_add_fusion.1.pos
  24.4 0.5 fusion.10
  24.9 4.8 %collective-permute-done.1.p2 = bf16[128,1280]{1,0:T(8,128)(2,1)S(1)} collective-permute-done((bf16[128,1280]{1,0:T(8,128)(2,1)S(1)}, bf16[128,1280]{1,0:T(8,128)(2,1)S(1)}, u32[]{:S(2)}, u32[]{:S(2)}) %collective-permute-start.1) | collective-permute-done | bytes 327712 | tf_op jit(solution)/shard_map/ppermute | solution.py:34
  29.7 0.7 copy-done.9
  30.4 0.7 copy-done.10
  31.2 2.6 %norm.1.h1 = bf16[2,512,640]{2,1,0:T(8,128)(2,1)S(1)} custom-call(s32[4]{0:T(128)S(1)} %pad_add_fusion.1.pos, bf16[128,1280]{1,0:T(8,128)(2,1)} %bitcast.41, bf16[128,1280]{1,0:T(8,128)(2,1)} %copy-done.8, bf16[128,1280]{1,0:T(8,128)(2,1)} %copy-done.9, bf16[128,1280]{1,0:T(8,128)(2,1)} %copy-done.10, f32[1,1280]{1,0:T(1,128)S(1)} %broadcast_in_dim.91.gain), custom_call_target="tpu_custom_call" | custom-call | tf_op jit(solution)/shard_map/norm/pallas_call | solution.py:280
  33.8 11.8 %collective-permute-done.4.refs_6_ = bf16[128,1280]{1,0:T(8,128)(2,1)} collective-permute-done((bf16[128,1280]{1,0:T(8,128)(2,1)S(1)}, bf16[128,1280]{1,0:T(8,128)(2,1)}, u32[]{:S(2)}, u32[]{:S(2)}) %collective-permute-start.4) | collective-permute-done | bytes 327712 | tf_op jit(solution)/shard_map/ppermute | solution.py:34
  45.6 3.6 %all-gather.5.cloned.1.call-done = bf16[2560,640]{1,0:T(8,128)(2,1)} async-done(((bf16[320,640]{1,0:T(8,128)(2,1)}), bf16[2560,640]{1,0:T(8,128)(2,1)}) %all-gather.5.cloned.1.call-update) | async-done | bytes 3276816 | tf_op jit(solution)/shard_map/all_gather | solution.py:264
  49.2 4.8 %qkv.1 = (bf16[240,512]{1,0:T(8,128)(2,1)S(1)}, bf16[240,512]{1,0:T(8,128)(2,1)}, bf16[240,512]{1,0:T(8,128)(2,1)}, bf16[240,512]{1,0:T(8,128)(2,1)S(1)}, bf16[4,80,640]{2,1,0:T(8,128)(2,1)S(1)}) custom-call(s32[4]{0:T(128)S(1)} %pad_add_fusion.1.pos, bf16[2,512,640]{2,1,0:T(8,128)(2,1)S(1)} %norm.1.h1, bf16[8,320,640]{2,1,0:T(8,128)(2,1)} %bitcast.38), custom_call_target="tpu_custom_call" | custom-call | tf_op jit(solution)/shard_map/qkv/pallas_call | solution.py:293
  54.1 0.4 collective-permute-start.10
  54.5 1.7 collective-permute-start.9
  56.2 2.2 %collective-permute-start.6 = (bf16[240,512]{1,0:T(8,128)(2,1)}, bf16[240,512]{1,0:T(8,128)(2,1)S(1)}, u32[]{:S(2)}, u32[]{:S(2)}) collective-permute-start(bf16[240,512]{1,0:T(8,128)(2,1)} %get-tuple-element.44), channel_id=1, source_target_pairs={{0,96},{32,0},{64,32},{96,64},{1,97},{33,1},{65,33},{97,65},{2,98}... | collective-permute-start | bytes 737288 | tf_op jit(solution)/shard_map/ppermute | solution.py:34
  58.4 1.8 %collective-permute-start.7 = (bf16[240,512]{1,0:T(8,128)(2,1)}, bf16[240,512]{1,0:T(8,128)(2,1)S(1)}, u32[]{:S(2)}, u32[]{:S(2)}) collective-permute-start(bf16[240,512]{1,0:T(8,128)(2,1)} %get-tuple-element.45), channel_id=1, source_target_pairs={{0,64},{32,96},{64,0},{96,32},{1,65},{33,97},{65,1},{97,33},{2,66}... | collective-permute-start | bytes 737288 | tf_op jit(solution)/shard_map/ppermute | solution.py:34
  60.2 0.1 select_reduce_fusion.2
  60.4 0.4 copy.15.id_col
  60.8 8.3 %collective-permute-done.6.r1 = bf16[240,512]{1,0:T(8,128)(2,1)S(1)} collective-permute-done((bf16[240,512]{1,0:T(8,128)(2,1)}, bf16[240,512]{1,0:T(8,128)(2,1)S(1)}, u32[]{:S(2)}, u32[]{:S(2)}) %collective-permute-start.6) | collective-permute-done | bytes 245792 | tf_op jit(solution)/shard_map/ppermute | solution.py:34
  69.1 3.6 %collective-permute-done.8.r3 = bf16[240,512]{1,0:T(8,128)(2,1)S(1)} collective-permute-done((bf16[240,512]{1,0:T(8,128)(2,1)S(1)}, bf16[240,512]{1,0:T(8,128)(2,1)S(1)}, u32[]{:S(2)}, u32[]{:S(2)}) %collective-permute-start.8) | collective-permute-done | bytes 245792 | tf_op jit(solution)/shard_map/ppermute | solution.py:34
  72.7 1.0 collective-permute-start.11
  73.7 0.5 collective-permute-start.13
  74.2 0.8 convert_reduce_fusion
  75.0 7.3 %attend.1 = (bf16[80,512]{1,0:T(8,128)(2,1)S(1)}, bf16[80,512]{1,0:T(8,128)(2,1)S(1)}, bf16[80,512]{1,0:T(8,128)(2,1)S(1)}, bf16[80,512]{1,0:T(8,128)(2,1)S(1)}) custom-call(s32[4]{0:T(128)S(1)} %pad_add_fusion.1.pos, s32[2,4]{1,0:T(2,128)S(1)} %pad_add_fusion.bounds, bf16[240,512]{1,0:T(8,128)(2,1)S(1)} %get-tuple-element.48.r0, ...), custom_call_target="tpu_custom_call" | custom-call | tf_op jit(solution)/shard_map/attend/pallas_call | solution.py:327
  82.3 12.7 %collective-permute-done.11.refs_12_ = bf16[4,80,640]{2,1,0:T(8,128)(2,1)S(1)} collective-permute-done((bf16[4,80,640]{2,1,0:T(8,128)(2,1)S(1)}, bf16[4,80,640]{2,1,0:T(8,128)(2,1)S(1)}, u32[]{:S(2)}, u32[]{:S(2)}) %collective-permute-start.11) | collective-permute-done | bytes 409632 | tf_op jit(solution)/shard_map/ppermute | solution.py:34
  95.0 0.7 collective-permute-start.14
  95.7 2.6 %collective-permute-start.15 = (bf16[80,512]{1,0:T(8,128)(2,1)S(1)}, bf16[80,512]{1,0:T(8,128)(2,1)S(1)}, u32[]{:S(2)}, u32[]{:S(2)}) collective-permute-start(bf16[80,512]{1,0:T(8,128)(2,1)S(1)} %get-tuple-element.61), channel_id=1, source_target_pairs={{0,16},{8,24},{16,0},{24,8},{1,17},{9,25},{17,1},{25,9},{2,18},{10... | collective-permute-start | bytes 245768 | tf_op jit(solution)/shard_map/ppermute | solution.py:34
  98.3 0.3 collective-permute-start.16
  98.7 0.6 fusion.8
  99.3 4.0 %collective-permute-done.14.g1 = bf16[80,512]{1,0:T(8,128)(2,1)S(1)} collective-permute-done((bf16[80,512]{1,0:T(8,128)(2,1)S(1)}, bf16[80,512]{1,0:T(8,128)(2,1)S(1)}, u32[]{:S(2)}, u32[]{:S(2)}) %collective-permute-start.14) | collective-permute-done | bytes 81952 | tf_op jit(solution)/shard_map/ppermute | solution.py:34
  103.3 1.9 %collective-permute-done.15.g2 = bf16[80,512]{1,0:T(8,128)(2,1)S(1)} collective-permute-done((bf16[80,512]{1,0:T(8,128)(2,1)S(1)}, bf16[80,512]{1,0:T(8,128)(2,1)S(1)}, u32[]{:S(2)}, u32[]{:S(2)}) %collective-permute-start.15) | collective-permute-done | bytes 81952 | tf_op jit(solution)/shard_map/ppermute | solution.py:34
  105.2 0.6 pack.1.refs_0_
  105.8 1.2 collective-permute-start.17
  107.0 1.7 collective-permute-start.18
  108.7 2.3 %collective-permute-start.19 = (bf16[4,80,512]{2,1,0:T(8,128)(2,1)S(1)}, bf16[4,80,512]{2,1,0:T(8,128)(2,1)S(1)}, u32[]{:S(2)}, u32[]{:S(2)}) collective-permute-start(bf16[4,80,512]{2,1,0:T(8,128)(2,1)S(1)} %pack.1.refs_0_), channel_id=1, source_target_pairs={{0,96},{32,0},{64,32},{96,64},{1,97},{33,1},{65,33},{97,65},{2,98}... | collective-permute-start | bytes 983048 | tf_op jit(solution)/shard_map/ppermute | solution.py:34
  111.0 0.1 select_reduce_fusion
  111.1 12.0 %collective-permute-done.17.refs_1_ = bf16[4,80,512]{2,1,0:T(8,128)(2,1)S(1)} collective-permute-done((bf16[4,80,512]{2,1,0:T(8,128)(2,1)S(1)}, bf16[4,80,512]{2,1,0:T(8,128)(2,1)S(1)}, u32[]{:S(2)}, u32[]{:S(2)}) %collective-permute-start.17) | collective-permute-done | bytes 327712 | tf_op jit(solution)/shard_map/ppermute | solution.py:34
  123.2 0.6 collective-permute-done.19.refs_3_
  123.9 0.8 copy-done.6
  124.6 11.5 %mlp.1 = (bf16[128,1280]{1,0:T(8,128)(2,1)S(1)}, bf16[128,1280]{1,0:T(8,128)(2,1)S(1)}, bf16[128,1280]{1,0:T(8,128)(2,1)S(1)}, bf16[128,1280]{1,0:T(8,128)(2,1)S...) custom-call(s32[4]{0:T(128)S(1)} %pad_add_fusion.1.pos, bf16[4,80,512]{2,1,0:T(8,128)(2,1)S(1)} %pack.1.refs_0_, ...), custom_call_target="tpu_custom_call" | custom-call | tf_op jit(solution)/shard_map/mlp/pallas_call | solution.py:357
  136.1 1.0 collective-permute-start.21
  137.1 3.2 %collective-permute-start.22 = (bf16[128,1280]{1,0:T(8,128)(2,1)S(1)}, bf16[128,1280]{1,0:T(8,128)(2,1)S(1)}, u32[]{:S(2)}, u32[]{:S(2)}) collective-permute-start(bf16[128,1280]{1,0:T(8,128)(2,1)S(1)} %get-tuple-element.74), channel_id=1, source_target_pairs={{0,64},{32,96},{64,0},{96,32},{1,65},{33,97},{65,1},{97,33},{2,66}... | collective-permute-start | bytes 983048 | tf_op jit(solution)/shard_map/ppermute | solution.py:34
  140.3 0.1 collective-permute-start.23
  140.4 0.1 select_convert_fusion.tail
  140.5 6.3 %collective-permute-done.21.t1 = bf16[128,1280]{1,0:T(8,128)(2,1)S(1)} collective-permute-done((bf16[128,1280]{1,0:T(8,128)(2,1)S(1)}, bf16[128,1280]{1,0:T(8,128)(2,1)S(1)}, u32[]{:S(2)}, u32[]{:S(2)}) %collective-permute-start.21) | collective-permute-done | bytes 327712 | tf_op jit(solution)/shard_map/ppermute | solution.py:34
  146.7 8.2 %collective-permute-done.22.t2 = bf16[128,1280]{1,0:T(8,128)(2,1)S(1)} collective-permute-done((bf16[128,1280]{1,0:T(8,128)(2,1)S(1)}, bf16[128,1280]{1,0:T(8,128)(2,1)S(1)}, u32[]{:S(2)}, u32[]{:S(2)}) %collective-permute-start.22) | collective-permute-done | bytes 327712 | tf_op jit(solution)/shard_map/ppermute | solution.py:34
  154.9 2.5 %merge.1 = bf16[32,1408]{1,0:T(8,128)(2,1)S(1)} custom-call(bf16[128,1280]{1,0:T(8,128)(2,1)S(1)} %get-tuple-element.71.resid, bf16[128,1280]{1,0:T(8,128)(2,1)S(1)} %get-tuple-element.72.t0, bf16[128,1280]{1,0:T(8,128)(2,1)S(1)} %collective-permute-done.21.t1, bf16[128,1280]{1,0:T(8,128)(2,1)S(1)} %collective-permute-done.22.t2, ...), custom_call_target="tpu_custom_call" | custom-call | tf_op jit(solution)/shard_map/merge/pallas_call | solution.py:398
  157.5 0.1 reshape.110
  157.5 11.3 %all_to_all.5 = bf16[16,2,1408]{2,1,0:T(2,128)(2,1)S(1)} all-to-all(bf16[16,2,1408]{2,1,0:T(2,128)(2,1)S(1)} %reshape.110), channel_id=1, replica_groups=mesh['x'=4,'y'=4,'z'=4,'c'=2] {'x','y'}, dimensions={0} | all-to-all | bytes 180224 | tf_op jit(solution)/shard_map/all_to_all | solution.py:407
  168.9 0.1 add_reduce_fusion
  169.0 0.1 fusion.4
  169.1 1.1 fusion
  (57 shorter events, 0.3 us)
Async XLA Ops:
  6.5 2.0 %copy-start = (bf16[320,1280]{1,0:T(8,128)(2,1)S(1)}, bf16[320,1280]{1,0:T(8,128)(2,1)}, u32[]{:S(2)}) copy-start(bf16[320,1280]{1,0:T(8,128)(2,1)} %param.18) | copy-start | bytes 2457604
  6.5 4.1 %copy-start.2 = (bf16[1,128,1280]{2,1,0:T(8,128)(2,1)S(1)}, bf16[1,128,1280]{2,1,0:T(8,128)(2,1)}, u32[]{:S(2)}) copy-start(bf16[1,128,1280]{2,1,0:T(8,128)(2,1)} %param.11) | copy-start | bytes 983044
  6.5 14.3 %copy-start.11 = (f32[1280]{0:T(1024)S(1)}, f32[1280]{0:T(1024)}, u32[]{:S(2)}) copy-start(f32[1280]{0:T(1024)} %param.13) | copy-start | bytes 15364
  6.5 14.8 %copy-start.1 = (s32[1,2048]{1,0:T(1,128)S(1)}, s32[1,2048]{1,0:T(1,128)}, u32[]{:S(2)}) copy-start(s32[1,2048]{1,0:T(1,128)} %id_row.1) | copy-start | bytes 24580
  6.5 17.8 %copy-start.13 = (s32[1,32]{1,0:T(1,128)S(1)}, s32[1,32]{1,0:T(1,128)}, u32[]{:S(2)}) copy-start(s32[1,32]{1,0:T(1,128)} %param.21) | copy-start | bytes 388
  6.5 42.7 %all-gather.5.cloned.1.call-start = ((), (), s32[]{:S(2)}) async-start(), calls=%async_computation.1 | async-start | bytes 3686400 | tf_op jit(solution)/shard_map/all_gather | solution.py:264
  8.5 115.4 %all-gather.7.cloned.1.call-start = ((), (), s32[]{:S(2)}) async-start(), calls=%async_computation.2 | async-start | bytes 7372800 | tf_op jit(solution)/shard_map/all_gather | solution.py:274
  10.6 11.8 %collective-permute-start = (bf16[128,1280]{1,0:T(8,128)(2,1)S(1)}, bf16[128,1280]{1,0:T(8,128)(2,1)S(1)}, u32[]{:S(2)}, u32[]{:S(2)}) collective-permute-start(bf16[128,1280]{1,0:T(8,128)(2,1)S(1)} %bitcast.43), channel_id=1, source_target_pairs={{0,8},{8,16},{16,24},{24,0},{1,9},{9,17},{17,25},{25,1},{2,10},{10... | collective-permute-start | bytes 983048 | tf_op jit(solution)/shard_map/ppermute | solution.py:34
  12.4 17.3 %collective-permute-start.1 = (bf16[128,1280]{1,0:T(8,128)(2,1)S(1)}, bf16[128,1280]{1,0:T(8,128)(2,1)S(1)}, u32[]{:S(2)}, u32[]{:S(2)}) collective-permute-start(bf16[128,1280]{1,0:T(8,128)(2,1)S(1)} %bitcast.44), channel_id=1, source_target_pairs={{0,16},{8,24},{16,0},{24,8},{1,17},{9,25},{17,1},{25,9},{2,18},{10... | collective-permute-start | bytes 983048 | tf_op jit(solution)/shard_map/ppermute | solution.py:34
  15.3 14.5 %collective-permute-start.2 = (bf16[128,1280]{1,0:T(8,128)(2,1)S(1)}, bf16[128,1280]{1,0:T(8,128)(2,1)S(1)}, u32[]{:S(2)}, u32[]{:S(2)}) collective-permute-start(bf16[128,1280]{1,0:T(8,128)(2,1)S(1)} %bitcast.45), channel_id=1, source_target_pairs={{0,24},{8,0},{16,8},{24,16},{1,25},{9,1},{17,9},{25,17},{2,26},{10... | collective-permute-start | bytes 983048 | tf_op jit(solution)/shard_map/ppermute | solution.py:34
  16.6 17.2 %collective-permute-start.3 = (bf16[128,1280]{1,0:T(8,128)(2,1)S(1)}, bf16[128,1280]{1,0:T(8,128)(2,1)}, u32[]{:S(2)}, u32[]{:S(2)}) collective-permute-start(bf16[128,1280]{1,0:T(8,128)(2,1)S(1)} %bitcast.46), channel_id=1, source_target_pairs={{0,32},{32,64},{64,96},{96,0},{1,33},{33,65},{65,97},{97,1},{2,34}... | collective-permute-start | bytes 983048 | tf_op jit(solution)/shard_map/ppermute | solution.py:34
  18.1 27.5 %collective-permute-start.4 = (bf16[128,1280]{1,0:T(8,128)(2,1)S(1)}, bf16[128,1280]{1,0:T(8,128)(2,1)}, u32[]{:S(2)}, u32[]{:S(2)}) collective-permute-start(bf16[128,1280]{1,0:T(8,128)(2,1)S(1)} %bitcast.47), channel_id=1, source_target_pairs={{0,64},{32,96},{64,0},{96,32},{1,65},{33,97},{65,1},{97,33},{2,66}... | collective-permute-start | bytes 983048 | tf_op jit(solution)/shard_map/ppermute | solution.py:34
  22.5 7.2 %copy-start.8 = (bf16[128,1280]{1,0:T(8,128)(2,1)}, bf16[128,1280]{1,0:T(8,128)(2,1)S(1)}, u32[]{:S(2)}) copy-start(bf16[128,1280]{1,0:T(8,128)(2,1)S(1)} %collective-permute-done.p1) | copy-start | bytes 983044
  22.5 23.1 %collective-permute-start.5 = (bf16[128,1280]{1,0:T(8,128)(2,1)S(1)}, bf16[128,1280]{1,0:T(8,128)(2,1)}, u32[]{:S(2)}, u32[]{:S(2)}) collective-permute-start(bf16[128,1280]{1,0:T(8,128)(2,1)S(1)} %bitcast.48), channel_id=1, source_target_pairs={{0,96},{32,0},{64,32},{96,64},{1,97},{33,1},{65,33},{97,65},{2,98}... | collective-permute-start | bytes 983048 | tf_op jit(solution)/shard_map/ppermute | solution.py:34
  29.7 0.7 copy-start.9
  30.4 0.7 copy-start.10
  49.2 50.0 %copy-start.12 = (f32[1280]{0:T(1024)S(1)}, f32[1280]{0:T(1024)}, u32[]{:S(2)}) copy-start(f32[1280]{0:T(1024)} %param.16) | copy-start | bytes 15364
  54.1 18.6 %collective-permute-start.10 = (bf16[4,80,640]{2,1,0:T(8,128)(2,1)S(1)}, bf16[4,80,640]{2,1,0:T(8,128)(2,1)}, u32[]{:S(2)}, u32[]{:S(2)}) collective-permute-start(bf16[4,80,640]{2,1,0:T(8,128)(2,1)S(1)} %get-tuple-element.56), channel_id=1, source_target_pairs={{0,24},{8,0},{16,8},{24,16},{1,25},{9,1},{17,9},{25,17},{2,26},{10... | collective-permute-start | bytes 1228808 | tf_op jit(solution)/shard_map/ppermute | solution.py:34
  54.5 18.2 %collective-permute-start.9 = (bf16[4,80,640]{2,1,0:T(8,128)(2,1)S(1)}, bf16[4,80,640]{2,1,0:T(8,128)(2,1)}, u32[]{:S(2)}, u32[]{:S(2)}) collective-permute-start(bf16[4,80,640]{2,1,0:T(8,128)(2,1)S(1)} %get-tuple-element.56), channel_id=1, source_target_pairs={{0,8},{8,16},{16,24},{24,0},{1,9},{9,17},{17,25},{25,1},{2,10},{10... | collective-permute-start | bytes 1228808 | tf_op jit(solution)/shard_map/ppermute | solution.py:34
  56.2 12.9 %collective-permute-start.6 = (bf16[240,512]{1,0:T(8,128)(2,1)}, bf16[240,512]{1,0:T(8,128)(2,1)S(1)}, u32[]{:S(2)}, u32[]{:S(2)}) collective-permute-start(bf16[240,512]{1,0:T(8,128)(2,1)} %get-tuple-element.44), channel_id=1, source_target_pairs={{0,96},{32,0},{64,32},{96,64},{1,97},{33,1},{65,33},{97,65},{2,98}... | collective-permute-start | bytes 737288 | tf_op jit(solution)/shard_map/ppermute | solution.py:34
  58.4 10.7 %collective-permute-start.7 = (bf16[240,512]{1,0:T(8,128)(2,1)}, bf16[240,512]{1,0:T(8,128)(2,1)S(1)}, u32[]{:S(2)}, u32[]{:S(2)}) collective-permute-start(bf16[240,512]{1,0:T(8,128)(2,1)} %get-tuple-element.45), channel_id=1, source_target_pairs={{0,64},{32,96},{64,0},{96,32},{1,65},{33,97},{65,1},{97,33},{2,66}... | collective-permute-start | bytes 737288 | tf_op jit(solution)/shard_map/ppermute | solution.py:34
  60.2 12.4 %collective-permute-start.8 = (bf16[240,512]{1,0:T(8,128)(2,1)S(1)}, bf16[240,512]{1,0:T(8,128)(2,1)S(1)}, u32[]{:S(2)}, u32[]{:S(2)}) collective-permute-start(bf16[240,512]{1,0:T(8,128)(2,1)S(1)} %get-tuple-element.46), channel_id=1, source_target_pairs={{0,32},{32,64},{64,96},{96,0},{1,33},{33,65},{65,97},{97,1},{2,34}... | collective-permute-start | bytes 737288 | tf_op jit(solution)/shard_map/ppermute | solution.py:34
  72.7 22.3 %collective-permute-start.11 = (bf16[4,80,640]{2,1,0:T(8,128)(2,1)S(1)}, bf16[4,80,640]{2,1,0:T(8,128)(2,1)S(1)}, u32[]{:S(2)}, u32[]{:S(2)}) collective-permute-start(bf16[4,80,640]{2,1,0:T(8,128)(2,1)S(1)} %get-tuple-element.56), channel_id=1, source_target_pairs={{0,16},{8,24},{16,0},{24,8},{1,17},{9,25},{17,1},{25,9},{2,18},{10... | collective-permute-start | bytes 1228808 | tf_op jit(solution)/shard_map/ppermute | solution.py:34
  73.7 21.3 %collective-permute-start.12 = (bf16[4,80,640]{2,1,0:T(8,128)(2,1)}, bf16[4,80,640]{2,1,0:T(8,128)(2,1)S(1)}, u32[]{:S(2)}, u32[]{:S(2)}) collective-permute-start(bf16[4,80,640]{2,1,0:T(8,128)(2,1)} %collective-permute-done.9.refs_11_), channel_id=1, source_target_pairs={{0,1},{1,0},{2,3},{3,2},{4,5},{5,4},{6,7},{7,6},{8,9},{9,8},{10,11... | collective-permute-start | bytes 1228808 | tf_op jit(solution)/shard_map/ppermute | solution.py:42
  73.7 21.3 %collective-permute-start.13 = (bf16[4,80,640]{2,1,0:T(8,128)(2,1)}, bf16[4,80,640]{2,1,0:T(8,128)(2,1)S(1)}, u32[]{:S(2)}, u32[]{:S(2)}) collective-permute-start(bf16[4,80,640]{2,1,0:T(8,128)(2,1)} %collective-permute-done.10.refs_13_), channel_id=1, source_target_pairs={{0,1},{1,0},{2,3},{3,2},{4,5},{5,4},{6,7},{7,6},{8,9},{9,8},{10,11... | collective-permute-start | bytes 1228808 | tf_op jit(solution)/shard_map/ppermute | solution.py:42
  95.0 28.8 %copy-start.3 = (bf16[4,80,640]{2,1,0:T(8,128)(2,1)}, bf16[4,80,640]{2,1,0:T(8,128)(2,1)S(1)}, u32[]{:S(2)}) copy-start(bf16[4,80,640]{2,1,0:T(8,128)(2,1)S(1)} %collective-permute-done.11.refs_12_) | copy-start | bytes 1228804
  95.0 28.8 %copy-start.4 = (bf16[4,80,640]{2,1,0:T(8,128)(2,1)}, bf16[4,80,640]{2,1,0:T(8,128)(2,1)S(1)}, u32[]{:S(2)}) copy-start(bf16[4,80,640]{2,1,0:T(8,128)(2,1)S(1)} %collective-permute-done.12.refs_14_) | copy-start | bytes 1228804
  95.0 28.8 %copy-start.5 = (bf16[4,80,640]{2,1,0:T(8,128)(2,1)}, bf16[4,80,640]{2,1,0:T(8,128)(2,1)S(1)}, u32[]{:S(2)}) copy-start(bf16[4,80,640]{2,1,0:T(8,128)(2,1)S(1)} %collective-permute-done.13.refs_16_) | copy-start | bytes 1228804
  95.0 8.3 %collective-permute-start.14 = (bf16[80,512]{1,0:T(8,128)(2,1)S(1)}, bf16[80,512]{1,0:T(8,128)(2,1)S(1)}, u32[]{:S(2)}, u32[]{:S(2)}) collective-permute-start(bf16[80,512]{1,0:T(8,128)(2,1)S(1)} %get-tuple-element.60), channel_id=1, source_target_pairs={{0,8},{8,16},{16,24},{24,0},{1,9},{9,17},{17,25},{25,1},{2,10},{10... | collective-permute-start | bytes 245768 | tf_op jit(solution)/shard_map/ppermute | solution.py:34
  95.7 9.5 %collective-permute-start.15 = (bf16[80,512]{1,0:T(8,128)(2,1)S(1)}, bf16[80,512]{1,0:T(8,128)(2,1)S(1)}, u32[]{:S(2)}, u32[]{:S(2)}) collective-permute-start(bf16[80,512]{1,0:T(8,128)(2,1)S(1)} %get-tuple-element.61), channel_id=1, source_target_pairs={{0,16},{8,24},{16,0},{24,8},{1,17},{9,25},{17,1},{25,9},{2,18},{10... | collective-permute-start | bytes 245768 | tf_op jit(solution)/shard_map/ppermute | solution.py:34
  98.3 6.9 %collective-permute-start.16 = (bf16[80,512]{1,0:T(8,128)(2,1)S(1)}, bf16[80,512]{1,0:T(8,128)(2,1)S(1)}, u32[]{:S(2)}, u32[]{:S(2)}) collective-permute-start(bf16[80,512]{1,0:T(8,128)(2,1)S(1)} %get-tuple-element.62), channel_id=1, source_target_pairs={{0,24},{8,0},{16,8},{24,16},{1,25},{9,1},{17,9},{25,17},{2,26},{10... | collective-permute-start | bytes 245768 | tf_op jit(solution)/shard_map/ppermute | solution.py:34
  98.7 25.2 %collective-permute-start.20 = (bf16[4,80,640]{2,1,0:T(8,128)(2,1)S(1)}, bf16[4,80,640]{2,1,0:T(8,128)(2,1)S(1)}, u32[]{:S(2)}, u32[]{:S(2)}) collective-permute-start(bf16[4,80,640]{2,1,0:T(8,128)(2,1)S(1)} %collective-permute-done.11.refs_12_), channel_id=1, source_target_pairs={{0,1},{1,0},{2,3},{3,2},{4,5},{5,4},{6,7},{7,6},{8,9},{9,8},{10,11... | collective-permute-start | bytes 1228808 | tf_op jit(solution)/shard_map/ppermute | solution.py:42
  105.8 17.4 %collective-permute-start.17 = (bf16[4,80,512]{2,1,0:T(8,128)(2,1)S(1)}, bf16[4,80,512]{2,1,0:T(8,128)(2,1)S(1)}, u32[]{:S(2)}, u32[]{:S(2)}) collective-permute-start(bf16[4,80,512]{2,1,0:T(8,128)(2,1)S(1)} %pack.1.refs_0_), channel_id=1, source_target_pairs={{0,32},{32,64},{64,96},{96,0},{1,33},{33,65},{65,97},{97,1},{2,34}... | collective-permute-start | bytes 983048 | tf_op jit(solution)/shard_map/ppermute | solution.py:34
  107.0 16.2 %collective-permute-start.18 = (bf16[4,80,512]{2,1,0:T(8,128)(2,1)S(1)}, bf16[4,80,512]{2,1,0:T(8,128)(2,1)S(1)}, u32[]{:S(2)}, u32[]{:S(2)}) collective-permute-start(bf16[4,80,512]{2,1,0:T(8,128)(2,1)S(1)} %pack.1.refs_0_), channel_id=1, source_target_pairs={{0,64},{32,96},{64,0},{96,32},{1,65},{33,97},{65,1},{97,33},{2,66}... | collective-permute-start | bytes 983048 | tf_op jit(solution)/shard_map/ppermute | solution.py:34
  108.7 15.1 %collective-permute-start.19 = (bf16[4,80,512]{2,1,0:T(8,128)(2,1)S(1)}, bf16[4,80,512]{2,1,0:T(8,128)(2,1)S(1)}, u32[]{:S(2)}, u32[]{:S(2)}) collective-permute-start(bf16[4,80,512]{2,1,0:T(8,128)(2,1)S(1)} %pack.1.refs_0_), channel_id=1, source_target_pairs={{0,96},{32,0},{64,32},{96,64},{1,97},{33,1},{65,33},{97,65},{2,98}... | collective-permute-start | bytes 983048 | tf_op jit(solution)/shard_map/ppermute | solution.py:34
  123.8 0.8 copy-start.6
  136.1 10.6 %collective-permute-start.21 = (bf16[128,1280]{1,0:T(8,128)(2,1)S(1)}, bf16[128,1280]{1,0:T(8,128)(2,1)S(1)}, u32[]{:S(2)}, u32[]{:S(2)}) collective-permute-start(bf16[128,1280]{1,0:T(8,128)(2,1)S(1)} %get-tuple-element.73), channel_id=1, source_target_pairs={{0,32},{32,64},{64,96},{96,0},{1,33},{33,65},{65,97},{97,1},{2,34}... | collective-permute-start | bytes 983048 | tf_op jit(solution)/shard_map/ppermute | solution.py:34
  137.1 17.8 %collective-permute-start.22 = (bf16[128,1280]{1,0:T(8,128)(2,1)S(1)}, bf16[128,1280]{1,0:T(8,128)(2,1)S(1)}, u32[]{:S(2)}, u32[]{:S(2)}) collective-permute-start(bf16[128,1280]{1,0:T(8,128)(2,1)S(1)} %get-tuple-element.74), channel_id=1, source_target_pairs={{0,64},{32,96},{64,0},{96,32},{1,65},{33,97},{65,1},{97,33},{2,66}... | collective-permute-start | bytes 983048 | tf_op jit(solution)/shard_map/ppermute | solution.py:34
  140.3 14.6 %collective-permute-start.23 = (bf16[128,1280]{1,0:T(8,128)(2,1)S(1)}, bf16[128,1280]{1,0:T(8,128)(2,1)S(1)}, u32[]{:S(2)}, u32[]{:S(2)}) collective-permute-start(bf16[128,1280]{1,0:T(8,128)(2,1)S(1)} %get-tuple-element.75), channel_id=1, source_target_pairs={{0,96},{32,0},{64,32},{96,64},{1,97},{33,1},{65,33},{97,65},{2,98}... | collective-permute-start | bytes 983048 | tf_op jit(solution)/shard_map/ppermute | solution.py:34
  154.9 14.1 %copy-start.7 = (bf16[128,1280]{1,0:T(8,128)(2,1)S(1)}, bf16[128,1280]{1,0:T(8,128)(2,1)}, u32[]{:S(2)}) copy-start(bf16[128,1280]{1,0:T(8,128)(2,1)} %param.20) | copy-start | bytes 983044
Sparse Core Ops, SparseCore 0:
  9.1 40.1 all-gather.4
  50.9 56.4 all-gather.6

commit v5 on v4

--- a/solution.py
+++ b/solution.py
@@ -90,8 +90,6 @@
     block = qs.shape[2]
     per = block // chunk
     scale = math.log2(math.e) / math.sqrt(HEAD)
-    rows = block // N
-    y = pos[1]
     for k, piece in enumerate((r0, r1, r2, r3)):
         at = lax.rem(x + k, N)
         qs[at] = piece[:HEAD, :]
@@ -131,18 +129,15 @@
             jnp.zeros((HEAD, block), F32),
         )
         top, total, acc = lax.fori_loop(low, high, step, start)
-        result = (acc / total).astype(BF)
-        for yb in range(N):
-            part = result[:, yb * rows : (yb + 1) * rows]
-            outs[lax.rem(yb - y + N, N), :, qb * rows : (qb + 1) * rows] = part
+        outs[lax.rem(qb - x + N, N)] = (acc / total).astype(BF)
     for k, out in enumerate((o0, o1, o2, o3)):
         out[...] = outs[k]
 
 
 def pack_kernel(pos, g0, g1, g2, g3, out):
-    y = pos[1]
+    x = pos[0]
     for k, piece in enumerate((g0, g1, g2, g3)):
-        out[lax.rem(y - k + N, N)] = piece[...]
+        out[lax.rem(x - k + N, N)] = piece[...]
 
 
 def mlp_kernel(pos, *refs):
@@ -153,46 +148,44 @@
     other = refs[14:17]
     merge_hbm = refs[17]
     t0, t1, t2, t3, own, w_merge, resid, w_mine, w_other, up, down, held, sems = refs[18:]
-    x = pos[0]
     y = pos[1]
     c = pos[3]
     rows = pieces[0].shape[0]
-    half = w_mine.shape[1]
+    half = w_mine.shape[2]
     group = N * HEAD
     skip = near.shape[1] - HEAD
-    first = []
+    moves = []
+    for j in range(N):
+        moves.append((near.at[2 * j + c, skip : skip + HEAD, :], w_mine.at[j]))
+        moves.append((near.at[2 * j + 1 - c, skip : skip + HEAD, :], w_other.at[j]))
+    for k in range(1, N):
+        to = slice(k * N, (k + 1) * N)
+        moves.append((mine[k - 1], w_mine.at[to]))
+        moves.append((other[k - 1], w_other.at[to]))
     for k in range(N):
-        for j in range(N):
-            at = (lax.rem(x - j + N, N) * N + lax.rem(y - k + N, N)) * HEAD
-            to = pl.ds(pl.multiple_of(at, 16), HEAD)
-            if k == 0:
-                sources = (
-                    near.at[2 * j + c, skip : skip + HEAD, :],
-                    near.at[2 * j + 1 - c, skip : skip + HEAD, :],
-                )
-            else:
-                sources = (mine[k - 1].at[j], other[k - 1].at[j])
-            for src, dst in zip(sources, (w_mine, w_other)):
-                sem = sems.at[len(first)]
-                first.append(pltpu.make_async_copy(src, dst.at[to, :], sem))
-    for k in range(N):
-        sem = sems.at[len(first)]
-        first.append(pltpu.make_async_copy(pieces[k], held.at[k], sem))
+        moves.append((pieces[k], held.at[k]))
+    early = len(moves)
     units = up.shape[1]
-    second = [
-        pltpu.make_async_copy(w_hbm.at[:, :units, :], up, sems.at[36]),
-        pltpu.make_async_copy(w_hbm.at[:, units:, :], down, sems.at[37]),
-    ]
-    ahead = pltpu.make_async_copy(merge_hbm, w_merge, sems.at[38])
-    for copy in first + second + [ahead]:
+    for h in (0, 1):
+        cols = slice(h * half, (h + 1) * half)
+        moves.append((w_hbm.at[:, h, :units, :], up.at[:, :, cols]))
+    for h in (0, 1):
+        cols = slice(h * half, (h + 1) * half)
+        moves.append((w_hbm.at[:, h, units:, :], down.at[:, :, cols]))
+    moves.append((merge_hbm, w_merge))
+    copies = [pltpu.make_async_copy(a, b, sems.at[i]) for i, (a, b) in enumerate(moves)]
+    for copy in copies:
         copy.start()
     lhs = jnp.concatenate([g[...].reshape(group, N * rows) for g in gathered], axis=0)
-    for copy in first:
+    for copy in copies[:early]:
         copy.wait()
-    resid[c] = lax.dot_general(lhs, w_mine[...], TN, preferred_element_type=F32)
-    resid[1 - c] = lax.dot_general(lhs, w_other[...], TN, preferred_element_type=F32)
+    heads = N * group
+    part = w_mine[...].reshape(heads, half)
+    resid[c] = lax.dot_general(lhs, part, TN, preferred_element_type=F32)
+    part = w_other[...].reshape(heads, half)
+    resid[1 - c] = lax.dot_general(lhs, part, TN, preferred_element_type=F32)
     for k in range(N):
-        at = pl.ds(pl.multiple_of(lax.rem(x - k + N, N) * rows, rows), rows)
+        at = pl.ds(pl.multiple_of(lax.rem(y - k + N, N) * rows, rows), rows)
         for h in (0, 1):
             start = held[k, :, h * half : (h + 1) * half].astype(F32)
             resid[h, at, :] = (resid[h, at, :] + start).astype(BF).astype(F32)
@@ -202,20 +195,22 @@
     normed = norm_rows(full, gain[...]).astype(BF)
     width = 2 * half
     count = up.shape[0] * units
-    second[0].wait()
+    copies[early].wait()
+    copies[early + 1].wait()
     hidden = lax.dot_general(
         normed, up[...].reshape(count, width), NT, preferred_element_type=F32
     )
     hidden = (0.5 * hidden * (1.0 + lax.erf(hidden * math.sqrt(0.5)))).astype(BF)
-    second[1].wait()
+    copies[early + 2].wait()
+    copies[early + 3].wait()
     result = jnp.dot(hidden, down[...].reshape(count, width), preferred_element_type=F32)
     resid[0] = result[:, :half]
     resid[1] = result[:, half:]
     for k, out in enumerate((t0, t1, t2, t3)):
-        at = pl.ds(pl.multiple_of(lax.rem(x + k, N) * rows, rows), rows)
+        at = pl.ds(pl.multiple_of(lax.rem(y + k, N) * rows, rows), rows)
         out[:, :half] = resid[0, at, :].astype(BF)
         out[:, half:] = resid[1, at, :].astype(BF)
-    ahead.wait()
+    copies[early + 4].wait()
 
 
 def merge_kernel(resid, t0, t1, t2, t3, w, select, tail, out, vision):
@@ -262,20 +257,21 @@
     w_heads = jnp.concatenate([w_heads, w_out], axis=0)
     w_half = lax.dynamic_slice_in_dim(w_heads, c * half, half, 1)
     near = lax.all_gather(w_half, ("x", "c"), axis=0, tiled=False)
-    units = w_down.shape[0] // 2
+    z = lax.axis_index("z")
+    units = w_down.shape[0] // N
+    sizes = (units, half)
     packed = jnp.concatenate(
         [
-            lax.dynamic_slice_in_dim(w_up.T, c * units, units, 0),
-            lax.dynamic_slice_in_dim(w_down, c * units, units, 0),
+            lax.dynamic_slice(w_up.T, (z * units, c * half), sizes),
+            lax.dynamic_slice(w_down, (z * units, c * half), sizes),
         ],
         axis=0,
     )
     packed, _ = lax.optimization_barrier((packed, w_half))
-    w_near = lax.all_gather(packed, ("y", "c"), axis=0, tiled=False)
+    w_near = lax.all_gather(packed, ("x", "z", "c"), axis=0, tiled=False)
+    w_near = w_near.reshape(N * N, 2, 2 * units, half)
 
     pieces = [rows] + [shift(rows, "y", k) for k in (1, 2, 3)]
-    across = [rows] + [shift(rows, "x", k) for k in (1, 2, 3)]
-
     total_rows = count * N
     h1 = pl.pallas_call(
         norm_kernel,
@@ -289,7 +285,7 @@
         compiler_params=params(16),
         name="norm",
     )(pos, *[far(piece) for piece in pieces], ln_attn[None, :])
-    near, h1, across = lax.optimization_barrier((near, h1, across))
+    near, h1 = lax.optimization_barrier((near, h1))
     *qkv, mine = pl.pallas_call(
         qkv_kernel,
         out_shape=[jax.ShapeDtypeStruct((3 * HEAD, total_rows), BF)] * N
@@ -340,7 +336,8 @@
         name="attend",
     )(pos, bounds, *blocks, ids[None, :], ids[:, None])
     attended, pass2, swap1, swap3 = lax.optimization_barrier((attended, pass2, swap1, swap3))
-    heads = [attended[0]] + [shift(attended[k], "y", k) for k in (1, 2, 3)]
+    swap2 = swap(pass2)
+    heads = [attended[0]] + [shift(attended[k], "x", k) for k in (1, 2, 3)]
     heads = pl.pallas_call(
         pack_kernel,
         out_shape=jax.ShapeDtypeStruct((N, HEAD, total_rows), BF),
@@ -349,10 +346,7 @@
         compiler_params=params(8),
         name="pack",
     )(pos, *heads)
-    gathered = [heads] + [shift(heads, "x", k) for k in (1, 2, 3)]
-    swap2 = swap(pass2)
-    passed = [pass1, pass2, pass3]
-    swapped = [swap1, swap2, swap3]
+    gathered = [heads] + [shift(heads, "y", k) for k in (1, 2, 3)]
 
     *part, resid, w_merge = pl.pallas_call(
         mlp_kernel,
@@ -362,23 +356,24 @@
         out_specs=[VMEM] * (N + 2),
         scratch_shapes=[
             pltpu.VMEM((2, total_rows, half), F32),
-            pltpu.VMEM((N * N * HEAD, half), BF),
-            pltpu.VMEM((N * N * HEAD, half), BF),
-            pltpu.VMEM((2 * N, units, width), BF),
-            pltpu.VMEM((2 * N, units, width), BF),
+            pltpu.VMEM((N * N, HEAD, half), BF),
+            pltpu.VMEM((N * N, HEAD, half), BF),
+            pltpu.VMEM((N * N, units, width), BF),
+            pltpu.VMEM((N * N, units, width), BF),
             pltpu.VMEM((N, count, width), BF),
-            pltpu.SemaphoreType.DMA((39,)),
+            pltpu.SemaphoreType.DMA((23,)),
         ],
         compiler_params=params(32),
         name="mlp",
     )(
         pos,
         *gathered,
-        *[far(v) for v in across],
+        *[far(v) for v in pieces],
         ln_mlp[None, :],
-        *[far(v) for v in (near, w_near, *passed, *swapped, w_merge)],
+        *[far(v) for v in (near, w_near, pass1, pass2, pass3)],
+        *[far(v) for v in (swap1, swap2, swap3, w_merge)],
     )
-    sums = [part[0]] + [shift(part[k], "x", k) for k in (1, 2, 3)]
+    sums = [part[0]] + [shift(part[k], "y", k) for k in (1, 2, 3)]
 
     merged_count = count // 4
     dest = slot_dest[0]

time: 177 us -> 164 us (0.927)
  waiting for transfers between devices: 77.9 us -> 68.7 us
  starting transfers between devices: 32.9 us -> 27.6 us
    ppermute x21 -> x18, waiting for transfers between devices: 74.2 us -> 62.4 us  [shift(): return lax.ppermute(value, axis, pairs)]
    ppermute x21 -> x18, starting transfers between devices: 32.3 us -> 27.3 us  [shift(): return lax.ppermute(value, axis, pairs)]
    all_gather x1, waiting for transfers between devices: 3.62 us -> 6.24 us  [local(): near = lax.all_gather(w_half, ('x', 'c'), axis=0, tiled=False)]
  transfers between devices with their start and end apart: 26 -> 23, of which waited for: 12 -> 14; matrix products, arithmetic and copies ran while one was open for 4% -> 5% of each run, Pallas kernels for 9% -> 9%
where the time goes in v5:
time: 164 us
  waiting for transfers between devices  68.7 us (42%)
  Pallas kernels  29.3 us (18%)
  starting transfers between devices  27.6 us (17%)
  between operations  13.6 us (8%)
  blocking collectives  11.2 us (7%)
  other arithmetic  7.56 us (5%)
  local copies, waits for them, and re-layouts  4.86 us (3%)
    ppermute x18, waiting for transfers between devices, shift(): return lax.ppermute(value, axis, pairs)  62.4 us
    ppermute x18, starting transfers between devices, shift(): return lax.ppermute(value, axis, pairs)  27.3 us
    pallas_call x1, Pallas kernels, local(): pl.pallas_call(mlp_kernel, out_shape=[jax.ShapeDtypeStruct((count, width)...  11.4 us
    all_to_all x1, blocking collectives, local(): lax.all_to_all(outgoing.reshape(req_count, slot_cap, width + 128), ('x',...  11.2 us
    pallas_call x1, Pallas kernels, local(): pl.pallas_call(attend_kernel, out_shape=[jax.ShapeDtypeStruct((HEAD, tota...  7.29 us
    all_gather x1, waiting for transfers between devices, local(): near = lax.all_gather(w_half, ('x', 'c'), axis=0, tiled=False)  6.24 us
    pallas_call x1, Pallas kernels, local(): pl.pallas_call(qkv_kernel, out_shape=[jax.ShapeDtypeStruct((3 * HEAD, tot...  4.88 us
  transfers between devices with their start and end apart: 23, of which 14 were waited for; matrix products, arithmetic and copies ran while one was open for 5% of the time, Pallas kernels for 9%

profile of v5, /device:TPU:0, one launch (start us, length us, event | category | flops | bytes accessed | tf_op | source)
XLA Modules:
  0.0 163.9 jit_solution(7697698185203057402)
XLA Ops:
  6.6 1.9 %fusion.1 = bf16[320,640]{1,0:T(8,128)(2,1)} fusion(s32[]{:T(128)S(6)} %select_n.78, bf16[240,1280]{1,0:T(8,128)(2,1)} %bitcast.46, bf16[80,1280]{1,0:T(8,128)(2,1)} %param.15), kind=kLoop, calls=%fused_computation.4 | loop fusion | flops 819200 | bytes 1228804 | tf_op jit(solution)/shard_map/concatenate | solution.py:257
  8.4 0.0 all-gather.7.cloned.1.call-start
  8.5 0.9 dynamic_slice.11
  9.4 0.7 pad_maximum_fusion
  10.2 1.7 %collective-permute-start = (bf16[128,1280]{1,0:T(8,128)(2,1)}, bf16[128,1280]{1,0:T(8,128)(2,1)S(1)}, u32[]{:S(2)}, u32[]{:S(2)}) collective-permute-start(bf16[128,1280]{1,0:T(8,128)(2,1)} %bitcast.41), channel_id=1, source_target_pairs={{0,8},{8,16},{16,24},{24,0},{1,9},{9,17},{17,25},{25,1},{2,10},{10... | collective-permute-start | bytes 983048 | tf_op jit(solution)/shard_map/ppermute | solution.py:34
  11.9 2.9 %collective-permute-start.1 = (bf16[128,1280]{1,0:T(8,128)(2,1)}, bf16[128,1280]{1,0:T(8,128)(2,1)S(1)}, u32[]{:S(2)}, u32[]{:S(2)}) collective-permute-start(bf16[128,1280]{1,0:T(8,128)(2,1)} %bitcast.42), channel_id=1, source_target_pairs={{0,16},{8,24},{16,0},{24,8},{1,17},{9,25},{17,1},{25,9},{2,18},{10... | collective-permute-start | bytes 983048 | tf_op jit(solution)/shard_map/ppermute | solution.py:34
  14.8 1.3 collective-permute-start.2
  16.2 0.7 broadcast_in_dim.91.gain
  16.9 0.5 broadcast.195
  17.4 1.3 reduce.5
  18.8 0.2 fusion.2
  19.0 0.2 and_reduce_fusion
  19.2 0.1 pad_add_fusion.1.pos
  19.3 1.2 fusion.10
  20.5 0.8 collective-permute-done.p1.refs_5_
  21.3 8.2 %collective-permute-done.1.p2.refs_6_ = bf16[128,1280]{1,0:T(8,128)(2,1)S(1)} collective-permute-done((bf16[128,1280]{1,0:T(8,128)(2,1)}, bf16[128,1280]{1,0:T(8,128)(2,1)S(1)}, u32[]{:S(2)}, u32[]{:S(2)}) %collective-permute-start.1) | collective-permute-done | bytes 327712 | tf_op jit(solution)/shard_map/ppermute | solution.py:34
  29.5 0.7 copy-done.3
  30.2 0.7 copy-done.4
  30.9 2.6 %norm.1.h1 = bf16[2,512,640]{2,1,0:T(8,128)(2,1)S(1)} custom-call(s32[4]{0:T(128)S(1)} %pad_add_fusion.1.pos, bf16[128,1280]{1,0:T(8,128)(2,1)} %bitcast.44, bf16[128,1280]{1,0:T(8,128)(2,1)} %copy-done.2, bf16[128,1280]{1,0:T(8,128)(2,1)} %copy-done.3, bf16[128,1280]{1,0:T(8,128)(2,1)} %copy-done.4, f32[1,1280]{1,0:T(1,128)S(1)} %broadcast_in_dim.91.gain), custom_call_target="tpu_custom_call" | custom-call | tf_op jit(solution)/shard_map/norm/pallas_call | solution.py:276
  33.6 6.2 %all-gather.5.cloned.1.call-done = bf16[2560,640]{1,0:T(8,128)(2,1)} async-done(((bf16[320,640]{1,0:T(8,128)(2,1)}), bf16[2560,640]{1,0:T(8,128)(2,1)}) %all-gather.5.cloned.1.call-update) | async-done | bytes 3276816 | tf_op jit(solution)/shard_map/all_gather | solution.py:259
  39.8 4.9 %qkv.1 = (bf16[240,512]{1,0:T(8,128)(2,1)S(1)}, bf16[240,512]{1,0:T(8,128)(2,1)}, bf16[240,512]{1,0:T(8,128)(2,1)}, bf16[240,512]{1,0:T(8,128)(2,1)S(1)}, bf16[4,80,640]{2,1,0:T(8,128)(2,1)S(1)}) custom-call(s32[4]{0:T(128)S(1)} %pad_add_fusion.1.pos, bf16[2,512,640]{2,1,0:T(8,128)(2,1)S(1)} %norm.1.h1, bf16[8,320,640]{2,1,0:T(8,128)(2,1)} %bitcast.38), custom_call_target="tpu_custom_call" | custom-call | tf_op jit(solution)/shard_map/qkv/pallas_call | solution.py:289
  44.7 1.5 collective-permute-start.6
  46.3 1.8 %collective-permute-start.7 = (bf16[4,80,640]{2,1,0:T(8,128)(2,1)S(1)}, bf16[4,80,640]{2,1,0:T(8,128)(2,1)}, u32[]{:S(2)}, u32[]{:S(2)}) collective-permute-start(bf16[4,80,640]{2,1,0:T(8,128)(2,1)S(1)} %get-tuple-element.52), channel_id=1, source_target_pairs={{0,24},{8,0},{16,8},{24,16},{1,25},{9,1},{17,9},{25,17},{2,26},{10... | collective-permute-start | bytes 1228808 | tf_op jit(solution)/shard_map/ppermute | solution.py:34
  48.0 1.5 collective-permute-start.3
  49.5 1.0 collective-permute-start.4
  50.5 0.6 collective-permute-start.5
  51.0 0.1 select_reduce_fusion.2
  51.2 0.4 copy.15.id_col
  51.6 6.6 %collective-permute-done.3.r1 = bf16[240,512]{1,0:T(8,128)(2,1)S(1)} collective-permute-done((bf16[240,512]{1,0:T(8,128)(2,1)}, bf16[240,512]{1,0:T(8,128)(2,1)S(1)}, u32[]{:S(2)}, u32[]{:S(2)}) %collective-permute-start.3) | collective-permute-done | bytes 245792 | tf_op jit(solution)/shard_map/ppermute | solution.py:34
  58.2 3.5 %collective-permute-done.4.r2 = bf16[240,512]{1,0:T(8,128)(2,1)S(1)} collective-permute-done((bf16[240,512]{1,0:T(8,128)(2,1)}, bf16[240,512]{1,0:T(8,128)(2,1)S(1)}, u32[]{:S(2)}, u32[]{:S(2)}) %collective-permute-start.4) | collective-permute-done | bytes 245792 | tf_op jit(solution)/shard_map/ppermute | solution.py:34
  61.6 5.1 %collective-permute-done.5.r3 = bf16[240,512]{1,0:T(8,128)(2,1)S(1)} collective-permute-done((bf16[240,512]{1,0:T(8,128)(2,1)S(1)}, bf16[240,512]{1,0:T(8,128)(2,1)S(1)}, u32[]{:S(2)}, u32[]{:S(2)}) %collective-permute-start.5) | collective-permute-done | bytes 245792 | tf_op jit(solution)/shard_map/ppermute | solution.py:34
  66.7 2.1 %collective-permute-start.8 = (bf16[4,80,640]{2,1,0:T(8,128)(2,1)S(1)}, bf16[4,80,640]{2,1,0:T(8,128)(2,1)S(1)}, u32[]{:S(2)}, u32[]{:S(2)}) collective-permute-start(bf16[4,80,640]{2,1,0:T(8,128)(2,1)S(1)} %get-tuple-element.52), channel_id=1, source_target_pairs={{0,16},{8,24},{16,0},{24,8},{1,17},{9,25},{17,1},{25,9},{2,18},{10... | collective-permute-start | bytes 1228808 | tf_op jit(solution)/shard_map/ppermute | solution.py:34
  68.8 0.2 collective-permute-start.9
  69.0 0.8 convert_reduce_fusion
  69.8 7.3 %attend.1 = (bf16[80,512]{1,0:T(8,128)(2,1)S(1)}, bf16[80,512]{1,0:T(8,128)(2,1)S(1)}, bf16[80,512]{1,0:T(8,128)(2,1)S(1)}, bf16[80,512]{1,0:T(8,128)(2,1)S(1)}) custom-call(s32[4]{0:T(128)S(1)} %pad_add_fusion.1.pos, s32[2,4]{1,0:T(2,128)S(1)} %pad_add_fusion.bounds, bf16[240,512]{1,0:T(8,128)(2,1)S(1)} %get-tuple-element.44.r0, ...), custom_call_target="tpu_custom_call" | custom-call | tf_op jit(solution)/shard_map/attend/pallas_call | solution.py:323
  77.1 3.0 %collective-permute-done.8.refs_12_ = bf16[4,80,640]{2,1,0:T(8,128)(2,1)S(1)} collective-permute-done((bf16[4,80,640]{2,1,0:T(8,128)(2,1)S(1)}, bf16[4,80,640]{2,1,0:T(8,128)(2,1)S(1)}, u32[]{:S(2)}, u32[]{:S(2)}) %collective-permute-start.8) | collective-permute-done | bytes 409632 | tf_op jit(solution)/shard_map/ppermute | solution.py:34
  80.1 0.1 collective-permute-start.11
  80.2 2.2 %collective-permute-start.12 = (bf16[80,512]{1,0:T(8,128)(2,1)S(1)}, bf16[80,512]{1,0:T(8,128)(2,1)S(1)}, u32[]{:S(2)}, u32[]{:S(2)}) collective-permute-start(bf16[80,512]{1,0:T(8,128)(2,1)S(1)} %get-tuple-element.57), channel_id=1, source_target_pairs={{0,64},{32,96},{64,0},{96,32},{1,65},{33,97},{65,1},{97,33},{2,66}... | collective-permute-start | bytes 245768 | tf_op jit(solution)/shard_map/ppermute | solution.py:34
  82.4 1.5 collective-permute-start.13
  83.9 0.6 fusion.8
  84.6 5.3 %collective-permute-done.11.g1 = bf16[80,512]{1,0:T(8,128)(2,1)S(1)} collective-permute-done((bf16[80,512]{1,0:T(8,128)(2,1)S(1)}, bf16[80,512]{1,0:T(8,128)(2,1)S(1)}, u32[]{:S(2)}, u32[]{:S(2)}) %collective-permute-start.11) | collective-permute-done | bytes 81952 | tf_op jit(solution)/shard_map/ppermute | solution.py:34
  89.8 0.1 collective-permute-done.12.g2
  90.0 2.3 %collective-permute-done.13.g3 = bf16[80,512]{1,0:T(8,128)(2,1)S(1)} collective-permute-done((bf16[80,512]{1,0:T(8,128)(2,1)S(1)}, bf16[80,512]{1,0:T(8,128)(2,1)S(1)}, u32[]{:S(2)}, u32[]{:S(2)}) %collective-permute-start.13) | collective-permute-done | bytes 81952 | tf_op jit(solution)/shard_map/ppermute | solution.py:34
  92.3 0.6 pack.1.refs_0_
  92.9 0.6 collective-permute-start.14
  93.5 2.6 %collective-permute-start.15 = (bf16[4,80,512]{2,1,0:T(8,128)(2,1)S(1)}, bf16[4,80,512]{2,1,0:T(8,128)(2,1)S(1)}, u32[]{:S(2)}, u32[]{:S(2)}) collective-permute-start(bf16[4,80,512]{2,1,0:T(8,128)(2,1)S(1)} %pack.1.refs_0_), channel_id=1, source_target_pairs={{0,16},{8,24},{16,0},{24,8},{1,17},{9,25},{17,1},{25,9},{2,18},{10... | collective-permute-start | bytes 983048 | tf_op jit(solution)/shard_map/ppermute | solution.py:34
  96.1 1.5 collective-permute-start.16
  97.6 0.1 select_reduce_fusion
  97.7 12.6 %collective-permute-done.14.refs_1_ = bf16[4,80,512]{2,1,0:T(8,128)(2,1)S(1)} collective-permute-done((bf16[4,80,512]{2,1,0:T(8,128)(2,1)S(1)}, bf16[4,80,512]{2,1,0:T(8,128)(2,1)S(1)}, u32[]{:S(2)}, u32[]{:S(2)}) %collective-permute-start.14) | collective-permute-done | bytes 327712 | tf_op jit(solution)/shard_map/ppermute | solution.py:34
  110.3 0.6 collective-permute-done.16.refs_3_
  111.0 0.7 copy-done.8
  111.7 11.4 %mlp.1 = (bf16[128,1280]{1,0:T(8,128)(2,1)S(1)}, bf16[128,1280]{1,0:T(8,128)(2,1)S(1)}, bf16[128,1280]{1,0:T(8,128)(2,1)S(1)}, bf16[128,1280]{1,0:T(8,128)(2,1)S...) custom-call(s32[4]{0:T(128)S(1)} %pad_add_fusion.1.pos, bf16[4,80,512]{2,1,0:T(8,128)(2,1)S(1)} %pack.1.refs_0_, ...), custom_call_target="tpu_custom_call" | custom-call | tf_op jit(solution)/shard_map/mlp/pallas_call | solution.py:351
  123.1 1.2 collective-permute-start.18
  124.2 3.0 %collective-permute-start.19 = (bf16[128,1280]{1,0:T(8,128)(2,1)S(1)}, bf16[128,1280]{1,0:T(8,128)(2,1)S(1)}, u32[]{:S(2)}, u32[]{:S(2)}) collective-permute-start(bf16[128,1280]{1,0:T(8,128)(2,1)S(1)} %get-tuple-element.66), channel_id=1, source_target_pairs={{0,16},{8,24},{16,0},{24,8},{1,17},{9,25},{17,1},{25,9},{2,18},{10... | collective-permute-start | bytes 983048 | tf_op jit(solution)/shard_map/ppermute | solution.py:34
  127.2 0.3 collective-permute-start.20
  127.5 0.1 select_convert_fusion.tail
  127.6 6.1 %collective-permute-done.18.t1 = bf16[128,1280]{1,0:T(8,128)(2,1)S(1)} collective-permute-done((bf16[128,1280]{1,0:T(8,128)(2,1)S(1)}, bf16[128,1280]{1,0:T(8,128)(2,1)S(1)}, u32[]{:S(2)}, u32[]{:S(2)}) %collective-permute-start.18) | collective-permute-done | bytes 327712 | tf_op jit(solution)/shard_map/ppermute | solution.py:34
  133.7 8.2 %collective-permute-done.19.t2 = bf16[128,1280]{1,0:T(8,128)(2,1)S(1)} collective-permute-done((bf16[128,1280]{1,0:T(8,128)(2,1)S(1)}, bf16[128,1280]{1,0:T(8,128)(2,1)S(1)}, u32[]{:S(2)}, u32[]{:S(2)}) %collective-permute-start.19) | collective-permute-done | bytes 327712 | tf_op jit(solution)/shard_map/ppermute | solution.py:34
  141.9 2.5 %merge.1 = bf16[32,1408]{1,0:T(8,128)(2,1)S(1)} custom-call(bf16[128,1280]{1,0:T(8,128)(2,1)S(1)} %get-tuple-element.63.resid, bf16[128,1280]{1,0:T(8,128)(2,1)S(1)} %get-tuple-element.64.t0, bf16[128,1280]{1,0:T(8,128)(2,1)S(1)} %collective-permute-done.18.t1, bf16[128,1280]{1,0:T(8,128)(2,1)S(1)} %collective-permute-done.19.t2, ...), custom_call_target="tpu_custom_call" | custom-call | tf_op jit(solution)/shard_map/merge/pallas_call | solution.py:393
  144.4 0.1 reshape.114
  144.5 11.2 %all_to_all.5 = bf16[16,2,1408]{2,1,0:T(2,128)(2,1)S(1)} all-to-all(bf16[16,2,1408]{2,1,0:T(2,128)(2,1)S(1)} %reshape.114), channel_id=1, replica_groups=mesh['x'=4,'y'=4,'z'=4,'c'=2] {'x','y'}, dimensions={0} | all-to-all | bytes 180224 | tf_op jit(solution)/shard_map/all_to_all | solution.py:402
  155.7 0.1 add_reduce_fusion
  155.9 0.1 fusion.4
  156.0 1.1 fusion
  (47 shorter events, 0.3 us)
Async XLA Ops:
  6.5 2.9 %copy-start = (bf16[1280,320]{0,1:T(8,128)(2,1)S(1)}, bf16[1280,320]{0,1:T(8,128)(2,1)}, u32[]{:S(2)}) copy-start(bf16[1280,320]{0,1:T(8,128)(2,1)} %param.17) | copy-start | bytes 2457604
  6.5 44.7 %copy-start.1 = (s32[1,2048]{1,0:T(1,128)S(1)}, s32[1,2048]{1,0:T(1,128)}, u32[]{:S(2)}) copy-start(s32[1,2048]{1,0:T(1,128)} %id_row.1) | copy-start | bytes 24580
  6.5 62.5 %copy-start.11 = (s32[1,32]{1,0:T(1,128)S(1)}, s32[1,32]{1,0:T(1,128)}, u32[]{:S(2)}) copy-start(s32[1,32]{1,0:T(1,128)} %param.21) | copy-start | bytes 388
  6.5 33.3 %all-gather.5.cloned.1.call-start = ((), (), s32[]{:S(2)}) async-start(), calls=%async_computation.1 | async-start | bytes 3686400 | tf_op jit(solution)/shard_map/all_gather | solution.py:259
  6.6 78.0 %copy-start.10 = (f32[1280]{0:T(1024)S(1)}, f32[1280]{0:T(1024)}, u32[]{:S(2)}) copy-start(f32[1280]{0:T(1024)} %param.16) | copy-start | bytes 15364
  8.4 102.5 %all-gather.7.cloned.1.call-start = ((), (), s32[]{:S(2)}) async-start(), calls=%async_computation.2 | async-start | bytes 6758400 | tf_op jit(solution)/shard_map/all_gather | solution.py:271
  10.2 11.1 %collective-permute-start = (bf16[128,1280]{1,0:T(8,128)(2,1)}, bf16[128,1280]{1,0:T(8,128)(2,1)S(1)}, u32[]{:S(2)}, u32[]{:S(2)}) collective-permute-start(bf16[128,1280]{1,0:T(8,128)(2,1)} %bitcast.41), channel_id=1, source_target_pairs={{0,8},{8,16},{16,24},{24,0},{1,9},{9,17},{17,25},{25,1},{2,10},{10... | collective-permute-start | bytes 983048 | tf_op jit(solution)/shard_map/ppermute | solution.py:34
  11.9 17.6 %collective-permute-start.1 = (bf16[128,1280]{1,0:T(8,128)(2,1)}, bf16[128,1280]{1,0:T(8,128)(2,1)S(1)}, u32[]{:S(2)}, u32[]{:S(2)}) collective-permute-start(bf16[128,1280]{1,0:T(8,128)(2,1)} %bitcast.42), channel_id=1, source_target_pairs={{0,16},{8,24},{16,0},{24,8},{1,17},{9,25},{17,1},{25,9},{2,18},{10... | collective-permute-start | bytes 983048 | tf_op jit(solution)/shard_map/ppermute | solution.py:34
  14.8 14.7 %collective-permute-start.2 = (bf16[128,1280]{1,0:T(8,128)(2,1)}, bf16[128,1280]{1,0:T(8,128)(2,1)S(1)}, u32[]{:S(2)}, u32[]{:S(2)}) collective-permute-start(bf16[128,1280]{1,0:T(8,128)(2,1)} %bitcast.43), channel_id=1, source_target_pairs={{0,24},{8,0},{16,8},{24,16},{1,25},{9,1},{17,9},{25,17},{2,26},{10... | collective-permute-start | bytes 983048 | tf_op jit(solution)/shard_map/ppermute | solution.py:34
  21.3 8.2 %copy-start.2 = (bf16[128,1280]{1,0:T(8,128)(2,1)}, bf16[128,1280]{1,0:T(8,128)(2,1)S(1)}, u32[]{:S(2)}) copy-start(bf16[128,1280]{1,0:T(8,128)(2,1)S(1)} %collective-permute-done.p1.refs_5_) | copy-start | bytes 983044
  29.5 0.7 copy-start.3
  30.2 0.7 copy-start.4
  44.7 22.0 %collective-permute-start.6 = (bf16[4,80,640]{2,1,0:T(8,128)(2,1)S(1)}, bf16[4,80,640]{2,1,0:T(8,128)(2,1)}, u32[]{:S(2)}, u32[]{:S(2)}) collective-permute-start(bf16[4,80,640]{2,1,0:T(8,128)(2,1)S(1)} %get-tuple-element.52), channel_id=1, source_target_pairs={{0,8},{8,16},{16,24},{24,0},{1,9},{9,17},{17,25},{25,1},{2,10},{10... | collective-permute-start | bytes 1228808 | tf_op jit(solution)/shard_map/ppermute | solution.py:34
  46.3 20.5 %collective-permute-start.7 = (bf16[4,80,640]{2,1,0:T(8,128)(2,1)S(1)}, bf16[4,80,640]{2,1,0:T(8,128)(2,1)}, u32[]{:S(2)}, u32[]{:S(2)}) collective-permute-start(bf16[4,80,640]{2,1,0:T(8,128)(2,1)S(1)} %get-tuple-element.52), channel_id=1, source_target_pairs={{0,24},{8,0},{16,8},{24,16},{1,25},{9,1},{17,9},{25,17},{2,26},{10... | collective-permute-start | bytes 1228808 | tf_op jit(solution)/shard_map/ppermute | solution.py:34
  48.0 10.2 %collective-permute-start.3 = (bf16[240,512]{1,0:T(8,128)(2,1)}, bf16[240,512]{1,0:T(8,128)(2,1)S(1)}, u32[]{:S(2)}, u32[]{:S(2)}) collective-permute-start(bf16[240,512]{1,0:T(8,128)(2,1)} %get-tuple-element.40), channel_id=1, source_target_pairs={{0,96},{32,0},{64,32},{96,64},{1,97},{33,1},{65,33},{97,65},{2,98}... | collective-permute-start | bytes 737288 | tf_op jit(solution)/shard_map/ppermute | solution.py:34
  49.5 12.2 %collective-permute-start.4 = (bf16[240,512]{1,0:T(8,128)(2,1)}, bf16[240,512]{1,0:T(8,128)(2,1)S(1)}, u32[]{:S(2)}, u32[]{:S(2)}) collective-permute-start(bf16[240,512]{1,0:T(8,128)(2,1)} %get-tuple-element.41), channel_id=1, source_target_pairs={{0,64},{32,96},{64,0},{96,32},{1,65},{33,97},{65,1},{97,33},{2,66}... | collective-permute-start | bytes 737288 | tf_op jit(solution)/shard_map/ppermute | solution.py:34
  50.5 16.2 %collective-permute-start.5 = (bf16[240,512]{1,0:T(8,128)(2,1)S(1)}, bf16[240,512]{1,0:T(8,128)(2,1)S(1)}, u32[]{:S(2)}, u32[]{:S(2)}) collective-permute-start(bf16[240,512]{1,0:T(8,128)(2,1)S(1)} %get-tuple-element.42), channel_id=1, source_target_pairs={{0,32},{32,64},{64,96},{96,0},{1,33},{33,65},{65,97},{97,1},{2,34}... | collective-permute-start | bytes 737288 | tf_op jit(solution)/shard_map/ppermute | solution.py:34
  66.7 10.4 %collective-permute-start.10 = (bf16[4,80,640]{2,1,0:T(8,128)(2,1)}, bf16[4,80,640]{2,1,0:T(8,128)(2,1)S(1)}, u32[]{:S(2)}, u32[]{:S(2)}) collective-permute-start(bf16[4,80,640]{2,1,0:T(8,128)(2,1)} %collective-permute-done.7.refs_13_), channel_id=1, source_target_pairs={{0,1},{1,0},{2,3},{3,2},{4,5},{5,4},{6,7},{7,6},{8,9},{9,8},{10,11... | collective-permute-start | bytes 1228808 | tf_op jit(solution)/shard_map/ppermute | solution.py:42
  66.7 13.4 %collective-permute-start.8 = (bf16[4,80,640]{2,1,0:T(8,128)(2,1)S(1)}, bf16[4,80,640]{2,1,0:T(8,128)(2,1)S(1)}, u32[]{:S(2)}, u32[]{:S(2)}) collective-permute-start(bf16[4,80,640]{2,1,0:T(8,128)(2,1)S(1)} %get-tuple-element.52), channel_id=1, source_target_pairs={{0,16},{8,24},{16,0},{24,8},{1,17},{9,25},{17,1},{25,9},{2,18},{10... | collective-permute-start | bytes 1228808 | tf_op jit(solution)/shard_map/ppermute | solution.py:34
  68.8 11.3 %collective-permute-start.9 = (bf16[4,80,640]{2,1,0:T(8,128)(2,1)}, bf16[4,80,640]{2,1,0:T(8,128)(2,1)S(1)}, u32[]{:S(2)}, u32[]{:S(2)}) collective-permute-start(bf16[4,80,640]{2,1,0:T(8,128)(2,1)} %collective-permute-done.6.refs_11_), channel_id=1, source_target_pairs={{0,1},{1,0},{2,3},{3,2},{4,5},{5,4},{6,7},{7,6},{8,9},{9,8},{10,11... | collective-permute-start | bytes 1228808 | tf_op jit(solution)/shard_map/ppermute | solution.py:42
  77.1 33.8 %copy-start.5 = (bf16[4,80,640]{2,1,0:T(8,128)(2,1)}, bf16[4,80,640]{2,1,0:T(8,128)(2,1)S(1)}, u32[]{:S(2)}) copy-start(bf16[4,80,640]{2,1,0:T(8,128)(2,1)S(1)} %collective-permute-done.10.refs_16_) | copy-start | bytes 1228804
  80.1 30.8 %copy-start.6 = (bf16[4,80,640]{2,1,0:T(8,128)(2,1)}, bf16[4,80,640]{2,1,0:T(8,128)(2,1)S(1)}, u32[]{:S(2)}) copy-start(bf16[4,80,640]{2,1,0:T(8,128)(2,1)S(1)} %collective-permute-done.8.refs_12_) | copy-start | bytes 1228804
  80.1 30.8 %copy-start.7 = (bf16[4,80,640]{2,1,0:T(8,128)(2,1)}, bf16[4,80,640]{2,1,0:T(8,128)(2,1)S(1)}, u32[]{:S(2)}) copy-start(bf16[4,80,640]{2,1,0:T(8,128)(2,1)S(1)} %collective-permute-done.9.refs_14_) | copy-start | bytes 1228804
  80.1 9.7 %collective-permute-start.11 = (bf16[80,512]{1,0:T(8,128)(2,1)S(1)}, bf16[80,512]{1,0:T(8,128)(2,1)S(1)}, u32[]{:S(2)}, u32[]{:S(2)}) collective-permute-start(bf16[80,512]{1,0:T(8,128)(2,1)S(1)} %get-tuple-element.56), channel_id=1, source_target_pairs={{0,32},{32,64},{64,96},{96,0},{1,33},{33,65},{65,97},{97,1},{2,34}... | collective-permute-start | bytes 245768 | tf_op jit(solution)/shard_map/ppermute | solution.py:34
  80.2 9.8 %collective-permute-start.12 = (bf16[80,512]{1,0:T(8,128)(2,1)S(1)}, bf16[80,512]{1,0:T(8,128)(2,1)S(1)}, u32[]{:S(2)}, u32[]{:S(2)}) collective-permute-start(bf16[80,512]{1,0:T(8,128)(2,1)S(1)} %get-tuple-element.57), channel_id=1, source_target_pairs={{0,64},{32,96},{64,0},{96,32},{1,65},{33,97},{65,1},{97,33},{2,66}... | collective-permute-start | bytes 245768 | tf_op jit(solution)/shard_map/ppermute | solution.py:34
  82.4 9.9 %collective-permute-start.13 = (bf16[80,512]{1,0:T(8,128)(2,1)S(1)}, bf16[80,512]{1,0:T(8,128)(2,1)S(1)}, u32[]{:S(2)}, u32[]{:S(2)}) collective-permute-start(bf16[80,512]{1,0:T(8,128)(2,1)S(1)} %get-tuple-element.58), channel_id=1, source_target_pairs={{0,96},{32,0},{64,32},{96,64},{1,97},{33,1},{65,33},{97,65},{2,98}... | collective-permute-start | bytes 245768 | tf_op jit(solution)/shard_map/ppermute | solution.py:34
  83.9 27.0 %collective-permute-start.17 = (bf16[4,80,640]{2,1,0:T(8,128)(2,1)S(1)}, bf16[4,80,640]{2,1,0:T(8,128)(2,1)S(1)}, u32[]{:S(2)}, u32[]{:S(2)}) collective-permute-start(bf16[4,80,640]{2,1,0:T(8,128)(2,1)S(1)} %collective-permute-done.8.refs_12_), channel_id=1, source_target_pairs={{0,1},{1,0},{2,3},{3,2},{4,5},{5,4},{6,7},{7,6},{8,9},{9,8},{10,11... | collective-permute-start | bytes 1228808 | tf_op jit(solution)/shard_map/ppermute | solution.py:42
  92.9 17.4 %collective-permute-start.14 = (bf16[4,80,512]{2,1,0:T(8,128)(2,1)S(1)}, bf16[4,80,512]{2,1,0:T(8,128)(2,1)S(1)}, u32[]{:S(2)}, u32[]{:S(2)}) collective-permute-start(bf16[4,80,512]{2,1,0:T(8,128)(2,1)S(1)} %pack.1.refs_0_), channel_id=1, source_target_pairs={{0,8},{8,16},{16,24},{24,0},{1,9},{9,17},{17,25},{25,1},{2,10},{10... | collective-permute-start | bytes 983048 | tf_op jit(solution)/shard_map/ppermute | solution.py:34
  93.5 16.8 %collective-permute-start.15 = (bf16[4,80,512]{2,1,0:T(8,128)(2,1)S(1)}, bf16[4,80,512]{2,1,0:T(8,128)(2,1)S(1)}, u32[]{:S(2)}, u32[]{:S(2)}) collective-permute-start(bf16[4,80,512]{2,1,0:T(8,128)(2,1)S(1)} %pack.1.refs_0_), channel_id=1, source_target_pairs={{0,16},{8,24},{16,0},{24,8},{1,17},{9,25},{17,1},{25,9},{2,18},{10... | collective-permute-start | bytes 983048 | tf_op jit(solution)/shard_map/ppermute | solution.py:34
  96.1 14.8 %collective-permute-start.16 = (bf16[4,80,512]{2,1,0:T(8,128)(2,1)S(1)}, bf16[4,80,512]{2,1,0:T(8,128)(2,1)S(1)}, u32[]{:S(2)}, u32[]{:S(2)}) collective-permute-start(bf16[4,80,512]{2,1,0:T(8,128)(2,1)S(1)} %pack.1.refs_0_), channel_id=1, source_target_pairs={{0,24},{8,0},{16,8},{24,16},{1,25},{9,1},{17,9},{25,17},{2,26},{10... | collective-permute-start | bytes 983048 | tf_op jit(solution)/shard_map/ppermute | solution.py:34
  110.9 0.8 copy-start.8
  123.1 10.6 %collective-permute-start.18 = (bf16[128,1280]{1,0:T(8,128)(2,1)S(1)}, bf16[128,1280]{1,0:T(8,128)(2,1)S(1)}, u32[]{:S(2)}, u32[]{:S(2)}) collective-permute-start(bf16[128,1280]{1,0:T(8,128)(2,1)S(1)} %get-tuple-element.65), channel_id=1, source_target_pairs={{0,8},{8,16},{16,24},{24,0},{1,9},{9,17},{17,25},{25,1},{2,10},{10... | collective-permute-start | bytes 983048 | tf_op jit(solution)/shard_map/ppermute | solution.py:34
  124.2 17.6 %collective-permute-start.19 = (bf16[128,1280]{1,0:T(8,128)(2,1)S(1)}, bf16[128,1280]{1,0:T(8,128)(2,1)S(1)}, u32[]{:S(2)}, u32[]{:S(2)}) collective-permute-start(bf16[128,1280]{1,0:T(8,128)(2,1)S(1)} %get-tuple-element.66), channel_id=1, source_target_pairs={{0,16},{8,24},{16,0},{24,8},{1,17},{9,25},{17,1},{25,9},{2,18},{10... | collective-permute-start | bytes 983048 | tf_op jit(solution)/shard_map/ppermute | solution.py:34
  127.2 14.6 %collective-permute-start.20 = (bf16[128,1280]{1,0:T(8,128)(2,1)S(1)}, bf16[128,1280]{1,0:T(8,128)(2,1)S(1)}, u32[]{:S(2)}, u32[]{:S(2)}) collective-permute-start(bf16[128,1280]{1,0:T(8,128)(2,1)S(1)} %get-tuple-element.67), channel_id=1, source_target_pairs={{0,24},{8,0},{16,8},{24,16},{1,25},{9,1},{17,9},{25,17},{2,26},{10... | collective-permute-start | bytes 983048 | tf_op jit(solution)/shard_map/ppermute | solution.py:34
  141.9 14.1 %copy-start.9 = (bf16[128,1280]{1,0:T(8,128)(2,1)S(1)}, bf16[128,1280]{1,0:T(8,128)(2,1)}, u32[]{:S(2)}) copy-start(bf16[128,1280]{1,0:T(8,128)(2,1)} %param.20) | copy-start | bytes 983044
Sparse Core Ops, SparseCore 0:
  9.0 30.7 all-gather.4
  42.1 55.8 all-gather.6

commit v6 on v5

v6 whole, which is shorter than its diff:
```python
import functools
import math

import jax
import jax.numpy as jnp
from jax import lax
from jax.experimental import pallas as pl
from jax.experimental.pallas import tpu as pltpu
from jax.sharding import Mesh
from jax.sharding import PartitionSpec as P

HEAD = 80
SCALE = math.log2(math.e) / math.sqrt(HEAD)
N = 4
BF = jnp.bfloat16
F32 = jnp.float32
NT = (((1,), (1,)), ((), ()))
TN = (((0,), (0,)), ((), ()))
HBM = pl.BlockSpec(memory_space=pltpu.HBM)
VMEM = pl.BlockSpec(memory_space=pltpu.VMEM)
SMEM = pl.BlockSpec(memory_space=pltpu.SMEM)


def params(mib):
    return pltpu.CompilerParams(vmem_limit_bytes=mib << 20)


def norm_rows(rows32, gain):
    center = rows32 - jnp.mean(rows32, axis=-1, keepdims=True)
    spread = jnp.mean(center * center, axis=-1, keepdims=True)
    return center * lax.rsqrt(spread + 1e-06) * gain


def shift(value, axis, step):
    pairs = [(i, (i + step) % N) for i in range(N)]
    return lax.ppermute(value, axis, pairs)


def far(value):
    return pltpu.with_memory_space_constraint(value, pltpu.HBM)


def swap(value):
    return lax.ppermute(value, "c", [(0, 1), (1, 0)])


def norm_kernel(pos, p0, p1, p2, p3, gain, h1, held, sems):
    y = pos[1]
    half = h1.shape[2]
    rows = p0.shape[0]
    copies = []
    for k, piece in enumerate((p0, p1, p2, p3)):
        copies.append(pltpu.make_async_copy(piece, held.at[k], sems.at[k]))
    for copy in copies:
        copy.start()
    for k in range(N):
        copies[k].wait()
        normed = norm_rows(held[k].astype(F32), gain[...]).astype(BF)
        at = pl.ds(pl.multiple_of(lax.rem(y - k + N, N) * rows, rows), rows)
        h1[0, at, :] = normed[:, :half]
        h1[1, at, :] = normed[:, half:]


def qkv_kernel(pos, h1, w_hbm, o0, o1, o2, o3, share, w, sems):
    x = pos[0]
    c = pos[3]
    cols = w.shape[1]
    copies = []
    for k in range(N):
        at = pl.ds(lax.rem(x - k + N, N) * 2, 2)
        copies.append(pltpu.make_async_copy(w_hbm.at[at, :cols, :], w.at[at], sems.at[k]))
    for j in range(N):
        src = w_hbm.at[2 * j + c, cols : cols + HEAD, :]
        copies.append(pltpu.make_async_copy(src, share.at[j], sems.at[N + j]))
    for copy in copies:
        copy.start()
    for k, out in enumerate((o0, o1, o2, o3)):
        at = lax.rem(x - k + N, N) * 2
        copies[k].wait()
        total = lax.dot_general(w[at], h1[0], NT, preferred_element_type=F32)
        total += lax.dot_general(w[at + 1], h1[1], NT, preferred_element_type=F32)
        out[:HEAD, :] = (total[:HEAD, :] * SCALE).astype(BF)
        out[HEAD:, :] = total[HEAD:, :].astype(BF)
    for copy in copies[N:]:
        copy.wait()


def attend_kernel(
    pos, work, r0, r1, r2, r3, id_row, id_col, o0, o1, o2, o3, qs, ks, vs, scores, outs
):
    x = pos[0]
    chunk = ks.shape[1]
    block = qs.shape[2]
    per = block // chunk
    for k, piece in enumerate((r0, r1, r2, r3)):
        at = lax.rem(x + k, N)
        qs[at] = piece[:HEAD, :]
        keys = jnp.transpose(piece[HEAD : 2 * HEAD, :])
        for j in range(per):
            ks[at * per + j] = keys[j * chunk : (j + 1) * chunk, :]
            vs[at * per + j] = piece[2 * HEAD :, j * chunk : (j + 1) * chunk]
    count = work[4, 0]

    def score(i):
        return jnp.dot(ks[work[1, i]], qs[work[0, i]], preferred_element_type=F32)

    scores[0] = score(0)

    def step(i, carry):
        top, total, acc = carry
        slot = lax.rem(i, 2)
        qb = work[0, i]
        kc = work[1, i]
        raw = scores[slot]
        scores[1 - slot] = score(jnp.minimum(i + 1, count - 1))
        key_ids = id_col[pl.ds(pl.multiple_of(kc * chunk, chunk), chunk), :]
        val = jnp.where(key_ids == id_row[qb], raw, -1e30)
        top = jnp.where(work[2, i] == 1, -1e30, top)
        new_top = jnp.maximum(top, jnp.max(val, axis=0, keepdims=True))
        alpha = jnp.exp2(top - new_top)
        alpha = jnp.where(work[2, i] == 1, 0.0, alpha)
        expo = jnp.exp2(val - new_top)
        total = total * alpha + jnp.sum(expo, axis=0, keepdims=True)
        acc = acc * alpha + jnp.dot(vs[kc], expo.astype(BF), preferred_element_type=F32)

        @pl.when(work[3, i] == 1)
        def _():
            outs[lax.rem(qb - x + N, N)] = (acc / total).astype(BF)

        return new_top, total, acc

    start = (
        jnp.full((1, block), -1e30, F32),
        jnp.zeros((1, block), F32),
        jnp.zeros((HEAD, block), F32),
    )
    lax.fori_loop(0, count, step, start)
    for k, out in enumerate((o0, o1, o2, o3)):
        out[...] = outs[k]


def pack_kernel(pos, g0, g1, g2, g3, out):
    x = pos[0]
    for k, piece in enumerate((g0, g1, g2, g3)):
        out[lax.rem(x - k + N, N)] = piece[...]


def copy_all(moves, sems):
    copies = [pltpu.make_async_copy(a, b, sems.at[i]) for i, (a, b) in enumerate(moves)]
    for copy in copies:
        copy.start()
    for copy in copies:
        copy.wait()


def fetch_kernel(pos, *refs):
    pieces = refs[0:4]
    near, w_hbm = refs[4:6]
    mine = refs[6:9]
    other = refs[9:12]
    w_all, up, down, held, sems = refs[12:]
    y = pos[1]
    c = pos[3]
    half = w_all.shape[3]
    skip = near.shape[1] - HEAD
    moves = []
    for j in range(N):
        moves.append((near.at[2 * j, skip : skip + HEAD, :], w_all.at[0, j]))
        moves.append((near.at[2 * j + 1, skip : skip + HEAD, :], w_all.at[1, j]))
    for k in range(1, N):
        to = slice(k * N, (k + 1) * N)
        moves.append((mine[k - 1], w_all.at[c, to]))
        moves.append((other[k - 1], w_all.at[1 - c, to]))
    for k in range(N):
        moves.append((pieces[k], held.at[lax.rem(y - k + N, N)]))
    units = up.shape[1]
    for h in (0, 1):
        cols = slice(h * half, (h + 1) * half)
        moves.append((w_hbm.at[:, h, :units, :], up.at[:, :, cols]))
        moves.append((w_hbm.at[:, h, units:, :], down.at[:, :, cols]))
    copy_all(moves, sems)


def fetch_merge_kernel(w_hbm, w, sems):
    parts = sems.shape[0]
    rows = w.shape[0] // parts
    cuts = [slice(i * rows, (i + 1) * rows) for i in range(parts)]
    copy_all([(w_hbm.at[cut], w.at[cut]) for cut in cuts], sems)


def mlp_kernel(offsets, pos, *refs):
    gathered = refs[0:4]
    w_all, up, down, held, gain = refs[4:9]
    outs = refs[9:]
    y = pos[1]
    rows = held.shape[1]
    width = held.shape[2]
    half = width // 2
    group = N * HEAD
    blocks = [lax.rem(y + k, N) for k in offsets]
    lhs = []
    start = []
    for block in blocks:
        cols = pl.ds(pl.multiple_of(block * rows, rows), rows)
        parts = [g[:, :, cols].reshape(group, rows) for g in gathered]
        lhs.append(jnp.transpose(jnp.concatenate(parts, axis=0)))
        start.append(held[block].astype(F32))
    lhs = jnp.concatenate(lhs, axis=0)
    start = jnp.concatenate(start, axis=0)
    heads = N * group
    attn = [
        jnp.dot(lhs, w_all[h].reshape(heads, half), preferred_element_type=F32) for h in (0, 1)
    ]
    resid = (start + jnp.concatenate(attn, axis=1)).astype(BF)
    normed = norm_rows(resid.astype(F32), gain[...]).astype(BF)
    count = up.shape[0] * up.shape[1]
    hidden = lax.dot_general(
        normed, up[...].reshape(count, width), NT, preferred_element_type=F32
    )
    hidden = (0.5 * hidden * (1.0 + lax.erf(hidden * math.sqrt(0.5)))).astype(BF)
    result = jnp.dot(hidden, down[...].reshape(count, width), preferred_element_type=F32)
    result = result.astype(BF)
    for i, k in enumerate(offsets):
        outs[i][...] = result[i * rows : (i + 1) * rows, :]
        if k == 0:
            outs[-1][...] = resid[i * rows : (i + 1) * rows, :]


def merge_kernel(early, late, w, select, tail, out, vision):
    sums = (early[...] + late[...].astype(F32)).astype(BF).astype(F32)
    full, width = early.shape
    count = full // 4
    tiles = width // 128
    for i in range(tiles):
        vision[i * full : (i + 1) * full, :] = sums[:, i * 128 : (i + 1) * 128]
    total = jnp.zeros((count, width), F32)
    for j in range(4):
        rows = [vision[pl.ds(i * full + j, count, stride=4), :] for i in range(tiles)]
        rows = jnp.concatenate(rows, axis=1).astype(BF)
        total += jnp.dot(rows, w[j * width : (j + 1) * width, :], preferred_element_type=F32)
    sent = jnp.dot(select[...], total.astype(BF), preferred_element_type=F32)
    out[:, :width] = sent.astype(BF)
    out[:, width:] = tail[...]


def local(
    patches,
    picture_ids,
    ln_attn,
    w_qkv,
    w_out,
    ln_mlp,
    w_up,
    w_down,
    w_merge,
    text_embed,
    slot_dest,
):
    rows = patches[0]
    count, width = rows.shape
    x = lax.axis_index("x")
    y = lax.axis_index("y")
    c = lax.axis_index("c")
    pos = jnp.stack([x, y, lax.axis_index("z"), c]).astype(jnp.int32)
    ids = picture_ids[0]

    half = width // 2
    w_heads = jnp.transpose(w_qkv, (0, 2, 1)).reshape(3 * HEAD, width)
    w_heads = jnp.concatenate([w_heads, w_out], axis=0)
    w_half = lax.dynamic_slice_in_dim(w_heads, c * half, half, 1)
    near = lax.all_gather(w_half, ("x", "c"), axis=0, tiled=False)
    z = lax.axis_index("z")
    units = w_down.shape[0] // N
    sizes = (units, half)
    packed = jnp.concatenate(
        [
            lax.dynamic_slice(w_up.T, (z * units, c * half), sizes),
            lax.dynamic_slice(w_down, (z * units, c * half), sizes),
        ],
        axis=0,
    )
    packed, _ = lax.optimization_barrier((packed, w_half))
    w_near = lax.all_gather(packed, ("x", "z", "c"), axis=0, tiled=False)
    w_near = w_near.reshape(N * N, 2, 2 * units, half)

    pieces = [rows] + [shift(rows, "y", k) for k in (1, 2, 3)]
    total_rows = count * N
    h1 = pl.pallas_call(
        norm_kernel,
        out_shape=jax.ShapeDtypeStruct((2, total_rows, half), BF),
        in_specs=[SMEM] + [HBM] * N + [VMEM],
        out_specs=VMEM,
        scratch_shapes=[
            pltpu.VMEM((N, count, width), BF),
            pltpu.SemaphoreType.DMA((N,)),
        ],
        compiler_params=params(16),
        name="norm",
    )(pos, *[far(piece) for piece in pieces], ln_attn[None, :])
    group_rows = ids.shape[0]
    chunk = 256
    chunks = group_rows // chunk
    held = (ids[:, None] == jnp.arange(16)[None, :]).reshape(chunks, chunk, 16)
    held = jnp.any(held, axis=1)
    per = chunks // N
    wanted = jnp.any(held.reshape(N, per, 16), axis=1)
    need = jnp.any(wanted[:, None, :] & held[None, :, :], axis=2)
    where = jnp.arange(chunks)[None, :]
    low = jnp.min(jnp.where(need, where, chunks - 1), axis=1)
    high = jnp.max(jnp.where(need, where + 1, 1), axis=1)
    low = jnp.minimum(low, high - 1)
    spans = high - low
    index = jnp.arange(N)
    ends = jnp.sum(jnp.where(index[None, :] <= index[:, None], spans[None, :], 0), axis=1)
    item = jnp.arange(N * chunks)
    block = jnp.sum((item[:, None] >= ends[None, :]).astype(jnp.int32), axis=1)
    block = jnp.minimum(block, N - 1)
    mark = block[:, None] == index[None, :]
    begin = jnp.sum(jnp.where(mark, (low + spans - ends)[None, :], 0), axis=1)
    key = jnp.clip(begin + item, 0, chunks - 1)
    is_first = jnp.any(mark & ((ends - spans)[None, :] == item[:, None]), axis=1)
    is_last = jnp.any(mark & ((ends - 1)[None, :] == item[:, None]), axis=1)
    total_items = jnp.full_like(item, 1) * ends[N - 1]
    work = jnp.stack([block, key, is_first, is_last, total_items]).astype(jnp.int32)

    merged_count = count // 4
    dest = slot_dest[0]
    prompt_rows = text_embed.shape[0]
    req_count = N * N
    row_count = lax.axis_size("z") * lax.axis_size("c")
    slot_cap = 2
    owner = jnp.where(dest >= 0, dest // prompt_rows // row_count, -1)
    order = jnp.arange(merged_count)
    same_owner = (owner[:, None] == owner[None, :]) & (order[None, :] < order[:, None])
    ranks = jnp.sum(same_owner.astype(jnp.int32), axis=1)
    target = jnp.where(owner >= 0, owner * slot_cap + ranks, -1)
    select = target[None, :] == jnp.arange(req_count * slot_cap)[:, None]
    places = jnp.sum(jnp.where(select, (dest % prompt_rows + 1)[None, :], 0), axis=1)
    lane = jnp.arange(128)[None, :] == 0
    tail = jnp.where(lane, places[:, None], 0).astype(BF)
    id_row = ids.reshape(N, 1, total_rows)
    id_col = ids[:, None]
    select = select.astype(BF)
    near, h1, work, id_col, select, tail = lax.optimization_barrier(
        (near, h1, work, id_col, select, tail)
    )
    *qkv, mine = pl.pallas_call(
        qkv_kernel,
        out_shape=[jax.ShapeDtypeStruct((3 * HEAD, total_rows), BF)] * N
        + [jax.ShapeDtypeStruct((N, HEAD, half), BF)],
        in_specs=[SMEM, VMEM, HBM],
        out_specs=[VMEM] * (N + 1),
        scratch_shapes=[
            pltpu.VMEM((2 * N, 3 * HEAD, half), BF),
            pltpu.SemaphoreType.DMA((2 * N,)),
        ],
        compiler_params=params(16),
        name="qkv",
    )(pos, h1, far(near))
    blocks = [qkv[0]] + [shift(qkv[k], "x", -k) for k in (1, 2, 3)]
    pass1 = shift(mine, "y", 1)
    pass3 = shift(mine, "y", 3)
    blocks, mine, pass1, pass3 = lax.optimization_barrier((blocks, mine, pass1, pass3))
    pass2 = shift(mine, "y", 2)
    swap1 = swap(pass1)
    swap3 = swap(pass3)

    attended = pl.pallas_call(
        attend_kernel,
        out_shape=[jax.ShapeDtypeStruct((HEAD, total_rows), BF)] * N,
        in_specs=[SMEM, SMEM] + [VMEM] * 6,
        out_specs=[VMEM] * N,
        scratch_shapes=[
            pltpu.VMEM((N, HEAD, total_rows), BF),
            pltpu.VMEM((chunks, chunk, HEAD), BF),
            pltpu.VMEM((chunks, HEAD, chunk), BF),
            pltpu.VMEM((2, chunk, total_rows), F32),
            pltpu.VMEM((N, HEAD, total_rows), BF),
        ],
        compiler_params=params(16),
        name="attend",
    )(pos, work, *blocks, id_row, id_col)
    attended, pass2, swap1, swap3 = lax.optimization_barrier((attended, pass2, swap1, swap3))
    swap2 = swap(pass2)
    heads = [attended[0]] + [shift(attended[k], "x", k) for k in (1, 2, 3)]
    heads = pl.pallas_call(
        pack_kernel,
        out_shape=jax.ShapeDtypeStruct((N, HEAD, total_rows), BF),
        in_specs=[SMEM] + [VMEM] * N,
        out_specs=VMEM,
        compiler_params=params(8),
        name="pack",
    )(pos, *heads)
    gathered = [heads] + [shift(heads, "y", k) for k in (1, 2, 3)]
    _, near, w_near, w_merge = lax.optimization_barrier((heads, near, w_near, w_merge))

    fetched = pl.pallas_call(
        fetch_kernel,
        out_shape=[
            jax.ShapeDtypeStruct((2, N * N, HEAD, half), BF),
            jax.ShapeDtypeStruct((N * N, units, width), BF),
            jax.ShapeDtypeStruct((N * N, units, width), BF),
            jax.ShapeDtypeStruct((N, count, width), BF),
        ],
        in_specs=[SMEM] + [HBM] * 12,
        out_specs=[VMEM] * 4,
        scratch_shapes=[pltpu.SemaphoreType.DMA((22,))],
        compiler_params=params(4),
        name="fetch",
    )(
        pos,
        *[far(v) for v in pieces],
        *[far(v) for v in (near, w_near, pass1, pass2, pass3, swap1, swap2, swap3)],
    )

    w_merge = pl.pallas_call(
        fetch_merge_kernel,
        out_shape=jax.ShapeDtypeStruct(w_merge.shape, BF),
        in_specs=[HBM],
        out_specs=VMEM,
        scratch_shapes=[pltpu.SemaphoreType.DMA((8,))],
        compiler_params=params(4),
        name="fetch_merge",
    )(far(w_merge))

    def mlp(offsets, name):
        outputs = len(offsets) + (0 in offsets)
        return pl.pallas_call(
            functools.partial(mlp_kernel, offsets),
            out_shape=[jax.ShapeDtypeStruct((count, width), BF)] * outputs,
            in_specs=[SMEM] + [VMEM] * 9,
            out_specs=[VMEM] * outputs,
            compiler_params=params(24),
            cost_estimate=pl.CostEstimate(
                flops=6 * len(offsets) * count * width * width,
                transcendentals=len(offsets) * count * width,
                bytes_accessed=6 * width * width,
            ),
            name=name,
        )(pos, *gathered, *fetched, ln_mlp[None, :])

    part2, part1 = mlp((2, 1), "mlp_first")
    gathered[0], w_merge, part2, part1 = lax.optimization_barrier(
        (gathered[0], w_merge, part2, part1)
    )
    part3, part0, resid = mlp((3, 0), "mlp_second")
    early = shift(part1, "y", 1).astype(F32) + shift(part2, "y", 2).astype(F32)
    sums = [resid.astype(F32) + part0.astype(F32) + early, shift(part3, "y", 3)]
    outgoing = pl.pallas_call(
        merge_kernel,
        out_shape=jax.ShapeDtypeStruct((req_count * slot_cap, width + 128), BF),
        in_specs=[VMEM] * 5,
        out_specs=VMEM,
        scratch_shapes=[pltpu.VMEM((count * width // 128, 128), F32)],
        compiler_params=params(8),
        name="merge",
    )(*sums, w_merge, select, tail)
    arrived = lax.all_to_all(
        outgoing.reshape(req_count, slot_cap, width + 128),
        ("x", "y"),
        split_axis=0,
        concat_axis=0,
        tiled=True,
    ).reshape(req_count * slot_cap, width + 128)
    landing = arrived[:, width].astype(jnp.int32) - 1
    placer = landing[None, :] == jnp.arange(prompt_rows)[:, None]
    placed = jnp.dot(
        placer.astype(BF), arrived[:, :width], preferred_element_type=F32
    ).astype(BF)
    filled = jnp.any(placer, axis=1)
    return jnp.where(filled[:, None], placed, text_embed)


def solution(mesh):
    grid = Mesh(mesh.devices.reshape(N, N, -1, 2), ("x", "y", "z", "c"))
    req = ("x", "y")
    row = ("z", "c")
    return jax.shard_map(
        local,
        mesh=grid,
        in_specs=(
            P(row, req, None),
            P(row, None),
            P(),
            P(None, None, req),
            P(req, None),
            P(),
            P(None, req),
            P(req, None),
            P(),
            P(("x", "y", "z", "c"), None),
            P(row, req),
        ),
        out_specs=P(("x", "y", "z", "c"), None),
        check_vma=False,
    )
```

time: 164 us -> 157 us (0.957)
  waiting for transfers between devices: 68.7 us -> 59.9 us
  Pallas kernels: 29.3 us -> 34.2 us
  starting transfers between devices: 27.6 us -> 23.6 us
    ppermute x18, waiting for transfers between devices: 62.4 us -> 52.8 us  [shift(): return lax.ppermute(value, axis, pairs)]
    pallas_call x1 -> x4, Pallas kernels: 11.4 us -> 18.1 us  [the longest x2 8.14 us: mlp(): pl.pallas_call(functools.partial(mlp_kernel, offsets), out_shape=[jax.Sha...]
    ppermute x18, starting transfers between devices: 27.3 us -> 23 us  [shift(): return lax.ppermute(value, axis, pairs)]
    all_gather x1, waiting for transfers between devices: 0.02 us -> 1.81 us  [local(): w_near = lax.all_gather(packed, ('x', 'z', 'c'), axis=0, tiled=False)]
  transfers between devices with their start and end apart: 23 -> 23, of which waited for: 14 -> 14; matrix products, arithmetic and copies ran while one was open for 5% -> 5% of each run, Pallas kernels for 9% -> 18%
where the time goes in v6:
time: 157 us
  waiting for transfers between devices  59.9 us (38%)
  Pallas kernels  34.2 us (22%)
  starting transfers between devices  23.6 us (15%)
  between operations  13.6 us (9%)
  blocking collectives  12.1 us (8%)
  other arithmetic  7 us (4%)
  local copies, waits for them, and re-layouts  5.24 us (3%)
    ppermute x18, waiting for transfers between devices, shift(): return lax.ppermute(value, axis, pairs)  52.8 us
    ppermute x18, starting transfers between devices, shift(): return lax.ppermute(value, axis, pairs)  23 us
    all_to_all x1, blocking collectives, local(): lax.all_to_all(outgoing.reshape(req_count, slot_cap, width + 128), ('x',...  12.1 us
    pallas_call x2, Pallas kernels, mlp(): pl.pallas_call(functools.partial(mlp_kernel, offsets), out_shape=[jax.Sha...  8.14 us
    pallas_call x1, Pallas kernels, local(): pl.pallas_call(attend_kernel, out_shape=[jax.ShapeDtypeStruct((HEAD, tota...  6.47 us
    all_gather x1, waiting for transfers between devices, local(): near = lax.all_gather(w_half, ('x', 'c'), axis=0, tiled=False)  5.24 us
    pallas_call x1, Pallas kernels, local(): pl.pallas_call(fetch_kernel, out_shape=[jax.ShapeDtypeStruct((2, N * N, H...  5.11 us
    pallas_call x1, Pallas kernels, local(): pl.pallas_call(fetch_merge_kernel, out_shape=jax.ShapeDtypeStruct(w_merge...  4.85 us
  transfers between devices with their start and end apart: 23, of which 14 were waited for; matrix products, arithmetic and copies ran while one was open for 5% of the time, Pallas kernels for 18%

profile of v6, /device:TPU:0, one launch (start us, length us, event | category | flops | bytes accessed | tf_op | source)
XLA Modules:
  0.0 156.8 jit_solution(9719996349126448718)
XLA Ops:
  6.5 1.9 %fusion.1 = bf16[320,640]{1,0:T(8,128)(2,1)} fusion(s32[]{:T(128)S(6)} %select_n.84, bf16[240,1280]{1,0:T(8,128)(2,1)} %bitcast.55, bf16[80,1280]{1,0:T(8,128)(2,1)} %param.15), kind=kLoop, calls=%fused_computation.5 | loop fusion | flops 819200 | bytes 1228804 | tf_op jit(solution)/shard_map/concatenate | solution.py:269
  8.5 0.9 dynamic_slice.11
  9.4 0.7 pad_maximum_fusion
  10.2 3.2 %collective-permute-start.2 = (bf16[128,1280]{1,0:T(8,128)(2,1)}, bf16[128,1280]{1,0:T(8,128)(2,1)S(1)}, u32[]{:S(2)}, u32[]{:S(2)}) collective-permute-start(bf16[128,1280]{1,0:T(8,128)(2,1)} %bitcast.50), channel_id=1, source_target_pairs={{0,24},{8,0},{16,8},{24,16},{1,25},{9,1},{17,9},{25,17},{2,26},{10... | collective-permute-start | bytes 983048 | tf_op jit(solution)/shard_map/ppermute | solution.py:36
  13.3 0.6 collective-permute-start.1
  14.0 1.0 collective-permute-start
  14.9 0.7 broadcast_in_dim.124.gain
  15.6 0.5 broadcast.211
  16.1 1.3 reduce.5
  17.4 0.2 fusion.2
  17.7 0.2 and_reduce_fusion
  17.8 0.2 select_reduce_fusion.3
  18.0 0.1 select_reduce_fusion.2
  18.1 0.6 slice.9
  18.8 0.1 select_reduce_fusion.1
  18.9 0.1 fusion.11
  19.0 0.5 stack.30
  19.6 0.7 compare_select_fusion
  20.2 0.7 fusion.14
  20.9 0.2 convert_reduce_fusion
  21.1 0.1 select_reduce_fusion
  21.4 6.3 %collective-permute-done.2.p3.refs_3_ = bf16[128,1280]{1,0:T(8,128)(2,1)S(1)} collective-permute-done((bf16[128,1280]{1,0:T(8,128)(2,1)}, bf16[128,1280]{1,0:T(8,128)(2,1)S(1)}, u32[]{:S(2)}, u32[]{:S(2)}) %collective-permute-start.2) | collective-permute-done | bytes 327712 | tf_op jit(solution)/shard_map/ppermute | solution.py:36
  27.7 3.6 %collective-permute-done.p1.refs_1_ = bf16[128,1280]{1,0:T(8,128)(2,1)S(1)} collective-permute-done((bf16[128,1280]{1,0:T(8,128)(2,1)}, bf16[128,1280]{1,0:T(8,128)(2,1)S(1)}, u32[]{:S(2)}, u32[]{:S(2)}) %collective-permute-start) | collective-permute-done | bytes 327712 | tf_op jit(solution)/shard_map/ppermute | solution.py:36
  31.3 0.7 copy-done.4
  32.0 2.6 %norm.1.h1 = bf16[2,512,640]{2,1,0:T(8,128)(2,1)S(1)} custom-call(s32[4]{0:T(128)S(1)} %pad_add_fusion.pos, bf16[128,1280]{1,0:T(8,128)(2,1)} %bitcast.53, bf16[128,1280]{1,0:T(8,128)(2,1)} %copy-done.4, bf16[128,1280]{1,0:T(8,128)(2,1)} %copy-done.3, bf16[128,1280]{1,0:T(8,128)(2,1)} %copy-done.2, f32[1,1280]{1,0:T(1,128)S(1)} %broadcast_in_dim.124.gain), custom_call_target="tpu_custom_call" | custom-call | tf_op jit(solution)/shard_map/norm/pallas_call | solution.py:288
  34.6 5.2 %all-gather.5.cloned.1.call-done = bf16[2560,640]{1,0:T(8,128)(2,1)} async-done(((bf16[320,640]{1,0:T(8,128)(2,1)}), bf16[2560,640]{1,0:T(8,128)(2,1)}) %all-gather.5.cloned.1.call-update) | async-done | bytes 3276816 | tf_op jit(solution)/shard_map/all_gather | solution.py:271
  39.8 4.1 %qkv.1 = (bf16[240,512]{1,0:T(8,128)(2,1)S(1)}, bf16[240,512]{1,0:T(8,128)(2,1)S(1)}, bf16[240,512]{1,0:T(8,128)(2,1)S(1)}, bf16[240,512]{1,0:T(8,128)(2,1)S(1)}, bf16[4,80,640]{2,1,0:T(8,128)(2,1)S(1)}) custom-call(s32[4]{0:T(128)S(1)} %pad_add_fusion.pos, bf16[2,512,640]{2,1,0:T(8,128)(2,1)S(1)} %norm.1.h1, bf16[8,320,640]{2,1,0:T(8,128)(2,1)} %bitcast.47), custom_call_target="tpu_custom_call" | custom-call | tf_op jit(solution)/shard_map/qkv/pallas_call | solution.py:347
  43.9 2.8 %collective-permute-start.7 = (bf16[4,80,640]{2,1,0:T(8,128)(2,1)S(1)}, bf16[4,80,640]{2,1,0:T(8,128)(2,1)}, u32[]{:S(2)}, u32[]{:S(2)}) collective-permute-start(bf16[4,80,640]{2,1,0:T(8,128)(2,1)S(1)} %get-tuple-element.68), channel_id=1, source_target_pairs={{0,24},{8,0},{16,8},{24,16},{1,25},{9,1},{17,9},{25,17},{2,26},{10... | collective-permute-start | bytes 1228808 | tf_op jit(solution)/shard_map/ppermute | solution.py:36
  46.7 1.4 collective-permute-start.3
  48.2 1.0 collective-permute-start.4
  49.2 0.6 collective-permute-start.5
  49.8 6.6 %collective-permute-done.3.r1 = bf16[240,512]{1,0:T(8,128)(2,1)S(1)} collective-permute-done((bf16[240,512]{1,0:T(8,128)(2,1)S(1)}, bf16[240,512]{1,0:T(8,128)(2,1)S(1)}, u32[]{:S(2)}, u32[]{:S(2)}) %collective-permute-start.3) | collective-permute-done | bytes 245792 | tf_op jit(solution)/shard_map/ppermute | solution.py:36
  56.4 3.6 %collective-permute-done.4.r2 = bf16[240,512]{1,0:T(8,128)(2,1)S(1)} collective-permute-done((bf16[240,512]{1,0:T(8,128)(2,1)S(1)}, bf16[240,512]{1,0:T(8,128)(2,1)S(1)}, u32[]{:S(2)}, u32[]{:S(2)}) %collective-permute-start.4) | collective-permute-done | bytes 245792 | tf_op jit(solution)/shard_map/ppermute | solution.py:36
  60.0 5.7 %collective-permute-done.5.r3 = bf16[240,512]{1,0:T(8,128)(2,1)S(1)} collective-permute-done((bf16[240,512]{1,0:T(8,128)(2,1)S(1)}, bf16[240,512]{1,0:T(8,128)(2,1)S(1)}, u32[]{:S(2)}, u32[]{:S(2)}) %collective-permute-start.5) | collective-permute-done | bytes 245792 | tf_op jit(solution)/shard_map/ppermute | solution.py:36
  65.6 1.6 %collective-permute-start.8 = (bf16[4,80,640]{2,1,0:T(8,128)(2,1)S(1)}, bf16[4,80,640]{2,1,0:T(8,128)(2,1)}, u32[]{:S(2)}, u32[]{:S(2)}) collective-permute-start(bf16[4,80,640]{2,1,0:T(8,128)(2,1)S(1)} %get-tuple-element.68), channel_id=1, source_target_pairs={{0,16},{8,24},{16,0},{24,8},{1,17},{9,25},{17,1},{25,9},{2,18},{10... | collective-permute-start | bytes 1228808 | tf_op jit(solution)/shard_map/ppermute | solution.py:36
  67.2 0.5 collective-permute-start.10
  67.7 0.4 copy.15.id_col
  68.1 6.5 %attend.1 = (bf16[80,512]{1,0:T(8,128)(2,1)S(1)}, bf16[80,512]{1,0:T(8,128)(2,1)S(1)}, bf16[80,512]{1,0:T(8,128)(2,1)S(1)}, bf16[80,512]{1,0:T(8,128)(2,1)S(1)}) custom-call(s32[4]{0:T(128)S(1)} %pad_add_fusion.pos, s32[5,32]{1,0:T(8,128)S(1)} %stack.31.work, bf16[240,512]{1,0:T(8,128)(2,1)S(1)} %get-tuple-element.59.r0, ...), custom_call_target="tpu_custom_call" | custom-call | tf_op jit(solution)/shard_map/attend/pallas_call | solution.py:368
  74.6 4.0 %collective-permute-done.8.refs_7_ = bf16[4,80,640]{2,1,0:T(8,128)(2,1)} collective-permute-done((bf16[4,80,640]{2,1,0:T(8,128)(2,1)S(1)}, bf16[4,80,640]{2,1,0:T(8,128)(2,1)}, u32[]{:S(2)}, u32[]{:S(2)}) %collective-permute-start.8) | collective-permute-done | bytes 409632 | tf_op jit(solution)/shard_map/ppermute | solution.py:36
  78.7 0.8 collective-permute-start.12
  79.5 2.5 %collective-permute-start.13 = (bf16[80,512]{1,0:T(8,128)(2,1)S(1)}, bf16[80,512]{1,0:T(8,128)(2,1)S(1)}, u32[]{:S(2)}, u32[]{:S(2)}) collective-permute-start(bf16[80,512]{1,0:T(8,128)(2,1)S(1)} %get-tuple-element.74), channel_id=1, source_target_pairs={{0,96},{32,0},{64,32},{96,64},{1,97},{33,1},{65,33},{97,65},{2,98}... | collective-permute-start | bytes 245768 | tf_op jit(solution)/shard_map/ppermute | solution.py:36
  82.0 6.0 %collective-permute-done.11.g1 = bf16[80,512]{1,0:T(8,128)(2,1)S(1)} collective-permute-done((bf16[80,512]{1,0:T(8,128)(2,1)S(1)}, bf16[80,512]{1,0:T(8,128)(2,1)S(1)}, u32[]{:S(2)}, u32[]{:S(2)}) %collective-permute-start.11) | collective-permute-done | bytes 81952 | tf_op jit(solution)/shard_map/ppermute | solution.py:36
  88.1 2.6 %collective-permute-done.13.g3 = bf16[80,512]{1,0:T(8,128)(2,1)S(1)} collective-permute-done((bf16[80,512]{1,0:T(8,128)(2,1)S(1)}, bf16[80,512]{1,0:T(8,128)(2,1)S(1)}, u32[]{:S(2)}, u32[]{:S(2)}) %collective-permute-start.13) | collective-permute-done | bytes 81952 | tf_op jit(solution)/shard_map/ppermute | solution.py:36
  90.7 0.6 pack.1.refs_0_
  91.3 3.2 %collective-permute-start.16 = (bf16[4,80,512]{2,1,0:T(8,128)(2,1)S(1)}, bf16[4,80,512]{2,1,0:T(8,128)(2,1)S(1)}, u32[]{:S(2)}, u32[]{:S(2)}) collective-permute-start(bf16[4,80,512]{2,1,0:T(8,128)(2,1)S(1)} %pack.1.refs_0_), channel_id=1, source_target_pairs={{0,24},{8,0},{16,8},{24,16},{1,25},{9,1},{17,9},{25,17},{2,26},{10... | collective-permute-start | bytes 983048 | tf_op jit(solution)/shard_map/ppermute | solution.py:36
  94.5 0.9 collective-permute-start.14
  95.5 1.8 %all-gather.7.cloned.1.call-done = bf16[5120,640]{1,0:T(8,128)(2,1)} async-done(((bf16[160,640]{1,0:T(8,128)(2,1)}), bf16[5120,640]{1,0:T(8,128)(2,1)}) %all-gather.7.cloned.1.call-update) | async-done | bytes 6553616 | tf_op jit(solution)/shard_map/all_gather | solution.py:283
  97.3 4.8 %fetch_merge.1.w = bf16[5120,1280]{1,0:T(8,128)(2,1)S(1)} custom-call(bf16[5120,1280]{1,0:T(8,128)(2,1)} %w_hbm), custom_call_target="tpu_custom_call" | custom-call | tf_op jit(solution)/shard_map/fetch_merge/pallas_call | solution.py:416
  102.1 0.8 copy-done.5
  102.9 5.1 %fetch.1 = (bf16[2,16,80,640]{3,2,1,0:T(8,128)(2,1)S(1)}, bf16[16,80,1280]{2,1,0:T(8,128)(2,1)S(1)}, bf16[16,80,1280]{2,1,0:T(8,128)(2,1)S(1)}, bf16[4,128,1280]{2,1,0:T(8,128)(2,1)S(1)}) custom-call(s32[4]{0:T(128)S(1)} %pad_add_fusion.pos, bf16[128,1280]{1,0:T(8,128)(2,1)} %bitcast.54, bf16[128,1280]{1,0:T(8,128)(2,1)} %copy-done.4, ...), custom_call_target="tpu_custom_call" | custom-call | tf_op jit(solution)/shard_map/fetch/pallas_call | solution.py:397
  108.0 0.4 collective-permute-done.16.refs_3_
  108.4 3.4 %collective-permute-done.14.refs_1_ = bf16[4,80,512]{2,1,0:T(8,128)(2,1)S(1)} collective-permute-done((bf16[4,80,512]{2,1,0:T(8,128)(2,1)S(1)}, bf16[4,80,512]{2,1,0:T(8,128)(2,1)S(1)}, u32[]{:S(2)}, u32[]{:S(2)}) %collective-permute-start.14) | collective-permute-done | bytes 327712 | tf_op jit(solution)/shard_map/ppermute | solution.py:36
  111.8 4.1 %mlp_first.1 = (bf16[128,1280]{1,0:T(8,128)(2,1)S(1)}, bf16[128,1280]{1,0:T(8,128)(2,1)S(1)}) custom-call(s32[4]{0:T(128)S(1)} %pad_add_fusion.pos, bf16[4,80,512]{2,1,0:T(8,128)(2,1)S(1)} %pack.1.refs_0_, bf16[4,80,512]{2,1,0:T(8,128)(2,1)S(1)} %collective-permute-done.14.refs_1_, bf16[4,80,512]{2,1,0:T(8,128)(2,1)S(1)} %collective-permute-done.15.refs_2_, ...), custom_call_target="tpu_custom_call" | custom-call | flops 2516582400 | bytes 9830400 | tf_op jit(solution)/shard_map/mlp_first/pallas_call | solution.py:428
  116.0 2.4 %collective-permute-start.19 = (bf16[128,1280]{1,0:T(8,128)(2,1)S(1)}, bf16[128,1280]{1,0:T(8,128)(2,1)S(1)}, u32[]{:S(2)}, u32[]{:S(2)}) collective-permute-start(bf16[128,1280]{1,0:T(8,128)(2,1)S(1)} %get-tuple-element.92), channel_id=1, source_target_pairs={{0,16},{8,24},{16,0},{24,8},{1,17},{9,25},{17,1},{25,9},{2,18},{10... | collective-permute-start | bytes 983048 | tf_op jit(solution)/shard_map/ppermute | solution.py:36
  118.3 4.1 %mlp_second.1 = (bf16[128,1280]{1,0:T(8,128)(2,1)S(1)}, bf16[128,1280]{1,0:T(8,128)(2,1)S(1)}, bf16[128,1280]{1,0:T(8,128)(2,1)S(1)}) custom-call(s32[4]{0:T(128)S(1)} %pad_add_fusion.pos, bf16[4,80,512]{2,1,0:T(8,128)(2,1)S(1)} %pack.1.refs_0_, bf16[4,80,512]{2,1,0:T(8,128)(2,1)S(1)} %collective-permute-done.14.refs_1_, ...), custom_call_target="tpu_custom_call" | custom-call | flops 2516582400 | bytes 9830400 | tf_op jit(solution)/shard_map/mlp_second/pallas_call | solution.py:428
  122.4 0.9 collective-permute-start.20
  123.3 10.1 %collective-permute-done.18 = bf16[128,1280]{1,0:T(8,128)(2,1)S(1)} collective-permute-done((bf16[128,1280]{1,0:T(8,128)(2,1)S(1)}, bf16[128,1280]{1,0:T(8,128)(2,1)S(1)}, u32[]{:S(2)}, u32[]{:S(2)}) %collective-permute-start.18) | collective-permute-done | bytes 327712 | tf_op jit(solution)/shard_map/ppermute | solution.py:36
  133.5 0.2 add_add_fusion.early
  133.6 0.4 collective-permute-done.20.late
  134.0 2.4 %merge.1 = bf16[32,1408]{1,0:T(8,128)(2,1)S(1)} custom-call(f32[128,1280]{1,0:T(8,128)S(1)} %add_add_fusion.early, bf16[128,1280]{1,0:T(8,128)(2,1)S(1)} %collective-permute-done.20.late, bf16[5120,1280]{1,0:T(8,128)(2,1)S(1)} %fetch_merge.1.w, bf16[32,32]{1,0:T(8,128)(2,1)S(1)} %fusion.5.select, bf16[32,128]{1,0:T(8,128)(2,1)S(1)} %select_convert_fusion.tail), custom_call_target="tpu_custom_call" | custom-call | tf_op jit(solution)/shard_map/merge/pallas_call | solution.py:449
  136.5 12.1 %all_to_all.5 = bf16[16,2,1408]{2,1,0:T(2,128)(2,1)S(1)} all-to-all(bf16[16,2,1408]{2,1,0:T(2,128)(2,1)S(1)} %reshape.167), channel_id=1, replica_groups=mesh['x'=4,'y'=4,'z'=4,'c'=2] {'x','y'}, dimensions={0} | all-to-all | bytes 180224 | tf_op jit(solution)/shard_map/all_to_all | solution.py:458
  148.7 0.1 add_reduce_fusion
  148.8 0.1 fusion.4
  148.9 1.1 fusion
  (53 shorter events, 0.8 us)
Async XLA Ops:
  6.5 2.9 %copy-start = (bf16[1280,320]{0,1:T(8,128)(2,1)S(1)}, bf16[1280,320]{0,1:T(8,128)(2,1)}, u32[]{:S(2)}) copy-start(bf16[1280,320]{0,1:T(8,128)(2,1)} %param.17) | copy-start | bytes 2457604
  6.5 33.3 %all-gather.5.cloned.1.call-start = ((), (), s32[]{:S(2)}) async-start(), calls=%async_computation.1 | async-start | bytes 3686400 | tf_op jit(solution)/shard_map/all_gather | solution.py:271
  8.4 88.8 %all-gather.7.cloned.1.call-start = ((), (), s32[]{:S(2)}) async-start(), calls=%async_computation.2 | async-start | bytes 6758400 | tf_op jit(solution)/shard_map/all_gather | solution.py:283
  10.2 17.5 %collective-permute-start.2 = (bf16[128,1280]{1,0:T(8,128)(2,1)}, bf16[128,1280]{1,0:T(8,128)(2,1)S(1)}, u32[]{:S(2)}, u32[]{:S(2)}) collective-permute-start(bf16[128,1280]{1,0:T(8,128)(2,1)} %bitcast.50), channel_id=1, source_target_pairs={{0,24},{8,0},{16,8},{24,16},{1,25},{9,1},{17,9},{25,17},{2,26},{10... | collective-permute-start | bytes 983048 | tf_op jit(solution)/shard_map/ppermute | solution.py:36
  13.3 14.3 %collective-permute-start.1 = (bf16[128,1280]{1,0:T(8,128)(2,1)}, bf16[128,1280]{1,0:T(8,128)(2,1)S(1)}, u32[]{:S(2)}, u32[]{:S(2)}) collective-permute-start(bf16[128,1280]{1,0:T(8,128)(2,1)} %bitcast.51), channel_id=1, source_target_pairs={{0,16},{8,24},{16,0},{24,8},{1,17},{9,25},{17,1},{25,9},{2,18},{10... | collective-permute-start | bytes 983048 | tf_op jit(solution)/shard_map/ppermute | solution.py:36
  14.0 17.3 %collective-permute-start = (bf16[128,1280]{1,0:T(8,128)(2,1)}, bf16[128,1280]{1,0:T(8,128)(2,1)S(1)}, u32[]{:S(2)}, u32[]{:S(2)}) collective-permute-start(bf16[128,1280]{1,0:T(8,128)(2,1)} %bitcast.52), channel_id=1, source_target_pairs={{0,8},{8,16},{16,24},{24,0},{1,9},{9,17},{17,25},{25,1},{2,10},{10... | collective-permute-start | bytes 983048 | tf_op jit(solution)/shard_map/ppermute | solution.py:36
  21.4 46.3 %copy-start.1 = (s32[1,2048]{1,0:T(1,128)S(1)}, s32[1,2048]{1,0:T(1,128)}, u32[]{:S(2)}) copy-start(s32[1,2048]{1,0:T(1,128)} %param.12) | copy-start | bytes 24580
  27.6 3.6 %copy-start.2 = (bf16[128,1280]{1,0:T(8,128)(2,1)}, bf16[128,1280]{1,0:T(8,128)(2,1)S(1)}, u32[]{:S(2)}) copy-start(bf16[128,1280]{1,0:T(8,128)(2,1)S(1)} %collective-permute-done.2.p3.refs_3_) | copy-start | bytes 983044
  27.7 3.6 %copy-start.3 = (bf16[128,1280]{1,0:T(8,128)(2,1)}, bf16[128,1280]{1,0:T(8,128)(2,1)S(1)}, u32[]{:S(2)}) copy-start(bf16[128,1280]{1,0:T(8,128)(2,1)S(1)} %collective-permute-done.1.p2.refs_2_) | copy-start | bytes 983044
  31.3 0.7 copy-start.4
  39.8 55.6 %copy-start.7 = (f32[1280]{0:T(1024)S(1)}, f32[1280]{0:T(1024)}, u32[]{:S(2)}) copy-start(f32[1280]{0:T(1024)} %param.16) | copy-start | bytes 15364
  43.9 21.7 %collective-permute-start.7 = (bf16[4,80,640]{2,1,0:T(8,128)(2,1)S(1)}, bf16[4,80,640]{2,1,0:T(8,128)(2,1)}, u32[]{:S(2)}, u32[]{:S(2)}) collective-permute-start(bf16[4,80,640]{2,1,0:T(8,128)(2,1)S(1)} %get-tuple-element.68), channel_id=1, source_target_pairs={{0,24},{8,0},{16,8},{24,16},{1,25},{9,1},{17,9},{25,17},{2,26},{10... | collective-permute-start | bytes 1228808 | tf_op jit(solution)/shard_map/ppermute | solution.py:36
  46.7 18.9 %collective-permute-start.6 = (bf16[4,80,640]{2,1,0:T(8,128)(2,1)S(1)}, bf16[4,80,640]{2,1,0:T(8,128)(2,1)}, u32[]{:S(2)}, u32[]{:S(2)}) collective-permute-start(bf16[4,80,640]{2,1,0:T(8,128)(2,1)S(1)} %get-tuple-element.68), channel_id=1, source_target_pairs={{0,8},{8,16},{16,24},{24,0},{1,9},{9,17},{17,25},{25,1},{2,10},{10... | collective-permute-start | bytes 1228808 | tf_op jit(solution)/shard_map/ppermute | solution.py:36
  46.7 9.7 %collective-permute-start.3 = (bf16[240,512]{1,0:T(8,128)(2,1)S(1)}, bf16[240,512]{1,0:T(8,128)(2,1)S(1)}, u32[]{:S(2)}, u32[]{:S(2)}) collective-permute-start(bf16[240,512]{1,0:T(8,128)(2,1)S(1)} %get-tuple-element.55), channel_id=1, source_target_pairs={{0,96},{32,0},{64,32},{96,64},{1,97},{33,1},{65,33},{97,65},{2,98}... | collective-permute-start | bytes 737288 | tf_op jit(solution)/shard_map/ppermute | solution.py:36
  48.2 11.8 %collective-permute-start.4 = (bf16[240,512]{1,0:T(8,128)(2,1)S(1)}, bf16[240,512]{1,0:T(8,128)(2,1)S(1)}, u32[]{:S(2)}, u32[]{:S(2)}) collective-permute-start(bf16[240,512]{1,0:T(8,128)(2,1)S(1)} %get-tuple-element.56), channel_id=1, source_target_pairs={{0,64},{32,96},{64,0},{96,32},{1,65},{33,97},{65,1},{97,33},{2,66}... | collective-permute-start | bytes 737288 | tf_op jit(solution)/shard_map/ppermute | solution.py:36
  49.2 16.4 %collective-permute-start.5 = (bf16[240,512]{1,0:T(8,128)(2,1)S(1)}, bf16[240,512]{1,0:T(8,128)(2,1)S(1)}, u32[]{:S(2)}, u32[]{:S(2)}) collective-permute-start(bf16[240,512]{1,0:T(8,128)(2,1)S(1)} %get-tuple-element.57), channel_id=1, source_target_pairs={{0,32},{32,64},{64,96},{96,0},{1,33},{33,65},{65,97},{97,1},{2,34}... | collective-permute-start | bytes 737288 | tf_op jit(solution)/shard_map/ppermute | solution.py:36
  65.6 13.0 %collective-permute-start.8 = (bf16[4,80,640]{2,1,0:T(8,128)(2,1)S(1)}, bf16[4,80,640]{2,1,0:T(8,128)(2,1)}, u32[]{:S(2)}, u32[]{:S(2)}) collective-permute-start(bf16[4,80,640]{2,1,0:T(8,128)(2,1)S(1)} %get-tuple-element.68), channel_id=1, source_target_pairs={{0,16},{8,24},{16,0},{24,8},{1,17},{9,25},{17,1},{25,9},{2,18},{10... | collective-permute-start | bytes 1228808 | tf_op jit(solution)/shard_map/ppermute | solution.py:36
  67.2 11.4 %collective-permute-start.9 = (bf16[4,80,640]{2,1,0:T(8,128)(2,1)}, bf16[4,80,640]{2,1,0:T(8,128)(2,1)}, u32[]{:S(2)}, u32[]{:S(2)}) collective-permute-start(bf16[4,80,640]{2,1,0:T(8,128)(2,1)} %collective-permute-done.6.refs_6_), channel_id=1, source_target_pairs={{0,1},{1,0},{2,3},{3,2},{4,5},{5,4},{6,7},{7,6},{8,9},{9,8},{10,11... | collective-permute-start | bytes 1228808 | tf_op jit(solution)/shard_map/ppermute | solution.py:44
  67.2 11.4 %collective-permute-start.10 = (bf16[4,80,640]{2,1,0:T(8,128)(2,1)}, bf16[4,80,640]{2,1,0:T(8,128)(2,1)}, u32[]{:S(2)}, u32[]{:S(2)}) collective-permute-start(bf16[4,80,640]{2,1,0:T(8,128)(2,1)} %collective-permute-done.7.refs_8_), channel_id=1, source_target_pairs={{0,1},{1,0},{2,3},{3,2},{4,5},{5,4},{6,7},{7,6},{8,9},{9,8},{10,11... | collective-permute-start | bytes 1228808 | tf_op jit(solution)/shard_map/ppermute | solution.py:44
  78.6 9.4 %collective-permute-start.11 = (bf16[80,512]{1,0:T(8,128)(2,1)S(1)}, bf16[80,512]{1,0:T(8,128)(2,1)S(1)}, u32[]{:S(2)}, u32[]{:S(2)}) collective-permute-start(bf16[80,512]{1,0:T(8,128)(2,1)S(1)} %get-tuple-element.72), channel_id=1, source_target_pairs={{0,32},{32,64},{64,96},{96,0},{1,33},{33,65},{65,97},{97,1},{2,34}... | collective-permute-start | bytes 245768 | tf_op jit(solution)/shard_map/ppermute | solution.py:36
  78.6 23.5 %collective-permute-start.17 = (bf16[4,80,640]{2,1,0:T(8,128)(2,1)}, bf16[4,80,640]{2,1,0:T(8,128)(2,1)S(1)}, u32[]{:S(2)}, u32[]{:S(2)}) collective-permute-start(bf16[4,80,640]{2,1,0:T(8,128)(2,1)} %collective-permute-done.8.refs_7_), channel_id=1, source_target_pairs={{0,1},{1,0},{2,3},{3,2},{4,5},{5,4},{6,7},{7,6},{8,9},{9,8},{10,11... | collective-permute-start | bytes 1228808 | tf_op jit(solution)/shard_map/ppermute | solution.py:44
  78.7 9.3 %collective-permute-start.12 = (bf16[80,512]{1,0:T(8,128)(2,1)S(1)}, bf16[80,512]{1,0:T(8,128)(2,1)S(1)}, u32[]{:S(2)}, u32[]{:S(2)}) collective-permute-start(bf16[80,512]{1,0:T(8,128)(2,1)S(1)} %get-tuple-element.73), channel_id=1, source_target_pairs={{0,64},{32,96},{64,0},{96,32},{1,65},{33,97},{65,1},{97,33},{2,66}... | collective-permute-start | bytes 245768 | tf_op jit(solution)/shard_map/ppermute | solution.py:36
  79.5 11.2 %collective-permute-start.13 = (bf16[80,512]{1,0:T(8,128)(2,1)S(1)}, bf16[80,512]{1,0:T(8,128)(2,1)S(1)}, u32[]{:S(2)}, u32[]{:S(2)}) collective-permute-start(bf16[80,512]{1,0:T(8,128)(2,1)S(1)} %get-tuple-element.74), channel_id=1, source_target_pairs={{0,96},{32,0},{64,32},{96,64},{1,97},{33,1},{65,33},{97,65},{2,98}... | collective-permute-start | bytes 245768 | tf_op jit(solution)/shard_map/ppermute | solution.py:36
  91.3 17.1 %collective-permute-start.16 = (bf16[4,80,512]{2,1,0:T(8,128)(2,1)S(1)}, bf16[4,80,512]{2,1,0:T(8,128)(2,1)S(1)}, u32[]{:S(2)}, u32[]{:S(2)}) collective-permute-start(bf16[4,80,512]{2,1,0:T(8,128)(2,1)S(1)} %pack.1.refs_0_), channel_id=1, source_target_pairs={{0,24},{8,0},{16,8},{24,16},{1,25},{9,1},{17,9},{25,17},{2,26},{10... | collective-permute-start | bytes 983048 | tf_op jit(solution)/shard_map/ppermute | solution.py:36
  94.5 13.9 %collective-permute-start.15 = (bf16[4,80,512]{2,1,0:T(8,128)(2,1)S(1)}, bf16[4,80,512]{2,1,0:T(8,128)(2,1)S(1)}, u32[]{:S(2)}, u32[]{:S(2)}) collective-permute-start(bf16[4,80,512]{2,1,0:T(8,128)(2,1)S(1)} %pack.1.refs_0_), channel_id=1, source_target_pairs={{0,16},{8,24},{16,0},{24,8},{1,17},{9,25},{17,1},{25,9},{2,18},{10... | collective-permute-start | bytes 983048 | tf_op jit(solution)/shard_map/ppermute | solution.py:36
  94.5 17.3 %collective-permute-start.14 = (bf16[4,80,512]{2,1,0:T(8,128)(2,1)S(1)}, bf16[4,80,512]{2,1,0:T(8,128)(2,1)S(1)}, u32[]{:S(2)}, u32[]{:S(2)}) collective-permute-start(bf16[4,80,512]{2,1,0:T(8,128)(2,1)S(1)} %pack.1.refs_0_), channel_id=1, source_target_pairs={{0,8},{8,16},{16,24},{24,0},{1,9},{9,17},{17,25},{25,1},{2,10},{10... | collective-permute-start | bytes 983048 | tf_op jit(solution)/shard_map/ppermute | solution.py:36
  102.1 0.8 copy-start.5
  115.9 17.6 %collective-permute-start.18 = (bf16[128,1280]{1,0:T(8,128)(2,1)S(1)}, bf16[128,1280]{1,0:T(8,128)(2,1)S(1)}, u32[]{:S(2)}, u32[]{:S(2)}) collective-permute-start(bf16[128,1280]{1,0:T(8,128)(2,1)S(1)} %get-tuple-element.91), channel_id=1, source_target_pairs={{0,8},{8,16},{16,24},{24,0},{1,9},{9,17},{17,25},{25,1},{2,10},{10... | collective-permute-start | bytes 983048 | tf_op jit(solution)/shard_map/ppermute | solution.py:36
  116.0 17.5 %collective-permute-start.19 = (bf16[128,1280]{1,0:T(8,128)(2,1)S(1)}, bf16[128,1280]{1,0:T(8,128)(2,1)S(1)}, u32[]{:S(2)}, u32[]{:S(2)}) collective-permute-start(bf16[128,1280]{1,0:T(8,128)(2,1)S(1)} %get-tuple-element.92), channel_id=1, source_target_pairs={{0,16},{8,24},{16,0},{24,8},{1,17},{9,25},{17,1},{25,9},{2,18},{10... | collective-permute-start | bytes 983048 | tf_op jit(solution)/shard_map/ppermute | solution.py:36
  122.4 11.6 %collective-permute-start.20 = (bf16[128,1280]{1,0:T(8,128)(2,1)S(1)}, bf16[128,1280]{1,0:T(8,128)(2,1)S(1)}, u32[]{:S(2)}, u32[]{:S(2)}) collective-permute-start(bf16[128,1280]{1,0:T(8,128)(2,1)S(1)} %get-tuple-element.93), channel_id=1, source_target_pairs={{0,24},{8,0},{16,8},{24,16},{1,25},{9,1},{17,9},{25,17},{2,26},{10... | collective-permute-start | bytes 983048 | tf_op jit(solution)/shard_map/ppermute | solution.py:36
  133.6 15.2 %copy-start.6 = (bf16[128,1280]{1,0:T(8,128)(2,1)S(1)}, bf16[128,1280]{1,0:T(8,128)(2,1)}, u32[]{:S(2)}) copy-start(bf16[128,1280]{1,0:T(8,128)(2,1)} %param.20) | copy-start | bytes 983044
Sparse Core Ops, SparseCore 0:
  9.0 30.7 all-gather.4
  42.1 55.1 all-gather.6

commit v7 on v6

--- a/solution.py
+++ b/solution.py
@@ -12,6 +12,7 @@
 HEAD = 80
 SCALE = math.log2(math.e) / math.sqrt(HEAD)
 N = 4
+SLOT = 8
 BF = jnp.bfloat16
 F32 = jnp.float32
 NT = (((1,), (1,)), ((), ()))
@@ -226,7 +227,7 @@
             outs[-1][...] = resid[i * rows : (i + 1) * rows, :]
 
 
-def merge_kernel(early, late, w, select, tail, out, vision):
+def merge_kernel(early, late, w, select, tail, o0, o1, o2, o3, vision):
     sums = (early[...] + late[...].astype(F32)).astype(BF).astype(F32)
     full, width = early.shape
     count = full // 4
@@ -238,9 +239,31 @@
         rows = [vision[pl.ds(i * full + j, count, stride=4), :] for i in range(tiles)]
         rows = jnp.concatenate(rows, axis=1).astype(BF)
         total += jnp.dot(rows, w[j * width : (j + 1) * width, :], preferred_element_type=F32)
-    sent = jnp.dot(select[...], total.astype(BF), preferred_element_type=F32)
-    out[:, :width] = sent.astype(BF)
-    out[:, width:] = tail[...]
+    sent = jnp.dot(select[...], total.astype(BF), preferred_element_type=F32).astype(BF)
+    for k, out in enumerate((o0, o1, o2, o3)):
+        for j in range(N):
+            at = slice((k * N + j) * SLOT, (k * N + j + 1) * SLOT)
+            out[j, :, :width] = sent[at, :]
+            out[j, :, width:] = tail[at, :]
+
+
+def turn_kernel(a0, a1, a2, a3, o0, o1, o2, o3):
+    for k, piece in enumerate((a0, a1, a2, a3)):
+        for j, out in enumerate((o0, o1, o2, o3)):
+            out[k] = piece[j]
+
+
+def place_kernel(b0, b1, b2, b3, text, out):
+    rows, width = text.shape
+    arrived = [b[...].reshape(N * SLOT, b.shape[2]) for b in (b0, b1, b2, b3)]
+    arrived = jnp.concatenate(arrived, axis=0)
+    landing = arrived[:, width : width + 1].astype(F32)
+    spot = lax.broadcasted_iota(jnp.int32, (arrived.shape[0], rows), 1) + 1
+    mark = jnp.where(landing == spot.astype(F32), 1.0, 0.0).astype(BF)
+    placed = lax.dot_general(mark, arrived[:, :width], TN, preferred_element_type=F32)
+    ones = jnp.ones((arrived.shape[0], 128), BF)
+    filled = lax.dot_general(mark, ones, TN, preferred_element_type=F32)
+    out[...] = jnp.where(filled[:, :1] > 0.5, placed.astype(BF), text[...])
 
 
 def local(
@@ -298,7 +321,7 @@
         name="norm",
     )(pos, *[far(piece) for piece in pieces], ln_attn[None, :])
     group_rows = ids.shape[0]
-    chunk = 256
+    chunk = 512
     chunks = group_rows // chunk
     held = (ids[:, None] == jnp.arange(16)[None, :]).reshape(chunks, chunk, 16)
     held = jnp.any(held, axis=1)
@@ -326,15 +349,14 @@
     merged_count = count // 4
     dest = slot_dest[0]
     prompt_rows = text_embed.shape[0]
-    req_count = N * N
     row_count = lax.axis_size("z") * lax.axis_size("c")
-    slot_cap = 2
     owner = jnp.where(dest >= 0, dest // prompt_rows // row_count, -1)
     order = jnp.arange(merged_count)
     same_owner = (owner[:, None] == owner[None, :]) & (order[None, :] < order[:, None])
     ranks = jnp.sum(same_owner.astype(jnp.int32), axis=1)
-    target = jnp.where(owner >= 0, owner * slot_cap + ranks, -1)
-    select = target[None, :] == jnp.arange(req_count * slot_cap)[:, None]
+    away = lax.rem(owner // N - x + N, N) * N + lax.rem(owner % N - y + N, N)
+    target = jnp.where(owner >= 0, away * SLOT + ranks, -1)
+    select = target[None, :] == jnp.arange(N * N * SLOT)[:, None]
     places = jnp.sum(jnp.where(select, (dest % prompt_rows + 1)[None, :], 0), axis=1)
     lane = jnp.arange(128)[None, :] == 0
     tail = jnp.where(lane, places[:, None], 0).astype(BF)
@@ -446,29 +468,34 @@
     part3, part0, resid = mlp((3, 0), "mlp_second")
     early = shift(part1, "y", 1).astype(F32) + shift(part2, "y", 2).astype(F32)
     sums = [resid.astype(F32) + part0.astype(F32) + early, shift(part3, "y", 3)]
-    outgoing = pl.pallas_call(
+    block = jax.ShapeDtypeStruct((N, SLOT, width + 128), BF)
+    sent = pl.pallas_call(
         merge_kernel,
-        out_shape=jax.ShapeDtypeStruct((req_count * slot_cap, width + 128), BF),
+        out_shape=[block] * N,
         in_specs=[VMEM] * 5,
-        out_specs=VMEM,
+        out_specs=[VMEM] * N,
         scratch_shapes=[pltpu.VMEM((count * width // 128, 128), F32)],
         compiler_params=params(8),
         name="merge",
     )(*sums, w_merge, select, tail)
-    arrived = lax.all_to_all(
-        outgoing.reshape(req_count, slot_cap, width + 128),
-        ("x", "y"),
-        split_axis=0,
-        concat_axis=0,
-        tiled=True,
-    ).reshape(req_count * slot_cap, width + 128)
-    landing = arrived[:, width].astype(jnp.int32) - 1
-    placer = landing[None, :] == jnp.arange(prompt_rows)[:, None]
-    placed = jnp.dot(
-        placer.astype(BF), arrived[:, :width], preferred_element_type=F32
-    ).astype(BF)
-    filled = jnp.any(placer, axis=1)
-    return jnp.where(filled[:, None], placed, text_embed)
+    sent = [sent[0]] + [shift(sent[k], "x", k) for k in (1, 2, 3)]
+    sent = pl.pallas_call(
+        turn_kernel,
+        out_shape=[block] * N,
+        in_specs=[VMEM] * N,
+        out_specs=[VMEM] * N,
+        compiler_params=params(4),
+        name="turn",
+    )(*sent)
+    sent = [sent[0]] + [shift(sent[k], "y", k) for k in (1, 2, 3)]
+    return pl.pallas_call(
+        place_kernel,
+        out_shape=jax.ShapeDtypeStruct(text_embed.shape, BF),
+        in_specs=[VMEM] * (N + 1),
+        out_specs=VMEM,
+        compiler_params=params(8),
+        name="place",
+    )(*sent, text_embed)
 
 
 def solution(mesh):

time: 157 us -> 162 us (1.032)
  blocking collectives: 12.1 us -> 0 us
  waiting for transfers between devices: 59.9 us -> 69.9 us
  starting transfers between devices: 23.6 us -> 32.7 us
    all_to_all x1 -> x0, blocking collectives: 12.1 us -> none  [local(): lax.all_to_all(outgoing.reshape(req_count, slot_cap, width + 128), ('x',...]
    ppermute x18 -> x24, waiting for transfers between devices: 52.8 us -> 62.9 us  [shift(): return lax.ppermute(value, axis, pairs)]
    ppermute x18 -> x24, starting transfers between devices: 23 us -> 32 us  [shift(): return lax.ppermute(value, axis, pairs)]
    pallas_call x1, Pallas kernels: 6.47 us -> 4.47 us  [local(): pl.pallas_call(attend_kernel, out_shape=[jax.ShapeDtypeStruct((HEAD, tota...]
    pallas_call x1 -> x3, Pallas kernels: 2.37 us -> 3.7 us  [the longest x1 2.49 us: local(): pl.pallas_call(merge_kernel, out_shape=[block] * N, in_specs=[VMEM] * 5,...]
  transfers between devices with their start and end apart: 23 -> 29, of which waited for: 14 -> 19; matrix products, arithmetic and copies ran while one was open for 5% -> 5% of each run, Pallas kernels for 18% -> 16%
where the time goes in v7:
time: 162 us
  waiting for transfers between devices  69.9 us (43%)
  Pallas kernels  33.5 us (21%)
  starting transfers between devices  32.7 us (20%)
  between operations  13.7 us (8%)
  other arithmetic  6.7 us (4%)
  local copies, waits for them, and re-layouts  5.2 us (3%)
    ppermute x24, waiting for transfers between devices, shift(): return lax.ppermute(value, axis, pairs)  62.9 us
    ppermute x24, starting transfers between devices, shift(): return lax.ppermute(value, axis, pairs)  32 us
    pallas_call x2, Pallas kernels, mlp(): pl.pallas_call(functools.partial(mlp_kernel, offsets), out_shape=[jax.Sha...  8.13 us
    all_gather x1, waiting for transfers between devices, local(): near = lax.all_gather(w_half, ('x', 'c'), axis=0, tiled=False)  5.26 us
    pallas_call x1, Pallas kernels, local(): pl.pallas_call(fetch_kernel, out_shape=[jax.ShapeDtypeStruct((2, N * N, H...  5.11 us
    pallas_call x1, Pallas kernels, local(): pl.pallas_call(fetch_merge_kernel, out_shape=jax.ShapeDtypeStruct(w_merge...  4.85 us
    pallas_call x1, Pallas kernels, local(): pl.pallas_call(attend_kernel, out_shape=[jax.ShapeDtypeStruct((HEAD, tota...  4.47 us
    pallas_call x1, Pallas kernels, local(): pl.pallas_call(qkv_kernel, out_shape=[jax.ShapeDtypeStruct((3 * HEAD, tot...  4.08 us
  transfers between devices with their start and end apart: 29, of which 19 were waited for; matrix products, arithmetic and copies ran while one was open for 5% of the time, Pallas kernels for 16%

profile of v7, /device:TPU:0, one launch (start us, length us, event | category | flops | bytes accessed | tf_op | source)
XLA Modules:
  0.0 161.7 jit_solution(5926092613645280739)
XLA Ops:
  6.5 1.8 %fusion = bf16[320,640]{1,0:T(8,128)(2,1)} fusion(s32[]{:T(128)S(6)} %select_n.88, bf16[240,1280]{1,0:T(8,128)(2,1)} %bitcast.55, bf16[80,1280]{1,0:T(8,128)(2,1)} %param.15), kind=kLoop, calls=%fused_computation.3 | loop fusion | flops 819200 | bytes 1228804 | tf_op jit(solution)/shard_map/concatenate | solution.py:292
  8.5 0.9 dynamic_slice.11
  9.4 0.7 pad_maximum_fusion
  10.1 3.2 %collective-permute-start.2 = (bf16[128,1280]{1,0:T(8,128)(2,1)}, bf16[128,1280]{1,0:T(8,128)(2,1)S(1)}, u32[]{:S(2)}, u32[]{:S(2)}) collective-permute-start(bf16[128,1280]{1,0:T(8,128)(2,1)} %bitcast.50), channel_id=1, source_target_pairs={{0,24},{8,0},{16,8},{24,16},{1,25},{9,1},{17,9},{25,17},{2,26},{10... | collective-permute-start | bytes 983048 | tf_op jit(solution)/shard_map/ppermute | solution.py:37
  13.3 0.6 collective-permute-start.1
  13.9 1.0 collective-permute-start
  14.9 0.7 broadcast_in_dim.107.gain
  15.6 0.5 broadcast.261
  16.1 1.3 reduce.3
  17.6 0.2 and_reduce_fusion
  17.7 0.2 select_reduce_fusion.3
  18.0 0.6 slice.3
  18.9 0.6 stack.30
  19.5 0.7 compare_select_fusion.4
  20.2 0.7 fusion.12
  20.8 0.2 convert_reduce_fusion
  21.4 6.2 %collective-permute-done.2.p3.refs_3_ = bf16[128,1280]{1,0:T(8,128)(2,1)S(1)} collective-permute-done((bf16[128,1280]{1,0:T(8,128)(2,1)}, bf16[128,1280]{1,0:T(8,128)(2,1)S(1)}, u32[]{:S(2)}, u32[]{:S(2)}) %collective-permute-start.2) | collective-permute-done | bytes 327712 | tf_op jit(solution)/shard_map/ppermute | solution.py:37
  27.6 3.6 %collective-permute-done.p1.refs_1_ = bf16[128,1280]{1,0:T(8,128)(2,1)S(1)} collective-permute-done((bf16[128,1280]{1,0:T(8,128)(2,1)}, bf16[128,1280]{1,0:T(8,128)(2,1)S(1)}, u32[]{:S(2)}, u32[]{:S(2)}) %collective-permute-start) | collective-permute-done | bytes 327712 | tf_op jit(solution)/shard_map/ppermute | solution.py:37
  31.2 0.7 copy-done.5
  32.0 2.6 %norm.1.h1 = bf16[2,512,640]{2,1,0:T(8,128)(2,1)S(1)} custom-call(s32[4]{0:T(128)S(1)} %pad_add_fusion.pos, bf16[128,1280]{1,0:T(8,128)(2,1)} %bitcast.53, bf16[128,1280]{1,0:T(8,128)(2,1)} %copy-done.5, bf16[128,1280]{1,0:T(8,128)(2,1)} %copy-done.4, bf16[128,1280]{1,0:T(8,128)(2,1)} %copy-done.3, f32[1,1280]{1,0:T(1,128)S(1)} %broadcast_in_dim.107.gain), custom_call_target="tpu_custom_call" | custom-call | tf_op jit(solution)/shard_map/norm/pallas_call | solution.py:311
  34.6 5.3 %all-gather.5.cloned.1.call-done = bf16[2560,640]{1,0:T(8,128)(2,1)} async-done(((bf16[320,640]{1,0:T(8,128)(2,1)}), bf16[2560,640]{1,0:T(8,128)(2,1)}) %all-gather.5.cloned.1.call-update) | async-done | bytes 3276816 | tf_op jit(solution)/shard_map/all_gather | solution.py:294
  39.8 4.1 %qkv.1 = (bf16[240,512]{1,0:T(8,128)(2,1)S(1)}, bf16[240,512]{1,0:T(8,128)(2,1)S(1)}, bf16[240,512]{1,0:T(8,128)(2,1)S(1)}, bf16[240,512]{1,0:T(8,128)(2,1)S(1)}, bf16[4,80,640]{2,1,0:T(8,128)(2,1)S(1)}) custom-call(s32[4]{0:T(128)S(1)} %pad_add_fusion.pos, bf16[2,512,640]{2,1,0:T(8,128)(2,1)S(1)} %norm.1.h1, bf16[8,320,640]{2,1,0:T(8,128)(2,1)} %bitcast.47), custom_call_target="tpu_custom_call" | custom-call | tf_op jit(solution)/shard_map/qkv/pallas_call | solution.py:369
  43.9 2.8 %collective-permute-start.7 = (bf16[4,80,640]{2,1,0:T(8,128)(2,1)S(1)}, bf16[4,80,640]{2,1,0:T(8,128)(2,1)}, u32[]{:S(2)}, u32[]{:S(2)}) collective-permute-start(bf16[4,80,640]{2,1,0:T(8,128)(2,1)S(1)} %get-tuple-element.76), channel_id=1, source_target_pairs={{0,24},{8,0},{16,8},{24,16},{1,25},{9,1},{17,9},{25,17},{2,26},{10... | collective-permute-start | bytes 1228808 | tf_op jit(solution)/shard_map/ppermute | solution.py:37
  46.7 1.4 collective-permute-start.3
  48.2 1.2 collective-permute-start.4
  49.4 0.4 collective-permute-start.5
  49.8 6.6 %collective-permute-done.3.r1 = bf16[240,512]{1,0:T(8,128)(2,1)S(1)} collective-permute-done((bf16[240,512]{1,0:T(8,128)(2,1)S(1)}, bf16[240,512]{1,0:T(8,128)(2,1)S(1)}, u32[]{:S(2)}, u32[]{:S(2)}) %collective-permute-start.3) | collective-permute-done | bytes 245792 | tf_op jit(solution)/shard_map/ppermute | solution.py:37
  56.4 3.6 %collective-permute-done.4.r2 = bf16[240,512]{1,0:T(8,128)(2,1)S(1)} collective-permute-done((bf16[240,512]{1,0:T(8,128)(2,1)S(1)}, bf16[240,512]{1,0:T(8,128)(2,1)S(1)}, u32[]{:S(2)}, u32[]{:S(2)}) %collective-permute-start.4) | collective-permute-done | bytes 245792 | tf_op jit(solution)/shard_map/ppermute | solution.py:37
  60.0 5.7 %collective-permute-done.5.r3 = bf16[240,512]{1,0:T(8,128)(2,1)S(1)} collective-permute-done((bf16[240,512]{1,0:T(8,128)(2,1)S(1)}, bf16[240,512]{1,0:T(8,128)(2,1)S(1)}, u32[]{:S(2)}, u32[]{:S(2)}) %collective-permute-start.5) | collective-permute-done | bytes 245792 | tf_op jit(solution)/shard_map/ppermute | solution.py:37
  65.7 1.6 collective-permute-start.8
  67.2 0.5 collective-permute-start.10
  67.8 0.4 copy.13.id_col
  68.1 4.5 %attend.1 = (bf16[80,512]{1,0:T(8,128)(2,1)S(1)}, bf16[80,512]{1,0:T(8,128)(2,1)S(1)}, bf16[80,512]{1,0:T(8,128)(2,1)S(1)}, bf16[80,512]{1,0:T(8,128)(2,1)S(1)}) custom-call(s32[4]{0:T(128)S(1)} %pad_add_fusion.pos, s32[5,16]{1,0:T(8,128)S(1)} %stack.31.work, bf16[240,512]{1,0:T(8,128)(2,1)S(1)} %get-tuple-element.67.r0, ...), custom_call_target="tpu_custom_call" | custom-call | tf_op jit(solution)/shard_map/attend/pallas_call | solution.py:390
  72.6 6.1 %collective-permute-done.8.refs_7_ = bf16[4,80,640]{2,1,0:T(8,128)(2,1)} collective-permute-done((bf16[4,80,640]{2,1,0:T(8,128)(2,1)S(1)}, bf16[4,80,640]{2,1,0:T(8,128)(2,1)}, u32[]{:S(2)}, u32[]{:S(2)}) %collective-permute-start.8) | collective-permute-done | bytes 409632 | tf_op jit(solution)/shard_map/ppermute | solution.py:37
  78.8 1.1 collective-permute-start.12
  79.9 2.5 %collective-permute-start.13 = (bf16[80,512]{1,0:T(8,128)(2,1)S(1)}, bf16[80,512]{1,0:T(8,128)(2,1)S(1)}, u32[]{:S(2)}, u32[]{:S(2)}) collective-permute-start(bf16[80,512]{1,0:T(8,128)(2,1)S(1)} %get-tuple-element.82), channel_id=1, source_target_pairs={{0,96},{32,0},{64,32},{96,64},{1,97},{33,1},{65,33},{97,65},{2,98}... | collective-permute-start | bytes 245768 | tf_op jit(solution)/shard_map/ppermute | solution.py:37
  82.3 5.7 %collective-permute-done.11.g1 = bf16[80,512]{1,0:T(8,128)(2,1)S(1)} collective-permute-done((bf16[80,512]{1,0:T(8,128)(2,1)S(1)}, bf16[80,512]{1,0:T(8,128)(2,1)S(1)}, u32[]{:S(2)}, u32[]{:S(2)}) %collective-permute-start.11) | collective-permute-done | bytes 81952 | tf_op jit(solution)/shard_map/ppermute | solution.py:37
  88.0 2.7 %collective-permute-done.13.g3 = bf16[80,512]{1,0:T(8,128)(2,1)S(1)} collective-permute-done((bf16[80,512]{1,0:T(8,128)(2,1)S(1)}, bf16[80,512]{1,0:T(8,128)(2,1)S(1)}, u32[]{:S(2)}, u32[]{:S(2)}) %collective-permute-start.13) | collective-permute-done | bytes 81952 | tf_op jit(solution)/shard_map/ppermute | solution.py:37
  90.8 0.6 pack.1.refs_0_
  91.3 3.2 %collective-permute-start.16 = (bf16[4,80,512]{2,1,0:T(8,128)(2,1)S(1)}, bf16[4,80,512]{2,1,0:T(8,128)(2,1)S(1)}, u32[]{:S(2)}, u32[]{:S(2)}) collective-permute-start(bf16[4,80,512]{2,1,0:T(8,128)(2,1)S(1)} %pack.1.refs_0_), channel_id=1, source_target_pairs={{0,24},{8,0},{16,8},{24,16},{1,25},{9,1},{17,9},{25,17},{2,26},{10... | collective-permute-start | bytes 983048 | tf_op jit(solution)/shard_map/ppermute | solution.py:37
  94.6 0.9 collective-permute-start.14
  95.5 1.7 %all-gather.7.cloned.1.call-done = bf16[5120,640]{1,0:T(8,128)(2,1)} async-done(((bf16[160,640]{1,0:T(8,128)(2,1)}), bf16[5120,640]{1,0:T(8,128)(2,1)}) %all-gather.7.cloned.1.call-update) | async-done | bytes 6553616 | tf_op jit(solution)/shard_map/all_gather | solution.py:306
  97.2 4.8 %fetch_merge.1.w = bf16[5120,1280]{1,0:T(8,128)(2,1)S(1)} custom-call(bf16[5120,1280]{1,0:T(8,128)(2,1)} %w_hbm), custom_call_target="tpu_custom_call" | custom-call | tf_op jit(solution)/shard_map/fetch_merge/pallas_call | solution.py:438
  102.1 0.8 copy-done.6
  102.9 5.1 %fetch.1 = (bf16[2,16,80,640]{3,2,1,0:T(8,128)(2,1)S(1)}, bf16[16,80,1280]{2,1,0:T(8,128)(2,1)S(1)}, bf16[16,80,1280]{2,1,0:T(8,128)(2,1)S(1)}, bf16[4,128,1280]{2,1,0:T(8,128)(2,1)S(1)}) custom-call(s32[4]{0:T(128)S(1)} %pad_add_fusion.pos, bf16[128,1280]{1,0:T(8,128)(2,1)} %bitcast.54, bf16[128,1280]{1,0:T(8,128)(2,1)} %copy-done.5, ...), custom_call_target="tpu_custom_call" | custom-call | tf_op jit(solution)/shard_map/fetch/pallas_call | solution.py:419
  108.0 0.5 collective-permute-done.16.refs_3_
  108.4 3.4 %collective-permute-done.14.refs_1_ = bf16[4,80,512]{2,1,0:T(8,128)(2,1)S(1)} collective-permute-done((bf16[4,80,512]{2,1,0:T(8,128)(2,1)S(1)}, bf16[4,80,512]{2,1,0:T(8,128)(2,1)S(1)}, u32[]{:S(2)}, u32[]{:S(2)}) %collective-permute-start.14) | collective-permute-done | bytes 327712 | tf_op jit(solution)/shard_map/ppermute | solution.py:37
  111.9 4.1 %mlp_first.1 = (bf16[128,1280]{1,0:T(8,128)(2,1)S(1)}, bf16[128,1280]{1,0:T(8,128)(2,1)S(1)}) custom-call(s32[4]{0:T(128)S(1)} %pad_add_fusion.pos, bf16[4,80,512]{2,1,0:T(8,128)(2,1)S(1)} %pack.1.refs_0_, bf16[4,80,512]{2,1,0:T(8,128)(2,1)S(1)} %collective-permute-done.14.refs_1_, bf16[4,80,512]{2,1,0:T(8,128)(2,1)S(1)} %collective-permute-done.15.refs_2_, ...), custom_call_target="tpu_custom_call" | custom-call | flops 2516582400 | bytes 9830400 | tf_op jit(solution)/shard_map/mlp_first/pallas_call | solution.py:450
  116.0 2.4 %collective-permute-start.19 = (bf16[128,1280]{1,0:T(8,128)(2,1)S(1)}, bf16[128,1280]{1,0:T(8,128)(2,1)S(1)}, u32[]{:S(2)}, u32[]{:S(2)}) collective-permute-start(bf16[128,1280]{1,0:T(8,128)(2,1)S(1)} %get-tuple-element.100), channel_id=1, source_target_pairs={{0,16},{8,24},{16,0},{24,8},{1,17},{9,25},{17,1},{25,9},{2,18},{10... | collective-permute-start | bytes 983048 | tf_op jit(solution)/shard_map/ppermute | solution.py:37
  118.4 4.1 %mlp_second.1 = (bf16[128,1280]{1,0:T(8,128)(2,1)S(1)}, bf16[128,1280]{1,0:T(8,128)(2,1)S(1)}, bf16[128,1280]{1,0:T(8,128)(2,1)S(1)}) custom-call(s32[4]{0:T(128)S(1)} %pad_add_fusion.pos, bf16[4,80,512]{2,1,0:T(8,128)(2,1)S(1)} %pack.1.refs_0_, bf16[4,80,512]{2,1,0:T(8,128)(2,1)S(1)} %collective-permute-done.14.refs_1_, ...), custom_call_target="tpu_custom_call" | custom-call | flops 2516582400 | bytes 9830400 | tf_op jit(solution)/shard_map/mlp_second/pallas_call | solution.py:450
  122.4 0.9 collective-permute-start.20
  123.4 10.1 %collective-permute-done.18 = bf16[128,1280]{1,0:T(8,128)(2,1)S(1)} collective-permute-done((bf16[128,1280]{1,0:T(8,128)(2,1)S(1)}, bf16[128,1280]{1,0:T(8,128)(2,1)S(1)}, u32[]{:S(2)}, u32[]{:S(2)}) %collective-permute-start.18) | collective-permute-done | bytes 327712 | tf_op jit(solution)/shard_map/ppermute | solution.py:37
  133.7 0.4 collective-permute-done.20.late
  134.1 2.5 %merge.1 = (bf16[4,8,1408]{2,1,0:T(8,128)(2,1)S(1)}, bf16[4,8,1408]{2,1,0:T(8,128)(2,1)S(1)}, bf16[4,8,1408]{2,1,0:T(8,128)(2,1)S(1)}, bf16[4,8,1408]{2,1,0:T(8,128)(2,1)S(1)}) custom-call(f32[128,1280]{1,0:T(8,128)S(1)} %add_add_fusion.early, bf16[128,1280]{1,0:T(8,128)(2,1)S(1)} %collective-permute-done.20.late, bf16[5120,1280]{1,0:T(8,128)(2,1)S(1)} %fetch_merge.1.w, ...), custom_call_target="tpu_custom_call" | custom-call | tf_op jit(solution)/shard_map/merge/pallas_call | solution.py:472
  136.7 2.4 %collective-permute-start.22 = (bf16[4,8,1408]{2,1,0:T(8,128)(2,1)S(1)}, bf16[4,8,1408]{2,1,0:T(8,128)(2,1)S(1)}, u32[]{:S(2)}, u32[]{:S(2)}) collective-permute-start(bf16[4,8,1408]{2,1,0:T(8,128)(2,1)S(1)} %get-tuple-element.107), channel_id=1, source_target_pairs={{0,64},{32,96},{64,0},{96,32},{1,65},{33,97},{65,1},{97,33},{2,66}... | collective-permute-start | bytes 270344 | tf_op jit(solution)/shard_map/ppermute | solution.py:37
  139.1 1.4 collective-permute-start.23
  140.4 2.9 %collective-permute-done.21.a1 = bf16[4,8,1408]{2,1,0:T(8,128)(2,1)S(1)} collective-permute-done((bf16[4,8,1408]{2,1,0:T(8,128)(2,1)S(1)}, bf16[4,8,1408]{2,1,0:T(8,128)(2,1)S(1)}, u32[]{:S(2)}, u32[]{:S(2)}) %collective-permute-start.21) | collective-permute-done | bytes 90144 | tf_op jit(solution)/shard_map/ppermute | solution.py:37
  143.4 0.9 collective-permute-done.23.a3
  144.2 0.4 collective-permute-start.24
  144.6 4.5 %collective-permute-start.25 = (bf16[4,8,1408]{2,1,0:T(8,128)(2,1)S(1)}, bf16[4,8,1408]{2,1,0:T(8,128)(2,1)S(1)}, u32[]{:S(2)}, u32[]{:S(2)}) collective-permute-start(bf16[4,8,1408]{2,1,0:T(8,128)(2,1)S(1)} %get-tuple-element.111), channel_id=1, source_target_pairs={{0,16},{8,24},{16,0},{24,8},{1,17},{9,25},{17,1},{25,9},{2,18},{10... | collective-permute-start | bytes 270344 | tf_op jit(solution)/shard_map/ppermute | solution.py:37
  149.1 2.0 %collective-permute-done.24.b1 = bf16[4,8,1408]{2,1,0:T(8,128)(2,1)S(1)} collective-permute-done((bf16[4,8,1408]{2,1,0:T(8,128)(2,1)S(1)}, bf16[4,8,1408]{2,1,0:T(8,128)(2,1)S(1)}, u32[]{:S(2)}, u32[]{:S(2)}) %collective-permute-start.24) | collective-permute-done | bytes 90144 | tf_op jit(solution)/shard_map/ppermute | solution.py:37
  151.2 1.5 collective-permute-done.25.b2
  152.6 1.1 collective-permute-done.26.b3
  153.7 1.2 place.1
  (59 shorter events, 1.5 us)
Async XLA Ops:
  6.5 2.8 %copy-start = (bf16[1280,320]{0,1:T(8,128)(2,1)S(1)}, bf16[1280,320]{0,1:T(8,128)(2,1)}, u32[]{:S(2)}) copy-start(bf16[1280,320]{0,1:T(8,128)(2,1)} %param.17) | copy-start | bytes 2457604
  6.5 33.3 %all-gather.5.cloned.1.call-start = ((), (), s32[]{:S(2)}) async-start(), calls=%async_computation | async-start | bytes 3686400 | tf_op jit(solution)/shard_map/all_gather | solution.py:294
  8.4 88.8 %all-gather.7.cloned.1.call-start = ((), (), s32[]{:S(2)}) async-start(), calls=%async_computation.1 | async-start | bytes 6758400 | tf_op jit(solution)/shard_map/all_gather | solution.py:306
  10.1 17.5 %collective-permute-start.2 = (bf16[128,1280]{1,0:T(8,128)(2,1)}, bf16[128,1280]{1,0:T(8,128)(2,1)S(1)}, u32[]{:S(2)}, u32[]{:S(2)}) collective-permute-start(bf16[128,1280]{1,0:T(8,128)(2,1)} %bitcast.50), channel_id=1, source_target_pairs={{0,24},{8,0},{16,8},{24,16},{1,25},{9,1},{17,9},{25,17},{2,26},{10... | collective-permute-start | bytes 983048 | tf_op jit(solution)/shard_map/ppermute | solution.py:37
  13.3 14.3 %collective-permute-start.1 = (bf16[128,1280]{1,0:T(8,128)(2,1)}, bf16[128,1280]{1,0:T(8,128)(2,1)S(1)}, u32[]{:S(2)}, u32[]{:S(2)}) collective-permute-start(bf16[128,1280]{1,0:T(8,128)(2,1)} %bitcast.51), channel_id=1, source_target_pairs={{0,16},{8,24},{16,0},{24,8},{1,17},{9,25},{17,1},{25,9},{2,18},{10... | collective-permute-start | bytes 983048 | tf_op jit(solution)/shard_map/ppermute | solution.py:37
  13.9 17.3 %collective-permute-start = (bf16[128,1280]{1,0:T(8,128)(2,1)}, bf16[128,1280]{1,0:T(8,128)(2,1)S(1)}, u32[]{:S(2)}, u32[]{:S(2)}) collective-permute-start(bf16[128,1280]{1,0:T(8,128)(2,1)} %bitcast.52), channel_id=1, source_target_pairs={{0,8},{8,16},{16,24},{24,0},{1,9},{9,17},{17,25},{25,1},{2,10},{10... | collective-permute-start | bytes 983048 | tf_op jit(solution)/shard_map/ppermute | solution.py:37
  21.4 46.4 %copy-start.2 = (s32[1,2048]{1,0:T(1,128)S(1)}, s32[1,2048]{1,0:T(1,128)}, u32[]{:S(2)}) copy-start(s32[1,2048]{1,0:T(1,128)} %param.12) | copy-start | bytes 24580
  27.6 3.6 %copy-start.3 = (bf16[128,1280]{1,0:T(8,128)(2,1)}, bf16[128,1280]{1,0:T(8,128)(2,1)S(1)}, u32[]{:S(2)}) copy-start(bf16[128,1280]{1,0:T(8,128)(2,1)S(1)} %collective-permute-done.2.p3.refs_3_) | copy-start | bytes 983044
  27.6 3.6 %copy-start.4 = (bf16[128,1280]{1,0:T(8,128)(2,1)}, bf16[128,1280]{1,0:T(8,128)(2,1)S(1)}, u32[]{:S(2)}) copy-start(bf16[128,1280]{1,0:T(8,128)(2,1)S(1)} %collective-permute-done.1.p2.refs_2_) | copy-start | bytes 983044
  31.2 0.7 copy-start.5
  39.8 55.7 %copy-start.7 = (f32[1280]{0:T(1024)S(1)}, f32[1280]{0:T(1024)}, u32[]{:S(2)}) copy-start(f32[1280]{0:T(1024)} %param.16) | copy-start | bytes 15364
  43.9 21.7 %collective-permute-start.7 = (bf16[4,80,640]{2,1,0:T(8,128)(2,1)S(1)}, bf16[4,80,640]{2,1,0:T(8,128)(2,1)}, u32[]{:S(2)}, u32[]{:S(2)}) collective-permute-start(bf16[4,80,640]{2,1,0:T(8,128)(2,1)S(1)} %get-tuple-element.76), channel_id=1, source_target_pairs={{0,24},{8,0},{16,8},{24,16},{1,25},{9,1},{17,9},{25,17},{2,26},{10... | collective-permute-start | bytes 1228808 | tf_op jit(solution)/shard_map/ppermute | solution.py:37
  46.7 18.9 %collective-permute-start.6 = (bf16[4,80,640]{2,1,0:T(8,128)(2,1)S(1)}, bf16[4,80,640]{2,1,0:T(8,128)(2,1)}, u32[]{:S(2)}, u32[]{:S(2)}) collective-permute-start(bf16[4,80,640]{2,1,0:T(8,128)(2,1)S(1)} %get-tuple-element.76), channel_id=1, source_target_pairs={{0,8},{8,16},{16,24},{24,0},{1,9},{9,17},{17,25},{25,1},{2,10},{10... | collective-permute-start | bytes 1228808 | tf_op jit(solution)/shard_map/ppermute | solution.py:37
  46.7 9.7 %collective-permute-start.3 = (bf16[240,512]{1,0:T(8,128)(2,1)S(1)}, bf16[240,512]{1,0:T(8,128)(2,1)S(1)}, u32[]{:S(2)}, u32[]{:S(2)}) collective-permute-start(bf16[240,512]{1,0:T(8,128)(2,1)S(1)} %get-tuple-element.63), channel_id=1, source_target_pairs={{0,96},{32,0},{64,32},{96,64},{1,97},{33,1},{65,33},{97,65},{2,98}... | collective-permute-start | bytes 737288 | tf_op jit(solution)/shard_map/ppermute | solution.py:37
  48.2 11.8 %collective-permute-start.4 = (bf16[240,512]{1,0:T(8,128)(2,1)S(1)}, bf16[240,512]{1,0:T(8,128)(2,1)S(1)}, u32[]{:S(2)}, u32[]{:S(2)}) collective-permute-start(bf16[240,512]{1,0:T(8,128)(2,1)S(1)} %get-tuple-element.64), channel_id=1, source_target_pairs={{0,64},{32,96},{64,0},{96,32},{1,65},{33,97},{65,1},{97,33},{2,66}... | collective-permute-start | bytes 737288 | tf_op jit(solution)/shard_map/ppermute | solution.py:37
  49.4 16.3 %collective-permute-start.5 = (bf16[240,512]{1,0:T(8,128)(2,1)S(1)}, bf16[240,512]{1,0:T(8,128)(2,1)S(1)}, u32[]{:S(2)}, u32[]{:S(2)}) collective-permute-start(bf16[240,512]{1,0:T(8,128)(2,1)S(1)} %get-tuple-element.65), channel_id=1, source_target_pairs={{0,32},{32,64},{64,96},{96,0},{1,33},{33,65},{65,97},{97,1},{2,34}... | collective-permute-start | bytes 737288 | tf_op jit(solution)/shard_map/ppermute | solution.py:37
  65.7 13.0 %collective-permute-start.8 = (bf16[4,80,640]{2,1,0:T(8,128)(2,1)S(1)}, bf16[4,80,640]{2,1,0:T(8,128)(2,1)}, u32[]{:S(2)}, u32[]{:S(2)}) collective-permute-start(bf16[4,80,640]{2,1,0:T(8,128)(2,1)S(1)} %get-tuple-element.76), channel_id=1, source_target_pairs={{0,16},{8,24},{16,0},{24,8},{1,17},{9,25},{17,1},{25,9},{2,18},{10... | collective-permute-start | bytes 1228808 | tf_op jit(solution)/shard_map/ppermute | solution.py:37
  67.2 11.4 %collective-permute-start.9 = (bf16[4,80,640]{2,1,0:T(8,128)(2,1)}, bf16[4,80,640]{2,1,0:T(8,128)(2,1)}, u32[]{:S(2)}, u32[]{:S(2)}) collective-permute-start(bf16[4,80,640]{2,1,0:T(8,128)(2,1)} %collective-permute-done.6.refs_6_), channel_id=1, source_target_pairs={{0,1},{1,0},{2,3},{3,2},{4,5},{5,4},{6,7},{7,6},{8,9},{9,8},{10,11... | collective-permute-start | bytes 1228808 | tf_op jit(solution)/shard_map/ppermute | solution.py:45
  67.2 11.4 %collective-permute-start.10 = (bf16[4,80,640]{2,1,0:T(8,128)(2,1)}, bf16[4,80,640]{2,1,0:T(8,128)(2,1)}, u32[]{:S(2)}, u32[]{:S(2)}) collective-permute-start(bf16[4,80,640]{2,1,0:T(8,128)(2,1)} %collective-permute-done.7.refs_8_), channel_id=1, source_target_pairs={{0,1},{1,0},{2,3},{3,2},{4,5},{5,4},{6,7},{7,6},{8,9},{9,8},{10,11... | collective-permute-start | bytes 1228808 | tf_op jit(solution)/shard_map/ppermute | solution.py:45
  78.7 9.4 %collective-permute-start.11 = (bf16[80,512]{1,0:T(8,128)(2,1)S(1)}, bf16[80,512]{1,0:T(8,128)(2,1)S(1)}, u32[]{:S(2)}, u32[]{:S(2)}) collective-permute-start(bf16[80,512]{1,0:T(8,128)(2,1)S(1)} %get-tuple-element.80), channel_id=1, source_target_pairs={{0,32},{32,64},{64,96},{96,0},{1,33},{33,65},{65,97},{97,1},{2,34}... | collective-permute-start | bytes 245768 | tf_op jit(solution)/shard_map/ppermute | solution.py:37
  78.7 23.4 %collective-permute-start.17 = (bf16[4,80,640]{2,1,0:T(8,128)(2,1)}, bf16[4,80,640]{2,1,0:T(8,128)(2,1)S(1)}, u32[]{:S(2)}, u32[]{:S(2)}) collective-permute-start(bf16[4,80,640]{2,1,0:T(8,128)(2,1)} %collective-permute-done.8.refs_7_), channel_id=1, source_target_pairs={{0,1},{1,0},{2,3},{3,2},{4,5},{5,4},{6,7},{7,6},{8,9},{9,8},{10,11... | collective-permute-start | bytes 1228808 | tf_op jit(solution)/shard_map/ppermute | solution.py:45
  78.8 9.3 %collective-permute-start.12 = (bf16[80,512]{1,0:T(8,128)(2,1)S(1)}, bf16[80,512]{1,0:T(8,128)(2,1)S(1)}, u32[]{:S(2)}, u32[]{:S(2)}) collective-permute-start(bf16[80,512]{1,0:T(8,128)(2,1)S(1)} %get-tuple-element.81), channel_id=1, source_target_pairs={{0,64},{32,96},{64,0},{96,32},{1,65},{33,97},{65,1},{97,33},{2,66}... | collective-permute-start | bytes 245768 | tf_op jit(solution)/shard_map/ppermute | solution.py:37
  79.9 10.9 %collective-permute-start.13 = (bf16[80,512]{1,0:T(8,128)(2,1)S(1)}, bf16[80,512]{1,0:T(8,128)(2,1)S(1)}, u32[]{:S(2)}, u32[]{:S(2)}) collective-permute-start(bf16[80,512]{1,0:T(8,128)(2,1)S(1)} %get-tuple-element.82), channel_id=1, source_target_pairs={{0,96},{32,0},{64,32},{96,64},{1,97},{33,1},{65,33},{97,65},{2,98}... | collective-permute-start | bytes 245768 | tf_op jit(solution)/shard_map/ppermute | solution.py:37
  91.3 17.1 %collective-permute-start.16 = (bf16[4,80,512]{2,1,0:T(8,128)(2,1)S(1)}, bf16[4,80,512]{2,1,0:T(8,128)(2,1)S(1)}, u32[]{:S(2)}, u32[]{:S(2)}) collective-permute-start(bf16[4,80,512]{2,1,0:T(8,128)(2,1)S(1)} %pack.1.refs_0_), channel_id=1, source_target_pairs={{0,24},{8,0},{16,8},{24,16},{1,25},{9,1},{17,9},{25,17},{2,26},{10... | collective-permute-start | bytes 983048 | tf_op jit(solution)/shard_map/ppermute | solution.py:37
  94.6 13.9 %collective-permute-start.15 = (bf16[4,80,512]{2,1,0:T(8,128)(2,1)S(1)}, bf16[4,80,512]{2,1,0:T(8,128)(2,1)S(1)}, u32[]{:S(2)}, u32[]{:S(2)}) collective-permute-start(bf16[4,80,512]{2,1,0:T(8,128)(2,1)S(1)} %pack.1.refs_0_), channel_id=1, source_target_pairs={{0,16},{8,24},{16,0},{24,8},{1,17},{9,25},{17,1},{25,9},{2,18},{10... | collective-permute-start | bytes 983048 | tf_op jit(solution)/shard_map/ppermute | solution.py:37
  94.6 17.3 %collective-permute-start.14 = (bf16[4,80,512]{2,1,0:T(8,128)(2,1)S(1)}, bf16[4,80,512]{2,1,0:T(8,128)(2,1)S(1)}, u32[]{:S(2)}, u32[]{:S(2)}) collective-permute-start(bf16[4,80,512]{2,1,0:T(8,128)(2,1)S(1)} %pack.1.refs_0_), channel_id=1, source_target_pairs={{0,8},{8,16},{16,24},{24,0},{1,9},{9,17},{17,25},{25,1},{2,10},{10... | collective-permute-start | bytes 983048 | tf_op jit(solution)/shard_map/ppermute | solution.py:37
  102.1 0.8 copy-start.6
  115.9 17.6 %collective-permute-start.18 = (bf16[128,1280]{1,0:T(8,128)(2,1)S(1)}, bf16[128,1280]{1,0:T(8,128)(2,1)S(1)}, u32[]{:S(2)}, u32[]{:S(2)}) collective-permute-start(bf16[128,1280]{1,0:T(8,128)(2,1)S(1)} %get-tuple-element.99), channel_id=1, source_target_pairs={{0,8},{8,16},{16,24},{24,0},{1,9},{9,17},{17,25},{25,1},{2,10},{10... | collective-permute-start | bytes 983048 | tf_op jit(solution)/shard_map/ppermute | solution.py:37
  116.0 17.5 %collective-permute-start.19 = (bf16[128,1280]{1,0:T(8,128)(2,1)S(1)}, bf16[128,1280]{1,0:T(8,128)(2,1)S(1)}, u32[]{:S(2)}, u32[]{:S(2)}) collective-permute-start(bf16[128,1280]{1,0:T(8,128)(2,1)S(1)} %get-tuple-element.100), channel_id=1, source_target_pairs={{0,16},{8,24},{16,0},{24,8},{1,17},{9,25},{17,1},{25,9},{2,18},{10... | collective-permute-start | bytes 983048 | tf_op jit(solution)/shard_map/ppermute | solution.py:37
  122.4 11.6 %collective-permute-start.20 = (bf16[128,1280]{1,0:T(8,128)(2,1)S(1)}, bf16[128,1280]{1,0:T(8,128)(2,1)S(1)}, u32[]{:S(2)}, u32[]{:S(2)}) collective-permute-start(bf16[128,1280]{1,0:T(8,128)(2,1)S(1)} %get-tuple-element.101), channel_id=1, source_target_pairs={{0,24},{8,0},{16,8},{24,16},{1,25},{9,1},{17,9},{25,17},{2,26},{10... | collective-permute-start | bytes 983048 | tf_op jit(solution)/shard_map/ppermute | solution.py:37
  133.7 20.0 %copy-start.1 = (bf16[128,1280]{1,0:T(8,128)(2,1)S(1)}, bf16[128,1280]{1,0:T(8,128)(2,1)}, u32[]{:S(2)}) copy-start(bf16[128,1280]{1,0:T(8,128)(2,1)} %text.1) | copy-start | bytes 983044
  136.6 6.8 %collective-permute-start.21 = (bf16[4,8,1408]{2,1,0:T(8,128)(2,1)S(1)}, bf16[4,8,1408]{2,1,0:T(8,128)(2,1)S(1)}, u32[]{:S(2)}, u32[]{:S(2)}) collective-permute-start(bf16[4,8,1408]{2,1,0:T(8,128)(2,1)S(1)} %get-tuple-element.106), channel_id=1, source_target_pairs={{0,32},{32,64},{64,96},{96,0},{1,33},{33,65},{65,97},{97,1},{2,34}... | collective-permute-start | bytes 270344 | tf_op jit(solution)/shard_map/ppermute | solution.py:37
  136.7 6.7 %collective-permute-start.22 = (bf16[4,8,1408]{2,1,0:T(8,128)(2,1)S(1)}, bf16[4,8,1408]{2,1,0:T(8,128)(2,1)S(1)}, u32[]{:S(2)}, u32[]{:S(2)}) collective-permute-start(bf16[4,8,1408]{2,1,0:T(8,128)(2,1)S(1)} %get-tuple-element.107), channel_id=1, source_target_pairs={{0,64},{32,96},{64,0},{96,32},{1,65},{33,97},{65,1},{97,33},{2,66}... | collective-permute-start | bytes 270344 | tf_op jit(solution)/shard_map/ppermute | solution.py:37
  139.1 5.1 %collective-permute-start.23 = (bf16[4,8,1408]{2,1,0:T(8,128)(2,1)S(1)}, bf16[4,8,1408]{2,1,0:T(8,128)(2,1)S(1)}, u32[]{:S(2)}, u32[]{:S(2)}) collective-permute-start(bf16[4,8,1408]{2,1,0:T(8,128)(2,1)S(1)} %get-tuple-element.108), channel_id=1, source_target_pairs={{0,96},{32,0},{64,32},{96,64},{1,97},{33,1},{65,33},{97,65},{2,98}... | collective-permute-start | bytes 270344 | tf_op jit(solution)/shard_map/ppermute | solution.py:37
  144.2 6.9 %collective-permute-start.24 = (bf16[4,8,1408]{2,1,0:T(8,128)(2,1)S(1)}, bf16[4,8,1408]{2,1,0:T(8,128)(2,1)S(1)}, u32[]{:S(2)}, u32[]{:S(2)}) collective-permute-start(bf16[4,8,1408]{2,1,0:T(8,128)(2,1)S(1)} %get-tuple-element.110), channel_id=1, source_target_pairs={{0,8},{8,16},{16,24},{24,0},{1,9},{9,17},{17,25},{25,1},{2,10},{10... | collective-permute-start | bytes 270344 | tf_op jit(solution)/shard_map/ppermute | solution.py:37
  144.6 8.0 %collective-permute-start.25 = (bf16[4,8,1408]{2,1,0:T(8,128)(2,1)S(1)}, bf16[4,8,1408]{2,1,0:T(8,128)(2,1)S(1)}, u32[]{:S(2)}, u32[]{:S(2)}) collective-permute-start(bf16[4,8,1408]{2,1,0:T(8,128)(2,1)S(1)} %get-tuple-element.111), channel_id=1, source_target_pairs={{0,16},{8,24},{16,0},{24,8},{1,17},{9,25},{17,1},{25,9},{2,18},{10... | collective-permute-start | bytes 270344 | tf_op jit(solution)/shard_map/ppermute | solution.py:37
  149.1 4.5 %collective-permute-start.26 = (bf16[4,8,1408]{2,1,0:T(8,128)(2,1)S(1)}, bf16[4,8,1408]{2,1,0:T(8,128)(2,1)S(1)}, u32[]{:S(2)}, u32[]{:S(2)}) collective-permute-start(bf16[4,8,1408]{2,1,0:T(8,128)(2,1)S(1)} %get-tuple-element.112), channel_id=1, source_target_pairs={{0,24},{8,0},{16,8},{24,16},{1,25},{9,1},{17,9},{25,17},{2,26},{10... | collective-permute-start | bytes 270344 | tf_op jit(solution)/shard_map/ppermute | solution.py:37
Sparse Core Ops, SparseCore 0:
  9.0 30.7 all-gather.4
  42.1 55.0 all-gather.6

commit v8 on v6

--- a/solution.py
+++ b/solution.py
@@ -38,10 +38,6 @@
 
 def far(value):
     return pltpu.with_memory_space_constraint(value, pltpu.HBM)
-
-
-def swap(value):
-    return lax.ppermute(value, "c", [(0, 1), (1, 0)])
 
 
 def norm_kernel(pos, p0, p1, p2, p3, gain, h1, held, sems):
@@ -63,15 +59,16 @@
 
 def qkv_kernel(pos, h1, w_hbm, o0, o1, o2, o3, share, w, sems):
     x = pos[0]
-    c = pos[3]
     cols = w.shape[1]
+    half = w.shape[2]
     copies = []
     for k in range(N):
         at = pl.ds(lax.rem(x - k + N, N) * 2, 2)
         copies.append(pltpu.make_async_copy(w_hbm.at[at, :cols, :], w.at[at], sems.at[k]))
-    for j in range(N):
-        src = w_hbm.at[2 * j + c, cols : cols + HEAD, :]
-        copies.append(pltpu.make_async_copy(src, share.at[j], sems.at[N + j]))
+    for j in range(2 * N):
+        src = w_hbm.at[j, cols : cols + HEAD, :]
+        dst = share.at[j // 2, :, j % 2 * half : (j % 2 + 1) * half]
+        copies.append(pltpu.make_async_copy(src, dst, sems.at[N + j]))
     for copy in copies:
         copy.start()
     for k, out in enumerate((o0, o1, o2, o3)):
@@ -156,21 +153,18 @@
 def fetch_kernel(pos, *refs):
     pieces = refs[0:4]
     near, w_hbm = refs[4:6]
-    mine = refs[6:9]
-    other = refs[9:12]
-    w_all, up, down, held, sems = refs[12:]
+    passed = refs[6:9]
+    w_all, up, down, held, sems = refs[9:]
     y = pos[1]
-    c = pos[3]
-    half = w_all.shape[3]
+    half = w_hbm.shape[3]
     skip = near.shape[1] - HEAD
     moves = []
     for j in range(N):
-        moves.append((near.at[2 * j, skip : skip + HEAD, :], w_all.at[0, j]))
-        moves.append((near.at[2 * j + 1, skip : skip + HEAD, :], w_all.at[1, j]))
+        for h in (0, 1):
+            cols = slice(h * half, (h + 1) * half)
+            moves.append((near.at[2 * j + h, skip : skip + HEAD, :], w_all.at[j, :, cols]))
     for k in range(1, N):
-        to = slice(k * N, (k + 1) * N)
-        moves.append((mine[k - 1], w_all.at[c, to]))
-        moves.append((other[k - 1], w_all.at[1 - c, to]))
+        moves.append((passed[k - 1], w_all.at[k * N : (k + 1) * N]))
     for k in range(N):
         moves.append((pieces[k], held.at[lax.rem(y - k + N, N)]))
     units = up.shape[1]
@@ -195,7 +189,6 @@
     y = pos[1]
     rows = held.shape[1]
     width = held.shape[2]
-    half = width // 2
     group = N * HEAD
     blocks = [lax.rem(y + k, N) for k in offsets]
     lhs = []
@@ -207,11 +200,8 @@
         start.append(held[block].astype(F32))
     lhs = jnp.concatenate(lhs, axis=0)
     start = jnp.concatenate(start, axis=0)
-    heads = N * group
-    attn = [
-        jnp.dot(lhs, w_all[h].reshape(heads, half), preferred_element_type=F32) for h in (0, 1)
-    ]
-    resid = (start + jnp.concatenate(attn, axis=1)).astype(BF)
+    attn = jnp.dot(lhs, w_all[...].reshape(N * group, width), preferred_element_type=F32)
+    resid = (start + attn).astype(BF)
     normed = norm_rows(resid.astype(F32), gain[...]).astype(BF)
     count = up.shape[0] * up.shape[1]
     hidden = lax.dot_general(
@@ -298,7 +288,7 @@
         name="norm",
     )(pos, *[far(piece) for piece in pieces], ln_attn[None, :])
     group_rows = ids.shape[0]
-    chunk = 256
+    chunk = 512
     chunks = group_rows // chunk
     held = (ids[:, None] == jnp.arange(16)[None, :]).reshape(chunks, chunk, 16)
     held = jnp.any(held, axis=1)
@@ -347,12 +337,12 @@
     *qkv, mine = pl.pallas_call(
         qkv_kernel,
         out_shape=[jax.ShapeDtypeStruct((3 * HEAD, total_rows), BF)] * N
-        + [jax.ShapeDtypeStruct((N, HEAD, half), BF)],
+        + [jax.ShapeDtypeStruct((N, HEAD, width), BF)],
         in_specs=[SMEM, VMEM, HBM],
         out_specs=[VMEM] * (N + 1),
         scratch_shapes=[
             pltpu.VMEM((2 * N, 3 * HEAD, half), BF),
-            pltpu.SemaphoreType.DMA((2 * N,)),
+            pltpu.SemaphoreType.DMA((3 * N,)),
         ],
         compiler_params=params(16),
         name="qkv",
@@ -360,10 +350,8 @@
     blocks = [qkv[0]] + [shift(qkv[k], "x", -k) for k in (1, 2, 3)]
     pass1 = shift(mine, "y", 1)
     pass3 = shift(mine, "y", 3)
-    blocks, mine, pass1, pass3 = lax.optimization_barrier((blocks, mine, pass1, pass3))
+    blocks, mine = lax.optimization_barrier((blocks, mine))
     pass2 = shift(mine, "y", 2)
-    swap1 = swap(pass1)
-    swap3 = swap(pass3)
 
     attended = pl.pallas_call(
         attend_kernel,
@@ -380,9 +368,9 @@
         compiler_params=params(16),
         name="attend",
     )(pos, work, *blocks, id_row, id_col)
-    attended, pass2, swap1, swap3 = lax.optimization_barrier((attended, pass2, swap1, swap3))
-    swap2 = swap(pass2)
+    attended, pass1, pass3 = lax.optimization_barrier((attended, pass1, pass3))
     heads = [attended[0]] + [shift(attended[k], "x", k) for k in (1, 2, 3)]
+    heads, pass1, pass2, pass3 = lax.optimization_barrier((heads, pass1, pass2, pass3))
     heads = pl.pallas_call(
         pack_kernel,
         out_shape=jax.ShapeDtypeStruct((N, HEAD, total_rows), BF),
@@ -397,20 +385,20 @@
     fetched = pl.pallas_call(
         fetch_kernel,
         out_shape=[
-            jax.ShapeDtypeStruct((2, N * N, HEAD, half), BF),
+            jax.ShapeDtypeStruct((N * N, HEAD, width), BF),
             jax.ShapeDtypeStruct((N * N, units, width), BF),
             jax.ShapeDtypeStruct((N * N, units, width), BF),
             jax.ShapeDtypeStruct((N, count, width), BF),
         ],
-        in_specs=[SMEM] + [HBM] * 12,
+        in_specs=[SMEM] + [HBM] * 9,
         out_specs=[VMEM] * 4,
-        scratch_shapes=[pltpu.SemaphoreType.DMA((22,))],
+        scratch_shapes=[pltpu.SemaphoreType.DMA((19,))],
         compiler_params=params(4),
         name="fetch",
     )(
         pos,
         *[far(v) for v in pieces],
-        *[far(v) for v in (near, w_near, pass1, pass2, pass3, swap1, swap2, swap3)],
+        *[far(v) for v in (near, w_near, pass1, pass2, pass3)],
     )
 
     w_merge = pl.pallas_call(

time: 157 us -> 155 us (0.987)
  waiting for transfers between devices: 59.9 us -> 52 us
  starting transfers between devices: 23.6 us -> 28.1 us
  blocking collectives: 12.1 us -> 14.9 us
    ppermute x18, waiting for transfers between devices: 52.8 us -> 46.7 us  [shift(): return lax.ppermute(value, axis, pairs)]
    ppermute x18, starting transfers between devices: 23 us -> 28 us  [shift(): return lax.ppermute(value, axis, pairs)]
    all_to_all x1, blocking collectives: 12.1 us -> 14.9 us  [local(): lax.all_to_all(outgoing.reshape(req_count, slot_cap, width + 128), ('x',...]
    all_gather x1, waiting for transfers between devices: 1.81 us -> 0.01 us  [local(): w_near = lax.all_gather(packed, ('x', 'z', 'c'), axis=0, tiled=False)]
  transfers between devices with their start and end apart: 23 -> 20, of which waited for: 14 -> 13; matrix products, arithmetic and copies ran while one was open for 5% -> 6% of each run, Pallas kernels for 18% -> 18%
where the time goes in v8:
time: 155 us
  waiting for transfers between devices  52 us (34%)
  Pallas kernels  33.9 us (22%)
  starting transfers between devices  28.1 us (18%)
  blocking collectives  14.9 us (10%)
  between operations  13.6 us (9%)
  other arithmetic  6.97 us (4%)
  local copies, waits for them, and re-layouts  4.62 us (3%)
    ppermute x18, waiting for transfers between devices, shift(): return lax.ppermute(value, axis, pairs)  46.7 us
    ppermute x18, starting transfers between devices, shift(): return lax.ppermute(value, axis, pairs)  28 us
    all_to_all x1, blocking collectives, local(): lax.all_to_all(outgoing.reshape(req_count, slot_cap, width + 128), ('x',...  14.9 us
    pallas_call x2, Pallas kernels, mlp(): pl.pallas_call(functools.partial(mlp_kernel, offsets), out_shape=[jax.Sha...  7.78 us
    pallas_call x1, Pallas kernels, local(): pl.pallas_call(attend_kernel, out_shape=[jax.ShapeDtypeStruct((HEAD, tota...  5.58 us
    all_gather x1, waiting for transfers between devices, local(): near = lax.all_gather(w_half, ('x', 'c'), axis=0, tiled=False)  5.29 us
    pallas_call x1, Pallas kernels, local(): pl.pallas_call(fetch_kernel, out_shape=[jax.ShapeDtypeStruct((N * N, HEAD...  5.08 us
    pallas_call x1, Pallas kernels, local(): pl.pallas_call(qkv_kernel, out_shape=[jax.ShapeDtypeStruct((3 * HEAD, tot...  5.06 us
  transfers between devices with their start and end apart: 20, of which 13 were waited for; matrix products, arithmetic and copies ran while one was open for 6% of the time, Pallas kernels for 18%

profile of v8, /device:TPU:0, one launch (start us, length us, event | category | flops | bytes accessed | tf_op | source)
XLA Modules:
  0.0 155.2 jit_solution(9404175132676512283)
XLA Ops:
  6.5 1.9 %fusion.1 = bf16[320,640]{1,0:T(8,128)(2,1)} fusion(s32[]{:T(128)S(6)} %select_n.83, bf16[240,1280]{1,0:T(8,128)(2,1)} %bitcast.55, bf16[80,1280]{1,0:T(8,128)(2,1)} %param.15), kind=kLoop, calls=%fused_computation.5 | loop fusion | flops 819200 | bytes 1228804 | tf_op jit(solution)/shard_map/concatenate | solution.py:259
  8.5 0.9 dynamic_slice.11
  9.4 0.7 pad_maximum_fusion
  10.2 3.2 %collective-permute-start.2 = (bf16[128,1280]{1,0:T(8,128)(2,1)}, bf16[128,1280]{1,0:T(8,128)(2,1)S(1)}, u32[]{:S(2)}, u32[]{:S(2)}) collective-permute-start(bf16[128,1280]{1,0:T(8,128)(2,1)} %bitcast.50), channel_id=1, source_target_pairs={{0,24},{8,0},{16,8},{24,16},{1,25},{9,1},{17,9},{25,17},{2,26},{10... | collective-permute-start | bytes 983048 | tf_op jit(solution)/shard_map/ppermute | solution.py:36
  13.3 0.6 collective-permute-start.1
  14.0 1.0 collective-permute-start
  14.9 0.7 broadcast_in_dim.118.gain
  15.6 0.5 broadcast.242
  16.2 1.3 reduce.5
  17.5 0.2 fusion.2
  17.7 0.2 and_reduce_fusion
  17.8 0.2 select_reduce_fusion.3
  18.0 0.1 select_reduce_fusion.2
  18.1 0.6 slice.9
  18.7 0.1 convert_reduce_fusion.1
  18.8 0.1 select_reduce_fusion.1
  18.9 0.1 fusion.11
  19.0 0.6 stack.30
  19.7 0.7 compare_select_fusion
  20.3 0.7 fusion.14
  21.0 0.2 convert_reduce_fusion
  21.2 0.1 select_reduce_fusion
  21.5 6.1 %collective-permute-done.2.p3.refs_3_ = bf16[128,1280]{1,0:T(8,128)(2,1)S(1)} collective-permute-done((bf16[128,1280]{1,0:T(8,128)(2,1)}, bf16[128,1280]{1,0:T(8,128)(2,1)S(1)}, u32[]{:S(2)}, u32[]{:S(2)}) %collective-permute-start.2) | collective-permute-done | bytes 327712 | tf_op jit(solution)/shard_map/ppermute | solution.py:36
  27.6 3.6 %collective-permute-done.p1.refs_1_ = bf16[128,1280]{1,0:T(8,128)(2,1)S(1)} collective-permute-done((bf16[128,1280]{1,0:T(8,128)(2,1)}, bf16[128,1280]{1,0:T(8,128)(2,1)S(1)}, u32[]{:S(2)}, u32[]{:S(2)}) %collective-permute-start) | collective-permute-done | bytes 327712 | tf_op jit(solution)/shard_map/ppermute | solution.py:36
  31.3 0.7 copy-done.4
  32.0 2.6 %norm.1.h1 = bf16[2,512,640]{2,1,0:T(8,128)(2,1)S(1)} custom-call(s32[4]{0:T(128)S(1)} %pad_add_fusion.pos, bf16[128,1280]{1,0:T(8,128)(2,1)} %bitcast.53, bf16[128,1280]{1,0:T(8,128)(2,1)} %copy-done.4, bf16[128,1280]{1,0:T(8,128)(2,1)} %copy-done.3, bf16[128,1280]{1,0:T(8,128)(2,1)} %copy-done.2, f32[1,1280]{1,0:T(1,128)S(1)} %broadcast_in_dim.118.gain), custom_call_target="tpu_custom_call" | custom-call | tf_op jit(solution)/shard_map/norm/pallas_call | solution.py:278
  34.6 5.3 %all-gather.5.cloned.1.call-done = bf16[2560,640]{1,0:T(8,128)(2,1)} async-done(((bf16[320,640]{1,0:T(8,128)(2,1)}), bf16[2560,640]{1,0:T(8,128)(2,1)}) %all-gather.5.cloned.1.call-update) | async-done | bytes 3276816 | tf_op jit(solution)/shard_map/all_gather | solution.py:261
  39.9 5.1 %qkv.1 = (bf16[240,512]{1,0:T(8,128)(2,1)S(1)}, bf16[240,512]{1,0:T(8,128)(2,1)S(1)}, bf16[240,512]{1,0:T(8,128)(2,1)S(1)}, bf16[240,512]{1,0:T(8,128)(2,1)S(1)}, bf16[4,80,1280]{2,1,0:T(8,128)(2,1)}) custom-call(s32[4]{0:T(128)S(1)} %pad_add_fusion.pos, bf16[2,512,640]{2,1,0:T(8,128)(2,1)S(1)} %norm.1.h1, bf16[8,320,640]{2,1,0:T(8,128)(2,1)} %bitcast.47), custom_call_target="tpu_custom_call" | custom-call | tf_op jit(solution)/shard_map/qkv/pallas_call | solution.py:337
  45.0 1.5 collective-permute-start.3
  46.5 1.0 collective-permute-start.4
  47.5 0.6 collective-permute-start.5
  48.1 2.7 %collective-permute-start.7 = (bf16[4,80,1280]{2,1,0:T(8,128)(2,1)}, bf16[4,80,1280]{2,1,0:T(8,128)(2,1)}, u32[]{:S(2)}, u32[]{:S(2)}) collective-permute-start(bf16[4,80,1280]{2,1,0:T(8,128)(2,1)} %get-tuple-element.77), channel_id=1, source_target_pairs={{0,24},{8,0},{16,8},{24,16},{1,25},{9,1},{17,9},{25,17},{2,26},{10... | collective-permute-start | bytes 2457608 | tf_op jit(solution)/shard_map/ppermute | solution.py:36
  50.8 3.0 %collective-permute-done.3.r1 = bf16[240,512]{1,0:T(8,128)(2,1)S(1)} collective-permute-done((bf16[240,512]{1,0:T(8,128)(2,1)S(1)}, bf16[240,512]{1,0:T(8,128)(2,1)S(1)}, u32[]{:S(2)}, u32[]{:S(2)}) %collective-permute-start.3) | collective-permute-done | bytes 245792 | tf_op jit(solution)/shard_map/ppermute | solution.py:36
  53.8 3.6 %collective-permute-done.4.r2 = bf16[240,512]{1,0:T(8,128)(2,1)S(1)} collective-permute-done((bf16[240,512]{1,0:T(8,128)(2,1)S(1)}, bf16[240,512]{1,0:T(8,128)(2,1)S(1)}, u32[]{:S(2)}, u32[]{:S(2)}) %collective-permute-start.4) | collective-permute-done | bytes 245792 | tf_op jit(solution)/shard_map/ppermute | solution.py:36
  57.4 6.1 %collective-permute-done.5.r3 = bf16[240,512]{1,0:T(8,128)(2,1)S(1)} collective-permute-done((bf16[240,512]{1,0:T(8,128)(2,1)S(1)}, bf16[240,512]{1,0:T(8,128)(2,1)S(1)}, u32[]{:S(2)}, u32[]{:S(2)}) %collective-permute-start.5) | collective-permute-done | bytes 245792 | tf_op jit(solution)/shard_map/ppermute | solution.py:36
  63.5 3.0 %collective-permute-start.11 = (bf16[4,80,1280]{2,1,0:T(8,128)(2,1)}, bf16[4,80,1280]{2,1,0:T(8,128)(2,1)}, u32[]{:S(2)}, u32[]{:S(2)}) collective-permute-start(bf16[4,80,1280]{2,1,0:T(8,128)(2,1)} %get-tuple-element.77), channel_id=1, source_target_pairs={{0,16},{8,24},{16,0},{24,8},{1,17},{9,25},{17,1},{25,9},{2,18},{10... | collective-permute-start | bytes 2457608 | tf_op jit(solution)/shard_map/ppermute | solution.py:36
  66.5 0.4 copy.15.id_col
  66.9 5.6 %attend.1 = (bf16[80,512]{1,0:T(8,128)(2,1)S(1)}, bf16[80,512]{1,0:T(8,128)(2,1)S(1)}, bf16[80,512]{1,0:T(8,128)(2,1)S(1)}, bf16[80,512]{1,0:T(8,128)(2,1)S(1)}) custom-call(s32[4]{0:T(128)S(1)} %pad_add_fusion.pos, s32[5,16]{1,0:T(8,128)S(1)} %stack.31.work, bf16[240,512]{1,0:T(8,128)(2,1)S(1)} %get-tuple-element.63.r0, ...), custom_call_target="tpu_custom_call" | custom-call | tf_op jit(solution)/shard_map/attend/pallas_call | solution.py:356
  72.5 13.2 %collective-permute-done.7.refs_8_ = bf16[4,80,1280]{2,1,0:T(8,128)(2,1)} collective-permute-done((bf16[4,80,1280]{2,1,0:T(8,128)(2,1)}, bf16[4,80,1280]{2,1,0:T(8,128)(2,1)}, u32[]{:S(2)}, u32[]{:S(2)}) %collective-permute-start.7) | collective-permute-done | bytes 819232 | tf_op jit(solution)/shard_map/ppermute | solution.py:36
  85.7 3.4 %collective-permute-done.6.refs_6_ = bf16[4,80,1280]{2,1,0:T(8,128)(2,1)} collective-permute-done((bf16[4,80,1280]{2,1,0:T(8,128)(2,1)}, bf16[4,80,1280]{2,1,0:T(8,128)(2,1)}, u32[]{:S(2)}, u32[]{:S(2)}) %collective-permute-start.6) | collective-permute-done | bytes 819232 | tf_op jit(solution)/shard_map/ppermute | solution.py:36
  89.1 1.9 %collective-permute-start.8 = (bf16[80,512]{1,0:T(8,128)(2,1)S(1)}, bf16[80,512]{1,0:T(8,128)(2,1)S(1)}, u32[]{:S(2)}, u32[]{:S(2)}) collective-permute-start(bf16[80,512]{1,0:T(8,128)(2,1)S(1)} %get-tuple-element.73), channel_id=1, source_target_pairs={{0,32},{32,64},{64,96},{96,0},{1,33},{33,65},{65,97},{97,1},{2,34}... | collective-permute-start | bytes 245768 | tf_op jit(solution)/shard_map/ppermute | solution.py:36
  91.0 2.2 %collective-permute-start.9 = (bf16[80,512]{1,0:T(8,128)(2,1)S(1)}, bf16[80,512]{1,0:T(8,128)(2,1)S(1)}, u32[]{:S(2)}, u32[]{:S(2)}) collective-permute-start(bf16[80,512]{1,0:T(8,128)(2,1)S(1)} %get-tuple-element.74), channel_id=1, source_target_pairs={{0,64},{32,96},{64,0},{96,32},{1,65},{33,97},{65,1},{97,33},{2,66}... | collective-permute-start | bytes 245768 | tf_op jit(solution)/shard_map/ppermute | solution.py:36
  93.3 1.6 %collective-permute-start.10 = (bf16[80,512]{1,0:T(8,128)(2,1)S(1)}, bf16[80,512]{1,0:T(8,128)(2,1)S(1)}, u32[]{:S(2)}, u32[]{:S(2)}) collective-permute-start(bf16[80,512]{1,0:T(8,128)(2,1)S(1)} %get-tuple-element.75), channel_id=1, source_target_pairs={{0,96},{32,0},{64,32},{96,64},{1,97},{33,1},{65,33},{97,65},{2,98}... | collective-permute-start | bytes 245768 | tf_op jit(solution)/shard_map/ppermute | solution.py:36
  94.9 2.1 %collective-permute-done.9.g2 = bf16[80,512]{1,0:T(8,128)(2,1)S(1)} collective-permute-done((bf16[80,512]{1,0:T(8,128)(2,1)S(1)}, bf16[80,512]{1,0:T(8,128)(2,1)S(1)}, u32[]{:S(2)}, u32[]{:S(2)}) %collective-permute-start.9) | collective-permute-done | bytes 81952 | tf_op jit(solution)/shard_map/ppermute | solution.py:36
  97.0 0.7 collective-permute-done.10.g3
  97.7 0.6 pack.1.refs_0_
  98.3 0.4 collective-permute-start.14
  98.6 1.7 %collective-permute-start.12 = (bf16[4,80,512]{2,1,0:T(8,128)(2,1)S(1)}, bf16[4,80,512]{2,1,0:T(8,128)(2,1)S(1)}, u32[]{:S(2)}, u32[]{:S(2)}) collective-permute-start(bf16[4,80,512]{2,1,0:T(8,128)(2,1)S(1)} %pack.1.refs_0_), channel_id=1, source_target_pairs={{0,8},{8,16},{16,24},{24,0},{1,9},{9,17},{17,25},{25,1},{2,10},{10... | collective-permute-start | bytes 983048 | tf_op jit(solution)/shard_map/ppermute | solution.py:36
  100.4 4.9 %fetch_merge.1.w = bf16[5120,1280]{1,0:T(8,128)(2,1)S(1)} custom-call(bf16[5120,1280]{1,0:T(8,128)(2,1)} %w_hbm), custom_call_target="tpu_custom_call" | custom-call | tf_op jit(solution)/shard_map/fetch_merge/pallas_call | solution.py:404
  105.3 5.1 %fetch.1 = (bf16[16,80,1280]{2,1,0:T(8,128)(2,1)S(1)}, bf16[16,80,1280]{2,1,0:T(8,128)(2,1)S(1)}, bf16[16,80,1280]{2,1,0:T(8,128)(2,1)S(1)}, bf16[4,128,1280]{2,1,0:T(8,128)(2,1)S(1)}) custom-call(s32[4]{0:T(128)S(1)} %pad_add_fusion.pos, bf16[128,1280]{1,0:T(8,128)(2,1)} %bitcast.54, bf16[128,1280]{1,0:T(8,128)(2,1)} %copy-done.4, ...), custom_call_target="tpu_custom_call" | custom-call | tf_op jit(solution)/shard_map/fetch/pallas_call | solution.py:385
  110.4 0.3 collective-permute-done.12.refs_1_
  110.7 3.9 %mlp_first.1 = (bf16[128,1280]{1,0:T(8,128)(2,1)S(1)}, bf16[128,1280]{1,0:T(8,128)(2,1)S(1)}) custom-call(s32[4]{0:T(128)S(1)} %pad_add_fusion.pos, bf16[4,80,512]{2,1,0:T(8,128)(2,1)S(1)} %pack.1.refs_0_, bf16[4,80,512]{2,1,0:T(8,128)(2,1)S(1)} %collective-permute-done.12.refs_1_, bf16[4,80,512]{2,1,0:T(8,128)(2,1)S(1)} %collective-permute-done.13.refs_2_, ...), custom_call_target="tpu_custom_call" | custom-call | flops 2516582400 | bytes 9830400 | tf_op jit(solution)/shard_map/mlp_first/pallas_call | solution.py:416
  114.6 1.5 collective-permute-start.15
  116.1 2.5 %collective-permute-start.16 = (bf16[128,1280]{1,0:T(8,128)(2,1)S(1)}, bf16[128,1280]{1,0:T(8,128)(2,1)S(1)}, u32[]{:S(2)}, u32[]{:S(2)}) collective-permute-start(bf16[128,1280]{1,0:T(8,128)(2,1)S(1)} %get-tuple-element.100), channel_id=1, source_target_pairs={{0,16},{8,24},{16,0},{24,8},{1,17},{9,25},{17,1},{25,9},{2,18},{10... | collective-permute-start | bytes 983048 | tf_op jit(solution)/shard_map/ppermute | solution.py:36
  118.6 3.9 %mlp_second.1 = (bf16[128,1280]{1,0:T(8,128)(2,1)S(1)}, bf16[128,1280]{1,0:T(8,128)(2,1)S(1)}, bf16[128,1280]{1,0:T(8,128)(2,1)S(1)}) custom-call(s32[4]{0:T(128)S(1)} %pad_add_fusion.pos, bf16[4,80,512]{2,1,0:T(8,128)(2,1)S(1)} %pack.1.refs_0_, bf16[4,80,512]{2,1,0:T(8,128)(2,1)S(1)} %collective-permute-done.12.refs_1_, ...), custom_call_target="tpu_custom_call" | custom-call | flops 2516582400 | bytes 9830400 | tf_op jit(solution)/shard_map/mlp_second/pallas_call | solution.py:416
  122.5 2.6 %collective-permute-start.17 = (bf16[128,1280]{1,0:T(8,128)(2,1)S(1)}, bf16[128,1280]{1,0:T(8,128)(2,1)S(1)}, u32[]{:S(2)}, u32[]{:S(2)}) collective-permute-start(bf16[128,1280]{1,0:T(8,128)(2,1)S(1)} %get-tuple-element.101), channel_id=1, source_target_pairs={{0,24},{8,0},{16,8},{24,16},{1,25},{9,1},{17,9},{25,17},{2,26},{10... | collective-permute-start | bytes 983048 | tf_op jit(solution)/shard_map/ppermute | solution.py:36
  125.1 2.0 %collective-permute-done.16 = bf16[128,1280]{1,0:T(8,128)(2,1)S(1)} collective-permute-done((bf16[128,1280]{1,0:T(8,128)(2,1)S(1)}, bf16[128,1280]{1,0:T(8,128)(2,1)S(1)}, u32[]{:S(2)}, u32[]{:S(2)}) %collective-permute-start.16) | collective-permute-done | bytes 327712 | tf_op jit(solution)/shard_map/ppermute | solution.py:36
  127.1 0.2 add_add_fusion.early
  127.2 2.4 %collective-permute-done.17.late = bf16[128,1280]{1,0:T(8,128)(2,1)S(1)} collective-permute-done((bf16[128,1280]{1,0:T(8,128)(2,1)S(1)}, bf16[128,1280]{1,0:T(8,128)(2,1)S(1)}, u32[]{:S(2)}, u32[]{:S(2)}) %collective-permute-start.17) | collective-permute-done | bytes 327712 | tf_op jit(solution)/shard_map/ppermute | solution.py:36
  129.7 2.4 %merge.1 = bf16[32,1408]{1,0:T(8,128)(2,1)S(1)} custom-call(f32[128,1280]{1,0:T(8,128)S(1)} %add_add_fusion.early, bf16[128,1280]{1,0:T(8,128)(2,1)S(1)} %collective-permute-done.17.late, bf16[5120,1280]{1,0:T(8,128)(2,1)S(1)} %fetch_merge.1.w, bf16[32,32]{1,0:T(8,128)(2,1)S(1)} %fusion.5.select, bf16[32,128]{1,0:T(8,128)(2,1)S(1)} %select_convert_fusion.tail), custom_call_target="tpu_custom_call" | custom-call | tf_op jit(solution)/shard_map/merge/pallas_call | solution.py:437
  132.1 14.9 %all_to_all.5 = bf16[16,2,1408]{2,1,0:T(2,128)(2,1)S(1)} all-to-all(bf16[16,2,1408]{2,1,0:T(2,128)(2,1)S(1)} %reshape.166), channel_id=1, replica_groups=mesh['x'=4,'y'=4,'z'=4,'c'=2] {'x','y'}, dimensions={0} | all-to-all | bytes 180224 | tf_op jit(solution)/shard_map/all_to_all | solution.py:446
  147.0 0.1 add_reduce_fusion
  147.1 0.1 fusion.4
  147.2 1.1 fusion
  (43 shorter events, 0.5 us)
Async XLA Ops:
  6.5 2.9 %copy-start = (bf16[1280,320]{0,1:T(8,128)(2,1)S(1)}, bf16[1280,320]{0,1:T(8,128)(2,1)}, u32[]{:S(2)}) copy-start(bf16[1280,320]{0,1:T(8,128)(2,1)} %param.17) | copy-start | bytes 2457604
  6.5 33.4 %all-gather.5.cloned.1.call-start = ((), (), s32[]{:S(2)}) async-start(), calls=%async_computation.1 | async-start | bytes 3686400 | tf_op jit(solution)/shard_map/all_gather | solution.py:261
  8.4 92.0 %all-gather.7.cloned.1.call-start = ((), (), s32[]{:S(2)}) async-start(), calls=%async_computation.2 | async-start | bytes 6758400 | tf_op jit(solution)/shard_map/all_gather | solution.py:273
  10.2 17.5 %collective-permute-start.2 = (bf16[128,1280]{1,0:T(8,128)(2,1)}, bf16[128,1280]{1,0:T(8,128)(2,1)S(1)}, u32[]{:S(2)}, u32[]{:S(2)}) collective-permute-start(bf16[128,1280]{1,0:T(8,128)(2,1)} %bitcast.50), channel_id=1, source_target_pairs={{0,24},{8,0},{16,8},{24,16},{1,25},{9,1},{17,9},{25,17},{2,26},{10... | collective-permute-start | bytes 983048 | tf_op jit(solution)/shard_map/ppermute | solution.py:36
  13.3 14.3 %collective-permute-start.1 = (bf16[128,1280]{1,0:T(8,128)(2,1)}, bf16[128,1280]{1,0:T(8,128)(2,1)S(1)}, u32[]{:S(2)}, u32[]{:S(2)}) collective-permute-start(bf16[128,1280]{1,0:T(8,128)(2,1)} %bitcast.51), channel_id=1, source_target_pairs={{0,16},{8,24},{16,0},{24,8},{1,17},{9,25},{17,1},{25,9},{2,18},{10... | collective-permute-start | bytes 983048 | tf_op jit(solution)/shard_map/ppermute | solution.py:36
  14.0 17.3 %collective-permute-start = (bf16[128,1280]{1,0:T(8,128)(2,1)}, bf16[128,1280]{1,0:T(8,128)(2,1)S(1)}, u32[]{:S(2)}, u32[]{:S(2)}) collective-permute-start(bf16[128,1280]{1,0:T(8,128)(2,1)} %bitcast.52), channel_id=1, source_target_pairs={{0,8},{8,16},{16,24},{24,0},{1,9},{9,17},{17,25},{25,1},{2,10},{10... | collective-permute-start | bytes 983048 | tf_op jit(solution)/shard_map/ppermute | solution.py:36
  21.5 45.0 %copy-start.1 = (s32[1,2048]{1,0:T(1,128)S(1)}, s32[1,2048]{1,0:T(1,128)}, u32[]{:S(2)}) copy-start(s32[1,2048]{1,0:T(1,128)} %param.12) | copy-start | bytes 24580
  27.6 3.6 %copy-start.2 = (bf16[128,1280]{1,0:T(8,128)(2,1)}, bf16[128,1280]{1,0:T(8,128)(2,1)S(1)}, u32[]{:S(2)}) copy-start(bf16[128,1280]{1,0:T(8,128)(2,1)S(1)} %collective-permute-done.2.p3.refs_3_) | copy-start | bytes 983044
  27.6 3.6 %copy-start.3 = (bf16[128,1280]{1,0:T(8,128)(2,1)}, bf16[128,1280]{1,0:T(8,128)(2,1)S(1)}, u32[]{:S(2)}) copy-start(bf16[128,1280]{1,0:T(8,128)(2,1)S(1)} %collective-permute-done.1.p2.refs_2_) | copy-start | bytes 983044
  31.2 0.7 copy-start.4
  39.9 60.5 %copy-start.6 = (f32[1280]{0:T(1024)S(1)}, f32[1280]{0:T(1024)}, u32[]{:S(2)}) copy-start(f32[1280]{0:T(1024)} %param.16) | copy-start | bytes 15364
  45.0 8.9 %collective-permute-start.3 = (bf16[240,512]{1,0:T(8,128)(2,1)S(1)}, bf16[240,512]{1,0:T(8,128)(2,1)S(1)}, u32[]{:S(2)}, u32[]{:S(2)}) collective-permute-start(bf16[240,512]{1,0:T(8,128)(2,1)S(1)} %get-tuple-element.59), channel_id=1, source_target_pairs={{0,96},{32,0},{64,32},{96,64},{1,97},{33,1},{65,33},{97,65},{2,98}... | collective-permute-start | bytes 737288 | tf_op jit(solution)/shard_map/ppermute | solution.py:36
  46.5 11.0 %collective-permute-start.4 = (bf16[240,512]{1,0:T(8,128)(2,1)S(1)}, bf16[240,512]{1,0:T(8,128)(2,1)S(1)}, u32[]{:S(2)}, u32[]{:S(2)}) collective-permute-start(bf16[240,512]{1,0:T(8,128)(2,1)S(1)} %get-tuple-element.60), channel_id=1, source_target_pairs={{0,64},{32,96},{64,0},{96,32},{1,65},{33,97},{65,1},{97,33},{2,66}... | collective-permute-start | bytes 737288 | tf_op jit(solution)/shard_map/ppermute | solution.py:36
  47.5 16.0 %collective-permute-start.5 = (bf16[240,512]{1,0:T(8,128)(2,1)S(1)}, bf16[240,512]{1,0:T(8,128)(2,1)S(1)}, u32[]{:S(2)}, u32[]{:S(2)}) collective-permute-start(bf16[240,512]{1,0:T(8,128)(2,1)S(1)} %get-tuple-element.61), channel_id=1, source_target_pairs={{0,32},{32,64},{64,96},{96,0},{1,33},{33,65},{65,97},{97,1},{2,34}... | collective-permute-start | bytes 737288 | tf_op jit(solution)/shard_map/ppermute | solution.py:36
  48.1 37.7 %collective-permute-start.7 = (bf16[4,80,1280]{2,1,0:T(8,128)(2,1)}, bf16[4,80,1280]{2,1,0:T(8,128)(2,1)}, u32[]{:S(2)}, u32[]{:S(2)}) collective-permute-start(bf16[4,80,1280]{2,1,0:T(8,128)(2,1)} %get-tuple-element.77), channel_id=1, source_target_pairs={{0,24},{8,0},{16,8},{24,16},{1,25},{9,1},{17,9},{25,17},{2,26},{10... | collective-permute-start | bytes 2457608 | tf_op jit(solution)/shard_map/ppermute | solution.py:36
  50.8 38.3 %collective-permute-start.6 = (bf16[4,80,1280]{2,1,0:T(8,128)(2,1)}, bf16[4,80,1280]{2,1,0:T(8,128)(2,1)}, u32[]{:S(2)}, u32[]{:S(2)}) collective-permute-start(bf16[4,80,1280]{2,1,0:T(8,128)(2,1)} %get-tuple-element.77), channel_id=1, source_target_pairs={{0,8},{8,16},{16,24},{24,0},{1,9},{9,17},{17,25},{25,1},{2,10},{10... | collective-permute-start | bytes 2457608 | tf_op jit(solution)/shard_map/ppermute | solution.py:36
  63.5 34.2 %collective-permute-start.11 = (bf16[4,80,1280]{2,1,0:T(8,128)(2,1)}, bf16[4,80,1280]{2,1,0:T(8,128)(2,1)}, u32[]{:S(2)}, u32[]{:S(2)}) collective-permute-start(bf16[4,80,1280]{2,1,0:T(8,128)(2,1)} %get-tuple-element.77), channel_id=1, source_target_pairs={{0,16},{8,24},{16,0},{24,8},{1,17},{9,25},{17,1},{25,9},{2,18},{10... | collective-permute-start | bytes 2457608 | tf_op jit(solution)/shard_map/ppermute | solution.py:36
  89.1 5.8 %collective-permute-start.8 = (bf16[80,512]{1,0:T(8,128)(2,1)S(1)}, bf16[80,512]{1,0:T(8,128)(2,1)S(1)}, u32[]{:S(2)}, u32[]{:S(2)}) collective-permute-start(bf16[80,512]{1,0:T(8,128)(2,1)S(1)} %get-tuple-element.73), channel_id=1, source_target_pairs={{0,32},{32,64},{64,96},{96,0},{1,33},{33,65},{65,97},{97,1},{2,34}... | collective-permute-start | bytes 245768 | tf_op jit(solution)/shard_map/ppermute | solution.py:36
  91.0 5.9 %collective-permute-start.9 = (bf16[80,512]{1,0:T(8,128)(2,1)S(1)}, bf16[80,512]{1,0:T(8,128)(2,1)S(1)}, u32[]{:S(2)}, u32[]{:S(2)}) collective-permute-start(bf16[80,512]{1,0:T(8,128)(2,1)S(1)} %get-tuple-element.74), channel_id=1, source_target_pairs={{0,64},{32,96},{64,0},{96,32},{1,65},{33,97},{65,1},{97,33},{2,66}... | collective-permute-start | bytes 245768 | tf_op jit(solution)/shard_map/ppermute | solution.py:36
  93.3 4.4 %collective-permute-start.10 = (bf16[80,512]{1,0:T(8,128)(2,1)S(1)}, bf16[80,512]{1,0:T(8,128)(2,1)S(1)}, u32[]{:S(2)}, u32[]{:S(2)}) collective-permute-start(bf16[80,512]{1,0:T(8,128)(2,1)S(1)} %get-tuple-element.75), channel_id=1, source_target_pairs={{0,96},{32,0},{64,32},{96,64},{1,97},{33,1},{65,33},{97,65},{2,98}... | collective-permute-start | bytes 245768 | tf_op jit(solution)/shard_map/ppermute | solution.py:36
  98.3 12.1 %collective-permute-start.14 = (bf16[4,80,512]{2,1,0:T(8,128)(2,1)S(1)}, bf16[4,80,512]{2,1,0:T(8,128)(2,1)S(1)}, u32[]{:S(2)}, u32[]{:S(2)}) collective-permute-start(bf16[4,80,512]{2,1,0:T(8,128)(2,1)S(1)} %pack.1.refs_0_), channel_id=1, source_target_pairs={{0,24},{8,0},{16,8},{24,16},{1,25},{9,1},{17,9},{25,17},{2,26},{10... | collective-permute-start | bytes 983048 | tf_op jit(solution)/shard_map/ppermute | solution.py:36
  98.6 11.7 %collective-permute-start.13 = (bf16[4,80,512]{2,1,0:T(8,128)(2,1)S(1)}, bf16[4,80,512]{2,1,0:T(8,128)(2,1)S(1)}, u32[]{:S(2)}, u32[]{:S(2)}) collective-permute-start(bf16[4,80,512]{2,1,0:T(8,128)(2,1)S(1)} %pack.1.refs_0_), channel_id=1, source_target_pairs={{0,16},{8,24},{16,0},{24,8},{1,17},{9,25},{17,1},{25,9},{2,18},{10... | collective-permute-start | bytes 983048 | tf_op jit(solution)/shard_map/ppermute | solution.py:36
  98.6 12.1 %collective-permute-start.12 = (bf16[4,80,512]{2,1,0:T(8,128)(2,1)S(1)}, bf16[4,80,512]{2,1,0:T(8,128)(2,1)S(1)}, u32[]{:S(2)}, u32[]{:S(2)}) collective-permute-start(bf16[4,80,512]{2,1,0:T(8,128)(2,1)S(1)} %pack.1.refs_0_), channel_id=1, source_target_pairs={{0,8},{8,16},{16,24},{24,0},{1,9},{9,17},{17,25},{25,1},{2,10},{10... | collective-permute-start | bytes 983048 | tf_op jit(solution)/shard_map/ppermute | solution.py:36
  114.6 10.5 %collective-permute-start.15 = (bf16[128,1280]{1,0:T(8,128)(2,1)S(1)}, bf16[128,1280]{1,0:T(8,128)(2,1)S(1)}, u32[]{:S(2)}, u32[]{:S(2)}) collective-permute-start(bf16[128,1280]{1,0:T(8,128)(2,1)S(1)} %get-tuple-element.99), channel_id=1, source_target_pairs={{0,8},{8,16},{16,24},{24,0},{1,9},{9,17},{17,25},{25,1},{2,10},{10... | collective-permute-start | bytes 983048 | tf_op jit(solution)/shard_map/ppermute | solution.py:36
  116.1 11.0 %collective-permute-start.16 = (bf16[128,1280]{1,0:T(8,128)(2,1)S(1)}, bf16[128,1280]{1,0:T(8,128)(2,1)S(1)}, u32[]{:S(2)}, u32[]{:S(2)}) collective-permute-start(bf16[128,1280]{1,0:T(8,128)(2,1)S(1)} %get-tuple-element.100), channel_id=1, source_target_pairs={{0,16},{8,24},{16,0},{24,8},{1,17},{9,25},{17,1},{25,9},{2,18},{10... | collective-permute-start | bytes 983048 | tf_op jit(solution)/shard_map/ppermute | solution.py:36
  122.5 7.2 %collective-permute-start.17 = (bf16[128,1280]{1,0:T(8,128)(2,1)S(1)}, bf16[128,1280]{1,0:T(8,128)(2,1)S(1)}, u32[]{:S(2)}, u32[]{:S(2)}) collective-permute-start(bf16[128,1280]{1,0:T(8,128)(2,1)S(1)} %get-tuple-element.101), channel_id=1, source_target_pairs={{0,24},{8,0},{16,8},{24,16},{1,25},{9,1},{17,9},{25,17},{2,26},{10... | collective-permute-start | bytes 983048 | tf_op jit(solution)/shard_map/ppermute | solution.py:36
  127.2 20.0 %copy-start.5 = (bf16[128,1280]{1,0:T(8,128)(2,1)S(1)}, bf16[128,1280]{1,0:T(8,128)(2,1)}, u32[]{:S(2)}) copy-start(bf16[128,1280]{1,0:T(8,128)(2,1)} %param.20) | copy-start | bytes 983044
Sparse Core Ops, SparseCore 0:
  9.0 30.7 all-gather.4
  42.1 51.6 all-gather.6

commit v9 on v8

--- a/solution.py
+++ b/solution.py
@@ -368,7 +368,6 @@
         compiler_params=params(16),
         name="attend",
     )(pos, work, *blocks, id_row, id_col)
-    attended, pass1, pass3 = lax.optimization_barrier((attended, pass1, pass3))
     heads = [attended[0]] + [shift(attended[k], "x", k) for k in (1, 2, 3)]
     heads, pass1, pass2, pass3 = lax.optimization_barrier((heads, pass1, pass2, pass3))
     heads = pl.pallas_call(

time: 155 us -> 154 us (level)
  waiting for transfers between devices: 52 us -> 59.3 us
  starting transfers between devices: 28.1 us -> 21.8 us
  blocking collectives: 14.9 us -> 12 us
    ppermute x18, starting transfers between devices: 28 us -> 21.8 us  [shift(): return lax.ppermute(value, axis, pairs)]
    all_gather x1, waiting for transfers between devices: 0.01 us -> 3.74 us  [local(): w_near = lax.all_gather(packed, ('x', 'z', 'c'), axis=0, tiled=False)]
    ppermute x18, waiting for transfers between devices: 46.7 us -> 50.2 us  [shift(): return lax.ppermute(value, axis, pairs)]
    all_to_all x1, blocking collectives: 14.9 us -> 12 us  [local(): lax.all_to_all(outgoing.reshape(req_count, slot_cap, width + 128), ('x',...]
where the time goes in v9:
time: 154 us; the launch traced here: 153 us
  waiting for transfers between devices  59.3 us (39%)
  Pallas kernels  33.9 us (22%)
  starting transfers between devices  21.8 us (14%)
  between operations  13.6 us (9%)
  blocking collectives  12 us (8%)
  other arithmetic  6.97 us (5%)
  local copies, waits for them, and re-layouts  4.62 us (3%)
    ppermute x18, waiting for transfers between devices, shift(): return lax.ppermute(value, axis, pairs)  50.2 us
    ppermute x18, starting transfers between devices, shift(): return lax.ppermute(value, axis, pairs)  21.8 us
    all_to_all x1, blocking collectives, local(): lax.all_to_all(outgoing.reshape(req_count, slot_cap, width + 128), ('x',...  12 us
    pallas_call x2, Pallas kernels, mlp(): pl.pallas_call(functools.partial(mlp_kernel, offsets), out_shape=[jax.Sha...  7.78 us
    pallas_call x1, Pallas kernels, local(): pl.pallas_call(attend_kernel, out_shape=[jax.ShapeDtypeStruct((HEAD, tota...  5.58 us
    all_gather x1, waiting for transfers between devices, local(): near = lax.all_gather(w_half, ('x', 'c'), axis=0, tiled=False)  5.29 us
    pallas_call x1, Pallas kernels, local(): pl.pallas_call(fetch_kernel, out_shape=[jax.ShapeDtypeStruct((N * N, HEAD...  5.08 us
    pallas_call x1, Pallas kernels, local(): pl.pallas_call(qkv_kernel, out_shape=[jax.ShapeDtypeStruct((3 * HEAD, tot...  5.06 us
  transfers between devices with their start and end apart: 20, of which 13 were waited for; matrix products, arithmetic and copies ran while one was open for 6% of the time, Pallas kernels for 18%

profile of v9, /device:TPU:0, one launch (start us, length us, event | category | flops | bytes accessed | tf_op | source)
XLA Modules:
  0.0 153.3 jit_solution(9935514399370525765)
XLA Ops:
  6.5 1.9 %fusion.1 = bf16[320,640]{1,0:T(8,128)(2,1)} fusion(s32[]{:T(128)S(6)} %select_n.83, bf16[240,1280]{1,0:T(8,128)(2,1)} %bitcast.55, bf16[80,1280]{1,0:T(8,128)(2,1)} %param.15), kind=kLoop, calls=%fused_computation.5 | loop fusion | flops 819200 | bytes 1228804 | tf_op jit(solution)/shard_map/concatenate | solution.py:259
  8.5 0.9 dynamic_slice.11
  9.4 0.7 pad_maximum_fusion
  10.2 3.2 %collective-permute-start.2 = (bf16[128,1280]{1,0:T(8,128)(2,1)}, bf16[128,1280]{1,0:T(8,128)(2,1)S(1)}, u32[]{:S(2)}, u32[]{:S(2)}) collective-permute-start(bf16[128,1280]{1,0:T(8,128)(2,1)} %bitcast.50), channel_id=1, source_target_pairs={{0,24},{8,0},{16,8},{24,16},{1,25},{9,1},{17,9},{25,17},{2,26},{10... | collective-permute-start | bytes 983048 | tf_op jit(solution)/shard_map/ppermute | solution.py:36
  13.3 0.6 collective-permute-start.1
  14.0 1.0 collective-permute-start
  14.9 0.7 broadcast_in_dim.118.gain
  15.6 0.5 broadcast.242
  16.2 1.3 reduce.5
  17.5 0.2 fusion.2
  17.7 0.2 and_reduce_fusion
  17.8 0.2 select_reduce_fusion.3
  18.0 0.1 select_reduce_fusion.2
  18.1 0.6 slice.9
  18.7 0.1 convert_reduce_fusion.1
  18.8 0.1 select_reduce_fusion.1
  18.9 0.1 fusion.11
  19.0 0.6 stack.30
  19.7 0.7 compare_select_fusion
  20.3 0.7 fusion.14
  21.0 0.2 convert_reduce_fusion
  21.2 0.1 select_reduce_fusion
  21.3 0.1 pad_add_fusion.pos
  21.5 6.1 %collective-permute-done.2.p3.refs_3_ = bf16[128,1280]{1,0:T(8,128)(2,1)S(1)} collective-permute-done((bf16[128,1280]{1,0:T(8,128)(2,1)}, bf16[128,1280]{1,0:T(8,128)(2,1)S(1)}, u32[]{:S(2)}, u32[]{:S(2)}) %collective-permute-start.2) | collective-permute-done | bytes 327712 | tf_op jit(solution)/shard_map/ppermute | solution.py:36
  27.6 3.6 %collective-permute-done.p1.refs_1_ = bf16[128,1280]{1,0:T(8,128)(2,1)S(1)} collective-permute-done((bf16[128,1280]{1,0:T(8,128)(2,1)}, bf16[128,1280]{1,0:T(8,128)(2,1)S(1)}, u32[]{:S(2)}, u32[]{:S(2)}) %collective-permute-start) | collective-permute-done | bytes 327712 | tf_op jit(solution)/shard_map/ppermute | solution.py:36
  31.3 0.7 copy-done.4
  32.0 2.6 %norm.1.h1 = bf16[2,512,640]{2,1,0:T(8,128)(2,1)S(1)} custom-call(s32[4]{0:T(128)S(1)} %pad_add_fusion.pos, bf16[128,1280]{1,0:T(8,128)(2,1)} %bitcast.53, bf16[128,1280]{1,0:T(8,128)(2,1)} %copy-done.4, bf16[128,1280]{1,0:T(8,128)(2,1)} %copy-done.3, bf16[128,1280]{1,0:T(8,128)(2,1)} %copy-done.2, f32[1,1280]{1,0:T(1,128)S(1)} %broadcast_in_dim.118.gain), custom_call_target="tpu_custom_call" | custom-call | tf_op jit(solution)/shard_map/norm/pallas_call | solution.py:278
  34.6 5.3 %all-gather.5.cloned.1.call-done = bf16[2560,640]{1,0:T(8,128)(2,1)} async-done(((bf16[320,640]{1,0:T(8,128)(2,1)}), bf16[2560,640]{1,0:T(8,128)(2,1)}) %all-gather.5.cloned.1.call-update) | async-done | bytes 3276816 | tf_op jit(solution)/shard_map/all_gather | solution.py:261
  39.9 5.1 %qkv.1 = (bf16[240,512]{1,0:T(8,128)(2,1)S(1)}, bf16[240,512]{1,0:T(8,128)(2,1)S(1)}, bf16[240,512]{1,0:T(8,128)(2,1)S(1)}, bf16[240,512]{1,0:T(8,128)(2,1)S(1)}, bf16[4,80,1280]{2,1,0:T(8,128)(2,1)}) custom-call(s32[4]{0:T(128)S(1)} %pad_add_fusion.pos, bf16[2,512,640]{2,1,0:T(8,128)(2,1)S(1)} %norm.1.h1, bf16[8,320,640]{2,1,0:T(8,128)(2,1)} %bitcast.47), custom_call_target="tpu_custom_call" | custom-call | tf_op jit(solution)/shard_map/qkv/pallas_call | solution.py:337
  45.0 1.5 collective-permute-start.3
  46.5 1.0 collective-permute-start.4
  47.5 0.6 collective-permute-start.5
  48.1 2.7 %collective-permute-start.11 = (bf16[4,80,1280]{2,1,0:T(8,128)(2,1)}, bf16[4,80,1280]{2,1,0:T(8,128)(2,1)}, u32[]{:S(2)}, u32[]{:S(2)}) collective-permute-start(bf16[4,80,1280]{2,1,0:T(8,128)(2,1)} %get-tuple-element.66), channel_id=1, source_target_pairs={{0,24},{8,0},{16,8},{24,16},{1,25},{9,1},{17,9},{25,17},{2,26},{10... | collective-permute-start | bytes 2457608 | tf_op jit(solution)/shard_map/ppermute | solution.py:36
  50.8 3.0 %collective-permute-done.3.r1 = bf16[240,512]{1,0:T(8,128)(2,1)S(1)} collective-permute-done((bf16[240,512]{1,0:T(8,128)(2,1)S(1)}, bf16[240,512]{1,0:T(8,128)(2,1)S(1)}, u32[]{:S(2)}, u32[]{:S(2)}) %collective-permute-start.3) | collective-permute-done | bytes 245792 | tf_op jit(solution)/shard_map/ppermute | solution.py:36
  53.8 3.6 %collective-permute-done.4.r2 = bf16[240,512]{1,0:T(8,128)(2,1)S(1)} collective-permute-done((bf16[240,512]{1,0:T(8,128)(2,1)S(1)}, bf16[240,512]{1,0:T(8,128)(2,1)S(1)}, u32[]{:S(2)}, u32[]{:S(2)}) %collective-permute-start.4) | collective-permute-done | bytes 245792 | tf_op jit(solution)/shard_map/ppermute | solution.py:36
  57.4 6.1 %collective-permute-done.5.r3 = bf16[240,512]{1,0:T(8,128)(2,1)S(1)} collective-permute-done((bf16[240,512]{1,0:T(8,128)(2,1)S(1)}, bf16[240,512]{1,0:T(8,128)(2,1)S(1)}, u32[]{:S(2)}, u32[]{:S(2)}) %collective-permute-start.5) | collective-permute-done | bytes 245792 | tf_op jit(solution)/shard_map/ppermute | solution.py:36
  63.5 3.0 %collective-permute-start.10 = (bf16[4,80,1280]{2,1,0:T(8,128)(2,1)}, bf16[4,80,1280]{2,1,0:T(8,128)(2,1)}, u32[]{:S(2)}, u32[]{:S(2)}) collective-permute-start(bf16[4,80,1280]{2,1,0:T(8,128)(2,1)} %get-tuple-element.66), channel_id=1, source_target_pairs={{0,16},{8,24},{16,0},{24,8},{1,17},{9,25},{17,1},{25,9},{2,18},{10... | collective-permute-start | bytes 2457608 | tf_op jit(solution)/shard_map/ppermute | solution.py:36
  66.5 0.4 copy.15.id_col
  66.9 5.6 %attend.1 = (bf16[80,512]{1,0:T(8,128)(2,1)S(1)}, bf16[80,512]{1,0:T(8,128)(2,1)S(1)}, bf16[80,512]{1,0:T(8,128)(2,1)S(1)}, bf16[80,512]{1,0:T(8,128)(2,1)S(1)}) custom-call(s32[4]{0:T(128)S(1)} %pad_add_fusion.pos, s32[5,16]{1,0:T(8,128)S(1)} %stack.31.work, bf16[240,512]{1,0:T(8,128)(2,1)S(1)} %get-tuple-element.57.r0, ...), custom_call_target="tpu_custom_call" | custom-call | tf_op jit(solution)/shard_map/attend/pallas_call | solution.py:356
  72.5 0.1 collective-permute-start.6
  72.6 2.1 %collective-permute-start.7 = (bf16[80,512]{1,0:T(8,128)(2,1)S(1)}, bf16[80,512]{1,0:T(8,128)(2,1)S(1)}, u32[]{:S(2)}, u32[]{:S(2)}) collective-permute-start(bf16[80,512]{1,0:T(8,128)(2,1)S(1)} %get-tuple-element.64), channel_id=1, source_target_pairs={{0,64},{32,96},{64,0},{96,32},{1,65},{33,97},{65,1},{97,33},{2,66}... | collective-permute-start | bytes 245768 | tf_op jit(solution)/shard_map/ppermute | solution.py:36
  74.6 7.6 %collective-permute-done.6.g1 = bf16[80,512]{1,0:T(8,128)(2,1)S(1)} collective-permute-done((bf16[80,512]{1,0:T(8,128)(2,1)S(1)}, bf16[80,512]{1,0:T(8,128)(2,1)S(1)}, u32[]{:S(2)}, u32[]{:S(2)}) %collective-permute-start.6) | collective-permute-done | bytes 81952 | tf_op jit(solution)/shard_map/ppermute | solution.py:36
  82.3 6.4 %collective-permute-done.8.g3 = bf16[80,512]{1,0:T(8,128)(2,1)S(1)} collective-permute-done((bf16[80,512]{1,0:T(8,128)(2,1)S(1)}, bf16[80,512]{1,0:T(8,128)(2,1)S(1)}, u32[]{:S(2)}, u32[]{:S(2)}) %collective-permute-start.8) | collective-permute-done | bytes 81952 | tf_op jit(solution)/shard_map/ppermute | solution.py:36
  88.7 0.4 collective-permute-done.9.refs_6_
  89.1 0.6 pack.1.refs_0_
  89.7 0.4 collective-permute-start.14
  90.1 0.5 collective-permute-start.13
  90.6 1.2 collective-permute-start.12
  91.8 3.7 %all-gather.7.cloned.1.call-done = bf16[5120,640]{1,0:T(8,128)(2,1)} async-done(((bf16[160,640]{1,0:T(8,128)(2,1)}), bf16[5120,640]{1,0:T(8,128)(2,1)}) %all-gather.7.cloned.1.call-update) | async-done | bytes 6553616 | tf_op jit(solution)/shard_map/all_gather | solution.py:273
  95.6 4.8 %fetch_merge.1.w = bf16[5120,1280]{1,0:T(8,128)(2,1)S(1)} custom-call(bf16[5120,1280]{1,0:T(8,128)(2,1)} %w_hbm), custom_call_target="tpu_custom_call" | custom-call | tf_op jit(solution)/shard_map/fetch_merge/pallas_call | solution.py:403
  100.4 5.1 %fetch.1 = (bf16[16,80,1280]{2,1,0:T(8,128)(2,1)S(1)}, bf16[16,80,1280]{2,1,0:T(8,128)(2,1)S(1)}, bf16[16,80,1280]{2,1,0:T(8,128)(2,1)S(1)}, bf16[4,128,1280]{2,1,0:T(8,128)(2,1)S(1)}) custom-call(s32[4]{0:T(128)S(1)} %pad_add_fusion.pos, bf16[128,1280]{1,0:T(8,128)(2,1)} %bitcast.54, bf16[128,1280]{1,0:T(8,128)(2,1)} %copy-done.4, ...), custom_call_target="tpu_custom_call" | custom-call | tf_op jit(solution)/shard_map/fetch/pallas_call | solution.py:384
  105.5 2.7 %collective-permute-done.12.refs_1_ = bf16[4,80,512]{2,1,0:T(8,128)(2,1)S(1)} collective-permute-done((bf16[4,80,512]{2,1,0:T(8,128)(2,1)S(1)}, bf16[4,80,512]{2,1,0:T(8,128)(2,1)S(1)}, u32[]{:S(2)}, u32[]{:S(2)}) %collective-permute-start.12) | collective-permute-done | bytes 327712 | tf_op jit(solution)/shard_map/ppermute | solution.py:36
  108.2 3.9 %mlp_first.1 = (bf16[128,1280]{1,0:T(8,128)(2,1)S(1)}, bf16[128,1280]{1,0:T(8,128)(2,1)S(1)}) custom-call(s32[4]{0:T(128)S(1)} %pad_add_fusion.pos, bf16[4,80,512]{2,1,0:T(8,128)(2,1)S(1)} %pack.1.refs_0_, bf16[4,80,512]{2,1,0:T(8,128)(2,1)S(1)} %collective-permute-done.12.refs_1_, bf16[4,80,512]{2,1,0:T(8,128)(2,1)S(1)} %collective-permute-done.13.refs_2_, ...), custom_call_target="tpu_custom_call" | custom-call | flops 2516582400 | bytes 9830400 | tf_op jit(solution)/shard_map/mlp_first/pallas_call | solution.py:415
  112.2 2.1 %collective-permute-start.16 = (bf16[128,1280]{1,0:T(8,128)(2,1)S(1)}, bf16[128,1280]{1,0:T(8,128)(2,1)S(1)}, u32[]{:S(2)}, u32[]{:S(2)}) collective-permute-start(bf16[128,1280]{1,0:T(8,128)(2,1)S(1)} %get-tuple-element.88), channel_id=1, source_target_pairs={{0,16},{8,24},{16,0},{24,8},{1,17},{9,25},{17,1},{25,9},{2,18},{10... | collective-permute-start | bytes 983048 | tf_op jit(solution)/shard_map/ppermute | solution.py:36
  114.3 3.9 %mlp_second.1 = (bf16[128,1280]{1,0:T(8,128)(2,1)S(1)}, bf16[128,1280]{1,0:T(8,128)(2,1)S(1)}, bf16[128,1280]{1,0:T(8,128)(2,1)S(1)}) custom-call(s32[4]{0:T(128)S(1)} %pad_add_fusion.pos, bf16[4,80,512]{2,1,0:T(8,128)(2,1)S(1)} %pack.1.refs_0_, bf16[4,80,512]{2,1,0:T(8,128)(2,1)S(1)} %collective-permute-done.12.refs_1_, ...), custom_call_target="tpu_custom_call" | custom-call | flops 2516582400 | bytes 9830400 | tf_op jit(solution)/shard_map/mlp_second/pallas_call | solution.py:415
  118.2 1.7 %collective-permute-start.17 = (bf16[128,1280]{1,0:T(8,128)(2,1)S(1)}, bf16[128,1280]{1,0:T(8,128)(2,1)S(1)}, u32[]{:S(2)}, u32[]{:S(2)}) collective-permute-start(bf16[128,1280]{1,0:T(8,128)(2,1)S(1)} %get-tuple-element.89), channel_id=1, source_target_pairs={{0,24},{8,0},{16,8},{24,16},{1,25},{9,1},{17,9},{25,17},{2,26},{10... | collective-permute-start | bytes 983048 | tf_op jit(solution)/shard_map/ppermute | solution.py:36
  120.0 10.1 %collective-permute-done.15 = bf16[128,1280]{1,0:T(8,128)(2,1)S(1)} collective-permute-done((bf16[128,1280]{1,0:T(8,128)(2,1)S(1)}, bf16[128,1280]{1,0:T(8,128)(2,1)S(1)}, u32[]{:S(2)}, u32[]{:S(2)}) %collective-permute-start.15) | collective-permute-done | bytes 327712 | tf_op jit(solution)/shard_map/ppermute | solution.py:36
  130.1 0.2 add_add_fusion.early
  130.2 0.4 collective-permute-done.17.late
  130.7 2.4 %merge.1 = bf16[32,1408]{1,0:T(8,128)(2,1)S(1)} custom-call(f32[128,1280]{1,0:T(8,128)S(1)} %add_add_fusion.early, bf16[128,1280]{1,0:T(8,128)(2,1)S(1)} %collective-permute-done.17.late, bf16[5120,1280]{1,0:T(8,128)(2,1)S(1)} %fetch_merge.1.w, bf16[32,32]{1,0:T(8,128)(2,1)S(1)} %fusion.5.select, bf16[32,128]{1,0:T(8,128)(2,1)S(1)} %select_convert_fusion.tail), custom_call_target="tpu_custom_call" | custom-call | tf_op jit(solution)/shard_map/merge/pallas_call | solution.py:436
  133.1 12.0 %all_to_all.5 = bf16[16,2,1408]{2,1,0:T(2,128)(2,1)S(1)} all-to-all(bf16[16,2,1408]{2,1,0:T(2,128)(2,1)S(1)} %reshape.166), channel_id=1, replica_groups=mesh['x'=4,'y'=4,'z'=4,'c'=2] {'x','y'}, dimensions={0} | all-to-all | bytes 180224 | tf_op jit(solution)/shard_map/all_to_all | solution.py:445
  145.2 0.1 add_reduce_fusion
  145.3 0.1 fusion.4
  145.4 1.1 fusion
  (43 shorter events, 0.5 us)
Async XLA Ops:
  6.5 2.9 %copy-start = (bf16[1280,320]{0,1:T(8,128)(2,1)S(1)}, bf16[1280,320]{0,1:T(8,128)(2,1)}, u32[]{:S(2)}) copy-start(bf16[1280,320]{0,1:T(8,128)(2,1)} %param.17) | copy-start | bytes 2457604
  6.5 33.4 %all-gather.5.cloned.1.call-start = ((), (), s32[]{:S(2)}) async-start(), calls=%async_computation.1 | async-start | bytes 3686400 | tf_op jit(solution)/shard_map/all_gather | solution.py:261
  8.4 87.1 %all-gather.7.cloned.1.call-start = ((), (), s32[]{:S(2)}) async-start(), calls=%async_computation.2 | async-start | bytes 6758400 | tf_op jit(solution)/shard_map/all_gather | solution.py:273
  10.2 17.5 %collective-permute-start.2 = (bf16[128,1280]{1,0:T(8,128)(2,1)}, bf16[128,1280]{1,0:T(8,128)(2,1)S(1)}, u32[]{:S(2)}, u32[]{:S(2)}) collective-permute-start(bf16[128,1280]{1,0:T(8,128)(2,1)} %bitcast.50), channel_id=1, source_target_pairs={{0,24},{8,0},{16,8},{24,16},{1,25},{9,1},{17,9},{25,17},{2,26},{10... | collective-permute-start | bytes 983048 | tf_op jit(solution)/shard_map/ppermute | solution.py:36
  13.3 14.3 %collective-permute-start.1 = (bf16[128,1280]{1,0:T(8,128)(2,1)}, bf16[128,1280]{1,0:T(8,128)(2,1)S(1)}, u32[]{:S(2)}, u32[]{:S(2)}) collective-permute-start(bf16[128,1280]{1,0:T(8,128)(2,1)} %bitcast.51), channel_id=1, source_target_pairs={{0,16},{8,24},{16,0},{24,8},{1,17},{9,25},{17,1},{25,9},{2,18},{10... | collective-permute-start | bytes 983048 | tf_op jit(solution)/shard_map/ppermute | solution.py:36
  14.0 17.3 %collective-permute-start = (bf16[128,1280]{1,0:T(8,128)(2,1)}, bf16[128,1280]{1,0:T(8,128)(2,1)S(1)}, u32[]{:S(2)}, u32[]{:S(2)}) collective-permute-start(bf16[128,1280]{1,0:T(8,128)(2,1)} %bitcast.52), channel_id=1, source_target_pairs={{0,8},{8,16},{16,24},{24,0},{1,9},{9,17},{17,25},{25,1},{2,10},{10... | collective-permute-start | bytes 983048 | tf_op jit(solution)/shard_map/ppermute | solution.py:36
  21.5 45.0 %copy-start.1 = (s32[1,2048]{1,0:T(1,128)S(1)}, s32[1,2048]{1,0:T(1,128)}, u32[]{:S(2)}) copy-start(s32[1,2048]{1,0:T(1,128)} %param.12) | copy-start | bytes 24580
  27.6 3.6 %copy-start.2 = (bf16[128,1280]{1,0:T(8,128)(2,1)}, bf16[128,1280]{1,0:T(8,128)(2,1)S(1)}, u32[]{:S(2)}) copy-start(bf16[128,1280]{1,0:T(8,128)(2,1)S(1)} %collective-permute-done.2.p3.refs_3_) | copy-start | bytes 983044
  27.6 3.6 %copy-start.3 = (bf16[128,1280]{1,0:T(8,128)(2,1)}, bf16[128,1280]{1,0:T(8,128)(2,1)S(1)}, u32[]{:S(2)}) copy-start(bf16[128,1280]{1,0:T(8,128)(2,1)S(1)} %collective-permute-done.1.p2.refs_2_) | copy-start | bytes 983044
  31.2 0.7 copy-start.4
  39.9 51.9 %copy-start.6 = (f32[1280]{0:T(1024)S(1)}, f32[1280]{0:T(1024)}, u32[]{:S(2)}) copy-start(f32[1280]{0:T(1024)} %param.16) | copy-start | bytes 15364
  45.0 8.9 %collective-permute-start.3 = (bf16[240,512]{1,0:T(8,128)(2,1)S(1)}, bf16[240,512]{1,0:T(8,128)(2,1)S(1)}, u32[]{:S(2)}, u32[]{:S(2)}) collective-permute-start(bf16[240,512]{1,0:T(8,128)(2,1)S(1)} %get-tuple-element.53), channel_id=1, source_target_pairs={{0,96},{32,0},{64,32},{96,64},{1,97},{33,1},{65,33},{97,65},{2,98}... | collective-permute-start | bytes 737288 | tf_op jit(solution)/shard_map/ppermute | solution.py:36
  46.5 11.0 %collective-permute-start.4 = (bf16[240,512]{1,0:T(8,128)(2,1)S(1)}, bf16[240,512]{1,0:T(8,128)(2,1)S(1)}, u32[]{:S(2)}, u32[]{:S(2)}) collective-permute-start(bf16[240,512]{1,0:T(8,128)(2,1)S(1)} %get-tuple-element.54), channel_id=1, source_target_pairs={{0,64},{32,96},{64,0},{96,32},{1,65},{33,97},{65,1},{97,33},{2,66}... | collective-permute-start | bytes 737288 | tf_op jit(solution)/shard_map/ppermute | solution.py:36
  47.5 16.0 %collective-permute-start.5 = (bf16[240,512]{1,0:T(8,128)(2,1)S(1)}, bf16[240,512]{1,0:T(8,128)(2,1)S(1)}, u32[]{:S(2)}, u32[]{:S(2)}) collective-permute-start(bf16[240,512]{1,0:T(8,128)(2,1)S(1)} %get-tuple-element.55), channel_id=1, source_target_pairs={{0,32},{32,64},{64,96},{96,0},{1,33},{33,65},{65,97},{97,1},{2,34}... | collective-permute-start | bytes 737288 | tf_op jit(solution)/shard_map/ppermute | solution.py:36
  48.1 40.6 %collective-permute-start.11 = (bf16[4,80,1280]{2,1,0:T(8,128)(2,1)}, bf16[4,80,1280]{2,1,0:T(8,128)(2,1)}, u32[]{:S(2)}, u32[]{:S(2)}) collective-permute-start(bf16[4,80,1280]{2,1,0:T(8,128)(2,1)} %get-tuple-element.66), channel_id=1, source_target_pairs={{0,24},{8,0},{16,8},{24,16},{1,25},{9,1},{17,9},{25,17},{2,26},{10... | collective-permute-start | bytes 2457608 | tf_op jit(solution)/shard_map/ppermute | solution.py:36
  50.8 38.3 %collective-permute-start.9 = (bf16[4,80,1280]{2,1,0:T(8,128)(2,1)}, bf16[4,80,1280]{2,1,0:T(8,128)(2,1)}, u32[]{:S(2)}, u32[]{:S(2)}) collective-permute-start(bf16[4,80,1280]{2,1,0:T(8,128)(2,1)} %get-tuple-element.66), channel_id=1, source_target_pairs={{0,8},{8,16},{16,24},{24,0},{1,9},{9,17},{17,25},{25,1},{2,10},{10... | collective-permute-start | bytes 2457608 | tf_op jit(solution)/shard_map/ppermute | solution.py:36
  63.5 25.6 %collective-permute-start.10 = (bf16[4,80,1280]{2,1,0:T(8,128)(2,1)}, bf16[4,80,1280]{2,1,0:T(8,128)(2,1)}, u32[]{:S(2)}, u32[]{:S(2)}) collective-permute-start(bf16[4,80,1280]{2,1,0:T(8,128)(2,1)} %get-tuple-element.66), channel_id=1, source_target_pairs={{0,16},{8,24},{16,0},{24,8},{1,17},{9,25},{17,1},{25,9},{2,18},{10... | collective-permute-start | bytes 2457608 | tf_op jit(solution)/shard_map/ppermute | solution.py:36
  72.5 9.8 %collective-permute-start.6 = (bf16[80,512]{1,0:T(8,128)(2,1)S(1)}, bf16[80,512]{1,0:T(8,128)(2,1)S(1)}, u32[]{:S(2)}, u32[]{:S(2)}) collective-permute-start(bf16[80,512]{1,0:T(8,128)(2,1)S(1)} %get-tuple-element.63), channel_id=1, source_target_pairs={{0,32},{32,64},{64,96},{96,0},{1,33},{33,65},{65,97},{97,1},{2,34}... | collective-permute-start | bytes 245768 | tf_op jit(solution)/shard_map/ppermute | solution.py:36
  72.6 9.7 %collective-permute-start.7 = (bf16[80,512]{1,0:T(8,128)(2,1)S(1)}, bf16[80,512]{1,0:T(8,128)(2,1)S(1)}, u32[]{:S(2)}, u32[]{:S(2)}) collective-permute-start(bf16[80,512]{1,0:T(8,128)(2,1)S(1)} %get-tuple-element.64), channel_id=1, source_target_pairs={{0,64},{32,96},{64,0},{96,32},{1,65},{33,97},{65,1},{97,33},{2,66}... | collective-permute-start | bytes 245768 | tf_op jit(solution)/shard_map/ppermute | solution.py:36
  82.2 6.5 %collective-permute-start.8 = (bf16[80,512]{1,0:T(8,128)(2,1)S(1)}, bf16[80,512]{1,0:T(8,128)(2,1)S(1)}, u32[]{:S(2)}, u32[]{:S(2)}) collective-permute-start(bf16[80,512]{1,0:T(8,128)(2,1)S(1)} %get-tuple-element.65), channel_id=1, source_target_pairs={{0,96},{32,0},{64,32},{96,64},{1,97},{33,1},{65,33},{97,65},{2,98}... | collective-permute-start | bytes 245768 | tf_op jit(solution)/shard_map/ppermute | solution.py:36
  89.7 15.8 %collective-permute-start.14 = (bf16[4,80,512]{2,1,0:T(8,128)(2,1)S(1)}, bf16[4,80,512]{2,1,0:T(8,128)(2,1)S(1)}, u32[]{:S(2)}, u32[]{:S(2)}) collective-permute-start(bf16[4,80,512]{2,1,0:T(8,128)(2,1)S(1)} %pack.1.refs_0_), channel_id=1, source_target_pairs={{0,24},{8,0},{16,8},{24,16},{1,25},{9,1},{17,9},{25,17},{2,26},{10... | collective-permute-start | bytes 983048 | tf_op jit(solution)/shard_map/ppermute | solution.py:36
  90.1 15.5 %collective-permute-start.13 = (bf16[4,80,512]{2,1,0:T(8,128)(2,1)S(1)}, bf16[4,80,512]{2,1,0:T(8,128)(2,1)S(1)}, u32[]{:S(2)}, u32[]{:S(2)}) collective-permute-start(bf16[4,80,512]{2,1,0:T(8,128)(2,1)S(1)} %pack.1.refs_0_), channel_id=1, source_target_pairs={{0,16},{8,24},{16,0},{24,8},{1,17},{9,25},{17,1},{25,9},{2,18},{10... | collective-permute-start | bytes 983048 | tf_op jit(solution)/shard_map/ppermute | solution.py:36
  90.6 17.6 %collective-permute-start.12 = (bf16[4,80,512]{2,1,0:T(8,128)(2,1)S(1)}, bf16[4,80,512]{2,1,0:T(8,128)(2,1)S(1)}, u32[]{:S(2)}, u32[]{:S(2)}) collective-permute-start(bf16[4,80,512]{2,1,0:T(8,128)(2,1)S(1)} %pack.1.refs_0_), channel_id=1, source_target_pairs={{0,8},{8,16},{16,24},{24,0},{1,9},{9,17},{17,25},{25,1},{2,10},{10... | collective-permute-start | bytes 983048 | tf_op jit(solution)/shard_map/ppermute | solution.py:36
  112.1 17.9 %collective-permute-start.15 = (bf16[128,1280]{1,0:T(8,128)(2,1)S(1)}, bf16[128,1280]{1,0:T(8,128)(2,1)S(1)}, u32[]{:S(2)}, u32[]{:S(2)}) collective-permute-start(bf16[128,1280]{1,0:T(8,128)(2,1)S(1)} %get-tuple-element.87), channel_id=1, source_target_pairs={{0,8},{8,16},{16,24},{24,0},{1,9},{9,17},{17,25},{25,1},{2,10},{10... | collective-permute-start | bytes 983048 | tf_op jit(solution)/shard_map/ppermute | solution.py:36
  112.2 17.9 %collective-permute-start.16 = (bf16[128,1280]{1,0:T(8,128)(2,1)S(1)}, bf16[128,1280]{1,0:T(8,128)(2,1)S(1)}, u32[]{:S(2)}, u32[]{:S(2)}) collective-permute-start(bf16[128,1280]{1,0:T(8,128)(2,1)S(1)} %get-tuple-element.88), channel_id=1, source_target_pairs={{0,16},{8,24},{16,0},{24,8},{1,17},{9,25},{17,1},{25,9},{2,18},{10... | collective-permute-start | bytes 983048 | tf_op jit(solution)/shard_map/ppermute | solution.py:36
  118.2 12.4 %collective-permute-start.17 = (bf16[128,1280]{1,0:T(8,128)(2,1)S(1)}, bf16[128,1280]{1,0:T(8,128)(2,1)S(1)}, u32[]{:S(2)}, u32[]{:S(2)}) collective-permute-start(bf16[128,1280]{1,0:T(8,128)(2,1)S(1)} %get-tuple-element.89), channel_id=1, source_target_pairs={{0,24},{8,0},{16,8},{24,16},{1,25},{9,1},{17,9},{25,17},{2,26},{10... | collective-permute-start | bytes 983048 | tf_op jit(solution)/shard_map/ppermute | solution.py:36
  130.2 15.2 %copy-start.5 = (bf16[128,1280]{1,0:T(8,128)(2,1)S(1)}, bf16[128,1280]{1,0:T(8,128)(2,1)}, u32[]{:S(2)}) copy-start(bf16[128,1280]{1,0:T(8,128)(2,1)} %param.20) | copy-start | bytes 983044
Sparse Core Ops, SparseCore 0:
  9.0 30.7 all-gather.4
  42.1 53.3 all-gather.6

commit v10 on v9

--- a/solution.py
+++ b/solution.py
@@ -38,6 +38,10 @@
 
 def far(value):
     return pltpu.with_memory_space_constraint(value, pltpu.HBM)
+
+
+def swap(value):
+    return lax.ppermute(value, "c", [(0, 1), (1, 0)])
 
 
 def norm_kernel(pos, p0, p1, p2, p3, gain, h1, held, sems):
@@ -57,7 +61,7 @@
         h1[1, at, :] = normed[:, half:]
 
 
-def qkv_kernel(pos, h1, w_hbm, o0, o1, o2, o3, share, w, sems):
+def qkv_kernel(pos, h1, w_hbm, o0, o1, o2, o3, share, share_half, w, sems):
     x = pos[0]
     cols = w.shape[1]
     half = w.shape[2]
@@ -69,6 +73,9 @@
         src = w_hbm.at[j, cols : cols + HEAD, :]
         dst = share.at[j // 2, :, j % 2 * half : (j % 2 + 1) * half]
         copies.append(pltpu.make_async_copy(src, dst, sems.at[N + j]))
+    for j in range(N):
+        src = w_hbm.at[2 * j + pos[3], cols : cols + HEAD, :]
+        copies.append(pltpu.make_async_copy(src, share_half.at[j], sems.at[3 * N + j]))
     for copy in copies:
         copy.start()
     for k, out in enumerate((o0, o1, o2, o3)):
@@ -153,8 +160,8 @@
 def fetch_kernel(pos, *refs):
     pieces = refs[0:4]
     near, w_hbm = refs[4:6]
-    passed = refs[6:9]
-    w_all, up, down, held, sems = refs[9:]
+    pass1, pass3, mine, other = refs[6:10]
+    w_all, up, down, held, sems = refs[10:]
     y = pos[1]
     half = w_hbm.shape[3]
     skip = near.shape[1] - HEAD
@@ -163,8 +170,8 @@
         for h in (0, 1):
             cols = slice(h * half, (h + 1) * half)
             moves.append((near.at[2 * j + h, skip : skip + HEAD, :], w_all.at[j, :, cols]))
-    for k in range(1, N):
-        moves.append((passed[k - 1], w_all.at[k * N : (k + 1) * N]))
+    moves.append((pass1, w_all.at[N : 2 * N]))
+    moves.append((pass3, w_all.at[3 * N :]))
     for k in range(N):
         moves.append((pieces[k], held.at[lax.rem(y - k + N, N)]))
     units = up.shape[1]
@@ -172,7 +179,15 @@
         cols = slice(h * half, (h + 1) * half)
         moves.append((w_hbm.at[:, h, :units, :], up.at[:, :, cols]))
         moves.append((w_hbm.at[:, h, units:, :], down.at[:, :, cols]))
-    copy_all(moves, sems)
+    for core in (0, 1):
+        low = slice(core * half, (core + 1) * half)
+        high = slice((1 - core) * half, (2 - core) * half)
+        rows = slice(2 * N, 3 * N)
+
+        @pl.when(pos[3] == core)
+        def _(low=low, high=high, rows=rows):
+            pair = [(mine, w_all.at[rows, :, low]), (other, w_all.at[rows, :, high])]
+            copy_all(moves + pair, sems)
 
 
 def fetch_merge_kernel(w_hbm, w, sems):
@@ -334,15 +349,18 @@
     near, h1, work, id_col, select, tail = lax.optimization_barrier(
         (near, h1, work, id_col, select, tail)
     )
-    *qkv, mine = pl.pallas_call(
+    *qkv, mine, mine_half = pl.pallas_call(
         qkv_kernel,
         out_shape=[jax.ShapeDtypeStruct((3 * HEAD, total_rows), BF)] * N
-        + [jax.ShapeDtypeStruct((N, HEAD, width), BF)],
+        + [
+            jax.ShapeDtypeStruct((N, HEAD, width), BF),
+            jax.ShapeDtypeStruct((N, HEAD, half), BF),
+        ],
         in_specs=[SMEM, VMEM, HBM],
-        out_specs=[VMEM] * (N + 1),
+        out_specs=[VMEM] * (N + 2),
         scratch_shapes=[
             pltpu.VMEM((2 * N, 3 * HEAD, half), BF),
-            pltpu.SemaphoreType.DMA((3 * N,)),
+            pltpu.SemaphoreType.DMA((4 * N,)),
         ],
         compiler_params=params(16),
         name="qkv",
@@ -350,8 +368,8 @@
     blocks = [qkv[0]] + [shift(qkv[k], "x", -k) for k in (1, 2, 3)]
     pass1 = shift(mine, "y", 1)
     pass3 = shift(mine, "y", 3)
-    blocks, mine = lax.optimization_barrier((blocks, mine))
-    pass2 = shift(mine, "y", 2)
+    blocks, mine_half = lax.optimization_barrier((blocks, mine_half))
+    pass2 = shift(mine_half, "y", 2)
 
     attended = pl.pallas_call(
         attend_kernel,
@@ -368,8 +386,10 @@
         compiler_params=params(16),
         name="attend",
     )(pos, work, *blocks, id_row, id_col)
+    attended, pass2 = lax.optimization_barrier((attended, pass2))
+    swap2 = swap(pass2)
     heads = [attended[0]] + [shift(attended[k], "x", k) for k in (1, 2, 3)]
-    heads, pass1, pass2, pass3 = lax.optimization_barrier((heads, pass1, pass2, pass3))
+    heads, pass1, pass3 = lax.optimization_barrier((heads, pass1, pass3))
     heads = pl.pallas_call(
         pack_kernel,
         out_shape=jax.ShapeDtypeStruct((N, HEAD, total_rows), BF),
@@ -389,15 +409,15 @@
             jax.ShapeDtypeStruct((N * N, units, width), BF),
             jax.ShapeDtypeStruct((N, count, width), BF),
         ],
-        in_specs=[SMEM] + [HBM] * 9,
+        in_specs=[SMEM] + [HBM] * 10,
         out_specs=[VMEM] * 4,
-        scratch_shapes=[pltpu.SemaphoreType.DMA((19,))],
+        scratch_shapes=[pltpu.SemaphoreType.DMA((20,))],
         compiler_params=params(4),
         name="fetch",
     )(
         pos,
         *[far(v) for v in pieces],
-        *[far(v) for v in (near, w_near, pass1, pass2, pass3)],
+        *[far(v) for v in (near, w_near, pass1, pass3, pass2, swap2)],
     )
 
     w_merge = pl.pallas_call(

time: 154 us -> 154 us (level)
  waiting for transfers between devices: 59.3 us -> 52.6 us
  starting transfers between devices: 21.8 us -> 26.7 us
    ppermute x18, starting transfers between devices: 21.8 us -> 26.6 us  [shift(): return lax.ppermute(value, axis, pairs)]
    ppermute x18, waiting for transfers between devices: 50.2 us -> 46.1 us  [shift(): return lax.ppermute(value, axis, pairs)]
    all_gather x1, waiting for transfers between devices: 3.74 us -> 1.24 us  [local(): w_near = lax.all_gather(packed, ('x', 'z', 'c'), axis=0, tiled=False)]
  transfers between devices with their start and end apart: 20 -> 21, of which waited for: 13 -> 14; matrix products, arithmetic and copies ran while one was open for 6% -> 6% of each run, Pallas kernels for 18% -> 18%
where the time goes in v10:
time: 154 us; the launch traced here: 153 us
  waiting for transfers between devices  52.6 us (34%)
  Pallas kernels  33.9 us (22%)
  starting transfers between devices  26.7 us (17%)
  between operations  13.6 us (9%)
  blocking collectives  13 us (8%)
  other arithmetic  6.99 us (5%)
  local copies, waits for them, and re-layouts  5.43 us (4%)
    ppermute x18, waiting for transfers between devices, shift(): return lax.ppermute(value, axis, pairs)  46.1 us
    ppermute x18, starting transfers between devices, shift(): return lax.ppermute(value, axis, pairs)  26.6 us
    all_to_all x1, blocking collectives, local(): lax.all_to_all(outgoing.reshape(req_count, slot_cap, width + 128), ('x',...  13 us
    pallas_call x2, Pallas kernels, mlp(): pl.pallas_call(functools.partial(mlp_kernel, offsets), out_shape=[jax.Sha...  7.78 us
    pallas_call x1, Pallas kernels, local(): pl.pallas_call(attend_kernel, out_shape=[jax.ShapeDtypeStruct((HEAD, tota...  5.59 us
    all_gather x1, waiting for transfers between devices, local(): near = lax.all_gather(w_half, ('x', 'c'), axis=0, tiled=False)  5.26 us
    pallas_call x1, Pallas kernels, local(): pl.pallas_call(qkv_kernel, out_shape=[jax.ShapeDtypeStruct((3 * HEAD, tot...  5.07 us
    pallas_call x1, Pallas kernels, local(): pl.pallas_call(fetch_kernel, out_shape=[jax.ShapeDtypeStruct((N * N, HEAD...  5 us
  transfers between devices with their start and end apart: 21, of which 14 were waited for; matrix products, arithmetic and copies ran while one was open for 6% of the time, Pallas kernels for 18%

profile of v10, /device:TPU:0, one launch (start us, length us, event | category | flops | bytes accessed | tf_op | source)
XLA Modules:
  0.0 153.3 jit_solution(8329289768448760845)
XLA Ops:
  6.5 1.9 %fusion.1 = bf16[320,640]{1,0:T(8,128)(2,1)} fusion(s32[]{:T(128)S(6)} %select_n.83, bf16[240,1280]{1,0:T(8,128)(2,1)} %bitcast.55, bf16[80,1280]{1,0:T(8,128)(2,1)} %param.15), kind=kLoop, calls=%fused_computation.5 | loop fusion | flops 819200 | bytes 1228804 | tf_op jit(solution)/shard_map/concatenate | solution.py:274
  8.5 0.9 dynamic_slice.11
  9.4 0.7 pad_maximum_fusion
  10.2 3.2 %collective-permute-start.2 = (bf16[128,1280]{1,0:T(8,128)(2,1)}, bf16[128,1280]{1,0:T(8,128)(2,1)S(1)}, u32[]{:S(2)}, u32[]{:S(2)}) collective-permute-start(bf16[128,1280]{1,0:T(8,128)(2,1)} %bitcast.50), channel_id=1, source_target_pairs={{0,24},{8,0},{16,8},{24,16},{1,25},{9,1},{17,9},{25,17},{2,26},{10... | collective-permute-start | bytes 983048 | tf_op jit(solution)/shard_map/ppermute | solution.py:36
  13.3 0.6 collective-permute-start.1
  14.0 1.0 collective-permute-start
  14.9 0.7 broadcast_in_dim.118.gain
  15.6 0.5 broadcast.242
  16.2 1.4 reduce.5
  17.5 0.2 fusion.2
  17.7 0.2 and_reduce_fusion
  17.9 0.2 select_reduce_fusion.3
  18.0 0.1 select_reduce_fusion.2
  18.2 0.6 slice.9
  19.1 0.6 stack.30
  19.7 0.7 compare_select_fusion
  20.4 0.7 fusion.14
  21.1 0.2 convert_reduce_fusion
  21.3 0.1 select_reduce_fusion
  21.6 6.1 %collective-permute-done.2.p3.refs_3_ = bf16[128,1280]{1,0:T(8,128)(2,1)S(1)} collective-permute-done((bf16[128,1280]{1,0:T(8,128)(2,1)}, bf16[128,1280]{1,0:T(8,128)(2,1)S(1)}, u32[]{:S(2)}, u32[]{:S(2)}) %collective-permute-start.2) | collective-permute-done | bytes 327712 | tf_op jit(solution)/shard_map/ppermute | solution.py:36
  27.6 3.6 %collective-permute-done.p1.refs_1_ = bf16[128,1280]{1,0:T(8,128)(2,1)S(1)} collective-permute-done((bf16[128,1280]{1,0:T(8,128)(2,1)}, bf16[128,1280]{1,0:T(8,128)(2,1)S(1)}, u32[]{:S(2)}, u32[]{:S(2)}) %collective-permute-start) | collective-permute-done | bytes 327712 | tf_op jit(solution)/shard_map/ppermute | solution.py:36
  31.2 0.7 copy-done.4
  32.0 2.6 %norm.1.h1 = bf16[2,512,640]{2,1,0:T(8,128)(2,1)S(1)} custom-call(s32[4]{0:T(128)S(1)} %pad_add_fusion.pos, bf16[128,1280]{1,0:T(8,128)(2,1)} %bitcast.53, bf16[128,1280]{1,0:T(8,128)(2,1)} %copy-done.4, bf16[128,1280]{1,0:T(8,128)(2,1)} %copy-done.3, bf16[128,1280]{1,0:T(8,128)(2,1)} %copy-done.2, f32[1,1280]{1,0:T(1,128)S(1)} %broadcast_in_dim.118.gain), custom_call_target="tpu_custom_call" | custom-call | tf_op jit(solution)/shard_map/norm/pallas_call | solution.py:293
  34.6 5.3 %all-gather.5.cloned.1.call-done = bf16[2560,640]{1,0:T(8,128)(2,1)} async-done(((bf16[320,640]{1,0:T(8,128)(2,1)}), bf16[2560,640]{1,0:T(8,128)(2,1)}) %all-gather.5.cloned.1.call-update) | async-done | bytes 3276816 | tf_op jit(solution)/shard_map/all_gather | solution.py:276
  39.9 5.1 %qkv.1 = (bf16[240,512]{1,0:T(8,128)(2,1)S(1)}, bf16[240,512]{1,0:T(8,128)(2,1)S(1)}, bf16[240,512]{1,0:T(8,128)(2,1)S(1)}, bf16[240,512]{1,0:T(8,128)(2,1)S(1)}...) custom-call(s32[4]{0:T(128)S(1)} %pad_add_fusion.pos, bf16[2,512,640]{2,1,0:T(8,128)(2,1)S(1)} %norm.1.h1, ...), custom_call_target="tpu_custom_call" | custom-call | tf_op jit(solution)/shard_map/qkv/pallas_call | solution.py:352
  44.9 1.5 collective-permute-start.3
  46.4 1.0 collective-permute-start.4
  47.5 0.6 collective-permute-start.5
  48.0 2.8 %collective-permute-start.11 = (bf16[4,80,1280]{2,1,0:T(8,128)(2,1)}, bf16[4,80,1280]{2,1,0:T(8,128)(2,1)}, u32[]{:S(2)}, u32[]{:S(2)}) collective-permute-start(bf16[4,80,1280]{2,1,0:T(8,128)(2,1)} %get-tuple-element.76), channel_id=1, source_target_pairs={{0,24},{8,0},{16,8},{24,16},{1,25},{9,1},{17,9},{25,17},{2,26},{10... | collective-permute-start | bytes 2457608 | tf_op jit(solution)/shard_map/ppermute | solution.py:36
  50.8 3.0 %collective-permute-done.3.r1 = bf16[240,512]{1,0:T(8,128)(2,1)S(1)} collective-permute-done((bf16[240,512]{1,0:T(8,128)(2,1)S(1)}, bf16[240,512]{1,0:T(8,128)(2,1)S(1)}, u32[]{:S(2)}, u32[]{:S(2)}) %collective-permute-start.3) | collective-permute-done | bytes 245792 | tf_op jit(solution)/shard_map/ppermute | solution.py:36
  53.8 3.7 %collective-permute-done.4.r2 = bf16[240,512]{1,0:T(8,128)(2,1)S(1)} collective-permute-done((bf16[240,512]{1,0:T(8,128)(2,1)S(1)}, bf16[240,512]{1,0:T(8,128)(2,1)S(1)}, u32[]{:S(2)}, u32[]{:S(2)}) %collective-permute-start.4) | collective-permute-done | bytes 245792 | tf_op jit(solution)/shard_map/ppermute | solution.py:36
  57.4 6.1 %collective-permute-done.5.r3 = bf16[240,512]{1,0:T(8,128)(2,1)S(1)} collective-permute-done((bf16[240,512]{1,0:T(8,128)(2,1)S(1)}, bf16[240,512]{1,0:T(8,128)(2,1)S(1)}, u32[]{:S(2)}, u32[]{:S(2)}) %collective-permute-start.5) | collective-permute-done | bytes 245792 | tf_op jit(solution)/shard_map/ppermute | solution.py:36
  63.5 3.0 %collective-permute-start.6 = (bf16[4,80,640]{2,1,0:T(8,128)(2,1)S(1)}, bf16[4,80,640]{2,1,0:T(8,128)(2,1)}, u32[]{:S(2)}, u32[]{:S(2)}) collective-permute-start(bf16[4,80,640]{2,1,0:T(8,128)(2,1)S(1)} %get-tuple-element.71), channel_id=1, source_target_pairs={{0,16},{8,24},{16,0},{24,8},{1,17},{9,25},{17,1},{25,9},{2,18},{10... | collective-permute-start | bytes 1228808 | tf_op jit(solution)/shard_map/ppermute | solution.py:36
  66.5 0.4 copy.15.id_col
  66.8 5.6 %attend.1 = (bf16[80,512]{1,0:T(8,128)(2,1)S(1)}, bf16[80,512]{1,0:T(8,128)(2,1)S(1)}, bf16[80,512]{1,0:T(8,128)(2,1)S(1)}, bf16[80,512]{1,0:T(8,128)(2,1)S(1)}) custom-call(s32[4]{0:T(128)S(1)} %pad_add_fusion.pos, s32[5,16]{1,0:T(8,128)S(1)} %stack.31.work, bf16[240,512]{1,0:T(8,128)(2,1)S(1)} %get-tuple-element.62.r0, ...), custom_call_target="tpu_custom_call" | custom-call | tf_op jit(solution)/shard_map/attend/pallas_call | solution.py:374
  72.4 7.2 %collective-permute-done.6.refs_8_ = bf16[4,80,640]{2,1,0:T(8,128)(2,1)} collective-permute-done((bf16[4,80,640]{2,1,0:T(8,128)(2,1)S(1)}, bf16[4,80,640]{2,1,0:T(8,128)(2,1)}, u32[]{:S(2)}, u32[]{:S(2)}) %collective-permute-start.6) | collective-permute-done | bytes 409632 | tf_op jit(solution)/shard_map/ppermute | solution.py:36
  79.6 1.7 %collective-permute-start.7 = (bf16[80,512]{1,0:T(8,128)(2,1)S(1)}, bf16[80,512]{1,0:T(8,128)(2,1)S(1)}, u32[]{:S(2)}, u32[]{:S(2)}) collective-permute-start(bf16[80,512]{1,0:T(8,128)(2,1)S(1)} %get-tuple-element.73), channel_id=1, source_target_pairs={{0,32},{32,64},{64,96},{96,0},{1,33},{33,65},{65,97},{97,1},{2,34}... | collective-permute-start | bytes 245768 | tf_op jit(solution)/shard_map/ppermute | solution.py:36
  81.3 2.4 %collective-permute-start.8 = (bf16[80,512]{1,0:T(8,128)(2,1)S(1)}, bf16[80,512]{1,0:T(8,128)(2,1)S(1)}, u32[]{:S(2)}, u32[]{:S(2)}) collective-permute-start(bf16[80,512]{1,0:T(8,128)(2,1)S(1)} %get-tuple-element.74), channel_id=1, source_target_pairs={{0,64},{32,96},{64,0},{96,32},{1,65},{33,97},{65,1},{97,33},{2,66}... | collective-permute-start | bytes 245768 | tf_op jit(solution)/shard_map/ppermute | solution.py:36
  83.7 1.7 %collective-permute-start.9 = (bf16[80,512]{1,0:T(8,128)(2,1)S(1)}, bf16[80,512]{1,0:T(8,128)(2,1)S(1)}, u32[]{:S(2)}, u32[]{:S(2)}) collective-permute-start(bf16[80,512]{1,0:T(8,128)(2,1)S(1)} %get-tuple-element.75), channel_id=1, source_target_pairs={{0,96},{32,0},{64,32},{96,64},{1,97},{33,1},{65,33},{97,65},{2,98}... | collective-permute-start | bytes 245768 | tf_op jit(solution)/shard_map/ppermute | solution.py:36
  85.4 2.2 %collective-permute-done.7.g1 = bf16[80,512]{1,0:T(8,128)(2,1)S(1)} collective-permute-done((bf16[80,512]{1,0:T(8,128)(2,1)S(1)}, bf16[80,512]{1,0:T(8,128)(2,1)S(1)}, u32[]{:S(2)}, u32[]{:S(2)}) %collective-permute-start.7) | collective-permute-done | bytes 81952 | tf_op jit(solution)/shard_map/ppermute | solution.py:36
  87.6 3.4 %collective-permute-done.8.g2 = bf16[80,512]{1,0:T(8,128)(2,1)S(1)} collective-permute-done((bf16[80,512]{1,0:T(8,128)(2,1)S(1)}, bf16[80,512]{1,0:T(8,128)(2,1)S(1)}, u32[]{:S(2)}, u32[]{:S(2)}) %collective-permute-start.8) | collective-permute-done | bytes 81952 | tf_op jit(solution)/shard_map/ppermute | solution.py:36
  91.0 0.1 collective-permute-done.9.g3
  91.2 0.6 pack.1.refs_0_
  91.8 0.2 collective-permute-start.14
  92.0 1.5 collective-permute-start.13
  93.5 1.1 collective-permute-start.12
  94.6 1.2 all-gather.7.cloned.1.call-done
  95.8 4.8 %fetch_merge.1.w = bf16[5120,1280]{1,0:T(8,128)(2,1)S(1)} custom-call(bf16[5120,1280]{1,0:T(8,128)(2,1)} %w_hbm), custom_call_target="tpu_custom_call" | custom-call | tf_op jit(solution)/shard_map/fetch_merge/pallas_call | solution.py:423
  100.7 0.8 copy-done.5
  101.4 5.0 %fetch.1 = (bf16[16,80,1280]{2,1,0:T(8,128)(2,1)S(1)}, bf16[16,80,1280]{2,1,0:T(8,128)(2,1)S(1)}, bf16[16,80,1280]{2,1,0:T(8,128)(2,1)S(1)}, bf16[4,128,1280]{2,1,0:T(8,128)(2,1)S(1)}) custom-call(s32[4]{0:T(128)S(1)} %pad_add_fusion.pos, bf16[128,1280]{1,0:T(8,128)(2,1)} %bitcast.54, bf16[128,1280]{1,0:T(8,128)(2,1)} %copy-done.4, ...), custom_call_target="tpu_custom_call" | custom-call | tf_op jit(solution)/shard_map/fetch/pallas_call | solution.py:404
  106.5 1.0 collective-permute-done.12.refs_1_
  107.4 3.9 %mlp_first.1 = (bf16[128,1280]{1,0:T(8,128)(2,1)S(1)}, bf16[128,1280]{1,0:T(8,128)(2,1)S(1)}) custom-call(s32[4]{0:T(128)S(1)} %pad_add_fusion.pos, bf16[4,80,512]{2,1,0:T(8,128)(2,1)S(1)} %pack.1.refs_0_, bf16[4,80,512]{2,1,0:T(8,128)(2,1)S(1)} %collective-permute-done.12.refs_1_, bf16[4,80,512]{2,1,0:T(8,128)(2,1)S(1)} %collective-permute-done.13.refs_2_, ...), custom_call_target="tpu_custom_call" | custom-call | flops 2516582400 | bytes 9830400 | tf_op jit(solution)/shard_map/mlp_first/pallas_call | solution.py:435
  111.3 0.3 collective-permute-start.16
  111.6 3.0 %collective-permute-start.17 = (bf16[128,1280]{1,0:T(8,128)(2,1)S(1)}, bf16[128,1280]{1,0:T(8,128)(2,1)S(1)}, u32[]{:S(2)}, u32[]{:S(2)}) collective-permute-start(bf16[128,1280]{1,0:T(8,128)(2,1)S(1)} %get-tuple-element.98), channel_id=1, source_target_pairs={{0,16},{8,24},{16,0},{24,8},{1,17},{9,25},{17,1},{25,9},{2,18},{10... | collective-permute-start | bytes 983048 | tf_op jit(solution)/shard_map/ppermute | solution.py:36
  114.6 3.9 %mlp_second.1 = (bf16[128,1280]{1,0:T(8,128)(2,1)S(1)}, bf16[128,1280]{1,0:T(8,128)(2,1)S(1)}, bf16[128,1280]{1,0:T(8,128)(2,1)S(1)}) custom-call(s32[4]{0:T(128)S(1)} %pad_add_fusion.pos, bf16[4,80,512]{2,1,0:T(8,128)(2,1)S(1)} %pack.1.refs_0_, bf16[4,80,512]{2,1,0:T(8,128)(2,1)S(1)} %collective-permute-done.12.refs_1_, ...), custom_call_target="tpu_custom_call" | custom-call | flops 2516582400 | bytes 9830400 | tf_op jit(solution)/shard_map/mlp_second/pallas_call | solution.py:435
  118.5 1.2 collective-permute-start.18
  119.7 1.8 %collective-permute-done.16 = bf16[128,1280]{1,0:T(8,128)(2,1)S(1)} collective-permute-done((bf16[128,1280]{1,0:T(8,128)(2,1)S(1)}, bf16[128,1280]{1,0:T(8,128)(2,1)S(1)}, u32[]{:S(2)}, u32[]{:S(2)}) %collective-permute-start.16) | collective-permute-done | bytes 327712 | tf_op jit(solution)/shard_map/ppermute | solution.py:36
  121.5 8.0 %collective-permute-done.17 = bf16[128,1280]{1,0:T(8,128)(2,1)S(1)} collective-permute-done((bf16[128,1280]{1,0:T(8,128)(2,1)S(1)}, bf16[128,1280]{1,0:T(8,128)(2,1)S(1)}, u32[]{:S(2)}, u32[]{:S(2)}) %collective-permute-start.17) | collective-permute-done | bytes 327712 | tf_op jit(solution)/shard_map/ppermute | solution.py:36
  129.5 0.2 add_add_fusion.early
  129.7 2.4 %merge.1 = bf16[32,1408]{1,0:T(8,128)(2,1)S(1)} custom-call(f32[128,1280]{1,0:T(8,128)S(1)} %add_add_fusion.early, bf16[128,1280]{1,0:T(8,128)(2,1)S(1)} %collective-permute-done.18.late, bf16[5120,1280]{1,0:T(8,128)(2,1)S(1)} %fetch_merge.1.w, bf16[32,32]{1,0:T(8,128)(2,1)S(1)} %fusion.5.select, bf16[32,128]{1,0:T(8,128)(2,1)S(1)} %select_convert_fusion.tail), custom_call_target="tpu_custom_call" | custom-call | tf_op jit(solution)/shard_map/merge/pallas_call | solution.py:456
  132.1 13.0 %all_to_all.5 = bf16[16,2,1408]{2,1,0:T(2,128)(2,1)S(1)} all-to-all(bf16[16,2,1408]{2,1,0:T(2,128)(2,1)S(1)} %reshape.166), channel_id=1, replica_groups=mesh['x'=4,'y'=4,'z'=4,'c'=2] {'x','y'}, dimensions={0} | all-to-all | bytes 180224 | tf_op jit(solution)/shard_map/all_to_all | solution.py:465
  145.1 0.1 add_reduce_fusion
  145.2 0.1 fusion.4
  145.4 1.1 fusion
  (47 shorter events, 0.8 us)
Async XLA Ops:
  6.5 2.9 %copy-start = (bf16[1280,320]{0,1:T(8,128)(2,1)S(1)}, bf16[1280,320]{0,1:T(8,128)(2,1)}, u32[]{:S(2)}) copy-start(bf16[1280,320]{0,1:T(8,128)(2,1)} %param.17) | copy-start | bytes 2457604
  6.5 33.3 %all-gather.5.cloned.1.call-start = ((), (), s32[]{:S(2)}) async-start(), calls=%async_computation.1 | async-start | bytes 3686400 | tf_op jit(solution)/shard_map/all_gather | solution.py:276
  8.4 87.4 %all-gather.7.cloned.1.call-start = ((), (), s32[]{:S(2)}) async-start(), calls=%async_computation.2 | async-start | bytes 6758400 | tf_op jit(solution)/shard_map/all_gather | solution.py:288
  10.2 17.5 %collective-permute-start.2 = (bf16[128,1280]{1,0:T(8,128)(2,1)}, bf16[128,1280]{1,0:T(8,128)(2,1)S(1)}, u32[]{:S(2)}, u32[]{:S(2)}) collective-permute-start(bf16[128,1280]{1,0:T(8,128)(2,1)} %bitcast.50), channel_id=1, source_target_pairs={{0,24},{8,0},{16,8},{24,16},{1,25},{9,1},{17,9},{25,17},{2,26},{10... | collective-permute-start | bytes 983048 | tf_op jit(solution)/shard_map/ppermute | solution.py:36
  13.3 14.3 %collective-permute-start.1 = (bf16[128,1280]{1,0:T(8,128)(2,1)}, bf16[128,1280]{1,0:T(8,128)(2,1)S(1)}, u32[]{:S(2)}, u32[]{:S(2)}) collective-permute-start(bf16[128,1280]{1,0:T(8,128)(2,1)} %bitcast.51), channel_id=1, source_target_pairs={{0,16},{8,24},{16,0},{24,8},{1,17},{9,25},{17,1},{25,9},{2,18},{10... | collective-permute-start | bytes 983048 | tf_op jit(solution)/shard_map/ppermute | solution.py:36
  14.0 17.3 %collective-permute-start = (bf16[128,1280]{1,0:T(8,128)(2,1)}, bf16[128,1280]{1,0:T(8,128)(2,1)S(1)}, u32[]{:S(2)}, u32[]{:S(2)}) collective-permute-start(bf16[128,1280]{1,0:T(8,128)(2,1)} %bitcast.52), channel_id=1, source_target_pairs={{0,8},{8,16},{16,24},{24,0},{1,9},{9,17},{17,25},{25,1},{2,10},{10... | collective-permute-start | bytes 983048 | tf_op jit(solution)/shard_map/ppermute | solution.py:36
  21.6 44.9 %copy-start.1 = (s32[1,2048]{1,0:T(1,128)S(1)}, s32[1,2048]{1,0:T(1,128)}, u32[]{:S(2)}) copy-start(s32[1,2048]{1,0:T(1,128)} %param.12) | copy-start | bytes 24580
  27.6 3.6 %copy-start.2 = (bf16[128,1280]{1,0:T(8,128)(2,1)}, bf16[128,1280]{1,0:T(8,128)(2,1)S(1)}, u32[]{:S(2)}) copy-start(bf16[128,1280]{1,0:T(8,128)(2,1)S(1)} %collective-permute-done.2.p3.refs_3_) | copy-start | bytes 983044
  27.6 3.6 %copy-start.3 = (bf16[128,1280]{1,0:T(8,128)(2,1)}, bf16[128,1280]{1,0:T(8,128)(2,1)S(1)}, u32[]{:S(2)}) copy-start(bf16[128,1280]{1,0:T(8,128)(2,1)S(1)} %collective-permute-done.1.p2.refs_2_) | copy-start | bytes 983044
  31.2 0.7 copy-start.4
  39.9 54.7 %copy-start.7 = (f32[1280]{0:T(1024)S(1)}, f32[1280]{0:T(1024)}, u32[]{:S(2)}) copy-start(f32[1280]{0:T(1024)} %param.16) | copy-start | bytes 15364
  44.9 8.9 %collective-permute-start.3 = (bf16[240,512]{1,0:T(8,128)(2,1)S(1)}, bf16[240,512]{1,0:T(8,128)(2,1)S(1)}, u32[]{:S(2)}, u32[]{:S(2)}) collective-permute-start(bf16[240,512]{1,0:T(8,128)(2,1)S(1)} %get-tuple-element.58), channel_id=1, source_target_pairs={{0,96},{32,0},{64,32},{96,64},{1,97},{33,1},{65,33},{97,65},{2,98}... | collective-permute-start | bytes 737288 | tf_op jit(solution)/shard_map/ppermute | solution.py:36
  46.4 11.0 %collective-permute-start.4 = (bf16[240,512]{1,0:T(8,128)(2,1)S(1)}, bf16[240,512]{1,0:T(8,128)(2,1)S(1)}, u32[]{:S(2)}, u32[]{:S(2)}) collective-permute-start(bf16[240,512]{1,0:T(8,128)(2,1)S(1)} %get-tuple-element.59), channel_id=1, source_target_pairs={{0,64},{32,96},{64,0},{96,32},{1,65},{33,97},{65,1},{97,33},{2,66}... | collective-permute-start | bytes 737288 | tf_op jit(solution)/shard_map/ppermute | solution.py:36
  47.5 16.0 %collective-permute-start.5 = (bf16[240,512]{1,0:T(8,128)(2,1)S(1)}, bf16[240,512]{1,0:T(8,128)(2,1)S(1)}, u32[]{:S(2)}, u32[]{:S(2)}) collective-permute-start(bf16[240,512]{1,0:T(8,128)(2,1)S(1)} %get-tuple-element.60), channel_id=1, source_target_pairs={{0,32},{32,64},{64,96},{96,0},{1,33},{33,65},{65,97},{97,1},{2,34}... | collective-permute-start | bytes 737288 | tf_op jit(solution)/shard_map/ppermute | solution.py:36
  48.0 43.1 %collective-permute-start.11 = (bf16[4,80,1280]{2,1,0:T(8,128)(2,1)}, bf16[4,80,1280]{2,1,0:T(8,128)(2,1)}, u32[]{:S(2)}, u32[]{:S(2)}) collective-permute-start(bf16[4,80,1280]{2,1,0:T(8,128)(2,1)} %get-tuple-element.76), channel_id=1, source_target_pairs={{0,24},{8,0},{16,8},{24,16},{1,25},{9,1},{17,9},{25,17},{2,26},{10... | collective-permute-start | bytes 2457608 | tf_op jit(solution)/shard_map/ppermute | solution.py:36
  50.8 40.4 %collective-permute-start.10 = (bf16[4,80,1280]{2,1,0:T(8,128)(2,1)}, bf16[4,80,1280]{2,1,0:T(8,128)(2,1)}, u32[]{:S(2)}, u32[]{:S(2)}) collective-permute-start(bf16[4,80,1280]{2,1,0:T(8,128)(2,1)} %get-tuple-element.76), channel_id=1, source_target_pairs={{0,8},{8,16},{16,24},{24,0},{1,9},{9,17},{17,25},{25,1},{2,10},{10... | collective-permute-start | bytes 2457608 | tf_op jit(solution)/shard_map/ppermute | solution.py:36
  63.5 16.1 %collective-permute-start.6 = (bf16[4,80,640]{2,1,0:T(8,128)(2,1)S(1)}, bf16[4,80,640]{2,1,0:T(8,128)(2,1)}, u32[]{:S(2)}, u32[]{:S(2)}) collective-permute-start(bf16[4,80,640]{2,1,0:T(8,128)(2,1)S(1)} %get-tuple-element.71), channel_id=1, source_target_pairs={{0,16},{8,24},{16,0},{24,8},{1,17},{9,25},{17,1},{25,9},{2,18},{10... | collective-permute-start | bytes 1228808 | tf_op jit(solution)/shard_map/ppermute | solution.py:36
  79.6 8.0 %collective-permute-start.7 = (bf16[80,512]{1,0:T(8,128)(2,1)S(1)}, bf16[80,512]{1,0:T(8,128)(2,1)S(1)}, u32[]{:S(2)}, u32[]{:S(2)}) collective-permute-start(bf16[80,512]{1,0:T(8,128)(2,1)S(1)} %get-tuple-element.73), channel_id=1, source_target_pairs={{0,32},{32,64},{64,96},{96,0},{1,33},{33,65},{65,97},{97,1},{2,34}... | collective-permute-start | bytes 245768 | tf_op jit(solution)/shard_map/ppermute | solution.py:36
  81.3 9.7 %collective-permute-start.8 = (bf16[80,512]{1,0:T(8,128)(2,1)S(1)}, bf16[80,512]{1,0:T(8,128)(2,1)S(1)}, u32[]{:S(2)}, u32[]{:S(2)}) collective-permute-start(bf16[80,512]{1,0:T(8,128)(2,1)S(1)} %get-tuple-element.74), channel_id=1, source_target_pairs={{0,64},{32,96},{64,0},{96,32},{1,65},{33,97},{65,1},{97,33},{2,66}... | collective-permute-start | bytes 245768 | tf_op jit(solution)/shard_map/ppermute | solution.py:36
  83.7 7.5 %collective-permute-start.9 = (bf16[80,512]{1,0:T(8,128)(2,1)S(1)}, bf16[80,512]{1,0:T(8,128)(2,1)S(1)}, u32[]{:S(2)}, u32[]{:S(2)}) collective-permute-start(bf16[80,512]{1,0:T(8,128)(2,1)S(1)} %get-tuple-element.75), channel_id=1, source_target_pairs={{0,96},{32,0},{64,32},{96,64},{1,97},{33,1},{65,33},{97,65},{2,98}... | collective-permute-start | bytes 245768 | tf_op jit(solution)/shard_map/ppermute | solution.py:36
  87.6 13.0 %collective-permute-start.15 = (bf16[4,80,640]{2,1,0:T(8,128)(2,1)}, bf16[4,80,640]{2,1,0:T(8,128)(2,1)S(1)}, u32[]{:S(2)}, u32[]{:S(2)}) collective-permute-start(bf16[4,80,640]{2,1,0:T(8,128)(2,1)} %collective-permute-done.6.refs_8_), channel_id=1, source_target_pairs={{0,1},{1,0},{2,3},{3,2},{4,5},{5,4},{6,7},{7,6},{8,9},{9,8},{10,11... | collective-permute-start | bytes 1228808 | tf_op jit(solution)/shard_map/ppermute | solution.py:44
  91.8 14.7 %collective-permute-start.14 = (bf16[4,80,512]{2,1,0:T(8,128)(2,1)S(1)}, bf16[4,80,512]{2,1,0:T(8,128)(2,1)S(1)}, u32[]{:S(2)}, u32[]{:S(2)}) collective-permute-start(bf16[4,80,512]{2,1,0:T(8,128)(2,1)S(1)} %pack.1.refs_0_), channel_id=1, source_target_pairs={{0,24},{8,0},{16,8},{24,16},{1,25},{9,1},{17,9},{25,17},{2,26},{10... | collective-permute-start | bytes 983048 | tf_op jit(solution)/shard_map/ppermute | solution.py:36
  92.0 14.5 %collective-permute-start.13 = (bf16[4,80,512]{2,1,0:T(8,128)(2,1)S(1)}, bf16[4,80,512]{2,1,0:T(8,128)(2,1)S(1)}, u32[]{:S(2)}, u32[]{:S(2)}) collective-permute-start(bf16[4,80,512]{2,1,0:T(8,128)(2,1)S(1)} %pack.1.refs_0_), channel_id=1, source_target_pairs={{0,16},{8,24},{16,0},{24,8},{1,17},{9,25},{17,1},{25,9},{2,18},{10... | collective-permute-start | bytes 983048 | tf_op jit(solution)/shard_map/ppermute | solution.py:36
  93.5 14.0 %collective-permute-start.12 = (bf16[4,80,512]{2,1,0:T(8,128)(2,1)S(1)}, bf16[4,80,512]{2,1,0:T(8,128)(2,1)S(1)}, u32[]{:S(2)}, u32[]{:S(2)}) collective-permute-start(bf16[4,80,512]{2,1,0:T(8,128)(2,1)S(1)} %pack.1.refs_0_), channel_id=1, source_target_pairs={{0,8},{8,16},{16,24},{24,0},{1,9},{9,17},{17,25},{25,1},{2,10},{10... | collective-permute-start | bytes 983048 | tf_op jit(solution)/shard_map/ppermute | solution.py:36
  100.7 0.8 copy-start.5
  111.3 10.2 %collective-permute-start.16 = (bf16[128,1280]{1,0:T(8,128)(2,1)S(1)}, bf16[128,1280]{1,0:T(8,128)(2,1)S(1)}, u32[]{:S(2)}, u32[]{:S(2)}) collective-permute-start(bf16[128,1280]{1,0:T(8,128)(2,1)S(1)} %get-tuple-element.97), channel_id=1, source_target_pairs={{0,8},{8,16},{16,24},{24,0},{1,9},{9,17},{17,25},{25,1},{2,10},{10... | collective-permute-start | bytes 983048 | tf_op jit(solution)/shard_map/ppermute | solution.py:36
  111.6 17.9 %collective-permute-start.17 = (bf16[128,1280]{1,0:T(8,128)(2,1)S(1)}, bf16[128,1280]{1,0:T(8,128)(2,1)S(1)}, u32[]{:S(2)}, u32[]{:S(2)}) collective-permute-start(bf16[128,1280]{1,0:T(8,128)(2,1)S(1)} %get-tuple-element.98), channel_id=1, source_target_pairs={{0,16},{8,24},{16,0},{24,8},{1,17},{9,25},{17,1},{25,9},{2,18},{10... | collective-permute-start | bytes 983048 | tf_op jit(solution)/shard_map/ppermute | solution.py:36
  118.5 11.1 %collective-permute-start.18 = (bf16[128,1280]{1,0:T(8,128)(2,1)S(1)}, bf16[128,1280]{1,0:T(8,128)(2,1)S(1)}, u32[]{:S(2)}, u32[]{:S(2)}) collective-permute-start(bf16[128,1280]{1,0:T(8,128)(2,1)S(1)} %get-tuple-element.99), channel_id=1, source_target_pairs={{0,24},{8,0},{16,8},{24,16},{1,25},{9,1},{17,9},{25,17},{2,26},{10... | collective-permute-start | bytes 983048 | tf_op jit(solution)/shard_map/ppermute | solution.py:36
  129.7 15.7 %copy-start.6 = (bf16[128,1280]{1,0:T(8,128)(2,1)S(1)}, bf16[128,1280]{1,0:T(8,128)(2,1)}, u32[]{:S(2)}) copy-start(bf16[128,1280]{1,0:T(8,128)(2,1)} %param.20) | copy-start | bytes 983044
Sparse Core Ops, SparseCore 0:
  9.0 30.7 all-gather.4
  42.1 53.6 all-gather.6

commit v11 on v10

--- a/solution.py
+++ b/solution.py
@@ -386,9 +386,9 @@
         compiler_params=params(16),
         name="attend",
     )(pos, work, *blocks, id_row, id_col)
-    attended, pass2 = lax.optimization_barrier((attended, pass2))
+    heads = [attended[0]] + [shift(attended[k], "x", k) for k in (1, 2, 3)]
+    heads[1], pass2 = lax.optimization_barrier((heads[1], pass2))
     swap2 = swap(pass2)
-    heads = [attended[0]] + [shift(attended[k], "x", k) for k in (1, 2, 3)]
     heads, pass1, pass3 = lax.optimization_barrier((heads, pass1, pass3))
     heads = pl.pallas_call(
         pack_kernel,
@@ -446,13 +446,13 @@
             name=name,
         )(pos, *gathered, *fetched, ln_mlp[None, :])
 
-    part2, part1 = mlp((2, 1), "mlp_first")
-    gathered[0], w_merge, part2, part1 = lax.optimization_barrier(
-        (gathered[0], w_merge, part2, part1)
-    )
-    part3, part0, resid = mlp((3, 0), "mlp_second")
-    early = shift(part1, "y", 1).astype(F32) + shift(part2, "y", 2).astype(F32)
-    sums = [resid.astype(F32) + part0.astype(F32) + early, shift(part3, "y", 3)]
+    part3, part1 = mlp((3, 1), "mlp_first")
+    gathered[0], w_merge, part3, part1 = lax.optimization_barrier(
+        (gathered[0], w_merge, part3, part1)
+    )
+    part2, part0, resid = mlp((2, 0), "mlp_second")
+    early = shift(part1, "y", 1).astype(F32) + shift(part3, "y", 3).astype(F32)
+    sums = [resid.astype(F32) + part0.astype(F32) + early, shift(part2, "y", 2)]
     outgoing = pl.pallas_call(
         merge_kernel,
         out_shape=jax.ShapeDtypeStruct((req_count * slot_cap, width + 128), BF),

time: 154 us -> 155 us (level)
  waiting for transfers between devices: 52.6 us -> 55.9 us
  starting transfers between devices: 26.7 us -> 23.6 us
    ppermute x18, starting transfers between devices: 26.6 us -> 23.6 us  [shift(): return lax.ppermute(value, axis, pairs)]
    all_gather x1, waiting for transfers between devices: 1.24 us -> 3.07 us  [local(): w_near = lax.all_gather(packed, ('x', 'z', 'c'), axis=0, tiled=False)]
  transfers between devices with their start and end apart: 21 -> 21, of which waited for: 14 -> 12; matrix products, arithmetic and copies ran while one was open for 6% -> 6% of each run, Pallas kernels for 18% -> 18%
where the time goes in v11:
time: 155 us; the launch traced here: 153 us
  waiting for transfers between devices  55.9 us (36%)
  Pallas kernels  33.8 us (22%)
  starting transfers between devices  23.6 us (15%)
  between operations  13.7 us (9%)
  blocking collectives  12.9 us (8%)
  other arithmetic  6.99 us (5%)
  local copies, waits for them, and re-layouts  5.43 us (4%)
    ppermute x18, waiting for transfers between devices, shift(): return lax.ppermute(value, axis, pairs)  47.6 us
    ppermute x18, starting transfers between devices, shift(): return lax.ppermute(value, axis, pairs)  23.6 us
    all_to_all x1, blocking collectives, local(): lax.all_to_all(outgoing.reshape(req_count, slot_cap, width + 128), ('x',...  12.9 us
    pallas_call x2, Pallas kernels, mlp(): pl.pallas_call(functools.partial(mlp_kernel, offsets), out_shape=[jax.Sha...  7.79 us
    pallas_call x1, Pallas kernels, local(): pl.pallas_call(attend_kernel, out_shape=[jax.ShapeDtypeStruct((HEAD, tota...  5.58 us
    all_gather x1, waiting for transfers between devices, local(): near = lax.all_gather(w_half, ('x', 'c'), axis=0, tiled=False)  5.26 us
    pallas_call x1, Pallas kernels, local(): pl.pallas_call(qkv_kernel, out_shape=[jax.ShapeDtypeStruct((3 * HEAD, tot...  5.07 us
    pallas_call x1, Pallas kernels, local(): pl.pallas_call(fetch_kernel, out_shape=[jax.ShapeDtypeStruct((N * N, HEAD...  5 us
  transfers between devices with their start and end apart: 21, of which 12 were waited for; matrix products, arithmetic and copies ran while one was open for 6% of the time, Pallas kernels for 18%

profile of v11, /device:TPU:0, one launch (start us, length us, event | category | flops | bytes accessed | tf_op | source)
XLA Modules:
  0.0 153.4 jit_solution(12242668664640488527)
XLA Ops:
  6.5 1.9 %fusion.1 = bf16[320,640]{1,0:T(8,128)(2,1)} fusion(s32[]{:T(128)S(6)} %select_n.83, bf16[240,1280]{1,0:T(8,128)(2,1)} %bitcast.55, bf16[80,1280]{1,0:T(8,128)(2,1)} %param.15), kind=kLoop, calls=%fused_computation.5 | loop fusion | flops 819200 | bytes 1228804 | tf_op jit(solution)/shard_map/concatenate | solution.py:274
  8.5 0.9 dynamic_slice.11
  9.4 0.7 pad_maximum_fusion
  10.2 3.2 %collective-permute-start.2 = (bf16[128,1280]{1,0:T(8,128)(2,1)}, bf16[128,1280]{1,0:T(8,128)(2,1)S(1)}, u32[]{:S(2)}, u32[]{:S(2)}) collective-permute-start(bf16[128,1280]{1,0:T(8,128)(2,1)} %bitcast.50), channel_id=1, source_target_pairs={{0,24},{8,0},{16,8},{24,16},{1,25},{9,1},{17,9},{25,17},{2,26},{10... | collective-permute-start | bytes 983048 | tf_op jit(solution)/shard_map/ppermute | solution.py:36
  13.3 0.6 collective-permute-start.1
  14.0 1.0 collective-permute-start
  14.9 0.7 broadcast_in_dim.118.gain
  15.6 0.5 broadcast.242
  16.2 1.4 reduce.5
  17.5 0.2 fusion.2
  17.7 0.2 and_reduce_fusion
  17.9 0.2 select_reduce_fusion.3
  18.0 0.1 select_reduce_fusion.2
  18.2 0.6 slice.9
  18.8 0.1 convert_reduce_fusion.1
  18.9 0.1 select_reduce_fusion.1
  18.9 0.1 fusion.11
  19.1 0.6 stack.30
  19.7 0.7 compare_select_fusion
  20.4 0.7 fusion.14
  21.1 0.2 convert_reduce_fusion
  21.3 0.1 select_reduce_fusion
  21.4 0.1 pad_add_fusion.pos
  21.6 6.1 %collective-permute-done.2.p3.refs_3_ = bf16[128,1280]{1,0:T(8,128)(2,1)S(1)} collective-permute-done((bf16[128,1280]{1,0:T(8,128)(2,1)}, bf16[128,1280]{1,0:T(8,128)(2,1)S(1)}, u32[]{:S(2)}, u32[]{:S(2)}) %collective-permute-start.2) | collective-permute-done | bytes 327712 | tf_op jit(solution)/shard_map/ppermute | solution.py:36
  27.6 3.6 %collective-permute-done.p1.refs_1_ = bf16[128,1280]{1,0:T(8,128)(2,1)S(1)} collective-permute-done((bf16[128,1280]{1,0:T(8,128)(2,1)}, bf16[128,1280]{1,0:T(8,128)(2,1)S(1)}, u32[]{:S(2)}, u32[]{:S(2)}) %collective-permute-start) | collective-permute-done | bytes 327712 | tf_op jit(solution)/shard_map/ppermute | solution.py:36
  31.2 0.7 copy-done.4
  32.0 2.6 %norm.1.h1 = bf16[2,512,640]{2,1,0:T(8,128)(2,1)S(1)} custom-call(s32[4]{0:T(128)S(1)} %pad_add_fusion.pos, bf16[128,1280]{1,0:T(8,128)(2,1)} %bitcast.53, bf16[128,1280]{1,0:T(8,128)(2,1)} %copy-done.4, bf16[128,1280]{1,0:T(8,128)(2,1)} %copy-done.3, bf16[128,1280]{1,0:T(8,128)(2,1)} %copy-done.2, f32[1,1280]{1,0:T(1,128)S(1)} %broadcast_in_dim.118.gain), custom_call_target="tpu_custom_call" | custom-call | tf_op jit(solution)/shard_map/norm/pallas_call | solution.py:293
  34.6 5.3 %all-gather.5.cloned.1.call-done = bf16[2560,640]{1,0:T(8,128)(2,1)} async-done(((bf16[320,640]{1,0:T(8,128)(2,1)}), bf16[2560,640]{1,0:T(8,128)(2,1)}) %all-gather.5.cloned.1.call-update) | async-done | bytes 3276816 | tf_op jit(solution)/shard_map/all_gather | solution.py:276
  39.9 5.1 %qkv.1 = (bf16[240,512]{1,0:T(8,128)(2,1)S(1)}, bf16[240,512]{1,0:T(8,128)(2,1)S(1)}, bf16[240,512]{1,0:T(8,128)(2,1)S(1)}, bf16[240,512]{1,0:T(8,128)(2,1)S(1)}...) custom-call(s32[4]{0:T(128)S(1)} %pad_add_fusion.pos, bf16[2,512,640]{2,1,0:T(8,128)(2,1)S(1)} %norm.1.h1, ...), custom_call_target="tpu_custom_call" | custom-call | tf_op jit(solution)/shard_map/qkv/pallas_call | solution.py:352
  44.9 2.8 %collective-permute-start.11 = (bf16[4,80,1280]{2,1,0:T(8,128)(2,1)}, bf16[4,80,1280]{2,1,0:T(8,128)(2,1)}, u32[]{:S(2)}, u32[]{:S(2)}) collective-permute-start(bf16[4,80,1280]{2,1,0:T(8,128)(2,1)} %get-tuple-element.70), channel_id=1, source_target_pairs={{0,24},{8,0},{16,8},{24,16},{1,25},{9,1},{17,9},{25,17},{2,26},{10... | collective-permute-start | bytes 2457608 | tf_op jit(solution)/shard_map/ppermute | solution.py:36
  47.8 1.5 collective-permute-start.3
  49.2 0.9 collective-permute-start.4
  50.2 0.6 collective-permute-start.5
  50.8 6.9 %collective-permute-done.3.r1 = bf16[240,512]{1,0:T(8,128)(2,1)S(1)} collective-permute-done((bf16[240,512]{1,0:T(8,128)(2,1)S(1)}, bf16[240,512]{1,0:T(8,128)(2,1)S(1)}, u32[]{:S(2)}, u32[]{:S(2)}) %collective-permute-start.3) | collective-permute-done | bytes 245792 | tf_op jit(solution)/shard_map/ppermute | solution.py:36
  57.7 3.5 %collective-permute-done.4.r2 = bf16[240,512]{1,0:T(8,128)(2,1)S(1)} collective-permute-done((bf16[240,512]{1,0:T(8,128)(2,1)S(1)}, bf16[240,512]{1,0:T(8,128)(2,1)S(1)}, u32[]{:S(2)}, u32[]{:S(2)}) %collective-permute-start.4) | collective-permute-done | bytes 245792 | tf_op jit(solution)/shard_map/ppermute | solution.py:36
  61.2 5.4 %collective-permute-done.5.r3 = bf16[240,512]{1,0:T(8,128)(2,1)S(1)} collective-permute-done((bf16[240,512]{1,0:T(8,128)(2,1)S(1)}, bf16[240,512]{1,0:T(8,128)(2,1)S(1)}, u32[]{:S(2)}, u32[]{:S(2)}) %collective-permute-start.5) | collective-permute-done | bytes 245792 | tf_op jit(solution)/shard_map/ppermute | solution.py:36
  66.5 2.1 %collective-permute-start.7 = (bf16[4,80,640]{2,1,0:T(8,128)(2,1)S(1)}, bf16[4,80,640]{2,1,0:T(8,128)(2,1)}, u32[]{:S(2)}, u32[]{:S(2)}) collective-permute-start(bf16[4,80,640]{2,1,0:T(8,128)(2,1)S(1)} %get-tuple-element.66), channel_id=1, source_target_pairs={{0,16},{8,24},{16,0},{24,8},{1,17},{9,25},{17,1},{25,9},{2,18},{10... | collective-permute-start | bytes 1228808 | tf_op jit(solution)/shard_map/ppermute | solution.py:36
  68.7 0.4 copy.15.id_col
  69.0 5.6 %attend.1 = (bf16[80,512]{1,0:T(8,128)(2,1)S(1)}, bf16[80,512]{1,0:T(8,128)(2,1)S(1)}, bf16[80,512]{1,0:T(8,128)(2,1)S(1)}, bf16[80,512]{1,0:T(8,128)(2,1)S(1)}) custom-call(s32[4]{0:T(128)S(1)} %pad_add_fusion.pos, s32[5,16]{1,0:T(8,128)S(1)} %stack.31.work, bf16[240,512]{1,0:T(8,128)(2,1)S(1)} %get-tuple-element.59.r0, ...), custom_call_target="tpu_custom_call" | custom-call | tf_op jit(solution)/shard_map/attend/pallas_call | solution.py:374
  74.6 0.1 collective-permute-start.6
  74.7 1.9 %collective-permute-start.8 = (bf16[80,512]{1,0:T(8,128)(2,1)S(1)}, bf16[80,512]{1,0:T(8,128)(2,1)S(1)}, u32[]{:S(2)}, u32[]{:S(2)}) collective-permute-start(bf16[80,512]{1,0:T(8,128)(2,1)S(1)} %get-tuple-element.68), channel_id=1, source_target_pairs={{0,64},{32,96},{64,0},{96,32},{1,65},{33,97},{65,1},{97,33},{2,66}... | collective-permute-start | bytes 245768 | tf_op jit(solution)/shard_map/ppermute | solution.py:36
  76.6 5.9 %collective-permute-done.6.g1 = bf16[80,512]{1,0:T(8,128)(2,1)S(1)} collective-permute-done((bf16[80,512]{1,0:T(8,128)(2,1)S(1)}, bf16[80,512]{1,0:T(8,128)(2,1)S(1)}, u32[]{:S(2)}, u32[]{:S(2)}) %collective-permute-start.6) | collective-permute-done | bytes 81952 | tf_op jit(solution)/shard_map/ppermute | solution.py:36
  82.5 6.2 %collective-permute-done.9.g3 = bf16[80,512]{1,0:T(8,128)(2,1)S(1)} collective-permute-done((bf16[80,512]{1,0:T(8,128)(2,1)S(1)}, bf16[80,512]{1,0:T(8,128)(2,1)S(1)}, u32[]{:S(2)}, u32[]{:S(2)}) %collective-permute-start.9) | collective-permute-done | bytes 81952 | tf_op jit(solution)/shard_map/ppermute | solution.py:36
  88.7 0.6 pack.1.refs_0_
  89.2 0.1 collective-permute-start.14
  89.3 4.2 %collective-permute-start.13 = (bf16[4,80,512]{2,1,0:T(8,128)(2,1)S(1)}, bf16[4,80,512]{2,1,0:T(8,128)(2,1)S(1)}, u32[]{:S(2)}, u32[]{:S(2)}) collective-permute-start(bf16[4,80,512]{2,1,0:T(8,128)(2,1)S(1)} %pack.1.refs_0_), channel_id=1, source_target_pairs={{0,16},{8,24},{16,0},{24,8},{1,17},{9,25},{17,1},{25,9},{2,18},{10... | collective-permute-start | bytes 983048 | tf_op jit(solution)/shard_map/ppermute | solution.py:36
  93.5 3.1 %all-gather.7.cloned.1.call-done = bf16[5120,640]{1,0:T(8,128)(2,1)} async-done(((bf16[160,640]{1,0:T(8,128)(2,1)}), bf16[5120,640]{1,0:T(8,128)(2,1)}) %all-gather.7.cloned.1.call-update) | async-done | bytes 6553616 | tf_op jit(solution)/shard_map/all_gather | solution.py:288
  96.6 4.8 %fetch_merge.1.w = bf16[5120,1280]{1,0:T(8,128)(2,1)S(1)} custom-call(bf16[5120,1280]{1,0:T(8,128)(2,1)} %w_hbm), custom_call_target="tpu_custom_call" | custom-call | tf_op jit(solution)/shard_map/fetch_merge/pallas_call | solution.py:423
  101.4 0.8 copy-done.5
  102.2 5.0 %fetch.1 = (bf16[16,80,1280]{2,1,0:T(8,128)(2,1)S(1)}, bf16[16,80,1280]{2,1,0:T(8,128)(2,1)S(1)}, bf16[16,80,1280]{2,1,0:T(8,128)(2,1)S(1)}, bf16[4,128,1280]{2,1,0:T(8,128)(2,1)S(1)}) custom-call(s32[4]{0:T(128)S(1)} %pad_add_fusion.pos, bf16[128,1280]{1,0:T(8,128)(2,1)} %bitcast.54, bf16[128,1280]{1,0:T(8,128)(2,1)} %copy-done.4, ...), custom_call_target="tpu_custom_call" | custom-call | tf_op jit(solution)/shard_map/fetch/pallas_call | solution.py:404
  107.2 3.9 %mlp_first.1 = (bf16[128,1280]{1,0:T(8,128)(2,1)S(1)}, bf16[128,1280]{1,0:T(8,128)(2,1)S(1)}) custom-call(s32[4]{0:T(128)S(1)} %pad_add_fusion.pos, bf16[4,80,512]{2,1,0:T(8,128)(2,1)S(1)} %pack.1.refs_0_, bf16[4,80,512]{2,1,0:T(8,128)(2,1)S(1)} %collective-permute-done.12.refs_1_, bf16[4,80,512]{2,1,0:T(8,128)(2,1)S(1)} %collective-permute-done.13.refs_2_, ...), custom_call_target="tpu_custom_call" | custom-call | flops 2516582400 | bytes 9830400 | tf_op jit(solution)/shard_map/mlp_first/pallas_call | solution.py:435
  111.1 1.7 %collective-permute-start.16 = (bf16[128,1280]{1,0:T(8,128)(2,1)S(1)}, bf16[128,1280]{1,0:T(8,128)(2,1)S(1)}, u32[]{:S(2)}, u32[]{:S(2)}) collective-permute-start(bf16[128,1280]{1,0:T(8,128)(2,1)S(1)} %get-tuple-element.91), channel_id=1, source_target_pairs={{0,8},{8,16},{16,24},{24,0},{1,9},{9,17},{17,25},{25,1},{2,10},{10... | collective-permute-start | bytes 983048 | tf_op jit(solution)/shard_map/ppermute | solution.py:36
  112.8 1.6 %collective-permute-start.17 = (bf16[128,1280]{1,0:T(8,128)(2,1)S(1)}, bf16[128,1280]{1,0:T(8,128)(2,1)S(1)}, u32[]{:S(2)}, u32[]{:S(2)}) collective-permute-start(bf16[128,1280]{1,0:T(8,128)(2,1)S(1)} %get-tuple-element.92), channel_id=1, source_target_pairs={{0,24},{8,0},{16,8},{24,16},{1,25},{9,1},{17,9},{25,17},{2,26},{10... | collective-permute-start | bytes 983048 | tf_op jit(solution)/shard_map/ppermute | solution.py:36
  114.4 3.9 %mlp_second.1 = (bf16[128,1280]{1,0:T(8,128)(2,1)S(1)}, bf16[128,1280]{1,0:T(8,128)(2,1)S(1)}, bf16[128,1280]{1,0:T(8,128)(2,1)S(1)}) custom-call(s32[4]{0:T(128)S(1)} %pad_add_fusion.pos, bf16[4,80,512]{2,1,0:T(8,128)(2,1)S(1)} %pack.1.refs_0_, bf16[4,80,512]{2,1,0:T(8,128)(2,1)S(1)} %collective-permute-done.12.refs_1_, ...), custom_call_target="tpu_custom_call" | custom-call | flops 2516582400 | bytes 9830400 | tf_op jit(solution)/shard_map/mlp_second/pallas_call | solution.py:435
  118.3 1.3 collective-permute-start.18
  119.7 2.7 %collective-permute-done.16 = bf16[128,1280]{1,0:T(8,128)(2,1)S(1)} collective-permute-done((bf16[128,1280]{1,0:T(8,128)(2,1)S(1)}, bf16[128,1280]{1,0:T(8,128)(2,1)S(1)}, u32[]{:S(2)}, u32[]{:S(2)}) %collective-permute-start.16) | collective-permute-done | bytes 327712 | tf_op jit(solution)/shard_map/ppermute | solution.py:36
  122.4 1.1 collective-permute-done.17
  123.4 0.2 add_add_fusion.early
  123.6 6.3 %collective-permute-done.18.late = bf16[128,1280]{1,0:T(8,128)(2,1)S(1)} collective-permute-done((bf16[128,1280]{1,0:T(8,128)(2,1)S(1)}, bf16[128,1280]{1,0:T(8,128)(2,1)S(1)}, u32[]{:S(2)}, u32[]{:S(2)}) %collective-permute-start.18) | collective-permute-done | bytes 327712 | tf_op jit(solution)/shard_map/ppermute | solution.py:36
  129.9 2.4 %merge.1 = bf16[32,1408]{1,0:T(8,128)(2,1)S(1)} custom-call(f32[128,1280]{1,0:T(8,128)S(1)} %add_add_fusion.early, bf16[128,1280]{1,0:T(8,128)(2,1)S(1)} %collective-permute-done.18.late, bf16[5120,1280]{1,0:T(8,128)(2,1)S(1)} %fetch_merge.1.w, bf16[32,32]{1,0:T(8,128)(2,1)S(1)} %fusion.5.select, bf16[32,128]{1,0:T(8,128)(2,1)S(1)} %select_convert_fusion.tail), custom_call_target="tpu_custom_call" | custom-call | tf_op jit(solution)/shard_map/merge/pallas_call | solution.py:456
  132.4 12.9 %all_to_all.5 = bf16[16,2,1408]{2,1,0:T(2,128)(2,1)S(1)} all-to-all(bf16[16,2,1408]{2,1,0:T(2,128)(2,1)S(1)} %reshape.166), channel_id=1, replica_groups=mesh['x'=4,'y'=4,'z'=4,'c'=2] {'x','y'}, dimensions={0} | all-to-all | bytes 180224 | tf_op jit(solution)/shard_map/all_to_all | solution.py:465
  145.3 0.1 add_reduce_fusion
  145.4 0.1 fusion.4
  145.5 1.1 fusion
  (47 shorter events, 0.4 us)
Async XLA Ops:
  6.5 2.9 %copy-start = (bf16[1280,320]{0,1:T(8,128)(2,1)S(1)}, bf16[1280,320]{0,1:T(8,128)(2,1)}, u32[]{:S(2)}) copy-start(bf16[1280,320]{0,1:T(8,128)(2,1)} %param.17) | copy-start | bytes 2457604
  6.5 33.3 %all-gather.5.cloned.1.call-start = ((), (), s32[]{:S(2)}) async-start(), calls=%async_computation.1 | async-start | bytes 3686400 | tf_op jit(solution)/shard_map/all_gather | solution.py:276
  8.4 88.1 %all-gather.7.cloned.1.call-start = ((), (), s32[]{:S(2)}) async-start(), calls=%async_computation.2 | async-start | bytes 6758400 | tf_op jit(solution)/shard_map/all_gather | solution.py:288
  10.2 17.5 %collective-permute-start.2 = (bf16[128,1280]{1,0:T(8,128)(2,1)}, bf16[128,1280]{1,0:T(8,128)(2,1)S(1)}, u32[]{:S(2)}, u32[]{:S(2)}) collective-permute-start(bf16[128,1280]{1,0:T(8,128)(2,1)} %bitcast.50), channel_id=1, source_target_pairs={{0,24},{8,0},{16,8},{24,16},{1,25},{9,1},{17,9},{25,17},{2,26},{10... | collective-permute-start | bytes 983048 | tf_op jit(solution)/shard_map/ppermute | solution.py:36
  13.3 14.3 %collective-permute-start.1 = (bf16[128,1280]{1,0:T(8,128)(2,1)}, bf16[128,1280]{1,0:T(8,128)(2,1)S(1)}, u32[]{:S(2)}, u32[]{:S(2)}) collective-permute-start(bf16[128,1280]{1,0:T(8,128)(2,1)} %bitcast.51), channel_id=1, source_target_pairs={{0,16},{8,24},{16,0},{24,8},{1,17},{9,25},{17,1},{25,9},{2,18},{10... | collective-permute-start | bytes 983048 | tf_op jit(solution)/shard_map/ppermute | solution.py:36
  14.0 17.3 %collective-permute-start = (bf16[128,1280]{1,0:T(8,128)(2,1)}, bf16[128,1280]{1,0:T(8,128)(2,1)S(1)}, u32[]{:S(2)}, u32[]{:S(2)}) collective-permute-start(bf16[128,1280]{1,0:T(8,128)(2,1)} %bitcast.52), channel_id=1, source_target_pairs={{0,8},{8,16},{16,24},{24,0},{1,9},{9,17},{17,25},{25,1},{2,10},{10... | collective-permute-start | bytes 983048 | tf_op jit(solution)/shard_map/ppermute | solution.py:36
  21.6 47.1 %copy-start.1 = (s32[1,2048]{1,0:T(1,128)S(1)}, s32[1,2048]{1,0:T(1,128)}, u32[]{:S(2)}) copy-start(s32[1,2048]{1,0:T(1,128)} %param.12) | copy-start | bytes 24580
  27.6 3.6 %copy-start.2 = (bf16[128,1280]{1,0:T(8,128)(2,1)}, bf16[128,1280]{1,0:T(8,128)(2,1)S(1)}, u32[]{:S(2)}) copy-start(bf16[128,1280]{1,0:T(8,128)(2,1)S(1)} %collective-permute-done.2.p3.refs_3_) | copy-start | bytes 983044
  27.6 3.6 %copy-start.3 = (bf16[128,1280]{1,0:T(8,128)(2,1)}, bf16[128,1280]{1,0:T(8,128)(2,1)S(1)}, u32[]{:S(2)}) copy-start(bf16[128,1280]{1,0:T(8,128)(2,1)S(1)} %collective-permute-done.1.p2.refs_2_) | copy-start | bytes 983044
  31.2 0.7 copy-start.4
  39.9 53.6 %copy-start.7 = (f32[1280]{0:T(1024)S(1)}, f32[1280]{0:T(1024)}, u32[]{:S(2)}) copy-start(f32[1280]{0:T(1024)} %param.16) | copy-start | bytes 15364
  44.9 43.7 %collective-permute-start.11 = (bf16[4,80,1280]{2,1,0:T(8,128)(2,1)}, bf16[4,80,1280]{2,1,0:T(8,128)(2,1)}, u32[]{:S(2)}, u32[]{:S(2)}) collective-permute-start(bf16[4,80,1280]{2,1,0:T(8,128)(2,1)} %get-tuple-element.70), channel_id=1, source_target_pairs={{0,24},{8,0},{16,8},{24,16},{1,25},{9,1},{17,9},{25,17},{2,26},{10... | collective-permute-start | bytes 2457608 | tf_op jit(solution)/shard_map/ppermute | solution.py:36
  47.8 40.9 %collective-permute-start.10 = (bf16[4,80,1280]{2,1,0:T(8,128)(2,1)}, bf16[4,80,1280]{2,1,0:T(8,128)(2,1)}, u32[]{:S(2)}, u32[]{:S(2)}) collective-permute-start(bf16[4,80,1280]{2,1,0:T(8,128)(2,1)} %get-tuple-element.70), channel_id=1, source_target_pairs={{0,8},{8,16},{16,24},{24,0},{1,9},{9,17},{17,25},{25,1},{2,10},{10... | collective-permute-start | bytes 2457608 | tf_op jit(solution)/shard_map/ppermute | solution.py:36
  47.8 9.9 %collective-permute-start.3 = (bf16[240,512]{1,0:T(8,128)(2,1)S(1)}, bf16[240,512]{1,0:T(8,128)(2,1)S(1)}, u32[]{:S(2)}, u32[]{:S(2)}) collective-permute-start(bf16[240,512]{1,0:T(8,128)(2,1)S(1)} %get-tuple-element.55), channel_id=1, source_target_pairs={{0,96},{32,0},{64,32},{96,64},{1,97},{33,1},{65,33},{97,65},{2,98}... | collective-permute-start | bytes 737288 | tf_op jit(solution)/shard_map/ppermute | solution.py:36
  49.2 11.9 %collective-permute-start.4 = (bf16[240,512]{1,0:T(8,128)(2,1)S(1)}, bf16[240,512]{1,0:T(8,128)(2,1)S(1)}, u32[]{:S(2)}, u32[]{:S(2)}) collective-permute-start(bf16[240,512]{1,0:T(8,128)(2,1)S(1)} %get-tuple-element.56), channel_id=1, source_target_pairs={{0,64},{32,96},{64,0},{96,32},{1,65},{33,97},{65,1},{97,33},{2,66}... | collective-permute-start | bytes 737288 | tf_op jit(solution)/shard_map/ppermute | solution.py:36
  50.2 16.4 %collective-permute-start.5 = (bf16[240,512]{1,0:T(8,128)(2,1)S(1)}, bf16[240,512]{1,0:T(8,128)(2,1)S(1)}, u32[]{:S(2)}, u32[]{:S(2)}) collective-permute-start(bf16[240,512]{1,0:T(8,128)(2,1)S(1)} %get-tuple-element.57), channel_id=1, source_target_pairs={{0,32},{32,64},{64,96},{96,0},{1,33},{33,65},{65,97},{97,1},{2,34}... | collective-permute-start | bytes 737288 | tf_op jit(solution)/shard_map/ppermute | solution.py:36
  66.5 15.9 %collective-permute-start.7 = (bf16[4,80,640]{2,1,0:T(8,128)(2,1)S(1)}, bf16[4,80,640]{2,1,0:T(8,128)(2,1)}, u32[]{:S(2)}, u32[]{:S(2)}) collective-permute-start(bf16[4,80,640]{2,1,0:T(8,128)(2,1)S(1)} %get-tuple-element.66), channel_id=1, source_target_pairs={{0,16},{8,24},{16,0},{24,8},{1,17},{9,25},{17,1},{25,9},{2,18},{10... | collective-permute-start | bytes 1228808 | tf_op jit(solution)/shard_map/ppermute | solution.py:36
  74.6 7.9 %collective-permute-start.6 = (bf16[80,512]{1,0:T(8,128)(2,1)S(1)}, bf16[80,512]{1,0:T(8,128)(2,1)S(1)}, u32[]{:S(2)}, u32[]{:S(2)}) collective-permute-start(bf16[80,512]{1,0:T(8,128)(2,1)S(1)} %get-tuple-element.65), channel_id=1, source_target_pairs={{0,32},{32,64},{64,96},{96,0},{1,33},{33,65},{65,97},{97,1},{2,34}... | collective-permute-start | bytes 245768 | tf_op jit(solution)/shard_map/ppermute | solution.py:36
  74.7 7.8 %collective-permute-start.8 = (bf16[80,512]{1,0:T(8,128)(2,1)S(1)}, bf16[80,512]{1,0:T(8,128)(2,1)S(1)}, u32[]{:S(2)}, u32[]{:S(2)}) collective-permute-start(bf16[80,512]{1,0:T(8,128)(2,1)S(1)} %get-tuple-element.68), channel_id=1, source_target_pairs={{0,64},{32,96},{64,0},{96,32},{1,65},{33,97},{65,1},{97,33},{2,66}... | collective-permute-start | bytes 245768 | tf_op jit(solution)/shard_map/ppermute | solution.py:36
  82.5 6.2 %collective-permute-start.9 = (bf16[80,512]{1,0:T(8,128)(2,1)S(1)}, bf16[80,512]{1,0:T(8,128)(2,1)S(1)}, u32[]{:S(2)}, u32[]{:S(2)}) collective-permute-start(bf16[80,512]{1,0:T(8,128)(2,1)S(1)} %get-tuple-element.69), channel_id=1, source_target_pairs={{0,96},{32,0},{64,32},{96,64},{1,97},{33,1},{65,33},{97,65},{2,98}... | collective-permute-start | bytes 245768 | tf_op jit(solution)/shard_map/ppermute | solution.py:36
  82.5 19.0 %collective-permute-start.15 = (bf16[4,80,640]{2,1,0:T(8,128)(2,1)}, bf16[4,80,640]{2,1,0:T(8,128)(2,1)S(1)}, u32[]{:S(2)}, u32[]{:S(2)}) collective-permute-start(bf16[4,80,640]{2,1,0:T(8,128)(2,1)} %collective-permute-done.7.refs_8_), channel_id=1, source_target_pairs={{0,1},{1,0},{2,3},{3,2},{4,5},{5,4},{6,7},{7,6},{8,9},{9,8},{10,11... | collective-permute-start | bytes 1228808 | tf_op jit(solution)/shard_map/ppermute | solution.py:44
  89.2 18.0 %collective-permute-start.14 = (bf16[4,80,512]{2,1,0:T(8,128)(2,1)S(1)}, bf16[4,80,512]{2,1,0:T(8,128)(2,1)S(1)}, u32[]{:S(2)}, u32[]{:S(2)}) collective-permute-start(bf16[4,80,512]{2,1,0:T(8,128)(2,1)S(1)} %pack.1.refs_0_), channel_id=1, source_target_pairs={{0,24},{8,0},{16,8},{24,16},{1,25},{9,1},{17,9},{25,17},{2,26},{10... | collective-permute-start | bytes 983048 | tf_op jit(solution)/shard_map/ppermute | solution.py:36
  89.3 17.9 %collective-permute-start.13 = (bf16[4,80,512]{2,1,0:T(8,128)(2,1)S(1)}, bf16[4,80,512]{2,1,0:T(8,128)(2,1)S(1)}, u32[]{:S(2)}, u32[]{:S(2)}) collective-permute-start(bf16[4,80,512]{2,1,0:T(8,128)(2,1)S(1)} %pack.1.refs_0_), channel_id=1, source_target_pairs={{0,16},{8,24},{16,0},{24,8},{1,17},{9,25},{17,1},{25,9},{2,18},{10... | collective-permute-start | bytes 983048 | tf_op jit(solution)/shard_map/ppermute | solution.py:36
  93.5 13.7 %collective-permute-start.12 = (bf16[4,80,512]{2,1,0:T(8,128)(2,1)S(1)}, bf16[4,80,512]{2,1,0:T(8,128)(2,1)S(1)}, u32[]{:S(2)}, u32[]{:S(2)}) collective-permute-start(bf16[4,80,512]{2,1,0:T(8,128)(2,1)S(1)} %pack.1.refs_0_), channel_id=1, source_target_pairs={{0,8},{8,16},{16,24},{24,0},{1,9},{9,17},{17,25},{25,1},{2,10},{10... | collective-permute-start | bytes 983048 | tf_op jit(solution)/shard_map/ppermute | solution.py:36
  101.4 0.8 copy-start.5
  111.1 11.2 %collective-permute-start.16 = (bf16[128,1280]{1,0:T(8,128)(2,1)S(1)}, bf16[128,1280]{1,0:T(8,128)(2,1)S(1)}, u32[]{:S(2)}, u32[]{:S(2)}) collective-permute-start(bf16[128,1280]{1,0:T(8,128)(2,1)S(1)} %get-tuple-element.91), channel_id=1, source_target_pairs={{0,8},{8,16},{16,24},{24,0},{1,9},{9,17},{17,25},{25,1},{2,10},{10... | collective-permute-start | bytes 983048 | tf_op jit(solution)/shard_map/ppermute | solution.py:36
  112.8 10.6 %collective-permute-start.17 = (bf16[128,1280]{1,0:T(8,128)(2,1)S(1)}, bf16[128,1280]{1,0:T(8,128)(2,1)S(1)}, u32[]{:S(2)}, u32[]{:S(2)}) collective-permute-start(bf16[128,1280]{1,0:T(8,128)(2,1)S(1)} %get-tuple-element.92), channel_id=1, source_target_pairs={{0,24},{8,0},{16,8},{24,16},{1,25},{9,1},{17,9},{25,17},{2,26},{10... | collective-permute-start | bytes 983048 | tf_op jit(solution)/shard_map/ppermute | solution.py:36
  118.3 11.6 %collective-permute-start.18 = (bf16[128,1280]{1,0:T(8,128)(2,1)S(1)}, bf16[128,1280]{1,0:T(8,128)(2,1)S(1)}, u32[]{:S(2)}, u32[]{:S(2)}) collective-permute-start(bf16[128,1280]{1,0:T(8,128)(2,1)S(1)} %get-tuple-element.93), channel_id=1, source_target_pairs={{0,16},{8,24},{16,0},{24,8},{1,17},{9,25},{17,1},{25,9},{2,18},{10... | collective-permute-start | bytes 983048 | tf_op jit(solution)/shard_map/ppermute | solution.py:36
  123.6 21.9 %copy-start.6 = (bf16[128,1280]{1,0:T(8,128)(2,1)S(1)}, bf16[128,1280]{1,0:T(8,128)(2,1)}, u32[]{:S(2)}) copy-start(bf16[128,1280]{1,0:T(8,128)(2,1)} %param.20) | copy-start | bytes 983044
Sparse Core Ops, SparseCore 0:
  9.0 30.7 all-gather.4
  42.1 54.4 all-gather.6

commit v12 on v10

--- a/solution.py
+++ b/solution.py
@@ -386,7 +386,8 @@
         compiler_params=params(16),
         name="attend",
     )(pos, work, *blocks, id_row, id_col)
-    attended, pass2 = lax.optimization_barrier((attended, pass2))
+    attended = list(attended)
+    attended[3], pass2 = lax.optimization_barrier((attended[3], pass2))
     swap2 = swap(pass2)
     heads = [attended[0]] + [shift(attended[k], "x", k) for k in (1, 2, 3)]
     heads, pass1, pass3 = lax.optimization_barrier((heads, pass1, pass3))

time: 154 us -> 155 us (level)
  waiting for transfers between devices: 52.6 us -> 56.4 us
  starting transfers between devices: 26.7 us -> 24.3 us
    all_gather x1, waiting for transfers between devices: 1.24 us -> 6.32 us  [local(): w_near = lax.all_gather(packed, ('x', 'z', 'c'), axis=0, tiled=False)]
    ppermute x18, starting transfers between devices: 26.6 us -> 23.3 us  [shift(): return lax.ppermute(value, axis, pairs)]
  transfers between devices with their start and end apart: 21 -> 21, of which waited for: 14 -> 13; matrix products, arithmetic and copies ran while one was open for 6% -> 6% of each run, Pallas kernels for 18% -> 18%
where the time goes in v12:
time: 155 us; the launch traced here: 154 us
  waiting for transfers between devices  56.4 us (36%)
  Pallas kernels  33.8 us (22%)
  starting transfers between devices  24.3 us (16%)
  between operations  13.6 us (9%)
  blocking collectives  12.6 us (8%)
  other arithmetic  6.99 us (5%)
  local copies, waits for them, and re-layouts  5.43 us (4%)
    ppermute x18, waiting for transfers between devices, shift(): return lax.ppermute(value, axis, pairs)  44.8 us
    ppermute x18, starting transfers between devices, shift(): return lax.ppermute(value, axis, pairs)  23.3 us
    all_to_all x1, blocking collectives, local(): lax.all_to_all(outgoing.reshape(req_count, slot_cap, width + 128), ('x',...  12.6 us
    pallas_call x2, Pallas kernels, mlp(): pl.pallas_call(functools.partial(mlp_kernel, offsets), out_shape=[jax.Sha...  7.79 us
    all_gather x1, waiting for transfers between devices, local(): w_near = lax.all_gather(packed, ('x', 'z', 'c'), axis=0, tiled=False)  6.32 us
    pallas_call x1, Pallas kernels, local(): pl.pallas_call(attend_kernel, out_shape=[jax.ShapeDtypeStruct((HEAD, tota...  5.58 us
    all_gather x1, waiting for transfers between devices, local(): near = lax.all_gather(w_half, ('x', 'c'), axis=0, tiled=False)  5.26 us
    pallas_call x1, Pallas kernels, local(): pl.pallas_call(qkv_kernel, out_shape=[jax.ShapeDtypeStruct((3 * HEAD, tot...  5.07 us
  transfers between devices with their start and end apart: 21, of which 13 were waited for; matrix products, arithmetic and copies ran while one was open for 6% of the time, Pallas kernels for 18%

profile of v12, /device:TPU:0, one launch (start us, length us, event | category | flops | bytes accessed | tf_op | source)
XLA Modules:
  0.0 154.4 jit_solution(13647728170536539041)
XLA Ops:
  6.5 1.9 %fusion.1 = bf16[320,640]{1,0:T(8,128)(2,1)} fusion(s32[]{:T(128)S(6)} %select_n.83, bf16[240,1280]{1,0:T(8,128)(2,1)} %bitcast.55, bf16[80,1280]{1,0:T(8,128)(2,1)} %param.15), kind=kLoop, calls=%fused_computation.5 | loop fusion | flops 819200 | bytes 1228804 | tf_op jit(solution)/shard_map/concatenate | solution.py:274
  8.5 0.9 dynamic_slice.11
  9.4 0.7 pad_maximum_fusion
  10.2 3.2 %collective-permute-start.2 = (bf16[128,1280]{1,0:T(8,128)(2,1)}, bf16[128,1280]{1,0:T(8,128)(2,1)S(1)}, u32[]{:S(2)}, u32[]{:S(2)}) collective-permute-start(bf16[128,1280]{1,0:T(8,128)(2,1)} %bitcast.50), channel_id=1, source_target_pairs={{0,24},{8,0},{16,8},{24,16},{1,25},{9,1},{17,9},{25,17},{2,26},{10... | collective-permute-start | bytes 983048 | tf_op jit(solution)/shard_map/ppermute | solution.py:36
  13.3 0.6 collective-permute-start.1
  14.0 1.0 collective-permute-start
  14.9 0.7 broadcast_in_dim.118.gain
  15.6 0.5 broadcast.242
  16.2 1.4 reduce.5
  17.5 0.2 fusion.2
  17.7 0.2 and_reduce_fusion
  17.9 0.2 select_reduce_fusion.3
  18.0 0.1 select_reduce_fusion.2
  18.2 0.6 slice.9
  18.8 0.1 convert_reduce_fusion.1
  18.9 0.1 select_reduce_fusion.1
  18.9 0.1 fusion.11
  19.1 0.6 stack.30
  19.7 0.7 compare_select_fusion
  20.4 0.7 fusion.14
  21.1 0.2 convert_reduce_fusion
  21.3 0.1 select_reduce_fusion
  21.6 6.1 %collective-permute-done.2.p3.refs_3_ = bf16[128,1280]{1,0:T(8,128)(2,1)S(1)} collective-permute-done((bf16[128,1280]{1,0:T(8,128)(2,1)}, bf16[128,1280]{1,0:T(8,128)(2,1)S(1)}, u32[]{:S(2)}, u32[]{:S(2)}) %collective-permute-start.2) | collective-permute-done | bytes 327712 | tf_op jit(solution)/shard_map/ppermute | solution.py:36
  27.6 3.6 %collective-permute-done.p1.refs_1_ = bf16[128,1280]{1,0:T(8,128)(2,1)S(1)} collective-permute-done((bf16[128,1280]{1,0:T(8,128)(2,1)}, bf16[128,1280]{1,0:T(8,128)(2,1)S(1)}, u32[]{:S(2)}, u32[]{:S(2)}) %collective-permute-start) | collective-permute-done | bytes 327712 | tf_op jit(solution)/shard_map/ppermute | solution.py:36
  31.2 0.7 copy-done.4
  32.0 2.6 %norm.1.h1 = bf16[2,512,640]{2,1,0:T(8,128)(2,1)S(1)} custom-call(s32[4]{0:T(128)S(1)} %pad_add_fusion.pos, bf16[128,1280]{1,0:T(8,128)(2,1)} %bitcast.53, bf16[128,1280]{1,0:T(8,128)(2,1)} %copy-done.4, bf16[128,1280]{1,0:T(8,128)(2,1)} %copy-done.3, bf16[128,1280]{1,0:T(8,128)(2,1)} %copy-done.2, f32[1,1280]{1,0:T(1,128)S(1)} %broadcast_in_dim.118.gain), custom_call_target="tpu_custom_call" | custom-call | tf_op jit(solution)/shard_map/norm/pallas_call | solution.py:293
  34.6 5.3 %all-gather.5.cloned.1.call-done = bf16[2560,640]{1,0:T(8,128)(2,1)} async-done(((bf16[320,640]{1,0:T(8,128)(2,1)}), bf16[2560,640]{1,0:T(8,128)(2,1)}) %all-gather.5.cloned.1.call-update) | async-done | bytes 3276816 | tf_op jit(solution)/shard_map/all_gather | solution.py:276
  39.9 5.1 %qkv.1 = (bf16[240,512]{1,0:T(8,128)(2,1)S(1)}, bf16[240,512]{1,0:T(8,128)(2,1)S(1)}, bf16[240,512]{1,0:T(8,128)(2,1)S(1)}, bf16[240,512]{1,0:T(8,128)(2,1)S(1)}...) custom-call(s32[4]{0:T(128)S(1)} %pad_add_fusion.pos, bf16[2,512,640]{2,1,0:T(8,128)(2,1)S(1)} %norm.1.h1, ...), custom_call_target="tpu_custom_call" | custom-call | tf_op jit(solution)/shard_map/qkv/pallas_call | solution.py:352
  44.9 2.8 %collective-permute-start.11 = (bf16[4,80,1280]{2,1,0:T(8,128)(2,1)}, bf16[4,80,1280]{2,1,0:T(8,128)(2,1)}, u32[]{:S(2)}, u32[]{:S(2)}) collective-permute-start(bf16[4,80,1280]{2,1,0:T(8,128)(2,1)} %get-tuple-element.70), channel_id=1, source_target_pairs={{0,24},{8,0},{16,8},{24,16},{1,25},{9,1},{17,9},{25,17},{2,26},{10... | collective-permute-start | bytes 2457608 | tf_op jit(solution)/shard_map/ppermute | solution.py:36
  47.8 1.5 collective-permute-start.3
  49.2 0.9 collective-permute-start.4
  50.2 0.6 collective-permute-start.5
  50.8 6.9 %collective-permute-done.3.r1 = bf16[240,512]{1,0:T(8,128)(2,1)S(1)} collective-permute-done((bf16[240,512]{1,0:T(8,128)(2,1)S(1)}, bf16[240,512]{1,0:T(8,128)(2,1)S(1)}, u32[]{:S(2)}, u32[]{:S(2)}) %collective-permute-start.3) | collective-permute-done | bytes 245792 | tf_op jit(solution)/shard_map/ppermute | solution.py:36
  57.7 3.5 %collective-permute-done.4.r2 = bf16[240,512]{1,0:T(8,128)(2,1)S(1)} collective-permute-done((bf16[240,512]{1,0:T(8,128)(2,1)S(1)}, bf16[240,512]{1,0:T(8,128)(2,1)S(1)}, u32[]{:S(2)}, u32[]{:S(2)}) %collective-permute-start.4) | collective-permute-done | bytes 245792 | tf_op jit(solution)/shard_map/ppermute | solution.py:36
  61.2 5.4 %collective-permute-done.5.r3 = bf16[240,512]{1,0:T(8,128)(2,1)S(1)} collective-permute-done((bf16[240,512]{1,0:T(8,128)(2,1)S(1)}, bf16[240,512]{1,0:T(8,128)(2,1)S(1)}, u32[]{:S(2)}, u32[]{:S(2)}) %collective-permute-start.5) | collective-permute-done | bytes 245792 | tf_op jit(solution)/shard_map/ppermute | solution.py:36
  66.5 2.1 %collective-permute-start.8 = (bf16[4,80,640]{2,1,0:T(8,128)(2,1)S(1)}, bf16[4,80,640]{2,1,0:T(8,128)(2,1)}, u32[]{:S(2)}, u32[]{:S(2)}) collective-permute-start(bf16[4,80,640]{2,1,0:T(8,128)(2,1)S(1)} %get-tuple-element.68), channel_id=1, source_target_pairs={{0,16},{8,24},{16,0},{24,8},{1,17},{9,25},{17,1},{25,9},{2,18},{10... | collective-permute-start | bytes 1228808 | tf_op jit(solution)/shard_map/ppermute | solution.py:36
  68.7 0.4 copy.15.id_col
  69.0 5.6 %attend.1 = (bf16[80,512]{1,0:T(8,128)(2,1)S(1)}, bf16[80,512]{1,0:T(8,128)(2,1)S(1)}, bf16[80,512]{1,0:T(8,128)(2,1)S(1)}, bf16[80,512]{1,0:T(8,128)(2,1)S(1)}) custom-call(s32[4]{0:T(128)S(1)} %pad_add_fusion.pos, s32[5,16]{1,0:T(8,128)S(1)} %stack.31.work, bf16[240,512]{1,0:T(8,128)(2,1)S(1)} %get-tuple-element.59.r0, ...), custom_call_target="tpu_custom_call" | custom-call | tf_op jit(solution)/shard_map/attend/pallas_call | solution.py:374
  74.7 1.9 %collective-permute-start.7 = (bf16[80,512]{1,0:T(8,128)(2,1)S(1)}, bf16[80,512]{1,0:T(8,128)(2,1)S(1)}, u32[]{:S(2)}, u32[]{:S(2)}) collective-permute-start(bf16[80,512]{1,0:T(8,128)(2,1)S(1)} %get-tuple-element.66), channel_id=1, source_target_pairs={{0,64},{32,96},{64,0},{96,32},{1,65},{33,97},{65,1},{97,33},{2,66}... | collective-permute-start | bytes 245768 | tf_op jit(solution)/shard_map/ppermute | solution.py:36
  76.6 3.1 %collective-permute-done.8.refs_8_ = bf16[4,80,640]{2,1,0:T(8,128)(2,1)} collective-permute-done((bf16[4,80,640]{2,1,0:T(8,128)(2,1)S(1)}, bf16[4,80,640]{2,1,0:T(8,128)(2,1)}, u32[]{:S(2)}, u32[]{:S(2)}) %collective-permute-start.8) | collective-permute-done | bytes 409632 | tf_op jit(solution)/shard_map/ppermute | solution.py:36
  79.7 4.3 %collective-permute-done.6.g1 = bf16[80,512]{1,0:T(8,128)(2,1)S(1)} collective-permute-done((bf16[80,512]{1,0:T(8,128)(2,1)S(1)}, bf16[80,512]{1,0:T(8,128)(2,1)S(1)}, u32[]{:S(2)}, u32[]{:S(2)}) %collective-permute-start.6) | collective-permute-done | bytes 81952 | tf_op jit(solution)/shard_map/ppermute | solution.py:36
  84.0 1.0 collective-permute-start.15
  84.9 2.0 %collective-permute-done.9.g3 = bf16[80,512]{1,0:T(8,128)(2,1)S(1)} collective-permute-done((bf16[80,512]{1,0:T(8,128)(2,1)S(1)}, bf16[80,512]{1,0:T(8,128)(2,1)S(1)}, u32[]{:S(2)}, u32[]{:S(2)}) %collective-permute-start.9) | collective-permute-done | bytes 81952 | tf_op jit(solution)/shard_map/ppermute | solution.py:36
  87.0 0.6 pack.1.refs_0_
  87.6 2.4 %collective-permute-start.14 = (bf16[4,80,512]{2,1,0:T(8,128)(2,1)S(1)}, bf16[4,80,512]{2,1,0:T(8,128)(2,1)S(1)}, u32[]{:S(2)}, u32[]{:S(2)}) collective-permute-start(bf16[4,80,512]{2,1,0:T(8,128)(2,1)S(1)} %pack.1.refs_0_), channel_id=1, source_target_pairs={{0,24},{8,0},{16,8},{24,16},{1,25},{9,1},{17,9},{25,17},{2,26},{10... | collective-permute-start | bytes 983048 | tf_op jit(solution)/shard_map/ppermute | solution.py:36
  90.0 1.5 collective-permute-start.13
  91.5 6.3 %all-gather.7.cloned.1.call-done = bf16[5120,640]{1,0:T(8,128)(2,1)} async-done(((bf16[160,640]{1,0:T(8,128)(2,1)}), bf16[5120,640]{1,0:T(8,128)(2,1)}) %all-gather.7.cloned.1.call-update) | async-done | bytes 6553616 | tf_op jit(solution)/shard_map/all_gather | solution.py:288
  97.8 4.8 %fetch_merge.1.w = bf16[5120,1280]{1,0:T(8,128)(2,1)S(1)} custom-call(bf16[5120,1280]{1,0:T(8,128)(2,1)} %w_hbm), custom_call_target="tpu_custom_call" | custom-call | tf_op jit(solution)/shard_map/fetch_merge/pallas_call | solution.py:424
  102.7 0.8 copy-done.5
  103.4 5.0 %fetch.1 = (bf16[16,80,1280]{2,1,0:T(8,128)(2,1)S(1)}, bf16[16,80,1280]{2,1,0:T(8,128)(2,1)S(1)}, bf16[16,80,1280]{2,1,0:T(8,128)(2,1)S(1)}, bf16[4,128,1280]{2,1,0:T(8,128)(2,1)S(1)}) custom-call(s32[4]{0:T(128)S(1)} %pad_add_fusion.pos, bf16[128,1280]{1,0:T(8,128)(2,1)} %bitcast.54, bf16[128,1280]{1,0:T(8,128)(2,1)} %copy-done.4, ...), custom_call_target="tpu_custom_call" | custom-call | tf_op jit(solution)/shard_map/fetch/pallas_call | solution.py:405
  108.5 3.9 %mlp_first.1 = (bf16[128,1280]{1,0:T(8,128)(2,1)S(1)}, bf16[128,1280]{1,0:T(8,128)(2,1)S(1)}) custom-call(s32[4]{0:T(128)S(1)} %pad_add_fusion.pos, bf16[4,80,512]{2,1,0:T(8,128)(2,1)S(1)} %pack.1.refs_0_, bf16[4,80,512]{2,1,0:T(8,128)(2,1)S(1)} %collective-permute-done.12.refs_1_, bf16[4,80,512]{2,1,0:T(8,128)(2,1)S(1)} %collective-permute-done.13.refs_2_, ...), custom_call_target="tpu_custom_call" | custom-call | flops 2516582400 | bytes 9830400 | tf_op jit(solution)/shard_map/mlp_first/pallas_call | solution.py:436
  112.4 1.8 %collective-permute-start.16 = (bf16[128,1280]{1,0:T(8,128)(2,1)S(1)}, bf16[128,1280]{1,0:T(8,128)(2,1)S(1)}, u32[]{:S(2)}, u32[]{:S(2)}) collective-permute-start(bf16[128,1280]{1,0:T(8,128)(2,1)S(1)} %get-tuple-element.91), channel_id=1, source_target_pairs={{0,8},{8,16},{16,24},{24,0},{1,9},{9,17},{17,25},{25,1},{2,10},{10... | collective-permute-start | bytes 983048 | tf_op jit(solution)/shard_map/ppermute | solution.py:36
  114.1 1.5 collective-permute-start.17
  115.6 3.9 %mlp_second.1 = (bf16[128,1280]{1,0:T(8,128)(2,1)S(1)}, bf16[128,1280]{1,0:T(8,128)(2,1)S(1)}, bf16[128,1280]{1,0:T(8,128)(2,1)S(1)}) custom-call(s32[4]{0:T(128)S(1)} %pad_add_fusion.pos, bf16[4,80,512]{2,1,0:T(8,128)(2,1)S(1)} %pack.1.refs_0_, bf16[4,80,512]{2,1,0:T(8,128)(2,1)S(1)} %collective-permute-done.12.refs_1_, ...), custom_call_target="tpu_custom_call" | custom-call | flops 2516582400 | bytes 9830400 | tf_op jit(solution)/shard_map/mlp_second/pallas_call | solution.py:436
  119.5 1.5 collective-permute-start.18
  121.0 3.2 %collective-permute-done.16 = bf16[128,1280]{1,0:T(8,128)(2,1)S(1)} collective-permute-done((bf16[128,1280]{1,0:T(8,128)(2,1)S(1)}, bf16[128,1280]{1,0:T(8,128)(2,1)S(1)}, u32[]{:S(2)}, u32[]{:S(2)}) %collective-permute-start.16) | collective-permute-done | bytes 327712 | tf_op jit(solution)/shard_map/ppermute | solution.py:36
  124.2 6.3 %collective-permute-done.17 = bf16[128,1280]{1,0:T(8,128)(2,1)S(1)} collective-permute-done((bf16[128,1280]{1,0:T(8,128)(2,1)S(1)}, bf16[128,1280]{1,0:T(8,128)(2,1)S(1)}, u32[]{:S(2)}, u32[]{:S(2)}) %collective-permute-start.17) | collective-permute-done | bytes 327712 | tf_op jit(solution)/shard_map/ppermute | solution.py:36
  130.5 0.2 add_add_fusion.early
  130.7 0.4 collective-permute-done.18.late
  131.1 2.4 %merge.1 = bf16[32,1408]{1,0:T(8,128)(2,1)S(1)} custom-call(f32[128,1280]{1,0:T(8,128)S(1)} %add_add_fusion.early, bf16[128,1280]{1,0:T(8,128)(2,1)S(1)} %collective-permute-done.18.late, bf16[5120,1280]{1,0:T(8,128)(2,1)S(1)} %fetch_merge.1.w, bf16[32,32]{1,0:T(8,128)(2,1)S(1)} %fusion.5.select, bf16[32,128]{1,0:T(8,128)(2,1)S(1)} %select_convert_fusion.tail), custom_call_target="tpu_custom_call" | custom-call | tf_op jit(solution)/shard_map/merge/pallas_call | solution.py:457
  133.5 12.6 %all_to_all.5 = bf16[16,2,1408]{2,1,0:T(2,128)(2,1)S(1)} all-to-all(bf16[16,2,1408]{2,1,0:T(2,128)(2,1)S(1)} %reshape.166), channel_id=1, replica_groups=mesh['x'=4,'y'=4,'z'=4,'c'=2] {'x','y'}, dimensions={0} | all-to-all | bytes 180224 | tf_op jit(solution)/shard_map/all_to_all | solution.py:466
  146.2 0.1 add_reduce_fusion
  146.3 0.1 fusion.4
  146.4 1.1 fusion
  (47 shorter events, 0.6 us)
Async XLA Ops:
  6.5 2.9 %copy-start = (bf16[1280,320]{0,1:T(8,128)(2,1)S(1)}, bf16[1280,320]{0,1:T(8,128)(2,1)}, u32[]{:S(2)}) copy-start(bf16[1280,320]{0,1:T(8,128)(2,1)} %param.17) | copy-start | bytes 2457604
  6.5 33.3 %all-gather.5.cloned.1.call-start = ((), (), s32[]{:S(2)}) async-start(), calls=%async_computation.1 | async-start | bytes 3686400 | tf_op jit(solution)/shard_map/all_gather | solution.py:276
  8.4 89.4 %all-gather.7.cloned.1.call-start = ((), (), s32[]{:S(2)}) async-start(), calls=%async_computation.2 | async-start | bytes 6758400 | tf_op jit(solution)/shard_map/all_gather | solution.py:288
  10.2 17.5 %collective-permute-start.2 = (bf16[128,1280]{1,0:T(8,128)(2,1)}, bf16[128,1280]{1,0:T(8,128)(2,1)S(1)}, u32[]{:S(2)}, u32[]{:S(2)}) collective-permute-start(bf16[128,1280]{1,0:T(8,128)(2,1)} %bitcast.50), channel_id=1, source_target_pairs={{0,24},{8,0},{16,8},{24,16},{1,25},{9,1},{17,9},{25,17},{2,26},{10... | collective-permute-start | bytes 983048 | tf_op jit(solution)/shard_map/ppermute | solution.py:36
  13.3 14.3 %collective-permute-start.1 = (bf16[128,1280]{1,0:T(8,128)(2,1)}, bf16[128,1280]{1,0:T(8,128)(2,1)S(1)}, u32[]{:S(2)}, u32[]{:S(2)}) collective-permute-start(bf16[128,1280]{1,0:T(8,128)(2,1)} %bitcast.51), channel_id=1, source_target_pairs={{0,16},{8,24},{16,0},{24,8},{1,17},{9,25},{17,1},{25,9},{2,18},{10... | collective-permute-start | bytes 983048 | tf_op jit(solution)/shard_map/ppermute | solution.py:36
  14.0 17.3 %collective-permute-start = (bf16[128,1280]{1,0:T(8,128)(2,1)}, bf16[128,1280]{1,0:T(8,128)(2,1)S(1)}, u32[]{:S(2)}, u32[]{:S(2)}) collective-permute-start(bf16[128,1280]{1,0:T(8,128)(2,1)} %bitcast.52), channel_id=1, source_target_pairs={{0,8},{8,16},{16,24},{24,0},{1,9},{9,17},{17,25},{25,1},{2,10},{10... | collective-permute-start | bytes 983048 | tf_op jit(solution)/shard_map/ppermute | solution.py:36
  21.6 47.1 %copy-start.1 = (s32[1,2048]{1,0:T(1,128)S(1)}, s32[1,2048]{1,0:T(1,128)}, u32[]{:S(2)}) copy-start(s32[1,2048]{1,0:T(1,128)} %param.12) | copy-start | bytes 24580
  27.6 3.6 %copy-start.2 = (bf16[128,1280]{1,0:T(8,128)(2,1)}, bf16[128,1280]{1,0:T(8,128)(2,1)S(1)}, u32[]{:S(2)}) copy-start(bf16[128,1280]{1,0:T(8,128)(2,1)S(1)} %collective-permute-done.2.p3.refs_3_) | copy-start | bytes 983044
  27.6 3.6 %copy-start.3 = (bf16[128,1280]{1,0:T(8,128)(2,1)}, bf16[128,1280]{1,0:T(8,128)(2,1)S(1)}, u32[]{:S(2)}) copy-start(bf16[128,1280]{1,0:T(8,128)(2,1)S(1)} %collective-permute-done.1.p2.refs_2_) | copy-start | bytes 983044
  31.2 0.7 copy-start.4
  39.9 51.6 %copy-start.7 = (f32[1280]{0:T(1024)S(1)}, f32[1280]{0:T(1024)}, u32[]{:S(2)}) copy-start(f32[1280]{0:T(1024)} %param.16) | copy-start | bytes 15364
  44.9 42.1 %collective-permute-start.11 = (bf16[4,80,1280]{2,1,0:T(8,128)(2,1)}, bf16[4,80,1280]{2,1,0:T(8,128)(2,1)}, u32[]{:S(2)}, u32[]{:S(2)}) collective-permute-start(bf16[4,80,1280]{2,1,0:T(8,128)(2,1)} %get-tuple-element.70), channel_id=1, source_target_pairs={{0,24},{8,0},{16,8},{24,16},{1,25},{9,1},{17,9},{25,17},{2,26},{10... | collective-permute-start | bytes 2457608 | tf_op jit(solution)/shard_map/ppermute | solution.py:36
  47.8 39.2 %collective-permute-start.10 = (bf16[4,80,1280]{2,1,0:T(8,128)(2,1)}, bf16[4,80,1280]{2,1,0:T(8,128)(2,1)}, u32[]{:S(2)}, u32[]{:S(2)}) collective-permute-start(bf16[4,80,1280]{2,1,0:T(8,128)(2,1)} %get-tuple-element.70), channel_id=1, source_target_pairs={{0,8},{8,16},{16,24},{24,0},{1,9},{9,17},{17,25},{25,1},{2,10},{10... | collective-permute-start | bytes 2457608 | tf_op jit(solution)/shard_map/ppermute | solution.py:36
  47.8 9.9 %collective-permute-start.3 = (bf16[240,512]{1,0:T(8,128)(2,1)S(1)}, bf16[240,512]{1,0:T(8,128)(2,1)S(1)}, u32[]{:S(2)}, u32[]{:S(2)}) collective-permute-start(bf16[240,512]{1,0:T(8,128)(2,1)S(1)} %get-tuple-element.55), channel_id=1, source_target_pairs={{0,96},{32,0},{64,32},{96,64},{1,97},{33,1},{65,33},{97,65},{2,98}... | collective-permute-start | bytes 737288 | tf_op jit(solution)/shard_map/ppermute | solution.py:36
  49.2 11.9 %collective-permute-start.4 = (bf16[240,512]{1,0:T(8,128)(2,1)S(1)}, bf16[240,512]{1,0:T(8,128)(2,1)S(1)}, u32[]{:S(2)}, u32[]{:S(2)}) collective-permute-start(bf16[240,512]{1,0:T(8,128)(2,1)S(1)} %get-tuple-element.56), channel_id=1, source_target_pairs={{0,64},{32,96},{64,0},{96,32},{1,65},{33,97},{65,1},{97,33},{2,66}... | collective-permute-start | bytes 737288 | tf_op jit(solution)/shard_map/ppermute | solution.py:36
  50.2 16.4 %collective-permute-start.5 = (bf16[240,512]{1,0:T(8,128)(2,1)S(1)}, bf16[240,512]{1,0:T(8,128)(2,1)S(1)}, u32[]{:S(2)}, u32[]{:S(2)}) collective-permute-start(bf16[240,512]{1,0:T(8,128)(2,1)S(1)} %get-tuple-element.57), channel_id=1, source_target_pairs={{0,32},{32,64},{64,96},{96,0},{1,33},{33,65},{65,97},{97,1},{2,34}... | collective-permute-start | bytes 737288 | tf_op jit(solution)/shard_map/ppermute | solution.py:36
  66.5 13.1 %collective-permute-start.8 = (bf16[4,80,640]{2,1,0:T(8,128)(2,1)S(1)}, bf16[4,80,640]{2,1,0:T(8,128)(2,1)}, u32[]{:S(2)}, u32[]{:S(2)}) collective-permute-start(bf16[4,80,640]{2,1,0:T(8,128)(2,1)S(1)} %get-tuple-element.68), channel_id=1, source_target_pairs={{0,16},{8,24},{16,0},{24,8},{1,17},{9,25},{17,1},{25,9},{2,18},{10... | collective-permute-start | bytes 1228808 | tf_op jit(solution)/shard_map/ppermute | solution.py:36
  74.6 9.4 %collective-permute-start.6 = (bf16[80,512]{1,0:T(8,128)(2,1)S(1)}, bf16[80,512]{1,0:T(8,128)(2,1)S(1)}, u32[]{:S(2)}, u32[]{:S(2)}) collective-permute-start(bf16[80,512]{1,0:T(8,128)(2,1)S(1)} %get-tuple-element.65), channel_id=1, source_target_pairs={{0,32},{32,64},{64,96},{96,0},{1,33},{33,65},{65,97},{97,1},{2,34}... | collective-permute-start | bytes 245768 | tf_op jit(solution)/shard_map/ppermute | solution.py:36
  74.7 10.3 %collective-permute-start.7 = (bf16[80,512]{1,0:T(8,128)(2,1)S(1)}, bf16[80,512]{1,0:T(8,128)(2,1)S(1)}, u32[]{:S(2)}, u32[]{:S(2)}) collective-permute-start(bf16[80,512]{1,0:T(8,128)(2,1)S(1)} %get-tuple-element.66), channel_id=1, source_target_pairs={{0,64},{32,96},{64,0},{96,32},{1,65},{33,97},{65,1},{97,33},{2,66}... | collective-permute-start | bytes 245768 | tf_op jit(solution)/shard_map/ppermute | solution.py:36
  79.6 7.3 %collective-permute-start.9 = (bf16[80,512]{1,0:T(8,128)(2,1)S(1)}, bf16[80,512]{1,0:T(8,128)(2,1)S(1)}, u32[]{:S(2)}, u32[]{:S(2)}) collective-permute-start(bf16[80,512]{1,0:T(8,128)(2,1)S(1)} %get-tuple-element.69), channel_id=1, source_target_pairs={{0,96},{32,0},{64,32},{96,64},{1,97},{33,1},{65,33},{97,65},{2,98}... | collective-permute-start | bytes 245768 | tf_op jit(solution)/shard_map/ppermute | solution.py:36
  84.0 18.7 %collective-permute-start.15 = (bf16[4,80,640]{2,1,0:T(8,128)(2,1)}, bf16[4,80,640]{2,1,0:T(8,128)(2,1)S(1)}, u32[]{:S(2)}, u32[]{:S(2)}) collective-permute-start(bf16[4,80,640]{2,1,0:T(8,128)(2,1)} %collective-permute-done.8.refs_8_), channel_id=1, source_target_pairs={{0,1},{1,0},{2,3},{3,2},{4,5},{5,4},{6,7},{7,6},{8,9},{9,8},{10,11... | collective-permute-start | bytes 1228808 | tf_op jit(solution)/shard_map/ppermute | solution.py:44
  87.6 20.9 %collective-permute-start.14 = (bf16[4,80,512]{2,1,0:T(8,128)(2,1)S(1)}, bf16[4,80,512]{2,1,0:T(8,128)(2,1)S(1)}, u32[]{:S(2)}, u32[]{:S(2)}) collective-permute-start(bf16[4,80,512]{2,1,0:T(8,128)(2,1)S(1)} %pack.1.refs_0_), channel_id=1, source_target_pairs={{0,24},{8,0},{16,8},{24,16},{1,25},{9,1},{17,9},{25,17},{2,26},{10... | collective-permute-start | bytes 983048 | tf_op jit(solution)/shard_map/ppermute | solution.py:36
  90.0 18.5 %collective-permute-start.13 = (bf16[4,80,512]{2,1,0:T(8,128)(2,1)S(1)}, bf16[4,80,512]{2,1,0:T(8,128)(2,1)S(1)}, u32[]{:S(2)}, u32[]{:S(2)}) collective-permute-start(bf16[4,80,512]{2,1,0:T(8,128)(2,1)S(1)} %pack.1.refs_0_), channel_id=1, source_target_pairs={{0,16},{8,24},{16,0},{24,8},{1,17},{9,25},{17,1},{25,9},{2,18},{10... | collective-permute-start | bytes 983048 | tf_op jit(solution)/shard_map/ppermute | solution.py:36
  91.5 17.0 %collective-permute-start.12 = (bf16[4,80,512]{2,1,0:T(8,128)(2,1)S(1)}, bf16[4,80,512]{2,1,0:T(8,128)(2,1)S(1)}, u32[]{:S(2)}, u32[]{:S(2)}) collective-permute-start(bf16[4,80,512]{2,1,0:T(8,128)(2,1)S(1)} %pack.1.refs_0_), channel_id=1, source_target_pairs={{0,8},{8,16},{16,24},{24,0},{1,9},{9,17},{17,25},{25,1},{2,10},{10... | collective-permute-start | bytes 983048 | tf_op jit(solution)/shard_map/ppermute | solution.py:36
  102.7 0.8 copy-start.5
  112.4 11.9 %collective-permute-start.16 = (bf16[128,1280]{1,0:T(8,128)(2,1)S(1)}, bf16[128,1280]{1,0:T(8,128)(2,1)S(1)}, u32[]{:S(2)}, u32[]{:S(2)}) collective-permute-start(bf16[128,1280]{1,0:T(8,128)(2,1)S(1)} %get-tuple-element.91), channel_id=1, source_target_pairs={{0,8},{8,16},{16,24},{24,0},{1,9},{9,17},{17,25},{25,1},{2,10},{10... | collective-permute-start | bytes 983048 | tf_op jit(solution)/shard_map/ppermute | solution.py:36
  114.1 16.4 %collective-permute-start.17 = (bf16[128,1280]{1,0:T(8,128)(2,1)S(1)}, bf16[128,1280]{1,0:T(8,128)(2,1)S(1)}, u32[]{:S(2)}, u32[]{:S(2)}) collective-permute-start(bf16[128,1280]{1,0:T(8,128)(2,1)S(1)} %get-tuple-element.92), channel_id=1, source_target_pairs={{0,16},{8,24},{16,0},{24,8},{1,17},{9,25},{17,1},{25,9},{2,18},{10... | collective-permute-start | bytes 983048 | tf_op jit(solution)/shard_map/ppermute | solution.py:36
  119.5 11.6 %collective-permute-start.18 = (bf16[128,1280]{1,0:T(8,128)(2,1)S(1)}, bf16[128,1280]{1,0:T(8,128)(2,1)S(1)}, u32[]{:S(2)}, u32[]{:S(2)}) collective-permute-start(bf16[128,1280]{1,0:T(8,128)(2,1)S(1)} %get-tuple-element.93), channel_id=1, source_target_pairs={{0,24},{8,0},{16,8},{24,16},{1,25},{9,1},{17,9},{25,17},{2,26},{10... | collective-permute-start | bytes 983048 | tf_op jit(solution)/shard_map/ppermute | solution.py:36
  130.7 15.7 %copy-start.6 = (bf16[128,1280]{1,0:T(8,128)(2,1)S(1)}, bf16[128,1280]{1,0:T(8,128)(2,1)}, u32[]{:S(2)}) copy-start(bf16[128,1280]{1,0:T(8,128)(2,1)} %param.20) | copy-start | bytes 983044
Sparse Core Ops, SparseCore 0:
  9.0 30.7 all-gather.4
  42.1 55.6 all-gather.6
